TPU v7x, 32 devices: a whole 2x2x4 slice. The times are simulated.
32 devices in a mesh: batch: 8 (over y, x, core), rows: 4 (over z).
Axes of the slice: x: 2, y: 2, z: 4, core: 2. Of those that a mesh axis runs over, the one named last changes fastest.
Arguments:
- atoms: bfloat16 [32, 256, 512], P('batch', 'rows'), may hold values from -6 to 6
- pair_bias: bfloat16 [32, 64, 256, 256], P('batch', None, 'rows'), may hold values from -6 to 6
- lengths: int32 [32], P('batch'), may hold values from 64 to 256, as said below
- first_gain: bfloat16 [512], replicated, may hold values from 0.099609375 to 1.8984375
- first_shift: bfloat16 [512], replicated, may hold values from -3 to 3
- query_weight: bfloat16 [512, 512], replicated, may hold values from -0.25 to 0.25
- query_bias: bfloat16 [512], replicated, may hold values from -3 to 3
- key_weight: bfloat16 [512, 512], replicated, may hold values from -0.25 to 0.25
- value_weight: bfloat16 [512, 512], replicated, may hold values from -0.25 to 0.25
- value_bias: bfloat16 [512], replicated, may hold values from -3 to 3
- out_weight: bfloat16 [512, 512], replicated, may hold values from -1 to 1
- out_bias: bfloat16 [512], replicated, may hold values from -3 to 3
- second_gain: bfloat16 [512], replicated, may hold values from 0.099609375 to 1.8984375
- second_shift: bfloat16 [512], replicated, may hold values from -3 to 3
- inner_weight: bfloat16 [512, 2048], replicated, may hold values from -0.25 to 0.25
- inner_bias: bfloat16 [2048], replicated, may hold values from -3 to 3
- outer_weight: bfloat16 [2048, 512], replicated, may hold values from -0.125 to 0.125
- outer_bias: bfloat16 [512], replicated, may hold values from -3 to 3
- atoms_cotangent: bfloat16 [32, 256, 512], P('batch', 'rows'), may hold values from -6 to 6
- pair_cotangent: bfloat16 [32, 64, 256, 256], P('batch', None, 'rows'), may hold values from -6 to 6
Outputs:
- atoms_out: bfloat16 [32, 256, 512], P('batch', 'rows')
- pair_out: bfloat16 [32, 64, 256, 256], P('batch', None, 'rows')
- atoms_grad: bfloat16 [32, 256, 512], P('batch', 'rows')
- pair_grad: bfloat16 [32, 64, 256, 256], P('batch', None, 'rows')
- first_gain_grad: float32 [512], P('batch')
- first_shift_grad: float32 [512], P('batch')
- query_weight_grad: float32 [512, 512], P('batch')
- query_bias_grad: float32 [512], P('batch')
- key_weight_grad: float32 [512, 512], P('batch')
- value_weight_grad: float32 [512, 512], P('batch')
- value_bias_grad: float32 [512], P('batch')
- out_weight_grad: float32 [512, 512], P('batch')
- out_bias_grad: float32 [512], P('batch')
- second_gain_grad: float32 [512], P('batch')
- second_shift_grad: float32 [512], P('batch')
- inner_weight_grad: float32 [512, 2048], P('batch')
- inner_bias_grad: float32 [2048], P('batch')
- outer_weight_grad: float32 [2048, 512], P('batch')
- outer_bias_grad: float32 [512], P('batch')
Inputs may be any that keep to these rules, and one draw needn't show every extreme that they name: Atoms at positions lengths[m] and beyond are padding and are masked as keys; of the 4 molecules at each index of batch, one (drawn from the seed) has exactly 256 atoms.
All inputs are finite; a program needn't handle non-finite values.
Results may differ from a plain program's by a relative error of at most 0.012.
Values may be sent and summed in bfloat16 or wider, within the bound.
No kernel may reach another device: no remote copies, remote signals or barrier semaphores. Data moves between devices by JAX's collectives and lax.ppermute only.
A program may use at most 128 MiB of HBM per device.

v0:
```python
from functools import partial

import jax
import jax.numpy as jnp
from jax import lax
from jax.sharding import PartitionSpec as P

EPSILON = 1e-05
MASKED = -1000000000.0


def norm_forward(values_in, gain, shift):
    centre = values_in - jnp.mean(values_in, -1, keepdims=True)
    inverse = lax.rsqrt(jnp.mean(centre * centre, -1, keepdims=True) + EPSILON)
    normed = centre * inverse
    return (normed * gain + shift, normed, inverse)


def norm_backward(upstream, normed, inverse, gain):
    scaled = upstream * gain
    result = inverse * (
        scaled
        - jnp.mean(scaled, -1, keepdims=True)
        - normed * jnp.mean(scaled * normed, -1, keepdims=True)
    )
    return (result, jnp.sum(upstream * normed, 0), jnp.sum(upstream, 0))


def across(left, right):
    return lax.dot_general(
        left, right, (((0,), (0,)), ((), ())), preferred_element_type=jnp.float32
    )


def against(left, right):
    return lax.dot_general(
        left, right, (((1,), (1,)), ((), ())), preferred_element_type=jnp.float32
    )


def column_sum(values_in):
    return jnp.sum(values_in.astype(jnp.float32), 0)


def project_keys(hidden_rows, key_weight, value_weight, value_bias):
    key_rows = jnp.dot(hidden_rows, key_weight, preferred_element_type=jnp.float32).astype(
        jnp.bfloat16
    )
    value_rows = (
        jnp.dot(hidden_rows, value_weight, preferred_element_type=jnp.float32)
        + value_bias.astype(jnp.float32)
    ).astype(jnp.bfloat16)
    return (key_rows, value_rows)


def scores_of(factor, query_rows, key_rows, pair_rows, length):
    scores = factor * jnp.einsum(
        "ihe,jhe->hij", query_rows, key_rows, preferred_element_type=jnp.float32
    )
    scores = scores + pair_rows.astype(jnp.float32)
    valid = lax.broadcasted_iota(jnp.int32, scores.shape, 2) < length
    return (scores, valid)


def attend_forward(factor, pieces):
    query_rows, key_rows, value_rows, pair_rows, length = pieces
    scores, valid = scores_of(factor, query_rows, key_rows, pair_rows, length)
    masked = jnp.where(valid, scores, MASKED)
    highest = jnp.max(masked, -1, keepdims=True)
    weights = jnp.exp(masked - highest)
    totals = jnp.sum(weights, -1, keepdims=True)
    low_probs = (weights / totals).astype(jnp.bfloat16)
    mixed_rows = jnp.einsum(
        "hij,jhe->ihe", low_probs, value_rows, preferred_element_type=jnp.float32
    )
    return (
        scores.astype(jnp.bfloat16),
        mixed_rows.astype(jnp.bfloat16),
        (highest + jnp.log(totals))[..., 0],
    )


def attend_backward(factor, pieces):
    query_rows, key_rows, value_rows, pair_rows, length, log_totals, mixed_grad, pair_cot = pieces
    scores, valid = scores_of(factor, query_rows, key_rows, pair_rows, length)
    probs = jnp.exp(jnp.where(valid, scores, MASKED) - log_totals[..., None])
    low_probs = probs.astype(jnp.bfloat16)
    probs_grad = jnp.einsum(
        "ihe,jhe->hij", mixed_grad, value_rows, preferred_element_type=jnp.float32
    )
    value_grad = jnp.einsum(
        "hij,ihe->jhe", low_probs, mixed_grad, preferred_element_type=jnp.float32
    )
    inner_sum = jnp.sum(probs * probs_grad, -1, keepdims=True)
    score_grad = (probs * (probs_grad - inner_sum) + pair_cot.astype(jnp.float32)).astype(
        jnp.bfloat16
    )
    query_grad = factor * jnp.einsum(
        "hij,jhe->ihe", score_grad, key_rows, preferred_element_type=jnp.float32
    )
    key_grad = factor * jnp.einsum(
        "hij,ihe->jhe", score_grad, query_rows, preferred_element_type=jnp.float32
    )
    return (score_grad, query_grad.astype(jnp.bfloat16), key_grad, value_grad)


def shards(
    atoms,
    pair_bias,
    lengths,
    first_gain,
    first_shift,
    query_weight,
    query_bias,
    key_weight,
    value_weight,
    value_bias,
    out_weight,
    out_bias,
    second_gain,
    second_shift,
    inner_weight,
    inner_bias,
    outer_weight,
    outer_bias,
    atoms_cotangent,
    pair_cotangent,
):
    floats = jnp.float32
    halves = jnp.bfloat16
    molecules, atom_rows, model_width = atoms.shape
    head_count = pair_bias.shape[1]
    head_size = model_width // head_count
    factor = head_size ** (-0.5)
    tokens = molecules * atom_rows
    atoms_float = atoms.astype(floats).reshape(tokens, model_width)
    first_out, first_normed, first_inverse = norm_forward(
        atoms_float, first_gain.astype(floats), first_shift.astype(floats)
    )
    first_low = first_out.astype(halves)
    query_low = (
        jnp.dot(first_low, query_weight, preferred_element_type=floats) + query_bias.astype(floats)
    ).astype(halves)
    first_grouped = first_low.reshape(molecules, atom_rows, model_width)
    key_local, value_local = project_keys(first_grouped, key_weight, value_weight, value_bias)
    all_keys, all_values = (
        lax.all_gather(key_local, "rows", axis=1, tiled=True),
        lax.all_gather(value_local, "rows", axis=1, tiled=True),
    )
    key_count = all_keys.shape[1]
    query_heads = query_low.reshape(molecules, atom_rows, head_count, head_size)
    key_heads = all_keys.reshape(molecules, key_count, head_count, head_size)
    value_heads = all_values.reshape(molecules, key_count, head_count, head_size)
    pair_out, mixed_heads, log_totals = lax.map(
        partial(attend_forward, factor), (query_heads, key_heads, value_heads, pair_bias, lengths)
    )
    mixed_low = mixed_heads.reshape(tokens, model_width)
    middle = (
        atoms_float
        + jnp.dot(mixed_low, out_weight, preferred_element_type=floats)
        + out_bias.astype(floats)
    )
    second_out, second_normed, second_inverse = norm_forward(
        middle, second_gain.astype(floats), second_shift.astype(floats)
    )
    second_low = second_out.astype(halves)
    inner_pre = jnp.dot(
        second_low, inner_weight, preferred_element_type=floats
    ) + inner_bias.astype(floats)
    activated, gelu_pull = jax.vjp(jax.nn.gelu, inner_pre)
    activated_low = activated.astype(halves)
    result_rows = (
        middle
        + jnp.dot(activated_low, outer_weight, preferred_element_type=floats)
        + outer_bias.astype(floats)
    )
    atoms_out = result_rows.astype(halves).reshape(molecules, atom_rows, model_width)
    grad_outer = atoms_cotangent.reshape(tokens, model_width)
    outer_weight_grad = across(activated_low, grad_outer)
    outer_bias_grad = column_sum(grad_outer)
    grad_activated = against(grad_outer, outer_weight)
    grad_inner = gelu_pull(grad_activated)[0].astype(halves)
    inner_weight_grad = across(second_low, grad_inner)
    inner_bias_grad = column_sum(grad_inner)
    grad_second = against(grad_inner, inner_weight)
    second_back, second_gain_grad, second_shift_grad = norm_backward(
        grad_second, second_normed, second_inverse, second_gain.astype(floats)
    )
    grad_middle = grad_outer.astype(floats) + second_back
    grad_branch = grad_middle.astype(halves)
    out_weight_grad = across(mixed_low, grad_branch)
    out_bias_grad = column_sum(grad_branch)
    grad_mixed = against(grad_branch, out_weight).astype(halves)
    pair_grad, query_grad, key_grad, value_grad = lax.map(
        partial(attend_backward, factor),
        (
            query_heads,
            key_heads,
            value_heads,
            pair_bias,
            lengths,
            log_totals,
            grad_mixed.reshape(molecules, atom_rows, head_count, head_size),
            pair_cotangent,
        ),
    )
    key_share, value_share = (
        lax.psum_scatter(
            key_grad.reshape(molecules, key_count, model_width),
            "rows",
            scatter_dimension=1,
            tiled=True,
        ),
        lax.psum_scatter(
            value_grad.reshape(molecules, key_count, model_width),
            "rows",
            scatter_dimension=1,
            tiled=True,
        ),
    )
    key_grad_low = key_share.reshape(tokens, model_width).astype(halves)
    value_grad_low = value_share.reshape(tokens, model_width).astype(halves)
    query_grad_low = query_grad.reshape(tokens, model_width)
    query_weight_grad = across(first_low, query_grad_low)
    query_bias_grad = column_sum(query_grad_low)
    key_weight_grad = across(first_low, key_grad_low)
    value_weight_grad = across(first_low, value_grad_low)
    value_bias_grad = column_sum(value_grad_low)
    grad_first = (
        against(query_grad_low, query_weight)
        + against(key_grad_low, key_weight)
        + against(value_grad_low, value_weight)
    )
    first_back, first_gain_grad, first_shift_grad = norm_backward(
        grad_first, first_normed, first_inverse, first_gain.astype(floats)
    )
    atoms_grad = (
        (grad_middle + first_back).astype(halves).reshape(molecules, atom_rows, model_width)
    )
    (
        first_gain_grad,
        first_shift_grad,
        query_weight_grad,
        query_bias_grad,
        key_weight_grad,
        value_weight_grad,
        value_bias_grad,
        out_weight_grad,
        out_bias_grad,
        second_gain_grad,
        second_shift_grad,
        inner_weight_grad,
        inner_bias_grad,
        outer_weight_grad,
        outer_bias_grad,
    ) = (
        lax.psum_scatter(first_gain_grad, "batch", scatter_dimension=0, tiled=True),
        lax.psum_scatter(first_shift_grad, "batch", scatter_dimension=0, tiled=True),
        lax.psum_scatter(query_weight_grad, "batch", scatter_dimension=0, tiled=True),
        lax.psum_scatter(query_bias_grad, "batch", scatter_dimension=0, tiled=True),
        lax.psum_scatter(key_weight_grad, "batch", scatter_dimension=0, tiled=True),
        lax.psum_scatter(value_weight_grad, "batch", scatter_dimension=0, tiled=True),
        lax.psum_scatter(value_bias_grad, "batch", scatter_dimension=0, tiled=True),
        lax.psum_scatter(out_weight_grad, "batch", scatter_dimension=0, tiled=True),
        lax.psum_scatter(out_bias_grad, "batch", scatter_dimension=0, tiled=True),
        lax.psum_scatter(second_gain_grad, "batch", scatter_dimension=0, tiled=True),
        lax.psum_scatter(second_shift_grad, "batch", scatter_dimension=0, tiled=True),
        lax.psum_scatter(inner_weight_grad, "batch", scatter_dimension=0, tiled=True),
        lax.psum_scatter(inner_bias_grad, "batch", scatter_dimension=0, tiled=True),
        lax.psum_scatter(outer_weight_grad, "batch", scatter_dimension=0, tiled=True),
        lax.psum_scatter(outer_bias_grad, "batch", scatter_dimension=0, tiled=True),
    )
    (
        first_gain_grad,
        first_shift_grad,
        query_weight_grad,
        query_bias_grad,
        key_weight_grad,
        value_weight_grad,
        value_bias_grad,
        out_weight_grad,
        out_bias_grad,
        second_gain_grad,
        second_shift_grad,
        inner_weight_grad,
        inner_bias_grad,
        outer_weight_grad,
        outer_bias_grad,
    ) = (
        lax.psum(first_gain_grad.astype(jnp.bfloat16), "rows").astype(jnp.float32),
        lax.psum(first_shift_grad.astype(jnp.bfloat16), "rows").astype(jnp.float32),
        lax.psum(query_weight_grad.astype(jnp.bfloat16), "rows").astype(jnp.float32),
        lax.psum(query_bias_grad.astype(jnp.bfloat16), "rows").astype(jnp.float32),
        lax.psum(key_weight_grad.astype(jnp.bfloat16), "rows").astype(jnp.float32),
        lax.psum(value_weight_grad.astype(jnp.bfloat16), "rows").astype(jnp.float32),
        lax.psum(value_bias_grad.astype(jnp.bfloat16), "rows").astype(jnp.float32),
        lax.psum(out_weight_grad.astype(jnp.bfloat16), "rows").astype(jnp.float32),
        lax.psum(out_bias_grad.astype(jnp.bfloat16), "rows").astype(jnp.float32),
        lax.psum(second_gain_grad.astype(jnp.bfloat16), "rows").astype(jnp.float32),
        lax.psum(second_shift_grad.astype(jnp.bfloat16), "rows").astype(jnp.float32),
        lax.psum(inner_weight_grad.astype(jnp.bfloat16), "rows").astype(jnp.float32),
        lax.psum(inner_bias_grad.astype(jnp.bfloat16), "rows").astype(jnp.float32),
        lax.psum(outer_weight_grad.astype(jnp.bfloat16), "rows").astype(jnp.float32),
        lax.psum(outer_bias_grad.astype(jnp.bfloat16), "rows").astype(jnp.float32),
    )
    return (
        atoms_out,
        pair_out,
        atoms_grad,
        pair_grad,
        first_gain_grad,
        first_shift_grad,
        query_weight_grad,
        query_bias_grad,
        key_weight_grad,
        value_weight_grad,
        value_bias_grad,
        out_weight_grad,
        out_bias_grad,
        second_gain_grad,
        second_shift_grad,
        inner_weight_grad,
        inner_bias_grad,
        outer_weight_grad,
        outer_bias_grad,
    )


def solution(mesh):
    placed = (
        P("batch", "rows", None),
        P("batch", None, "rows", None),
        P("batch"),
        P(),
        P(),
        P(),
        P(),
        P(),
        P(),
        P(),
        P(),
        P(),
        P(),
        P(),
        P(),
        P(),
        P(),
        P(),
        P("batch", "rows", None),
        P("batch", None, "rows", None),
    )
    return jax.shard_map(
        shards,
        mesh=mesh,
        in_specs=placed,
        out_specs=(
            P("batch", "rows", None),
            P("batch", None, "rows", None),
            P("batch", "rows", None),
            P("batch", None, "rows", None),
            P("batch"),
            P("batch"),
            P("batch", None),
            P("batch"),
            P("batch", None),
            P("batch", None),
            P("batch"),
            P("batch", None),
            P("batch"),
            P("batch"),
            P("batch"),
            P("batch", None),
            P("batch"),
            P("batch", None),
            P("batch"),
        ),
        check_vma=False,
    )
```

profile of v0, /device:TPU:0, one launch (start us, length us, event | category | flops | bytes accessed | tf_op | source)
XLA Modules:
  0.0 693.5 jit_solution(6744688574644620447)
XLA Ops:
  25.2 20.6 %all-gather.5.cloned.1.call-done = bf16[4,256,512]{2,1,0:T(8,128)(2,1)} async-done(((bf16[4,64,512]{2,1,0:T(8,128)(2,1)}), bf16[4,256,512]{2,1,0:T(8,128)(2,1)}) %all-gather.5.cloned.1.call-update) | async-done | bytes 1048592 | tf_op jit(solution)/shard_map/all_gather | solution.py:148
  48.2 27.3 %all-gather.3.cloned.1.call-done = bf16[4,256,512]{2,1,0:T(8,128)(2,1)} async-done(((bf16[4,64,512]{2,1,0:T(8,128)(2,1)}), bf16[4,256,512]{2,1,0:T(8,128)(2,1)}) %all-gather.3.cloned.1.call-update) | async-done | bytes 1048592 | tf_op jit(solution)/shard_map/all_gather | solution.py:147
  77.8 4.5 broadcast.188.clone
  82.3 43.1 %while.30 = (s32[]{:T(128)}, bf16[4,64,64,256]{3,2,1,0:T(8,128)(2,1)}, bf16[4,64,64,8]{1,3,2,0:T(8,128)(2,1)}, f32[4,64,64]{2,1,0:T(8,128)S(1)}, bf16[4,64,64,8]...) while((s32[]{:T(128)}, ...), condition=%wide.region_5.6_spmd, body=%wide.region_2.5_spmd.sunk | while | flops 47214848 | bytes 21941888 | solution.py:154
  132.1 4.8 convert_reduce_fusion
  145.5 124.5 %while.31 = (s32[]{:T(128)}, bf16[4,64,64,256]{3,2,1,0:T(8,128)(2,1)}, bf16[4,64,64,8]{1,3,2,0:T(8,128)(2,1)}, f32[4,256,64,8]{1,3,2,0:T(8,128)}, f32[4,256,64,8...) while((s32[]{:T(128)}, ...), condition=%wide.region_12.13_spmd, body=%wide.region_10.12_spmd.sunk | while | flops 193147904 | bytes 48575392 | solution.py:194
  147.4 5.2 fusion.229
  152.5 6.8 fusion.230
  162.7 7.0 %fusion.231 = f32[4,256,64,8]{1,3,2,0:T(8,128)} fusion(f32[4,256,64,8]{1,3,2,0:T(8,128)} %get-tuple-element.487, s32[]{:T(128)S(6)} %copy.94, f32[64,64,256]{2,1,0:T(8,128)} %fusion.229, bf16[4,64,64,256]{3,2,1,0:T(8,128)(2,1)} %get-tuple-element.510, bf16[4,256,64,8]{1,3,2,0:T(8,128)(2,1)S(1)} %get-tuple-element.509, ...), kind=kOutput, calls=%fused_computation.37.clone.1 | convolution fusion | flops 56758528 | bytes 11931136 | tf_op jit(solution)/shard_map/while/body/eval_jaxpr/hij,ihe->jhe/dot_general | solution.py:101
  169.6 6.9 %bitcast_dynamic-update-slice_fusion.8 = bf16[4,64,64,256]{3,2,1,0:T(8,128)(2,1)} fusion(bf16[4,64,64,256]{3,2,1,0:T(8,128)(2,1)} %get-tuple-element.485, s32[]{:T(128)S(6)} %copy.94, bf16[4,64,64,256]{3,2,1,0:T(8,128)(2,1)} %get-tuple-element.510, f32[64,64,256]{2,1,0:T(8,128)} %fusion.229, bf16[4,256,64,8]{1,3,2,0:T(8,128)(2,1)S(1)} %get-tuple-element.509, ...), kind=kOutput, calls=%fused_computation.30.clone.1 | convolution fusion | flops 39850240 | bytes 13371904 | tf_op jit(solution)/shard_map/while/body/eval_jaxpr/sub | solution.py:95
  178.5 5.1 fusion.229
  183.6 6.8 fusion.230
  193.8 7.0 %fusion.231 = f32[4,256,64,8]{1,3,2,0:T(8,128)} fusion(f32[4,256,64,8]{1,3,2,0:T(8,128)} %get-tuple-element.487, s32[]{:T(128)S(6)} %copy.94, f32[64,64,256]{2,1,0:T(8,128)} %fusion.229, bf16[4,64,64,256]{3,2,1,0:T(8,128)(2,1)} %get-tuple-element.510, bf16[4,256,64,8]{1,3,2,0:T(8,128)(2,1)S(1)} %get-tuple-element.509, ...), kind=kOutput, calls=%fused_computation.37.clone.1 | convolution fusion | flops 56758528 | bytes 11931136 | tf_op jit(solution)/shard_map/while/body/eval_jaxpr/hij,ihe->jhe/dot_general | solution.py:101
  200.8 6.9 %bitcast_dynamic-update-slice_fusion.8 = bf16[4,64,64,256]{3,2,1,0:T(8,128)(2,1)} fusion(bf16[4,64,64,256]{3,2,1,0:T(8,128)(2,1)} %get-tuple-element.485, s32[]{:T(128)S(6)} %copy.94, bf16[4,64,64,256]{3,2,1,0:T(8,128)(2,1)} %get-tuple-element.510, f32[64,64,256]{2,1,0:T(8,128)} %fusion.229, bf16[4,256,64,8]{1,3,2,0:T(8,128)(2,1)S(1)} %get-tuple-element.509, ...), kind=kOutput, calls=%fused_computation.30.clone.1 | convolution fusion | flops 39850240 | bytes 13371904 | tf_op jit(solution)/shard_map/while/body/eval_jaxpr/sub | solution.py:95
  209.6 5.2 fusion.229
  214.8 6.8 fusion.230
  224.9 7.0 %fusion.231 = f32[4,256,64,8]{1,3,2,0:T(8,128)} fusion(f32[4,256,64,8]{1,3,2,0:T(8,128)} %get-tuple-element.487, s32[]{:T(128)S(6)} %copy.94, f32[64,64,256]{2,1,0:T(8,128)} %fusion.229, bf16[4,64,64,256]{3,2,1,0:T(8,128)(2,1)} %get-tuple-element.510, bf16[4,256,64,8]{1,3,2,0:T(8,128)(2,1)S(1)} %get-tuple-element.509, ...), kind=kOutput, calls=%fused_computation.37.clone.1 | convolution fusion | flops 56758528 | bytes 11931136 | tf_op jit(solution)/shard_map/while/body/eval_jaxpr/hij,ihe->jhe/dot_general | solution.py:101
  231.9 6.9 %bitcast_dynamic-update-slice_fusion.8 = bf16[4,64,64,256]{3,2,1,0:T(8,128)(2,1)} fusion(bf16[4,64,64,256]{3,2,1,0:T(8,128)(2,1)} %get-tuple-element.485, s32[]{:T(128)S(6)} %copy.94, bf16[4,64,64,256]{3,2,1,0:T(8,128)(2,1)} %get-tuple-element.510, f32[64,64,256]{2,1,0:T(8,128)} %fusion.229, bf16[4,256,64,8]{1,3,2,0:T(8,128)(2,1)S(1)} %get-tuple-element.509, ...), kind=kOutput, calls=%fused_computation.30.clone.1 | convolution fusion | flops 39850240 | bytes 13371904 | tf_op jit(solution)/shard_map/while/body/eval_jaxpr/sub | solution.py:95
  240.7 5.2 fusion.229
  245.9 6.8 fusion.230
  256.1 7.0 %fusion.231 = f32[4,256,64,8]{1,3,2,0:T(8,128)} fusion(f32[4,256,64,8]{1,3,2,0:T(8,128)} %get-tuple-element.487, s32[]{:T(128)S(6)} %copy.94, f32[64,64,256]{2,1,0:T(8,128)} %fusion.229, bf16[4,64,64,256]{3,2,1,0:T(8,128)(2,1)} %get-tuple-element.510, bf16[4,256,64,8]{1,3,2,0:T(8,128)(2,1)S(1)} %get-tuple-element.509, ...), kind=kOutput, calls=%fused_computation.37.clone.1 | convolution fusion | flops 56758528 | bytes 11931136 | tf_op jit(solution)/shard_map/while/body/eval_jaxpr/hij,ihe->jhe/dot_general | solution.py:101
  263.0 6.9 %bitcast_dynamic-update-slice_fusion.8 = bf16[4,64,64,256]{3,2,1,0:T(8,128)(2,1)} fusion(bf16[4,64,64,256]{3,2,1,0:T(8,128)(2,1)} %get-tuple-element.485, s32[]{:T(128)S(6)} %copy.94, bf16[4,64,64,256]{3,2,1,0:T(8,128)(2,1)} %get-tuple-element.510, f32[64,64,256]{2,1,0:T(8,128)} %fusion.229, bf16[4,256,64,8]{1,3,2,0:T(8,128)(2,1)S(1)} %get-tuple-element.509, ...), kind=kOutput, calls=%fused_computation.30.clone.1 | convolution fusion | flops 39850240 | bytes 13371904 | tf_op jit(solution)/shard_map/while/body/eval_jaxpr/sub | solution.py:95
  280.7 35.7 %reduce-scatter.11.cloned.1.call-done = f32[4,64,512]{2,1,0:T(8,128)} async-done(((f32[4,256,512]{2,1,0:T(8,128)}), f32[4,64,512]{2,1,0:T(8,128)}) %reduce-scatter.11.cloned.1.call-update) | async-done | bytes 524304 | tf_op jit(solution)/shard_map/reduce_scatter | solution.py:214
  319.0 43.0 %reduce-scatter.9.cloned.1.call-done = f32[4,64,512]{2,1,0:T(8,128)} async-done(((f32[4,256,512]{2,1,0:T(8,128)}), f32[4,64,512]{2,1,0:T(8,128)}) %reduce-scatter.9.cloned.1.call-update) | async-done | bytes 524304 | tf_op jit(solution)/shard_map/reduce_scatter | solution.py:208
  379.3 20.9 %reduce-scatter.19.cloned.1.call-done = f32[64,512]{1,0:T(8,128)} async-done(((f32[512,512]{1,0:T(8,128)}), f32[64,512]{1,0:T(8,128)}) %reduce-scatter.19.cloned.1.call-update) | async-done | bytes 131088 | tf_op jit(solution)/shard_map/reduce_scatter | solution.py:264
  401.8 37.5 %reduce-scatter.13.cloned.1.call-done = f32[64,512]{1,0:T(8,128)} async-done(((f32[512,512]{1,0:T(8,128)}), f32[64,512]{1,0:T(8,128)}) %reduce-scatter.13.cloned.1.call-update) | async-done | bytes 131088 | tf_op jit(solution)/shard_map/reduce_scatter | solution.py:259
  442.1 36.5 %reduce-scatter.17.cloned.1.call-done = f32[64,512]{1,0:T(8,128)} async-done(((f32[512,512]{1,0:T(8,128)}), f32[64,512]{1,0:T(8,128)}) %reduce-scatter.17.cloned.1.call-update) | async-done | bytes 131088 | tf_op jit(solution)/shard_map/reduce_scatter | solution.py:262
  480.1 37.7 %reduce-scatter.15.cloned.1.call-done = f32[64,512]{1,0:T(8,128)} async-done(((f32[512,512]{1,0:T(8,128)}), f32[64,512]{1,0:T(8,128)}) %reduce-scatter.15.cloned.1.call-update) | async-done | bytes 131088 | tf_op jit(solution)/shard_map/reduce_scatter | solution.py:261
  519.3 53.2 %reduce-scatter.23.cloned.1.call-done = f32[256,512]{1,0:T(8,128)} async-done(((f32[2048,512]{1,0:T(8,128)}), f32[256,512]{1,0:T(8,128)}) %reduce-scatter.23.cloned.1.call-update) | async-done | bytes 524304 | tf_op jit(solution)/shard_map/reduce_scatter | solution.py:270
  574.3 53.1 %reduce-scatter.21.cloned.1.call-done = f32[64,2048]{1,0:T(8,128)} async-done(((f32[512,2048]{1,0:T(8,128)}), f32[64,2048]{1,0:T(8,128)}) %reduce-scatter.21.cloned.1.call-update) | async-done | bytes 524304 | tf_op jit(solution)/shard_map/reduce_scatter | solution.py:268
  631.8 24.1 %all-reduce.9 = (bf16[512]{0:T(512)(128)(2,1)S(1)}, bf16[512]{0:T(512)(128)(2,1)S(1)}, bf16[512]{0:T(512)(128)(2,1)S(1)}, bf16[512]{0:T(512)(128)(2,1)S(1)}, bf1...) all-reduce(f32[512]{0:T(512)S(1)} %get-tuple-element.213, ...), channel_id=4, replica_groups=mesh['batch'=8,'rows'=4] {'batch'}, use_global_device_ids=true, to_apply=%region_18.19.clone | all-reduce | flops 6144 | bytes 36864
  656.6 12.1 %all-reduce.10 = (bf16[64]{0:T(256)(128)(2,1)S(1)}, bf16[64]{0:T(256)(128)(2,1)S(1)}, bf16[64]{0:T(256)(128)(2,1)S(1)}, bf16[64]{0:T(256)(128)(2,1)S(1)}, bf16[6...) all-reduce(bf16[64]{0:T(256)(128)(2,1)S(1)} %dynamic-slice.35, ...), channel_id=1, replica_groups=mesh['batch'=8,'rows'=4] {'rows'}, use_global_device_ids=true, to_apply=%region_19.20 | all-reduce | flops 768 | bytes 3072 | tf_op jit(solution)/shard_map/psum | solution.py:290
  (257 shorter events, 163.2 us)
Async XLA Ops:
  7.2 124.8 %copy-start = (bf16[512,2048]{1,0:T(8,128)(2,1)S(1)}, bf16[512,2048]{1,0:T(8,128)(2,1)}, u32[]{:S(2)}) copy-start(bf16[512,2048]{1,0:T(8,128)(2,1)} %param.38) | copy-start | bytes 6291460
  7.2 9.9 %copy-start.5 = (bf16[4,64,512]{2,1,0:T(8,128)(2,1)S(1)}, bf16[4,64,512]{2,1,0:T(8,128)(2,1)}, u32[]{:S(2)}) copy-start(bf16[4,64,512]{2,1,0:T(8,128)(2,1)} %param.24) | copy-start | bytes 786436
  7.2 9.2 %copy-start.41 = (bf16[512]{0:T(512)(128)(2,1)S(1)}, bf16[512]{0:T(512)(128)(2,1)}, u32[]{:S(2)}) copy-start(bf16[512]{0:T(512)(128)(2,1)} %param.37) | copy-start | bytes 3076
  7.3 9.2 %copy-start.42 = (bf16[512]{0:T(512)(128)(2,1)S(1)}, bf16[512]{0:T(512)(128)(2,1)}, u32[]{:S(2)}) copy-start(bf16[512]{0:T(512)(128)(2,1)} %param.30) | copy-start | bytes 3076
  7.3 9.2 %copy-start.43 = (bf16[512]{0:T(512)(128)(2,1)S(1)}, bf16[512]{0:T(512)(128)(2,1)}, u32[]{:S(2)}) copy-start(bf16[512]{0:T(512)(128)(2,1)} %param.35) | copy-start | bytes 3076
  7.3 9.2 %copy-start.37 = (bf16[2048]{0:T(1024)(128)(2,1)S(1)}, bf16[2048]{0:T(1024)(128)(2,1)}, u32[]{:S(2)}) copy-start(bf16[2048]{0:T(1024)(128)(2,1)} %param.39) | copy-start | bytes 12292
  7.3 38.6 %all-gather.5.cloned.1.call-start = ((), (), s32[]{:S(2)}) async-start(), calls=%async_computation.9 | async-start | bytes 1310720 | tf_op jit(solution)/shard_map/all_gather | solution.py:148
  15.1 60.4 %all-gather.3.cloned.1.call-start = ((), (), s32[]{:S(2)}) async-start(), calls=%async_computation.8 | async-start | bytes 1310720 | tf_op jit(solution)/shard_map/all_gather | solution.py:147
  16.2 300.3 %reduce-scatter.11.cloned.1.call-start = ((), (), s32[]{:S(2)}) async-start(), calls=%async_computation.11 | async-start | bytes 2621440 | tf_op jit(solution)/shard_map/reduce_scatter | solution.py:214
  139.1 136.9 %copy-start.8 = (f32[256,512]{1,0:T(8,128)}, f32[256,512]{1,0:T(8,128)S(1)}, u32[]{:S(2)}) copy-start(f32[256,512]{1,0:T(8,128)S(1)} %get-tuple-element.290) | copy-start | bytes 1572868
  272.9 89.0 %reduce-scatter.9.cloned.1.call-start = ((), (), s32[]{:S(2)}) async-start(), calls=%async_computation.10 | async-start | bytes 2621440 | tf_op jit(solution)/shard_map/reduce_scatter | solution.py:208
  275.9 124.3 %reduce-scatter.19.cloned.1.call-start = ((), (), s32[]{:S(2)}) async-start(), calls=%async_computation.15 | async-start | bytes 1179648 | tf_op jit(solution)/shard_map/reduce_scatter | solution.py:264
  278.2 161.2 %reduce-scatter.13.cloned.1.call-start = ((), (), s32[]{:S(2)}) async-start(), calls=%async_computation.12 | async-start | bytes 1179648 | tf_op jit(solution)/shard_map/reduce_scatter | solution.py:259
  279.2 39.6 %copy-start.16 = (bf16[256,512]{0,1:T(8,128)(2,1)}, bf16[256,512]{0,1:T(8,128)(2,1)S(1)}, u32[]{:S(2)}) copy-start(bf16[256,512]{0,1:T(8,128)(2,1)S(1)} %reshape.266) | copy-start | bytes 786436
  280.7 197.9 %reduce-scatter.17.cloned.1.call-start = ((), (), s32[]{:S(2)}) async-start(), calls=%async_computation.14 | async-start | bytes 1179648 | tf_op jit(solution)/shard_map/reduce_scatter | solution.py:262
  318.9 46.2 %copy-start.10 = (f32[256,2048]{1,0:T(8,128)S(1)}, f32[256,2048]{1,0:T(8,128)}, u32[]{:S(2)}) copy-start(f32[256,2048]{1,0:T(8,128)} %get-tuple-element.297) | copy-start | bytes 6291460
  318.9 46.2 %copy-start.14 = (bf16[4,64,512]{2,1,0:T(8,128)(2,1)S(1)}, bf16[4,64,512]{2,1,0:T(8,128)(2,1)}, u32[]{:S(2)}) copy-start(bf16[4,64,512]{2,1,0:T(8,128)(2,1)} %param.42) | copy-start | bytes 786436
  318.9 198.9 %reduce-scatter.15.cloned.1.call-start = ((), (), s32[]{:S(2)}) async-start(), calls=%async_computation.13 | async-start | bytes 1179648 | tf_op jit(solution)/shard_map/reduce_scatter | solution.py:261
  365.0 207.5 %reduce-scatter.23.cloned.1.call-start = ((), (), s32[]{:S(2)}) async-start(), calls=%async_computation.17 | async-start | bytes 4718592 | tf_op jit(solution)/shard_map/reduce_scatter | solution.py:270
  368.0 259.4 %reduce-scatter.21.cloned.1.call-start = ((), (), s32[]{:S(2)}) async-start(), calls=%async_computation.16 | async-start | bytes 4718592 | tf_op jit(solution)/shard_map/reduce_scatter | solution.py:268
  372.2 305.2 %all-reduce.14.cloned.1.call-start = ((), (), s32[]{:S(2)}) async-start(), calls=%async_computation.18 | async-start | bytes 1572864 | tf_op jit(solution)/shard_map/psum | solution.py:292
  375.5 65.5 %copy-start.19 = (bf16[4,64,512]{2,1,0:T(8,128)(2,1)S(1)}, bf16[4,64,512]{2,1,0:T(8,128)(2,1)}, u32[]{:S(2)}) copy-start(bf16[4,64,512]{2,1,0:T(8,128)(2,1)} %copy-done.18) | copy-start | bytes 786436
  375.5 65.4 %copy-start.21 = (bf16[512,512]{1,0:T(8,128)(2,1)S(1)}, bf16[512,512]{1,0:T(8,128)(2,1)}, u32[]{:S(2)}) copy-start(bf16[512,512]{1,0:T(8,128)(2,1)} %param.31) | copy-start | bytes 1572868
  440.9 188.3 %copy-start.28 = (bf16[4,64,512]{2,1,0:T(8,128)(2,1)S(1)}, bf16[4,64,512]{2,1,0:T(8,128)(2,1)}, u32[]{:S(2)}) copy-start(bf16[4,64,512]{2,1,0:T(8,128)(2,1)} %copy-done.27) | copy-start | bytes 786436
  440.9 188.3 %copy-start.32 = (f32[256]{0:T(256)S(1)}, f32[256]{0:T(256)}, u32[]{:S(2)}) copy-start(f32[256]{0:T(256)} %copy-done.31) | copy-start | bytes 3076
  440.9 188.3 %copy-start.34 = (f32[256]{0:T(256)S(1)}, f32[256]{0:T(256)}, u32[]{:S(2)}) copy-start(f32[256]{0:T(256)} %copy-done.33) | copy-start | bytes 3076
  574.3 57.5 %copy-start.35 = (f32[512]{0:T(512)S(1)}, f32[512]{0:T(512)}, u32[]{:S(2)}) copy-start(f32[512]{0:T(512)} %get-tuple-element.289) | copy-start | bytes 6148
  574.3 57.5 %copy-start.36 = (f32[2048]{0:T(1024)S(1)}, f32[2048]{0:T(1024)}, u32[]{:S(2)}) copy-start(f32[2048]{0:T(1024)} %get-tuple-element.287) | copy-start | bytes 24580
  574.3 57.5 %copy-start.38 = (f32[512]{0:T(512)S(1)}, f32[512]{0:T(512)}, u32[]{:S(2)}) copy-start(f32[512]{0:T(512)} %get-tuple-element.211) | copy-start | bytes 6148
  574.3 57.5 %copy-start.39 = (f32[512]{0:T(512)S(1)}, f32[512]{0:T(512)}, u32[]{:S(2)}) copy-start(f32[512]{0:T(512)} %get-tuple-element.217) | copy-start | bytes 6148
  574.3 99.1 %copy-start.9 = (f32[256,512]{1,0:T(8,128)S(1)}, f32[256,512]{1,0:T(8,128)}, u32[]{:S(2)}) copy-start(f32[256,512]{1,0:T(8,128)} %copy-done.8) | copy-start | bytes 1572868
  629.2 57.8 %copy-start.1 = (bf16[512,2048]{1,0:T(8,128)(2,1)S(1)}, bf16[512,2048]{1,0:T(8,128)(2,1)}, u32[]{:S(2)}) copy-start(bf16[512,2048]{1,0:T(8,128)(2,1)} %param.38) | copy-start | bytes 6291460
  (25 other events, 74.1 us)
Sparse Core Ops, SparseCore 0:
  15.2 30.6 all-gather.4
  48.0 27.4 all-gather.2
  273.1 43.3 reduce-scatter.10
  318.7 43.1 reduce-scatter.8
  364.9 35.3 reduce-scatter.18
  403.3 35.9 reduce-scatter.12
  442.5 35.9 reduce-scatter.16
  481.7 35.9 reduce-scatter.14
  521.1 51.3 reduce-scatter.22
  576.1 51.2 reduce-scatter.20
  631.4 45.9 all-reduce.13
where the time goes:
time: 696 us; the launch traced here: 694 us
  waiting for transfers between devices  368 us (53%)
  matrix products  179 us (26%)
  other arithmetic  49.1 us (7%)
  local copies, waits for them, and re-layouts  44.4 us (6%)
  blocking collectives  36.2 us (5%)
  between operations  15.8 us (2%)
    reduce_scatter x1, waiting for transfers between devices, shards(): lax.psum_scatter(outer_weight_grad, 'batch', scatter_dimension=0, tiled=T...  53.2 us
    reduce_scatter x1, waiting for transfers between devices, shards(): lax.psum_scatter(inner_weight_grad, 'batch', scatter_dimension=0, tiled=T...  53.1 us
    reduce_scatter x1, waiting for transfers between devices, shards(): lax.psum_scatter(key_grad.reshape(molecules, key_count, model_width), 'ro...  43 us
    reduce_scatter x1, waiting for transfers between devices, shards(): lax.psum_scatter(key_weight_grad, 'batch', scatter_dimension=0, tiled=True)  37.7 us
    reduce_scatter x1, waiting for transfers between devices, shards(): lax.psum_scatter(query_weight_grad, 'batch', scatter_dimension=0, tiled=T...  37.5 us
    reduce_scatter x1, waiting for transfers between devices, shards(): lax.psum_scatter(value_weight_grad, 'batch', scatter_dimension=0, tiled=T...  36.5 us
    dot_general x8, matrix products, scores_of(): jnp.einsum('ihe,jhe->hij', query_rows, key_rows, preferred_element_type=j...  35.8 us
    reduce_scatter x1, waiting for transfers between devices, shards(): lax.psum_scatter(value_grad.reshape(molecules, key_count, model_width), '...  35.7 us
  transfers between devices with their start and end apart: 11, of which 11 were waited for; matrix products, arithmetic and copies ran while one was open for 8% of the time, Pallas kernels for 0%

commit v1 on v0

v1 whole, which is shorter than its diff:
```python
import functools

import jax
import jax.numpy as jnp
from jax import lax
from jax.experimental import pallas as pl
from jax.experimental.pallas import tpu as pltpu
from jax.sharding import PartitionSpec as P

EPSILON = 1e-05
MASKED = -1000000000.0
F32 = jnp.float32
BF16 = jnp.bfloat16
LANES = 128


def norm_forward(values_in, gain, shift):
    centre = values_in - jnp.mean(values_in, -1, keepdims=True)
    inverse = lax.rsqrt(jnp.mean(centre * centre, -1, keepdims=True) + EPSILON)
    normed = centre * inverse
    return (normed * gain + shift, normed, inverse)


def norm_backward(upstream, normed, inverse, gain):
    scaled = upstream * gain
    return inverse * (
        scaled
        - jnp.mean(scaled, -1, keepdims=True)
        - normed * jnp.mean(scaled * normed, -1, keepdims=True)
    )


def dot(left, right):
    return jnp.dot(left, right, preferred_element_type=F32)


def across(left, right):
    return lax.dot_general(left, right, (((0,), (0,)), ((), ())), preferred_element_type=F32)


def against(left, right):
    return lax.dot_general(left, right, (((1,), (1,)), ((), ())), preferred_element_type=F32)


def column_sum(values_in):
    return jnp.sum(values_in.astype(F32), 0)


def forward_kernel(
    head_size,
    chunk,
    length_ref,
    all_ref,
    own_ref,
    pair_ref,
    gain_ref,
    shift_ref,
    query_weight_ref,
    query_bias_ref,
    key_weight_ref,
    value_weight_ref,
    value_bias_ref,
    pair_out_ref,
    weights_ref,
    mixed_ref,
    inverse_ref,
    hidden_ref,
    query_ref,
    key_ref,
    value_ref,
    query_scratch,
    key_scratch,
    value_scratch,
):
    molecule = pl.program_id(0)
    group = pl.program_id(1)
    groups, keys, width = key_scratch.shape
    heads = width // head_size
    rows, model_width = own_ref.shape[1:]
    factor = head_size**-0.5

    @pl.when(group == 0)
    def _():
        gain = gain_ref[...].astype(F32)
        shift = shift_ref[...].astype(F32)
        hidden = norm_forward(all_ref[...].reshape(keys, model_width).astype(F32), gain, shift)[0]
        hidden = hidden.astype(BF16)
        hidden_ref[...] = hidden.reshape(hidden_ref.shape)
        key_rows = dot(hidden, key_weight_ref[...]).astype(BF16)
        value_rows = dot(hidden, value_weight_ref[...]) + value_bias_ref[...].astype(F32)
        value_rows = value_rows.astype(BF16)
        own = norm_forward(own_ref[0].astype(F32), gain, shift)[0].astype(BF16)
        query_rows = dot(own, query_weight_ref[...]) + query_bias_ref[...].astype(F32)
        query_rows = (query_rows * factor).astype(BF16)
        ones = jnp.ones((keys, width), BF16)
        for t in range(groups):
            lanes = slice(t * width, (t + 1) * width)
            key_scratch[t] = key_rows[:, lanes]
            query_scratch[t] = query_rows[:, lanes]
            value_scratch[t, :, :width] = value_rows[:, lanes]
            value_scratch[t, :, width:] = ones

    query = query_scratch[group]
    key = key_scratch[group]
    value = value_scratch[group]
    query_ref[...] = query[None]
    key_ref[...] = key[None]
    value_ref[...] = value[None]
    valid = lax.broadcasted_iota(jnp.int32, (1, keys), 1) < length_ref[molecule]
    lane = lax.broadcasted_iota(jnp.int32, (1, width), 1) // head_size
    lane_pair = lax.broadcasted_iota(jnp.int32, (1, 2 * width), 1) % width // head_size
    total = jnp.zeros((rows, 2 * width), F32)
    zero = jnp.zeros((), BF16)
    for c in range(0, heads, chunk):
        here = slice(c, c + chunk)
        spread = jnp.concatenate([jnp.where(lane == c + t, query, zero) for t in range(chunk)], 0)
        scores = against(spread, key) + pair_ref[0, here].reshape(chunk * rows, keys).astype(F32)
        pair_out_ref[0, here] = scores.astype(BF16).reshape(chunk, rows, keys)
        masked = jnp.where(valid, scores, MASKED)
        weights = jnp.exp(masked - jnp.max(masked, -1, keepdims=True)).astype(BF16)
        weights_ref[0, here] = weights.reshape(chunk, rows, keys)
        product = dot(weights, value)
        for t in range(chunk):
            total = jnp.where(lane_pair == c + t, product[t * rows : (t + 1) * rows], total)
    inverse = 1.0 / total[:, width:]
    inverse_ref[...] = inverse[None]
    mixed_ref[...] = (total[:, :width] * inverse)[None]


def attention_forward(head_size, chunk, lengths, atoms_all, atoms, pair_bias, parameters):
    spans, molecules, rows, model_width = atoms_all.shape
    keys = pair_bias.shape[3]
    groups = model_width // LANES
    heads = LANES // head_size
    pair_spec = pl.BlockSpec((1, heads, rows, keys), lambda m, g, n: (m, g, 0, 0))
    row_spec = pl.BlockSpec((1, rows, LANES), lambda m, g, n: (m, 0, g))
    all_spec = pl.BlockSpec((spans, 1, rows, model_width), lambda m, g, n: (0, m, 0, 0))
    fixed = [pl.BlockSpec(a.shape, lambda m, g, n: (0, 0)) for a in parameters]
    token_shape = (molecules, rows, model_width)
    return pl.pallas_call(
        functools.partial(forward_kernel, head_size, chunk),
        grid_spec=pltpu.PrefetchScalarGridSpec(
            num_scalar_prefetch=1,
            grid=(molecules, groups),
            in_specs=[
                all_spec,
                pl.BlockSpec((1, rows, model_width), lambda m, g, n: (m, 0, 0)),
                pair_spec,
            ]
            + fixed,
            out_specs=[
                pair_spec,
                pair_spec,
                row_spec,
                row_spec,
                all_spec,
                row_spec,
                pl.BlockSpec((1, keys, LANES), lambda m, g, n: (m, 0, g)),
                pl.BlockSpec((1, keys, 2 * LANES), lambda m, g, n: (m, 0, g)),
            ],
            scratch_shapes=[
                pltpu.VMEM((groups, rows, LANES), BF16),
                pltpu.VMEM((groups, keys, LANES), BF16),
                pltpu.VMEM((groups, keys, 2 * LANES), BF16),
            ],
        ),
        out_shape=[
            jax.ShapeDtypeStruct(pair_bias.shape, BF16),
            jax.ShapeDtypeStruct(pair_bias.shape, BF16),
            jax.ShapeDtypeStruct(token_shape, F32),
            jax.ShapeDtypeStruct(token_shape, F32),
            jax.ShapeDtypeStruct(atoms_all.shape, BF16),
            jax.ShapeDtypeStruct(token_shape, BF16),
            jax.ShapeDtypeStruct((molecules, keys, model_width), BF16),
            jax.ShapeDtypeStruct((molecules, keys, 2 * model_width), BF16),
        ],
        compiler_params=pltpu.CompilerParams(vmem_limit_bytes=40 << 20),
        name="attention_forward",
    )(lengths, atoms_all, atoms, pair_bias, *parameters)


def backward_kernel(
    head_size,
    chunk,
    weights_ref,
    cotangent_ref,
    grad_mixed_ref,
    mixed_ref,
    inverse_ref,
    query_ref,
    key_ref,
    value_ref,
    pair_grad_ref,
    grad_query_ref,
    grad_key_ref,
    grad_value_ref,
):
    rows, width = query_ref.shape[1:]
    keys = key_ref.shape[1]
    heads = width // head_size
    factor = head_size**-0.5
    query = query_ref[0]
    key = key_ref[0]
    value = value_ref[0]
    upstream = (grad_mixed_ref[0].astype(F32) * inverse_ref[0]).astype(BF16)
    offset = (-(upstream.astype(F32) * mixed_ref[0])).astype(BF16)
    both = jnp.concatenate([upstream, offset], 1)
    lane = lax.broadcasted_iota(jnp.int32, (1, width), 1) // head_size
    lane_pair = lax.broadcasted_iota(jnp.int32, (1, 2 * width), 1) % width // head_size
    query_turned = jnp.transpose(query.astype(F32)).astype(BF16)
    upstream_turned = jnp.transpose(upstream.astype(F32)).astype(BF16)
    query_turned = jnp.concatenate([query_turned] * chunk, 1)
    upstream_turned = jnp.concatenate([upstream_turned] * chunk, 1)
    turned_shape = (chunk * head_size, chunk * rows)
    same = (
        lax.broadcasted_iota(jnp.int32, turned_shape, 0) // head_size
        == lax.broadcasted_iota(jnp.int32, turned_shape, 1) // rows
    )
    zero = jnp.zeros((), BF16)
    total = jnp.zeros((rows, width), F32)
    key_parts = []
    value_parts = []
    for c in range(0, heads, chunk):
        here = slice(c, c + chunk)
        feature = slice(c * head_size, (c + chunk) * head_size)
        spread = jnp.concatenate([jnp.where(lane_pair == c + t, both, zero) for t in range(chunk)], 0)
        centred = against(spread, value)
        weights = weights_ref[0, here].reshape(chunk * rows, keys)
        cotangent = cotangent_ref[0, here].reshape(chunk * rows, keys)
        grad = (weights.astype(F32) * centred + cotangent.astype(F32)).astype(BF16)
        pair_grad_ref[0, here] = grad.reshape(chunk, rows, keys)
        product = dot(grad, key)
        for t in range(chunk):
            total = jnp.where(lane == c + t, product[t * rows : (t + 1) * rows], total)
        key_parts.append(dot(jnp.where(same, query_turned[feature], zero), grad))
        value_parts.append(dot(jnp.where(same, upstream_turned[feature], zero), weights))
    grad_query_ref[...] = (total * factor).astype(BF16)[None]
    grad_key = jnp.transpose(jnp.concatenate(key_parts, 0)).astype(BF16)
    grad_value = jnp.transpose(jnp.concatenate(value_parts, 0)).astype(BF16)
    grad_key_ref[...] = grad_key.reshape(grad_key_ref.shape)
    grad_value_ref[...] = grad_value.reshape(grad_value_ref.shape)


def attention_backward(
    head_size, chunk, spans, weights, cotangent, grad_mixed, mixed, inverse, query, key, value
):
    molecules, _, rows, keys = weights.shape
    model_width = query.shape[2]
    groups = model_width // LANES
    heads = LANES // head_size
    pair_spec = pl.BlockSpec((1, heads, rows, keys), lambda m, g: (m, g, 0, 0))
    row_spec = pl.BlockSpec((1, rows, LANES), lambda m, g: (m, 0, g))
    span_spec = pl.BlockSpec((spans, 1, rows, LANES), lambda m, g: (0, m, 0, g))
    span_shape = jax.ShapeDtypeStruct((spans, molecules, rows, model_width), BF16)
    return pl.pallas_call(
        functools.partial(backward_kernel, head_size, chunk),
        grid=(molecules, groups),
        in_specs=[
            pair_spec,
            pair_spec,
            row_spec,
            row_spec,
            row_spec,
            row_spec,
            pl.BlockSpec((1, keys, LANES), lambda m, g: (m, 0, g)),
            pl.BlockSpec((1, keys, 2 * LANES), lambda m, g: (m, 0, g)),
        ],
        out_specs=[pair_spec, row_spec, span_spec, span_spec],
        out_shape=[
            jax.ShapeDtypeStruct(weights.shape, BF16),
            jax.ShapeDtypeStruct((molecules, rows, model_width), BF16),
            span_shape,
            span_shape,
        ],
        compiler_params=pltpu.CompilerParams(vmem_limit_bytes=40 << 20),
        name="attention_backward",
    )(weights, cotangent, grad_mixed, mixed, inverse, query, key, value)


def swap(value, axis, mask):
    size = lax.axis_size(axis)
    return lax.ppermute(value, axis, [(i, i ^ mask) for i in range(size)])


def gather_rows(value):
    size = lax.axis_size("rows")
    if size != 4:
        return lax.all_gather(value, "rows", axis=0, tiled=False)
    half = value.shape[0] // 2
    me = lax.axis_index("rows")
    one = swap(value, "rows", 1)
    three = swap(value, "rows", 3)
    two = jnp.concatenate([swap(one[:half], "rows", 3), swap(three[half:], "rows", 1)], 0)
    stacked = jnp.stack([value, one, two, three])
    return jnp.concatenate(
        [lax.dynamic_index_in_dim(stacked, me ^ i, 0, keepdims=True) for i in range(4)], 0
    )


def pick(value, index):
    return lax.dynamic_index_in_dim(value, index, 0, keepdims=False)


def scatter_rows(value):
    size = lax.axis_size("rows")
    if size != 4:
        return lax.psum_scatter(
            value, "rows", scatter_dimension=0, tiled=False
        ).astype(F32)
    me = lax.axis_index("rows")
    half = value.shape[1] // 2
    results = []
    for part, first, second in ((slice(0, half), 1, 3), (slice(half, None), 3, 1)):
        piece = value[:, part]
        sent = jnp.stack([pick(piece, me ^ first), pick(piece, me ^ 2)]).astype(BF16)
        came = swap(sent, "rows", first).astype(F32)
        mine = pick(piece, me) + came[0]
        other = (pick(piece, me ^ second) + came[1]).astype(BF16)
        results.append(mine + swap(other, "rows", second).astype(F32))
    return jnp.concatenate(results, 0)


def reduce_slices(value, flip):
    count = lax.axis_size("batch")
    spans = lax.axis_size("rows")
    bits = count.bit_length() - 1
    if count != 1 << bits or spans != 4:
        part = lax.psum_scatter(value, "batch", scatter_dimension=0, tiled=True)
        return lax.psum(part.astype(BF16), "rows").astype(F32)
    me = lax.axis_index("batch")
    shape = (count, value.shape[0] // count) + value.shape[1:]
    total = value.reshape(shape)
    order = [0] + (list(range(bits - 1, 0, -1)) if flip else list(range(1, bits)))
    left = list(range(bits - 1, -1, -1))
    total = total.reshape((2,) * bits + shape[1:])
    for bit in order:
        axis = left.index(bit)
        mine = (me >> bit) & 1
        sent = lax.dynamic_index_in_dim(total, 1 - mine, axis, keepdims=False).astype(BF16)
        kept = lax.dynamic_index_in_dim(total, mine, axis, keepdims=False).astype(F32)
        total = kept + swap(sent, "batch", 1 << bit).astype(F32)
        left.remove(bit)
    for mask in (3, 1) if flip else (1, 3):
        low = total.astype(BF16)
        total = low.astype(F32) + swap(low, "rows", mask).astype(F32)
    return total


def shards(
    atoms,
    pair_bias,
    lengths,
    first_gain,
    first_shift,
    query_weight,
    query_bias,
    key_weight,
    value_weight,
    value_bias,
    out_weight,
    out_bias,
    second_gain,
    second_shift,
    inner_weight,
    inner_bias,
    outer_weight,
    outer_bias,
    atoms_cotangent,
    pair_cotangent,
):
    molecules, rows, model_width = atoms.shape
    head_count = pair_bias.shape[1]
    head_size = model_width // head_count
    spans = lax.axis_size("rows")
    batch_count = lax.axis_size("batch")
    tokens = molecules * rows
    flat = lambda a: a.reshape(-1, model_width)
    atoms_all = gather_rows(atoms)
    pair_out, weights, mixed, inverse, hidden_all, query, key, value = attention_forward(
        head_size,
        4,
        lengths,
        atoms_all,
        atoms,
        pair_bias,
        (
            first_gain[None],
            first_shift[None],
            query_weight,
            query_bias[None],
            key_weight,
            value_weight,
            value_bias[None],
        ),
    )
    atoms_float = flat(atoms).astype(F32)
    mixed_low = flat(mixed).astype(BF16)
    middle = atoms_float + dot(mixed_low, out_weight) + out_bias.astype(F32)
    second_out, second_normed, second_inverse = norm_forward(
        middle, second_gain.astype(F32), second_shift.astype(F32)
    )
    second_low = second_out.astype(BF16)
    inner_pre = dot(second_low, inner_weight) + inner_bias.astype(F32)
    activated, gelu_pull = jax.vjp(jax.nn.gelu, inner_pre)
    activated_low = activated.astype(BF16)
    result_rows = middle + dot(activated_low, outer_weight) + outer_bias.astype(F32)
    atoms_out = result_rows.astype(BF16).reshape(atoms.shape)
    grad_outer = flat(atoms_cotangent)
    outer_weight_grad = across(activated_low, grad_outer)
    outer_bias_grad = column_sum(grad_outer)
    grad_activated = against(grad_outer, outer_weight)
    grad_inner = gelu_pull(grad_activated)[0].astype(BF16)
    inner_weight_grad = across(second_low, grad_inner)
    inner_bias_grad = column_sum(grad_inner)
    grad_second = against(grad_inner, inner_weight)
    second_gain_grad = jnp.sum(grad_second * second_normed, 0)
    second_shift_grad = jnp.sum(grad_second, 0)
    grad_middle = grad_outer.astype(F32) + norm_backward(
        grad_second, second_normed, second_inverse, second_gain.astype(F32)
    )
    grad_branch = grad_middle.astype(BF16)
    out_weight_grad = across(mixed_low, grad_branch)
    out_bias_grad = column_sum(grad_branch)
    grad_mixed = against(grad_branch, out_weight).astype(BF16)

    outer_weight_grad = reduce_slices(outer_weight_grad, False)
    inner_weight_grad = reduce_slices(inner_weight_grad, True)
    out_weight_grad = reduce_slices(out_weight_grad, True)

    pair_grad, query_grad, key_grad, value_grad = attention_backward(
        head_size,
        4,
        spans,
        weights,
        pair_cotangent,
        grad_mixed.reshape(atoms.shape),
        mixed,
        inverse,
        query,
        key,
        value,
    )
    query_flat, key_flat, value_flat = flat(query_grad), flat(key_grad), flat(value_grad)
    hidden_flat = flat(hidden_all)
    _, normed_all, _ = norm_forward(
        flat(atoms_all).astype(F32), first_gain.astype(F32), first_shift.astype(F32)
    )
    _, first_normed, first_inverse = norm_forward(
        atoms_float, first_gain.astype(F32), first_shift.astype(F32)
    )
    grad_shared = against(key_flat, key_weight) + against(value_flat, value_weight)
    grad_local = against(query_flat, query_weight)
    grad_first = (
        scatter_rows(grad_shared.reshape((spans,) + atoms.shape)).reshape(tokens, model_width)
        + grad_local
    )
    hidden_own = flat(lax.dynamic_index_in_dim(hidden_all, lax.axis_index("rows"), 0))
    query_weight_grad = reduce_slices(across(hidden_own, query_flat), False)
    key_weight_grad = reduce_slices(across(hidden_flat, key_flat), False)
    value_weight_grad = reduce_slices(across(hidden_flat, value_flat), True)
    vectors = [
        jnp.sum(grad_shared * normed_all, 0) + jnp.sum(grad_local * first_normed, 0),
        jnp.sum(grad_shared, 0) + jnp.sum(grad_local, 0),
        column_sum(query_flat),
        column_sum(value_flat),
        out_bias_grad,
        second_gain_grad,
        second_shift_grad,
        inner_bias_grad,
        outer_bias_grad,
    ]
    packed = jnp.concatenate([v.reshape(batch_count, -1) for v in vectors], 1)
    packed = reduce_slices(packed, True)[0]
    small = []
    start = 0
    for v in vectors:
        size = v.shape[0] // batch_count
        small.append(packed[start : start + size])
        start += size
    atoms_grad = grad_middle + norm_backward(
        grad_first, first_normed, first_inverse, first_gain.astype(F32)
    )
    return (
        atoms_out,
        pair_out,
        atoms_grad.astype(BF16).reshape(atoms.shape),
        pair_grad,
        small[0],
        small[1],
        query_weight_grad,
        small[2],
        key_weight_grad,
        value_weight_grad,
        small[3],
        out_weight_grad,
        small[4],
        small[5],
        small[6],
        inner_weight_grad,
        small[7],
        outer_weight_grad,
        small[8],
    )


def solution(mesh):
    tokens = P("batch", "rows", None)
    pairs = P("batch", None, "rows", None)
    vector = P("batch")
    matrix = P("batch", None)
    return jax.shard_map(
        shards,
        mesh=mesh,
        in_specs=(tokens, pairs, P("batch")) + (P(),) * 15 + (tokens, pairs),
        out_specs=(
            tokens,
            pairs,
            tokens,
            pairs,
            vector,
            vector,
            matrix,
            vector,
            matrix,
            matrix,
            vector,
            matrix,
            vector,
            vector,
            vector,
            matrix,
            vector,
            matrix,
            vector,
        ),
        check_vma=False,
    )
```

time: 696 us -> 242 us (0.35)
  waiting for transfers between devices: 368 us -> 64.9 us
  matrix products: 179 us -> 23.9 us
  starting transfers between devices: 0.68 us -> 51.8 us
  Pallas kernels: 0 us -> 38.8 us
  blocking collectives: 36.2 us -> 0 us
  other arithmetic: 49.1 us -> 27.2 us
  between operations: 15.8 us -> 1.75 us
  local copies, waits for them, and re-layouts: 44.4 us -> 31.5 us
    reduce_scatter x8 -> x0, waiting for transfers between devices: 318 us -> none  [the longest x1 53.2 us: shards(): lax.psum_scatter(outer_weight_grad, 'batch', scatter_dimension=0, tiled=T...]
    dot_general x30 -> x3, matrix products: 131 us -> 6.99 us  [dot(): return jnp.dot(left, right, preferred_element_type=F32)]
    ppermute x0 -> x43, waiting for transfers between devices: none -> 64.9 us  [swap(): return lax.ppermute(value, axis, [(i, i ^ mask) for i in range(size)])]
    ppermute x0 -> x43, starting transfers between devices: none -> 51.8 us  [swap(): return lax.ppermute(value, axis, [(i, i ^ mask) for i in range(size)])]
    all_gather x2 -> x0, waiting for transfers between devices: 48 us -> none  [the longest x1 27.3 us: shards(): lax.all_gather(key_local, 'rows', axis=1, tiled=True)]
    pallas_call x0 -> x2, Pallas kernels: none -> 38.8 us  [the longest x1 19.8 us: attention_forward(): pl.pallas_call(functools.partial(forward_kernel, head_size, chunk), grid_...]
    sub x4 -> x0, matrix products: 27.8 us -> none  [attend_backward(): probs_grad - inner_sum]
    unnamed x1 -> x0, blocking collectives: 24.1 us -> none
  transfers between devices with their start and end apart: 11 -> 43, of which waited for: 11 -> 19; matrix products, arithmetic and copies ran while one was open for 8% -> 18% of each run, Pallas kernels for 0% -> 0%
where the time goes in v1:
time: 242 us; the launch traced here: 240 us
  waiting for transfers between devices  64.9 us (27%)
  starting transfers between devices  51.8 us (21%)
  Pallas kernels  38.8 us (16%)
  local copies, waits for them, and re-layouts  31.5 us (13%)
  other arithmetic  27.2 us (11%)
  matrix products  23.9 us (10%)
    ppermute x43, waiting for transfers between devices, swap(): return lax.ppermute(value, axis, [(i, i ^ mask) for i in range(size)])  64.9 us
    ppermute x43, starting transfers between devices, swap(): return lax.ppermute(value, axis, [(i, i ^ mask) for i in range(size)])  51.8 us
    pallas_call x1, Pallas kernels, attention_forward(): pl.pallas_call(functools.partial(forward_kernel, head_size, chunk), grid_...  19.8 us
    pallas_call x1, Pallas kernels, attention_backward(): pl.pallas_call(functools.partial(backward_kernel, head_size, chunk), grid...  19 us
    unnamed x101, local copies, waits for them, and re-layouts  10.6 us
    dot_general x6, matrix products, against(): lax.dot_general(left, right, (((1,), (1,)), ((), ())), preferred_element_...  10.3 us
    add x14, other arithmetic, reduce_slices(): total = kept + swap(sent, 'batch', 1 << bit).astype(F32)  7 us
    dot_general x3, matrix products, dot(): return jnp.dot(left, right, preferred_element_type=F32)  6.99 us
  transfers between devices with their start and end apart: 43, of which 19 were waited for; matrix products, arithmetic and copies ran while one was open for 18% of the time, Pallas kernels for 0%

profile of v1, /device:TPU:0, one launch (start us, length us, event | category | flops | bytes accessed | tf_op | source)
XLA Modules:
  0.0 239.8 jit_solution(17420241539212843067)
XLA Ops:
  0.7 3.1 %collective-permute-start = (bf16[4,64,512]{2,1,0:T(8,128)(2,1)}, bf16[4,64,512]{2,1,0:T(8,128)(2,1)S(1)}, u32[]{:S(2)}, u32[]{:S(2)}) collective-permute-start(bf16[4,64,512]{2,1,0:T(8,128)(2,1)} %own_ref.1), channel_id=1, source_target_pairs={{0,1},{1,0},{2,3},{3,2},{4,5},{5,4},{6,7},{7,6},{8,9},{9,8},{10,11... | collective-permute-start | bytes 786440 | tf_op jit(solution)/shard_map/ppermute | solution.py:282
  3.8 2.5 %collective-permute-start.2 = (bf16[4,64,512]{2,1,0:T(8,128)(2,1)}, bf16[4,64,512]{2,1,0:T(8,128)(2,1)S(1)}, u32[]{:S(2)}, u32[]{:S(2)}) collective-permute-start(bf16[4,64,512]{2,1,0:T(8,128)(2,1)} %own_ref.1), channel_id=1, source_target_pairs={{0,3},{1,2},{2,1},{3,0},{4,7},{5,6},{6,5},{7,4},{8,11},{9,10},{10,... | collective-permute-start | bytes 786440 | tf_op jit(solution)/shard_map/ppermute | solution.py:282
  16.9 3.8 %fusion.84 = f32[256,2048]{1,0:T(8,128)} fusion(bf16[256,512]{1,0:T(8,128)(2,1)} %bitcast.251, bf16[2048,512]{1,0:T(8,128)(2,1)} %param.36), kind=kOutput, calls=%fused_computation.208 | convolution fusion | flops 536870912 | bytes 4456448 | tf_op jit(solution)/shard_map/dot_general | solution.py:42
  22.9 5.8 %collective-permute-done.1 = bf16[2,64,512]{2,1,0:T(8,128)(2,1)S(1)} collective-permute-done((bf16[2,64,512]{2,1,0:T(8,128)(2,1)S(1)}, bf16[2,64,512]{2,1,0:T(8,128)(2,1)S(1)}, u32[]{:S(2)}, u32[]{:S(2)}) %collective-permute-start.1) | collective-permute-done | bytes 131104 | tf_op jit(solution)/shard_map/ppermute | solution.py:282
  34.7 19.8 %attention_forward.1 = (bf16[4,64,64,256]{3,2,1,0:T(8,128)(2,1)}, bf16[4,64,64,256]{3,2,1,0:T(8,128)(2,1)}, f32[4,64,512]{2,1,0:T(8,128)S(1)}, f32[4,64,512]{2,1...) custom-call(s32[4]{0:T(128)S(1)} %copy-done.25, ...), custom_call_target="tpu_custom_call" | custom-call | tf_op jit(solution)/shard_map/attention_forward/pallas_call | solution.py:140
  55.2 2.5 %copy-done.40 = f32[256,2048]{1,0:T(8,128)S(1)} copy-done((f32[256,2048]{1,0:T(8,128)S(1)}, f32[256,2048]{1,0:T(8,128)}, u32[]{:S(2)}) %copy-start.40) | copy-done | bytes 2097176
  57.7 3.4 %convert_reduce_fusion = (f32[2048]{0:T(1024)S(1)}, bf16[256,2048]{1,0:T(8,128)(2,1)S(1)}, f32[256,2048]{1,0:T(8,128)}) fusion(f32[256,2048]{1,0:T(8,128)S(1)} %copy-done.40, f32[2048]{0:T(1024)S(1)} %convert_element_type.463, bf16[512,2048]{1,0:T(8,128)(2,1)S(1)} %copy-done, f32[256,512]{1,0:T(8,128)S(1)} %get-tuple-element.82, ...), kind=kOutput, calls=%fused_computation.27 | convolution fusion | flops 549582848 | bytes 7886848 | tf_op jit(solution)/shard_map/dot_general | solution.py:34
  62.9 2.9 %fusion.76 = f32[512,2048]{1,0:T(8,128)} fusion(bf16[256,2048]{1,0:T(8,128)(2,1)S(1)} %get-tuple-element.54, f32[256,512]{1,0:T(8,128)S(1)} %get-tuple-element.82, f32[512]{0:T(512)S(1)} %convert_element_type.461, f32[512]{0:T(512)S(1)} %convert_element_type.460, f32[256]{0:T(256)S(1)} %add_rsqrt_fusion.2, f32[256]{0:T(256)S(1)} %broadcast_multiply_fusion.6), kind=kOutput, calls=%fused_computation.202 | convolution fusion | flops 537526272 | bytes 5773312 | tf_op jit(solution)/shard_map/dot_general | solution.py:38
  69.0 2.4 fusion.14
  71.4 3.2 %fusion.20 = bf16[256,512]{1,0:T(8,128)(2,1)} fusion(f32[256,512]{1,0:T(8,128)S(1)} %copy-done.30, bf16[2048,512]{1,0:T(8,128)(2,1)} %param.36, f32[256,2048]{1,0:T(8,128)S(1)} %copy-done.39, f32[512]{0:T(512)S(1)} %convert_element_type.465), kind=kOutput, calls=%fused_computation.36 | convolution fusion | flops 541982720 | bytes 4982784 | tf_op jit(solution)/shard_map/dot_general | solution.py:34
  84.1 19.0 %attention_backward.1 = (bf16[4,64,64,256]{3,2,1,0:T(8,128)(2,1)}, bf16[4,64,512]{2,1,0:T(8,128)(2,1)S(1)}, bf16[4,4,64,512]{3,2,1,0:T(8,128)(2,1)S(1)}, bf16[4,4,64,512]{3,2,1,0:T(8,128)(2,1)S(1)}) custom-call(bf16[4,64,64,256]{3,2,1,0:T(8,128)(2,1)} %get-tuple-element.33.weights_ref, bf16[4,64,64,256]{3,2,1,0:T(8,128)(2,1)} %cotangent_ref.1, ...), custom_call_target="tpu_custom_call" | custom-call | tf_op jit(solution)/shard_map/attention_backward/pallas_call | solution.py:255
  115.9 4.0 %fusion.22 = bf16[2,2,64,2048]{3,2,1,0:T(8,128)(2,1)} fusion(f32[2,2,2,64,2048]{4,3,2,1,0:T(8,128)} %bitcast.247, s32[]{:T(128)S(6)} %select_n.96), kind=kLoop, calls=%fused_computation.39 | loop fusion | bytes 2097156 | tf_op jit(solution)/shard_map/convert_element_type | solution.py:339
  120.0 3.4 %collective-permute-done.6 = bf16[2,2,64,512]{3,2,1,0:T(8,128)(2,1)S(1)} collective-permute-done((bf16[2,2,64,512]{3,2,1,0:T(8,128)(2,1)S(1)}, bf16[2,2,64,512]{3,2,1,0:T(8,128)(2,1)S(1)}, u32[]{:S(2)}, u32[]{:S(2)}) %collective-permute-start.6) | collective-permute-done | bytes 262176 | tf_op jit(solution)/shard_map/ppermute | solution.py:282
  123.4 3.9 %collective-permute-start.4 = (bf16[2,2,64,512]{3,2,1,0:T(8,128)(2,1)S(1)}, bf16[2,2,64,512]{3,2,1,0:T(8,128)(2,1)S(1)}, u32[]{:S(2)}, u32[]{:S(2)}) collective-permute-start(bf16[2,2,64,512]{3,2,1,0:T(8,128)(2,1)S(1)} %pad_maximum_fusion.3), channel_id=1, source_target_pairs={{0,1},{1,0},{2,3},{3,2},{4,5},{5,4},{6,7},{7,6},{8,9},{9,8},{10,11... | collective-permute-start | bytes 786440 | tf_op jit(solution)/shard_map/ppermute | solution.py:282
  128.9 4.5 %collective-permute-done.4 = bf16[2,2,64,512]{3,2,1,0:T(8,128)(2,1)S(1)} collective-permute-done((bf16[2,2,64,512]{3,2,1,0:T(8,128)(2,1)S(1)}, bf16[2,2,64,512]{3,2,1,0:T(8,128)(2,1)S(1)}, u32[]{:S(2)}, u32[]{:S(2)}) %collective-permute-start.4) | collective-permute-done | bytes 262176 | tf_op jit(solution)/shard_map/ppermute | solution.py:282
  139.9 2.4 %collective-permute-done.7 = bf16[2,64,512]{2,1,0:T(8,128)(2,1)S(1)} collective-permute-done((bf16[2,64,512]{2,1,0:T(8,128)(2,1)S(1)}, bf16[2,64,512]{2,1,0:T(8,128)(2,1)S(1)}, u32[]{:S(2)}, u32[]{:S(2)}) %collective-permute-start.7) | collective-permute-done | bytes 131104 | tf_op jit(solution)/shard_map/ppermute | solution.py:282
  142.4 2.4 %collective-permute-start.5 = (bf16[2,64,512]{2,1,0:T(8,128)(2,1)S(1)}, bf16[2,64,512]{2,1,0:T(8,128)(2,1)S(1)}, u32[]{:S(2)}, u32[]{:S(2)}) collective-permute-start(bf16[2,64,512]{2,1,0:T(8,128)(2,1)S(1)} %fusion.50), channel_id=1, source_target_pairs={{0,3},{1,2},{2,1},{3,0},{4,7},{5,6},{6,5},{7,4},{8,11},{9,10},{10,... | collective-permute-start | bytes 393224 | tf_op jit(solution)/shard_map/ppermute | solution.py:282
  144.9 4.4 %collective-permute-done.5 = bf16[2,64,512]{2,1,0:T(8,128)(2,1)S(1)} collective-permute-done((bf16[2,64,512]{2,1,0:T(8,128)(2,1)S(1)}, bf16[2,64,512]{2,1,0:T(8,128)(2,1)S(1)}, u32[]{:S(2)}, u32[]{:S(2)}) %collective-permute-start.5) | collective-permute-done | bytes 131104 | tf_op jit(solution)/shard_map/ppermute | solution.py:282
  159.8 3.1 %collective-permute-done.9 = bf16[2,1,768]{2,0,1:T(2,128)(2,1)S(1)} collective-permute-done((bf16[2,1,768]{2,0,1:T(2,128)(2,1)S(1)}, bf16[2,1,768]{2,0,1:T(2,128)(2,1)S(1)}, u32[]{:S(2)}, u32[]{:S(2)}) %collective-permute-start.9) | collective-permute-done | bytes 3104 | tf_op jit(solution)/shard_map/ppermute | solution.py:282
  165.0 3.0 %collective-permute-done.10 = bf16[1,768]{1,0:T(2,128)(2,1)S(1)} collective-permute-done((bf16[1,768]{1,0:T(2,128)(2,1)S(1)}, bf16[1,768]{1,0:T(2,128)(2,1)S(1)}, u32[]{:S(2)}, u32[]{:S(2)}) %collective-permute-start.10) | collective-permute-done | bytes 1568 | tf_op jit(solution)/shard_map/ppermute | solution.py:282
  168.1 2.5 %collective-permute-start.11 = (bf16[1,768]{1,0:T(2,128)(2,1)S(1)}, bf16[1,768]{1,0:T(2,128)(2,1)S(1)}, u32[]{:S(2)}, u32[]{:S(2)}) collective-permute-start(bf16[1,768]{1,0:T(2,128)(2,1)S(1)} %fusion.67), channel_id=1, source_target_pairs={{0,3},{1,2},{2,1},{3,0},{4,7},{5,6},{6,5},{7,4},{8,11},{9,10},{10,... | collective-permute-start | bytes 4616 | tf_op jit(solution)/shard_map/ppermute | solution.py:282
  170.6 3.0 %collective-permute-done.11 = bf16[1,768]{1,0:T(2,128)(2,1)S(1)} collective-permute-done((bf16[1,768]{1,0:T(2,128)(2,1)S(1)}, bf16[1,768]{1,0:T(2,128)(2,1)S(1)}, u32[]{:S(2)}, u32[]{:S(2)}) %collective-permute-start.11) | collective-permute-done | bytes 1568 | tf_op jit(solution)/shard_map/ppermute | solution.py:282
  173.6 3.6 %collective-permute-done.12 = bf16[1,768]{1,0:T(2,128)(2,1)S(1)} collective-permute-done((bf16[1,768]{1,0:T(2,128)(2,1)S(1)}, bf16[1,768]{1,0:T(2,128)(2,1)S(1)}, u32[]{:S(2)}, u32[]{:S(2)}) %collective-permute-start.12) | collective-permute-done | bytes 1568 | tf_op jit(solution)/shard_map/ppermute | solution.py:282
  181.5 2.4 %collective-permute-start.31 = (bf16[64,512]{1,0:T(8,128)(2,1)S(1)}, bf16[64,512]{1,0:T(8,128)(2,1)S(1)}, u32[]{:S(2)}, u32[]{:S(2)}) collective-permute-start(bf16[64,512]{1,0:T(8,128)(2,1)S(1)} %fusion.52), channel_id=1, source_target_pairs={{0,3},{1,2},{2,1},{3,0},{4,7},{5,6},{6,5},{7,4},{8,11},{9,10},{10,... | collective-permute-start | bytes 196616 | tf_op jit(solution)/shard_map/ppermute | solution.py:282
  187.9 2.5 %collective-permute-start.17 = (bf16[64,512]{1,0:T(8,128)(2,1)S(1)}, bf16[64,512]{1,0:T(8,128)(2,1)S(1)}, u32[]{:S(2)}, u32[]{:S(2)}) collective-permute-start(bf16[64,512]{1,0:T(8,128)(2,1)S(1)} %add_convert_fusion.7), channel_id=1, source_target_pairs={{0,3},{1,2},{2,1},{3,0},{4,7},{5,6},{6,5},{7,4},{8,11},{9,10},{10,... | collective-permute-start | bytes 196616 | tf_op jit(solution)/shard_map/ppermute | solution.py:282
  194.0 2.6 %collective-permute-start.22 = (bf16[64,512]{1,0:T(8,128)(2,1)S(1)}, bf16[64,512]{1,0:T(8,128)(2,1)S(1)}, u32[]{:S(2)}, u32[]{:S(2)}) collective-permute-start(bf16[64,512]{1,0:T(8,128)(2,1)S(1)} %add_convert_fusion.6), channel_id=1, source_target_pairs={{0,3},{1,2},{2,1},{3,0},{4,7},{5,6},{6,5},{7,4},{8,11},{9,10},{10,... | collective-permute-start | bytes 196616 | tf_op jit(solution)/shard_map/ppermute | solution.py:282
  203.0 8.2 %collective-permute-done.34 = bf16[2,64,2048]{2,1,0:T(8,128)(2,1)S(1)} collective-permute-done((bf16[2,64,2048]{2,1,0:T(8,128)(2,1)S(1)}, bf16[2,64,2048]{2,1,0:T(8,128)(2,1)S(1)}, u32[]{:S(2)}, u32[]{:S(2)}) %collective-permute-start.34) | collective-permute-done | bytes 524320 | tf_op jit(solution)/shard_map/ppermute | solution.py:282
  213.1 4.7 %collective-permute-done.35 = bf16[64,2048]{1,0:T(8,128)(2,1)S(1)} collective-permute-done((bf16[64,2048]{1,0:T(8,128)(2,1)S(1)}, bf16[64,2048]{1,0:T(8,128)(2,1)S(1)}, u32[]{:S(2)}, u32[]{:S(2)}) %collective-permute-start.35) | collective-permute-done | bytes 262176 | tf_op jit(solution)/shard_map/ppermute | solution.py:282
  219.9 6.4 %collective-permute-done.36 = bf16[64,2048]{1,0:T(8,128)(2,1)S(1)} collective-permute-done((bf16[64,2048]{1,0:T(8,128)(2,1)S(1)}, bf16[64,2048]{1,0:T(8,128)(2,1)S(1)}, u32[]{:S(2)}, u32[]{:S(2)}) %collective-permute-start.36) | collective-permute-done | bytes 262176 | tf_op jit(solution)/shard_map/ppermute | solution.py:282
  226.4 3.1 %collective-permute-start.37 = (bf16[64,2048]{1,0:T(8,128)(2,1)S(1)}, bf16[64,2048]{1,0:T(8,128)(2,1)S(1)}, u32[]{:S(2)}, u32[]{:S(2)}) collective-permute-start(bf16[64,2048]{1,0:T(8,128)(2,1)S(1)} %add_convert_fusion.1), channel_id=1, source_target_pairs={{0,1},{1,0},{2,3},{3,2},{4,5},{5,4},{6,7},{7,6},{8,9},{9,8},{10,11... | collective-permute-start | bytes 786440 | tf_op jit(solution)/shard_map/ppermute | solution.py:282
  230.3 2.2 collective-permute-start.42
  234.7 4.2 %collective-permute-done.42 = bf16[256,512]{1,0:T(8,128)(2,1)S(1)} collective-permute-done((bf16[256,512]{1,0:T(8,128)(2,1)S(1)}, bf16[256,512]{1,0:T(8,128)(2,1)S(1)}, u32[]{:S(2)}, u32[]{:S(2)}) %collective-permute-start.42) | collective-permute-done | bytes 262176 | tf_op jit(solution)/shard_map/ppermute | solution.py:282
  (300 shorter events, 93.1 us)
Async XLA Ops:
  0.7 20.0 %collective-permute-start = (bf16[4,64,512]{2,1,0:T(8,128)(2,1)}, bf16[4,64,512]{2,1,0:T(8,128)(2,1)S(1)}, u32[]{:S(2)}, u32[]{:S(2)}) collective-permute-start(bf16[4,64,512]{2,1,0:T(8,128)(2,1)} %own_ref.1), channel_id=1, source_target_pairs={{0,1},{1,0},{2,3},{3,2},{4,5},{5,4},{6,7},{7,6},{8,9},{9,8},{10,11... | collective-permute-start | bytes 786440 | tf_op jit(solution)/shard_map/ppermute | solution.py:282
  3.8 18.4 %collective-permute-start.2 = (bf16[4,64,512]{2,1,0:T(8,128)(2,1)}, bf16[4,64,512]{2,1,0:T(8,128)(2,1)S(1)}, u32[]{:S(2)}, u32[]{:S(2)}) collective-permute-start(bf16[4,64,512]{2,1,0:T(8,128)(2,1)} %own_ref.1), channel_id=1, source_target_pairs={{0,3},{1,2},{2,1},{3,0},{4,7},{5,6},{6,5},{7,4},{8,11},{9,10},{10,... | collective-permute-start | bytes 786440 | tf_op jit(solution)/shard_map/ppermute | solution.py:282
  20.7 8.0 %collective-permute-start.1 = (bf16[2,64,512]{2,1,0:T(8,128)(2,1)S(1)}, bf16[2,64,512]{2,1,0:T(8,128)(2,1)S(1)}, u32[]{:S(2)}, u32[]{:S(2)}) collective-permute-start(bf16[2,64,512]{2,1,0:T(8,128)(2,1)S(1)} %slice.104), channel_id=1, source_target_pairs={{0,3},{1,2},{2,1},{3,0},{4,7},{5,6},{6,5},{7,4},{8,11},{9,10},{10,... | collective-permute-start | bytes 393224 | tf_op jit(solution)/shard_map/ppermute | solution.py:282
  22.1 7.3 %collective-permute-start.3 = (bf16[2,64,512]{2,1,0:T(8,128)(2,1)S(1)}, bf16[2,64,512]{2,1,0:T(8,128)(2,1)S(1)}, u32[]{:S(2)}, u32[]{:S(2)}) collective-permute-start(bf16[2,64,512]{2,1,0:T(8,128)(2,1)S(1)} %slice.105), channel_id=1, source_target_pairs={{0,1},{1,0},{2,3},{3,2},{4,5},{5,4},{6,7},{7,6},{8,9},{9,8},{10,11... | collective-permute-start | bytes 393224 | tf_op jit(solution)/shard_map/ppermute | solution.py:282
  107.0 20.4 %collective-permute-start.13 = (bf16[2,2,64,512]{3,2,1,0:T(8,128)(2,1)S(1)}, bf16[2,2,64,512]{3,2,1,0:T(8,128)(2,1)S(1)}, u32[]{:S(2)}, u32[]{:S(2)}) collective-permute-start(bf16[2,2,64,512]{3,2,1,0:T(8,128)(2,1)S(1)} %fusion.32), channel_id=1, source_target_pairs={{0,4},{4,0},{8,12},{12,8},{16,20},{20,16},{24,28},{28,24},{1,5},{5... | collective-permute-start | bytes 786440 | tf_op jit(solution)/shard_map/ppermute | solution.py:282
  107.5 20.8 %collective-permute-start.28 = (bf16[2,2,64,512]{3,2,1,0:T(8,128)(2,1)S(1)}, bf16[2,2,64,512]{3,2,1,0:T(8,128)(2,1)S(1)}, u32[]{:S(2)}, u32[]{:S(2)}) collective-permute-start(bf16[2,2,64,512]{3,2,1,0:T(8,128)(2,1)S(1)} %fusion.35), channel_id=1, source_target_pairs={{0,4},{4,0},{8,12},{12,8},{16,20},{20,16},{24,28},{28,24},{1,5},{5... | collective-permute-start | bytes 786440 | tf_op jit(solution)/shard_map/ppermute | solution.py:282
  109.6 26.1 %collective-permute-start.23 = (bf16[2,2,64,512]{3,2,1,0:T(8,128)(2,1)S(1)}, bf16[2,2,64,512]{3,2,1,0:T(8,128)(2,1)S(1)}, u32[]{:S(2)}, u32[]{:S(2)}) collective-permute-start(bf16[2,2,64,512]{3,2,1,0:T(8,128)(2,1)S(1)} %fusion.34), channel_id=1, source_target_pairs={{0,4},{4,0},{8,12},{12,8},{16,20},{20,16},{24,28},{28,24},{1,5},{5... | collective-permute-start | bytes 786440 | tf_op jit(solution)/shard_map/ppermute | solution.py:282
  110.0 27.3 %collective-permute-start.18 = (bf16[2,2,64,512]{3,2,1,0:T(8,128)(2,1)S(1)}, bf16[2,2,64,512]{3,2,1,0:T(8,128)(2,1)S(1)}, u32[]{:S(2)}, u32[]{:S(2)}) collective-permute-start(bf16[2,2,64,512]{3,2,1,0:T(8,128)(2,1)S(1)} %fusion.33), channel_id=1, source_target_pairs={{0,4},{4,0},{8,12},{12,8},{16,20},{20,16},{24,28},{28,24},{1,5},{5... | collective-permute-start | bytes 786440 | tf_op jit(solution)/shard_map/ppermute | solution.py:282
  112.9 10.6 %collective-permute-start.6 = (bf16[2,2,64,512]{3,2,1,0:T(8,128)(2,1)S(1)}, bf16[2,2,64,512]{3,2,1,0:T(8,128)(2,1)S(1)}, u32[]{:S(2)}, u32[]{:S(2)}) collective-permute-start(bf16[2,2,64,512]{3,2,1,0:T(8,128)(2,1)S(1)} %pad_maximum_fusion.4), channel_id=1, source_target_pairs={{0,3},{1,2},{2,1},{3,0},{4,7},{5,6},{6,5},{7,4},{8,11},{9,10},{10,... | collective-permute-start | bytes 786440 | tf_op jit(solution)/shard_map/ppermute | solution.py:282
  123.4 10.0 %collective-permute-start.4 = (bf16[2,2,64,512]{3,2,1,0:T(8,128)(2,1)S(1)}, bf16[2,2,64,512]{3,2,1,0:T(8,128)(2,1)S(1)}, u32[]{:S(2)}, u32[]{:S(2)}) collective-permute-start(bf16[2,2,64,512]{3,2,1,0:T(8,128)(2,1)S(1)} %pad_maximum_fusion.3), channel_id=1, source_target_pairs={{0,1},{1,0},{2,3},{3,2},{4,5},{5,4},{6,7},{7,6},{8,9},{9,8},{10,11... | collective-permute-start | bytes 786440 | tf_op jit(solution)/shard_map/ppermute | solution.py:282
  127.4 69.8 %collective-permute-start.33 = (bf16[2,2,64,2048]{3,2,1,0:T(8,128)(2,1)}, bf16[2,2,64,2048]{3,2,1,0:T(8,128)(2,1)}, u32[]{:S(2)}, u32[]{:S(2)}) collective-permute-start(bf16[2,2,64,2048]{3,2,1,0:T(8,128)(2,1)} %fusion.22), channel_id=1, source_target_pairs={{0,4},{4,0},{8,12},{12,8},{16,20},{20,16},{24,28},{28,24},{1,5},{5... | collective-permute-start | bytes 3145736 | tf_op jit(solution)/shard_map/ppermute | solution.py:282
  128.3 72.2 %collective-permute-start.38 = (bf16[2,2,256,512]{3,2,1,0:T(8,128)(2,1)S(1)}, bf16[2,2,256,512]{3,2,1,0:T(8,128)(2,1)}, u32[]{:S(2)}, u32[]{:S(2)}) collective-permute-start(bf16[2,2,256,512]{3,2,1,0:T(8,128)(2,1)S(1)} %fusion.21), channel_id=1, source_target_pairs={{0,4},{4,0},{8,12},{12,8},{16,20},{20,16},{24,28},{28,24},{1,5},{5... | collective-permute-start | bytes 3145736 | tf_op jit(solution)/shard_map/ppermute | solution.py:282
  133.4 20.2 %collective-permute-start.14 = (bf16[2,64,512]{2,1,0:T(8,128)(2,1)}, bf16[2,64,512]{2,1,0:T(8,128)(2,1)}, u32[]{:S(2)}, u32[]{:S(2)}) collective-permute-start(bf16[2,64,512]{2,1,0:T(8,128)(2,1)} %fusion.46), channel_id=1, source_target_pairs={{0,8},{4,12},{8,0},{12,4},{16,24},{20,28},{24,16},{28,20},{1,9},{5... | collective-permute-start | bytes 393224 | tf_op jit(solution)/shard_map/ppermute | solution.py:282
  135.7 19.6 %collective-permute-start.29 = (bf16[2,64,512]{2,1,0:T(8,128)(2,1)}, bf16[2,64,512]{2,1,0:T(8,128)(2,1)}, u32[]{:S(2)}, u32[]{:S(2)}) collective-permute-start(bf16[2,64,512]{2,1,0:T(8,128)(2,1)} %fusion.49), channel_id=1, source_target_pairs={{0,16},{4,20},{8,24},{12,28},{16,0},{20,4},{24,8},{28,12},{1,17},{... | collective-permute-start | bytes 393224 | tf_op jit(solution)/shard_map/ppermute | solution.py:282
  142.4 6.9 %collective-permute-start.5 = (bf16[2,64,512]{2,1,0:T(8,128)(2,1)S(1)}, bf16[2,64,512]{2,1,0:T(8,128)(2,1)S(1)}, u32[]{:S(2)}, u32[]{:S(2)}) collective-permute-start(bf16[2,64,512]{2,1,0:T(8,128)(2,1)S(1)} %fusion.50), channel_id=1, source_target_pairs={{0,3},{1,2},{2,1},{3,0},{4,7},{5,6},{6,5},{7,4},{8,11},{9,10},{10,... | collective-permute-start | bytes 393224 | tf_op jit(solution)/shard_map/ppermute | solution.py:282
  149.2 8.7 %collective-permute-start.24 = (bf16[2,64,512]{2,1,0:T(8,128)(2,1)}, bf16[2,64,512]{2,1,0:T(8,128)(2,1)}, u32[]{:S(2)}, u32[]{:S(2)}) collective-permute-start(bf16[2,64,512]{2,1,0:T(8,128)(2,1)} %fusion.48), channel_id=1, source_target_pairs={{0,16},{4,20},{8,24},{12,28},{16,0},{20,4},{24,8},{28,12},{1,17},{... | collective-permute-start | bytes 393224 | tf_op jit(solution)/shard_map/ppermute | solution.py:282
  153.6 10.7 %collective-permute-start.19 = (bf16[2,64,512]{2,1,0:T(8,128)(2,1)S(1)}, bf16[2,64,512]{2,1,0:T(8,128)(2,1)S(1)}, u32[]{:S(2)}, u32[]{:S(2)}) collective-permute-start(bf16[2,64,512]{2,1,0:T(8,128)(2,1)S(1)} %fusion.47), channel_id=1, source_target_pairs={{0,8},{4,12},{8,0},{12,4},{16,24},{20,28},{24,16},{28,20},{1,9},{5... | collective-permute-start | bytes 393224 | tf_op jit(solution)/shard_map/ppermute | solution.py:282
  155.2 23.8 %collective-permute-start.15 = (bf16[64,512]{1,0:T(8,128)(2,1)S(1)}, bf16[64,512]{1,0:T(8,128)(2,1)S(1)}, u32[]{:S(2)}, u32[]{:S(2)}) collective-permute-start(bf16[64,512]{1,0:T(8,128)(2,1)S(1)} %fusion.56), channel_id=1, source_target_pairs={{0,16},{4,20},{8,24},{12,28},{16,0},{20,4},{24,8},{28,12},{1,17},{... | collective-permute-start | bytes 196616 | tf_op jit(solution)/shard_map/ppermute | solution.py:282
  162.9 16.7 %collective-permute-start.30 = (bf16[64,512]{1,0:T(8,128)(2,1)S(1)}, bf16[64,512]{1,0:T(8,128)(2,1)S(1)}, u32[]{:S(2)}, u32[]{:S(2)}) collective-permute-start(bf16[64,512]{1,0:T(8,128)(2,1)S(1)} %fusion.59), channel_id=1, source_target_pairs={{0,8},{4,12},{8,0},{12,4},{16,24},{20,28},{24,16},{28,20},{1,9},{5... | collective-permute-start | bytes 196616 | tf_op jit(solution)/shard_map/ppermute | solution.py:282
  181.5 6.4 %collective-permute-start.31 = (bf16[64,512]{1,0:T(8,128)(2,1)S(1)}, bf16[64,512]{1,0:T(8,128)(2,1)S(1)}, u32[]{:S(2)}, u32[]{:S(2)}) collective-permute-start(bf16[64,512]{1,0:T(8,128)(2,1)S(1)} %fusion.52), channel_id=1, source_target_pairs={{0,3},{1,2},{2,1},{3,0},{4,7},{5,6},{6,5},{7,4},{8,11},{9,10},{10,... | collective-permute-start | bytes 196616 | tf_op jit(solution)/shard_map/ppermute | solution.py:282
  183.9 6.5 %collective-permute-start.26 = (bf16[64,512]{1,0:T(8,128)(2,1)S(1)}, bf16[64,512]{1,0:T(8,128)(2,1)S(1)}, u32[]{:S(2)}, u32[]{:S(2)}) collective-permute-start(bf16[64,512]{1,0:T(8,128)(2,1)S(1)} %fusion.53), channel_id=1, source_target_pairs={{0,3},{1,2},{2,1},{3,0},{4,7},{5,6},{6,5},{7,4},{8,11},{9,10},{10,... | collective-permute-start | bytes 196616 | tf_op jit(solution)/shard_map/ppermute | solution.py:282
  190.5 9.4 %collective-permute-start.32 = (bf16[64,512]{1,0:T(8,128)(2,1)S(1)}, bf16[64,512]{1,0:T(8,128)(2,1)S(1)}, u32[]{:S(2)}, u32[]{:S(2)}) collective-permute-start(bf16[64,512]{1,0:T(8,128)(2,1)S(1)} %add_convert_fusion.4), channel_id=1, source_target_pairs={{0,1},{1,0},{2,3},{3,2},{4,5},{5,4},{6,7},{7,6},{8,9},{9,8},{10,11... | collective-permute-start | bytes 196616 | tf_op jit(solution)/shard_map/ppermute | solution.py:282
  191.5 27.6 %collective-permute-start.27 = (bf16[64,512]{1,0:T(8,128)(2,1)S(1)}, bf16[64,512]{1,0:T(8,128)(2,1)S(1)}, u32[]{:S(2)}, u32[]{:S(2)}) collective-permute-start(bf16[64,512]{1,0:T(8,128)(2,1)S(1)} %add_convert_fusion.5), channel_id=1, source_target_pairs={{0,1},{1,0},{2,3},{3,2},{4,5},{5,4},{6,7},{7,6},{8,9},{9,8},{10,11... | collective-permute-start | bytes 196616 | tf_op jit(solution)/shard_map/ppermute | solution.py:282
  194.0 35.6 %collective-permute-start.22 = (bf16[64,512]{1,0:T(8,128)(2,1)S(1)}, bf16[64,512]{1,0:T(8,128)(2,1)S(1)}, u32[]{:S(2)}, u32[]{:S(2)}) collective-permute-start(bf16[64,512]{1,0:T(8,128)(2,1)S(1)} %add_convert_fusion.6), channel_id=1, source_target_pairs={{0,3},{1,2},{2,1},{3,0},{4,7},{5,6},{6,5},{7,4},{8,11},{9,10},{10,... | collective-permute-start | bytes 196616 | tf_op jit(solution)/shard_map/ppermute | solution.py:282
  199.1 12.1 %collective-permute-start.34 = (bf16[2,64,2048]{2,1,0:T(8,128)(2,1)S(1)}, bf16[2,64,2048]{2,1,0:T(8,128)(2,1)S(1)}, u32[]{:S(2)}, u32[]{:S(2)}) collective-permute-start(bf16[2,64,2048]{2,1,0:T(8,128)(2,1)S(1)} %fusion.26), channel_id=1, source_target_pairs={{0,16},{4,20},{8,24},{12,28},{16,0},{20,4},{24,8},{28,12},{1,17},{... | collective-permute-start | bytes 1572872 | tf_op jit(solution)/shard_map/ppermute | solution.py:282
  202.2 9.9 %collective-permute-start.39 = (bf16[2,256,512]{2,1,0:T(8,128)(2,1)S(1)}, bf16[2,256,512]{2,1,0:T(8,128)(2,1)S(1)}, u32[]{:S(2)}, u32[]{:S(2)}) collective-permute-start(bf16[2,256,512]{2,1,0:T(8,128)(2,1)S(1)} %fusion.27), channel_id=1, source_target_pairs={{0,8},{4,12},{8,0},{12,4},{16,24},{20,28},{24,16},{28,20},{1,9},{5... | collective-permute-start | bytes 1572872 | tf_op jit(solution)/shard_map/ppermute | solution.py:282
  211.3 6.4 %collective-permute-start.35 = (bf16[64,2048]{1,0:T(8,128)(2,1)S(1)}, bf16[64,2048]{1,0:T(8,128)(2,1)S(1)}, u32[]{:S(2)}, u32[]{:S(2)}) collective-permute-start(bf16[64,2048]{1,0:T(8,128)(2,1)S(1)} %fusion.36), channel_id=1, source_target_pairs={{0,8},{4,12},{8,0},{12,4},{16,24},{20,28},{24,16},{28,20},{1,9},{5... | collective-permute-start | bytes 786440 | tf_op jit(solution)/shard_map/ppermute | solution.py:282
  212.4 7.4 %collective-permute-start.40 = (bf16[256,512]{1,0:T(8,128)(2,1)S(1)}, bf16[256,512]{1,0:T(8,128)(2,1)S(1)}, u32[]{:S(2)}, u32[]{:S(2)}) collective-permute-start(bf16[256,512]{1,0:T(8,128)(2,1)S(1)} %fusion.37), channel_id=1, source_target_pairs={{0,16},{4,20},{8,24},{12,28},{16,0},{20,4},{24,8},{28,12},{1,17},{... | collective-permute-start | bytes 786440 | tf_op jit(solution)/shard_map/ppermute | solution.py:282
  217.8 8.5 %collective-permute-start.36 = (bf16[64,2048]{1,0:T(8,128)(2,1)S(1)}, bf16[64,2048]{1,0:T(8,128)(2,1)S(1)}, u32[]{:S(2)}, u32[]{:S(2)}) collective-permute-start(bf16[64,2048]{1,0:T(8,128)(2,1)S(1)} %fusion.29), channel_id=1, source_target_pairs={{0,3},{1,2},{2,1},{3,0},{4,7},{5,6},{6,5},{7,4},{8,11},{9,10},{10,... | collective-permute-start | bytes 786440 | tf_op jit(solution)/shard_map/ppermute | solution.py:282
  219.8 10.4 %collective-permute-start.41 = (bf16[256,512]{1,0:T(8,128)(2,1)S(1)}, bf16[256,512]{1,0:T(8,128)(2,1)S(1)}, u32[]{:S(2)}, u32[]{:S(2)}) collective-permute-start(bf16[256,512]{1,0:T(8,128)(2,1)S(1)} %fusion.28), channel_id=1, source_target_pairs={{0,1},{1,0},{2,3},{3,2},{4,5},{5,4},{6,7},{7,6},{8,9},{9,8},{10,11... | collective-permute-start | bytes 786440 | tf_op jit(solution)/shard_map/ppermute | solution.py:282
  226.4 7.5 %collective-permute-start.37 = (bf16[64,2048]{1,0:T(8,128)(2,1)S(1)}, bf16[64,2048]{1,0:T(8,128)(2,1)S(1)}, u32[]{:S(2)}, u32[]{:S(2)}) collective-permute-start(bf16[64,2048]{1,0:T(8,128)(2,1)S(1)} %add_convert_fusion.1), channel_id=1, source_target_pairs={{0,1},{1,0},{2,3},{3,2},{4,5},{5,4},{6,7},{7,6},{8,9},{9,8},{10,11... | collective-permute-start | bytes 786440 | tf_op jit(solution)/shard_map/ppermute | solution.py:282
  230.3 8.7 %collective-permute-start.42 = (bf16[256,512]{1,0:T(8,128)(2,1)S(1)}, bf16[256,512]{1,0:T(8,128)(2,1)S(1)}, u32[]{:S(2)}, u32[]{:S(2)}) collective-permute-start(bf16[256,512]{1,0:T(8,128)(2,1)S(1)} %add_convert_fusion), channel_id=1, source_target_pairs={{0,3},{1,2},{2,1},{3,0},{4,7},{5,6},{6,5},{7,4},{8,11},{9,10},{10,... | collective-permute-start | bytes 786440 | tf_op jit(solution)/shard_map/ppermute | solution.py:282
  (61 other events, 408.0 us)

commit v2 on v1

v2 whole, which is shorter than its diff:
```python
import functools
import math

import jax
import jax.numpy as jnp
from jax import lax
from jax.experimental import pallas as pl
from jax.experimental.pallas import tpu as pltpu
from jax.sharding import PartitionSpec as P

EPSILON = 1e-05
MASKED = -1000000000.0
F32 = jnp.float32
BF16 = jnp.bfloat16
LANES = 128
STAGES = 2
VMEM_LIMIT = 56 << 20


def shape_of(shape, dtype):
    return jax.ShapeDtypeStruct(tuple(shape), dtype)


def norm_forward(values_in, gain, shift):
    centre = values_in - jnp.mean(values_in, -1, keepdims=True)
    inverse = lax.rsqrt(jnp.mean(centre * centre, -1, keepdims=True) + EPSILON)
    normed = centre * inverse
    return (normed * gain + shift, normed, inverse)


def norm_backward(upstream, normed, inverse, gain):
    scaled = upstream * gain
    return inverse * (
        scaled
        - jnp.mean(scaled, -1, keepdims=True)
        - normed * jnp.mean(scaled * normed, -1, keepdims=True)
    )


def dot(left, right):
    return jnp.dot(left, right, preferred_element_type=F32)


def across(left, right):
    return lax.dot_general(left, right, (((0,), (0,)), ((), ())), preferred_element_type=F32)


def against(left, right):
    return lax.dot_general(left, right, (((1,), (1,)), ((), ())), preferred_element_type=F32)


def column_sum(values_in):
    return jnp.sum(values_in.astype(F32), 0, keepdims=True)


def whole(array):
    return pl.BlockSpec(array.shape, lambda *_: (0,) * array.ndim)


def params(**extra):
    return pltpu.CompilerParams(vmem_limit_bytes=VMEM_LIMIT, **extra)


def forward_kernel(
    head_size,
    chunk,
    place_ref,
    length_ref,
    own_ref,
    one_ref,
    two_ref,
    three_ref,
    pair_ref,
    gain_ref,
    shift_ref,
    query_weight_ref,
    query_bias_ref,
    key_weight_ref,
    value_weight_ref,
    value_bias_ref,
    _,
    pair_out_ref,
    weights_ref,
    mixed_ref,
    inverse_ref,
    hidden_ref,
    normed_ref,
    query_ref,
    key_ref,
    value_ref,
    atoms_scratch,
    query_scratch,
    key_scratch,
    value_scratch,
    *,
    first,
):
    molecule = pl.program_id(0)
    group = pl.program_id(1)
    groups, keys, width = key_scratch.shape
    heads = width // head_size
    rows = own_ref.shape[1]
    factor = head_size**-0.5
    row = place_ref[1]

    @pl.when(group == 0)
    def _():
        for i, piece in enumerate((own_ref, one_ref, two_ref, three_ref)):
            start = pl.multiple_of((row ^ i) * rows, rows)
            atoms_scratch[pl.ds(start, rows)] = piece[0]
        gain = gain_ref[...].astype(F32)
        shift = shift_ref[...].astype(F32)
        hidden, normed, _ = norm_forward(atoms_scratch[...].astype(F32), gain, shift)
        hidden = hidden.astype(BF16)
        hidden_ref[0] = hidden
        normed_ref[0] = normed.astype(BF16)
        key_rows = dot(hidden, key_weight_ref[...]).astype(BF16)
        value_rows = dot(hidden, value_weight_ref[...]) + value_bias_ref[...].astype(F32)
        value_rows = value_rows.astype(BF16)
        own = norm_forward(own_ref[0].astype(F32), gain, shift)[0].astype(BF16)
        query_rows = dot(own, query_weight_ref[...]) + query_bias_ref[...].astype(F32)
        query_rows = (query_rows * factor).astype(BF16)
        ones = jnp.ones((keys, width), BF16)
        for t in range(groups):
            lanes = slice(t * width, (t + 1) * width)
            key_scratch[t] = key_rows[:, lanes]
            query_scratch[t] = query_rows[:, lanes]
            value_scratch[t, :, :width] = value_rows[:, lanes]
            value_scratch[t, :, width:] = ones

    query = query_scratch[group]
    key = key_scratch[group]
    value = value_scratch[group]
    query_ref[...] = query[None]
    key_ref[...] = key[None]
    value_ref[...] = value[None]
    valid = lax.broadcasted_iota(jnp.int32, (1, keys), 1) < length_ref[molecule + first]
    lane = lax.broadcasted_iota(jnp.int32, (1, width), 1) // head_size
    lane_pair = lax.broadcasted_iota(jnp.int32, (1, 2 * width), 1) % width // head_size
    total = jnp.zeros((rows, 2 * width), F32)
    zero = jnp.zeros((), BF16)
    for c in range(0, heads, chunk):
        here = slice(c, c + chunk)
        spread = jnp.concatenate([jnp.where(lane == c + t, query, zero) for t in range(chunk)], 0)
        scores = against(spread, key) + pair_ref[0, here].reshape(chunk * rows, keys).astype(F32)
        pair_out_ref[0, here] = scores.astype(BF16).reshape(chunk, rows, keys)
        masked = jnp.where(valid, scores, MASKED)
        weights = jnp.exp(masked - jnp.max(masked, -1, keepdims=True)).astype(BF16)
        weights_ref[0, here] = weights.reshape(chunk, rows, keys)
        product = dot(weights, value)
        for t in range(chunk):
            total = jnp.where(lane_pair == c + t, product[t * rows : (t + 1) * rows], total)
    inverse = 1.0 / total[:, width:]
    inverse_ref[...] = inverse[None]
    mixed_ref[...] = (total[:, :width] * inverse)[None]


def attention_forward(head_size, first, count, place, lengths, pieces, pair_bias, parameters, held):
    _, _, rows, keys = pair_bias.shape
    model_width = pieces[0].shape[2]
    groups = model_width // LANES
    heads = LANES // head_size
    pair_spec = pl.BlockSpec((1, heads, rows, keys), lambda m, g, *_: (m + first, g, 0, 0))
    stage_spec = pl.BlockSpec((1, heads, rows, keys), lambda m, g, *_: (m, g, 0, 0))
    row_spec = pl.BlockSpec((1, rows, LANES), lambda m, g, *_: (m, 0, g))
    all_spec = pl.BlockSpec((1, keys, model_width), lambda m, g, *_: (m, 0, 0))
    piece_specs = [
        pl.BlockSpec(
            (1, rows, model_width), lambda m, g, *_, base=first if i == 0 else 0: (m + base, 0, 0)
        )
        for i in range(len(pieces))
    ]
    token_shape = (count, rows, model_width)
    key_shape = (count, keys, model_width)
    elements = count * pair_bias.shape[1] * rows * keys
    operands = (place, lengths, *pieces, pair_bias, *parameters, held)
    return pl.pallas_call(
        functools.partial(forward_kernel, head_size, 4, first=first),
        grid_spec=pltpu.PrefetchScalarGridSpec(
            num_scalar_prefetch=2,
            grid=(count, groups),
            in_specs=piece_specs
            + [pair_spec]
            + [whole(a) for a in parameters]
            + [pl.BlockSpec(memory_space=pl.ANY)],
            out_specs=[
                pair_spec,
                stage_spec,
                row_spec,
                row_spec,
                all_spec,
                all_spec,
                row_spec,
                pl.BlockSpec((1, keys, LANES), lambda m, g, *_: (m, 0, g)),
                pl.BlockSpec((1, keys, 2 * LANES), lambda m, g, *_: (m, 0, g)),
            ],
            scratch_shapes=[
                pltpu.VMEM((keys, model_width), BF16),
                pltpu.VMEM((groups, rows, LANES), BF16),
                pltpu.VMEM((groups, keys, LANES), BF16),
                pltpu.VMEM((groups, keys, 2 * LANES), BF16),
            ],
        ),
        out_shape=[
            shape_of(pair_bias.shape, BF16),
            shape_of((count,) + pair_bias.shape[1:], BF16),
            shape_of(token_shape, F32),
            shape_of(token_shape, F32),
            shape_of(key_shape, BF16),
            shape_of(key_shape, BF16),
            shape_of(token_shape, BF16),
            shape_of(key_shape, BF16),
            shape_of((count, keys, 2 * model_width), BF16),
        ],
        input_output_aliases={} if held.ndim == 1 else {len(operands) - 1: 0},
        compiler_params=params(),
        cost_estimate=pl.CostEstimate(
            flops=elements * 2 * 384, transcendentals=elements, bytes_accessed=elements * 6
        ),
        name="attention_forward",
    )(*operands)


def dense_kernel(
    mixed_count,
    place_ref,
    *refs,
):
    mixed_refs = refs[:mixed_count]
    (
        atoms_ref,
        cotangent_ref,
        out_weight_ref,
        out_bias_ref,
        gain_ref,
        shift_ref,
        inner_weight_ref,
        inner_bias_ref,
        outer_weight_ref,
        outer_bias_ref,
        atoms_out_ref,
        outer_send_ref,
        outer_keep_ref,
        inner_send_ref,
        inner_keep_ref,
        out_send_ref,
        out_keep_ref,
        grad_middle_ref,
        grad_mixed_ref,
        vectors_ref,
        hidden_scratch,
        turned_scratch,
        normed_scratch,
        inverse_scratch,
        result_scratch,
        upstream_scratch,
        outer_scratch,
        inner_scratch,
    ) = refs[mixed_count:]
    step = pl.program_id(0)
    steps = pl.num_programs(0)
    core = place_ref[2]
    tokens, model_width = hidden_scratch.shape
    cotangent = cotangent_ref[...].reshape(tokens, model_width)

    def mixed_rows():
        return jnp.concatenate([m[...].reshape(-1, model_width) for m in mixed_refs], 0)

    @pl.when(step == 0)
    def _():
        mixed_low = mixed_rows().astype(BF16)
        middle = (
            atoms_ref[...].reshape(tokens, model_width).astype(F32)
            + dot(mixed_low, out_weight_ref[...])
            + out_bias_ref[...].astype(F32)
        )
        hidden, normed, inverse = norm_forward(
            middle, gain_ref[...].astype(F32), shift_ref[...].astype(F32)
        )
        hidden_scratch[...] = hidden.astype(BF16)
        turned_scratch[...] = jnp.transpose(hidden).astype(BF16)
        normed_scratch[...] = normed
        inverse_scratch[...] = inverse
        result_scratch[...] = middle + outer_bias_ref[...].astype(F32)
        upstream_scratch[...] = jnp.zeros_like(upstream_scratch)
        vectors_ref[0:1] = column_sum(cotangent)

    hidden = hidden_scratch[...]
    pre = dot(hidden, inner_weight_ref[...]) + inner_bias_ref[...].astype(F32)
    slope = math.sqrt(2.0 / math.pi)
    square = pre * pre
    tanh = jnp.tanh(slope * (pre + 0.044715 * (pre * square)))
    half = 0.5 * (1.0 + tanh)
    active = (pre * half).astype(BF16)
    result_scratch[...] += dot(active, outer_weight_ref[...])
    derivative = half + (0.5 * slope) * pre * (1.0 - tanh * tanh) * (1.0 + 0.134145 * square)
    grad_pre = against(cotangent, outer_weight_ref[...]) * derivative
    vectors_ref[pl.ds(4 + step, 1)] = column_sum(grad_pre.astype(BF16))
    grad_pre = grad_pre.astype(BF16)
    outer_scratch[...] = across(active, cotangent).reshape(outer_scratch.shape)
    outer_send_ref[...] = outer_scratch[:, 1 - core].astype(BF16).reshape(outer_send_ref.shape)
    outer_keep_ref[...] = outer_scratch[:, core].astype(BF16).reshape(outer_keep_ref.shape)
    inner_scratch[...] = dot(turned_scratch[...], grad_pre).reshape(inner_scratch.shape)
    inner_send_ref[:, 0] = inner_scratch[:, 1 - core].astype(BF16)
    inner_keep_ref[:, 0] = inner_scratch[:, core].astype(BF16)
    upstream_scratch[...] += against(grad_pre, inner_weight_ref[...])

    @pl.when(step == steps - 1)
    def _():
        atoms_out_ref[...] = result_scratch[...].astype(BF16).reshape(atoms_out_ref.shape)
        upstream = upstream_scratch[...]
        normed = normed_scratch[...]
        vectors_ref[1:2] = column_sum(upstream * normed)
        vectors_ref[2:3] = column_sum(upstream)
        grad_middle = cotangent.astype(F32) + norm_backward(
            upstream, normed, inverse_scratch[...], gain_ref[...].astype(F32)
        )
        grad_middle_ref[...] = grad_middle.reshape(grad_middle_ref.shape)
        branch = grad_middle.astype(BF16)
        vectors_ref[3:4] = column_sum(branch)
        grad_mixed = against(branch, out_weight_ref[...]).astype(BF16)
        grad_mixed_ref[...] = grad_mixed.reshape(grad_mixed_ref.shape)
        turned = jnp.transpose(mixed_rows()).astype(BF16)
        inner_scratch[...] = dot(turned, branch).reshape(inner_scratch.shape)
        out_send_ref[...] = inner_scratch[:, 1 - core].astype(BF16)
        out_keep_ref[...] = inner_scratch[:, core].astype(BF16)


def dense(place, mixed, atoms, cotangent, parameters, batch_count):
    (
        out_weight,
        out_bias,
        gain,
        shift,
        inner_weight,
        inner_bias,
        outer_weight,
        outer_bias,
    ) = parameters
    model_width, inner_width = inner_weight.shape
    tokens = atoms.shape[0] * atoms.shape[1]
    width = model_width
    steps = inner_width // width
    pairs = batch_count // 2
    outer_rows = inner_width // batch_count
    outer_pairs = width // (2 * outer_rows)
    own_rows = model_width // batch_count
    operands = (
        place,
        *mixed,
        atoms,
        cotangent,
        out_weight,
        out_bias,
        gain,
        shift,
        inner_weight,
        inner_bias,
        outer_weight,
        outer_bias,
    )
    outer_spec = pl.BlockSpec((outer_pairs, outer_rows, model_width), lambda s, *_: (s, 0, 0))
    inner_spec = pl.BlockSpec((pairs, 1, own_rows, width), lambda s, *_: (0, s, 0, 0))
    outer_shape = shape_of((pairs, outer_rows, model_width), BF16)
    inner_shape = shape_of((pairs, steps, own_rows, width), BF16)
    out_shape = shape_of((pairs, own_rows, model_width), BF16)
    out_shapes = [
        shape_of(atoms.shape, BF16),
        outer_shape,
        outer_shape,
        inner_shape,
        inner_shape,
        out_shape,
        out_shape,
        shape_of(atoms.shape, F32),
        shape_of(atoms.shape, BF16),
        shape_of((4 + steps, model_width), F32),
    ]
    fixed = lambda s: pl.BlockSpec(s.shape, lambda *_: (0,) * len(s.shape))
    out_specs = [fixed(s) for s in out_shapes]
    out_specs[1:5] = [outer_spec, outer_spec, inner_spec, inner_spec]
    in_specs = [whole(a) for a in operands[1:]]
    in_specs[-4] = pl.BlockSpec((model_width, width), lambda s, *_: (0, s))
    in_specs[-3] = pl.BlockSpec((1, width), lambda s, *_: (0, s))
    in_specs[-2] = pl.BlockSpec((width, model_width), lambda s, *_: (s, 0))
    return pl.pallas_call(
        functools.partial(dense_kernel, len(mixed)),
        grid_spec=pltpu.PrefetchScalarGridSpec(
            num_scalar_prefetch=1,
            grid=(steps,),
            in_specs=in_specs,
            out_specs=out_specs,
            scratch_shapes=[
                pltpu.VMEM((tokens, model_width), BF16),
                pltpu.VMEM((model_width, tokens), BF16),
                pltpu.VMEM((tokens, model_width), F32),
                pltpu.VMEM((tokens, 1), F32),
                pltpu.VMEM((tokens, model_width), F32),
                pltpu.VMEM((tokens, model_width), F32),
                pltpu.VMEM((outer_pairs, 2, outer_rows, model_width), F32),
                pltpu.VMEM((pairs, 2, own_rows, width), F32),
            ],
        ),
        out_shape=out_shapes,
        compiler_params=params(),
        cost_estimate=pl.CostEstimate(
            flops=12 * tokens * model_width * inner_width,
            transcendentals=tokens * inner_width,
            bytes_accessed=12 * model_width * inner_width,
        ),
        name="dense",
    )(*operands)


def backward_kernel(
    head_size,
    chunk,
    place_ref,
    weights_ref,
    cotangent_ref,
    grad_mixed_ref,
    mixed_ref,
    inverse_ref,
    query_ref,
    key_ref,
    value_ref,
    hidden_ref,
    normed_ref,
    query_weight_ref,
    key_weight_ref,
    value_weight_ref,
    _after,
    _held,
    pair_grad_ref,
    near_ref,
    cross_ref,
    own_ref,
    send_ref,
    keep_ref,
    vectors_ref,
    grad_query_scratch,
    grad_key_scratch,
    grad_value_scratch,
    total_scratch,
    grad_scratch,
):
    molecule = pl.program_id(0)
    group = pl.program_id(1)
    rows, width = query_ref.shape[1:]
    keys = key_ref.shape[1]
    groups = grad_key_scratch.shape[0]
    heads = width // head_size
    factor = head_size**-0.5
    query = query_ref[0]
    key = key_ref[0]
    value = value_ref[0]
    upstream = (grad_mixed_ref[0].astype(F32) * inverse_ref[0]).astype(BF16)
    offset = (-(upstream.astype(F32) * mixed_ref[0])).astype(BF16)
    both = jnp.concatenate([upstream, offset], 1)
    lane = lax.broadcasted_iota(jnp.int32, (1, width), 1) // head_size
    lane_pair = lax.broadcasted_iota(jnp.int32, (1, 2 * width), 1) % width // head_size
    query_turned = jnp.transpose(query.astype(F32)).astype(BF16)
    upstream_turned = jnp.transpose(upstream.astype(F32)).astype(BF16)
    query_turned = jnp.concatenate([query_turned] * chunk, 1)
    upstream_turned = jnp.concatenate([upstream_turned] * chunk, 1)
    turned_shape = (chunk * head_size, chunk * rows)
    same = (
        lax.broadcasted_iota(jnp.int32, turned_shape, 0) // head_size
        == lax.broadcasted_iota(jnp.int32, turned_shape, 1) // rows
    )
    zero = jnp.zeros((), BF16)
    total = jnp.zeros((rows, width), F32)
    key_parts = []
    value_parts = []
    for c in range(0, heads, chunk):
        here = slice(c, c + chunk)
        feature = slice(c * head_size, (c + chunk) * head_size)
        spread = jnp.concatenate([jnp.where(lane_pair == c + t, both, zero) for t in range(chunk)], 0)
        centred = against(spread, value)
        weights = weights_ref[0, here].reshape(chunk * rows, keys)
        cotangent = cotangent_ref[0, here].reshape(chunk * rows, keys)
        grad = (weights.astype(F32) * centred + cotangent.astype(F32)).astype(BF16)
        pair_grad_ref[0, here] = grad.reshape(chunk, rows, keys)
        product = dot(grad, key)
        for t in range(chunk):
            total = jnp.where(lane == c + t, product[t * rows : (t + 1) * rows], total)
        key_parts.append(dot(jnp.where(same, query_turned[feature], zero), grad))
        value_parts.append(dot(jnp.where(same, upstream_turned[feature], zero), weights))
    grad_query_scratch[group] = (total * factor).astype(BF16)
    grad_key_scratch[group] = jnp.transpose(jnp.concatenate(key_parts, 0)).astype(BF16)
    grad_value_scratch[group] = jnp.transpose(jnp.concatenate(value_parts, 0)).astype(BF16)

    @pl.when((molecule == 0) & (group == 0))
    def _():
        total_scratch[...] = jnp.zeros_like(total_scratch)
        vectors_ref[...] = jnp.zeros_like(vectors_ref)

    @pl.when(group == groups - 1)
    def _():
        row = place_ref[1]
        mine = pl.ds(pl.multiple_of(row * rows, rows), rows)
        join = lambda ref: jnp.concatenate([ref[t] for t in range(groups)], 1)
        grad_query = join(grad_query_scratch)
        grad_key = join(grad_key_scratch)
        grad_value = join(grad_value_scratch)
        hidden_turned = jnp.transpose(hidden_ref[0].astype(F32)).astype(BF16)
        own_turned = jnp.transpose(hidden_ref[0, mine].astype(F32)).astype(BF16)
        part_shape = (total_scratch.shape[0],) + total_scratch.shape[2:]
        total_scratch[:, 0] += dot(own_turned, grad_query).reshape(part_shape)
        total_scratch[:, 1] += dot(hidden_turned, grad_key).reshape(part_shape)
        total_scratch[:, 2] += dot(hidden_turned, grad_value).reshape(part_shape)
        grad_scratch[...] = against(grad_key, key_weight_ref[...]) + against(
            grad_value, value_weight_ref[...]
        )
        grad_scratch[mine] += against(grad_query, query_weight_ref[...])
        grad = grad_scratch[...]
        vectors_ref[0:1] += column_sum(grad * normed_ref[0].astype(F32))
        vectors_ref[1:2] += column_sum(grad)
        vectors_ref[2:3] += column_sum(grad_query)
        vectors_ref[3:4] += column_sum(grad_value)
        at = lambda other: pl.ds(pl.multiple_of((row ^ other) * rows, rows), rows)
        near_ref[0, 0] = grad_scratch[at(1)].astype(BF16)
        near_ref[1, 0] = grad_scratch[at(3)].astype(BF16)
        cross_ref[0] = grad_scratch[at(2)].astype(BF16)
        own_ref[0] = grad_scratch[mine]

    @pl.when((molecule == pl.num_programs(0) - 1) & (group == groups - 1))
    def _():
        core = place_ref[2]
        pairs, parts, count = send_ref.shape[0], send_ref.shape[1], 2
        for i in range(pairs):
            for j in range(parts):
                send_ref[i, j] = total_scratch[i * count + (1 - core), j].astype(BF16)
                keep_ref[i, j] = total_scratch[i * count + core, j].astype(BF16)


def attention_backward(
    head_size,
    first,
    place,
    stage,
    cotangent,
    grad_mixed,
    parameters,
    held,
    batch_count,
    after,
):
    weights, mixed, inverse, hidden, normed, query, key, value = stage
    count, _, rows, keys = weights.shape
    model_width = query.shape[2]
    groups = model_width // LANES
    heads = LANES // head_size
    pairs = batch_count // 2
    own_rows = model_width // batch_count
    stage_spec = pl.BlockSpec((1, heads, rows, keys), lambda m, g, *_: (m, g, 0, 0))
    pair_spec = pl.BlockSpec((1, heads, rows, keys), lambda m, g, *_: (m + first, g, 0, 0))
    row_spec = pl.BlockSpec((1, rows, LANES), lambda m, g, *_: (m, 0, g))
    all_spec = pl.BlockSpec((1, keys, model_width), lambda m, g, *_: (m, 0, 0))
    part_shape = shape_of((pairs, 3, own_rows, model_width), BF16)
    part_spec = pl.BlockSpec(part_shape.shape, lambda m, g, *_: (0, 0, 0, 0))
    token_spec = pl.BlockSpec((1, rows, model_width), lambda m, g, *_: (m, 0, 0))
    elements = math.prod(weights.shape)
    operands = (
        place,
        weights,
        cotangent,
        grad_mixed,
        mixed,
        inverse,
        query,
        key,
        value,
        hidden,
        normed,
        *parameters,
        after,
        held,
    )
    return pl.pallas_call(
        functools.partial(backward_kernel, head_size, 4),
        grid_spec=pltpu.PrefetchScalarGridSpec(
            num_scalar_prefetch=1,
            grid=(count, groups),
            in_specs=[
                stage_spec,
                pair_spec,
                pl.BlockSpec((1, rows, LANES), lambda m, g, *_: (m + first, 0, g)),
                row_spec,
                row_spec,
                row_spec,
                pl.BlockSpec((1, keys, LANES), lambda m, g, *_: (m, 0, g)),
                pl.BlockSpec((1, keys, 2 * LANES), lambda m, g, *_: (m, 0, g)),
                all_spec,
                all_spec,
            ]
            + [whole(a) for a in parameters]
            + [pl.BlockSpec(memory_space=pl.ANY)] * 2,
            out_specs=[
                pair_spec,
                pl.BlockSpec((2, 1, rows, model_width), lambda m, g, *_: (0, m, 0, 0)),
                token_spec,
                token_spec,
                part_spec,
                part_spec,
                pl.BlockSpec((8, model_width), lambda m, g, *_: (0, 0)),
            ],
            scratch_shapes=[
                pltpu.VMEM((groups, rows, LANES), BF16),
                pltpu.VMEM((groups, keys, LANES), BF16),
                pltpu.VMEM((groups, keys, LANES), BF16),
                pltpu.VMEM((batch_count, 3, own_rows, model_width), F32),
                pltpu.VMEM((keys, model_width), F32),
            ],
        ),
        out_shape=[
            shape_of(cotangent.shape, BF16),
            shape_of((2, count, rows, model_width), BF16),
            shape_of((count, rows, model_width), BF16),
            shape_of((count, rows, model_width), F32),
            part_shape,
            part_shape,
            shape_of((8, model_width), F32),
        ],
        input_output_aliases={} if held.ndim == 1 else {len(operands) - 1: 0},
        compiler_params=params(),
        cost_estimate=pl.CostEstimate(
            flops=elements * 2 * 768, transcendentals=0, bytes_accessed=elements * 6
        ),
        name="attention_backward",
    )(*operands)


def swap(value, axis, mask):
    size = lax.axis_size(axis)
    return lax.ppermute(value, axis, [(i, i ^ mask) for i in range(size)])


def first_sum_kernel(counts, place_ref, *refs):
    terms = sum(counts)
    mine_ref, other_ref = refs[terms : terms + 2]
    along_x_ref, along_y_ref, keep_x_ref, keep_y_ref, vectors_ref = refs[terms + 2 :]
    x, y = place_ref[3], place_ref[4]
    half = along_x_ref.shape[2]
    slots = keep_x_ref.shape[1]
    slot = 0
    start = 0
    for count in counts:
        group = refs[start : start + count]
        start += count
        for s in range(group[0].shape[1]):

            def total(at, lanes):
                values = [r[at, s, :, lanes].astype(F32) for r in group]
                return functools.reduce(lambda a, b: a + b, values)

            low, high = slice(0, half), slice(half, None)
            for k in range(2):
                along_x_ref[k * slots + slot] = total(2 * k + (1 - x), low).astype(BF16)
                keep_x_ref[k, slot] = total(2 * k + x, low)
                along_y_ref[k * slots + slot] = total(2 * (1 - y) + k, high).astype(BF16)
                keep_y_ref[k, slot] = total(2 * y + k, high)
            slot += 1
    vectors = (mine_ref[...] + other_ref[...]).astype(BF16)
    vectors_ref[...] = vectors
    put_vectors(vectors, along_x_ref, along_y_ref)


def put_vectors(vectors, low_ref, high_ref):
    count = vectors.shape[0]
    for ref, lanes in ((low_ref, vectors[:, : vectors.shape[1] // 2]), (high_ref, vectors[:, vectors.shape[1] // 2 :])):
        last = ref.shape[0] - 1
        ref[last] = jnp.zeros(ref.shape[1:], ref.dtype)
        ref[last, :count] = lanes


def get_vectors(low_ref, high_ref, count):
    last = low_ref.shape[0] - 1
    return jnp.concatenate([low_ref[last, :count], high_ref[last, :count]], 1).astype(F32)


def second_sum_kernel(
    place_ref,
    keep_x_ref,
    came_x_ref,
    keep_y_ref,
    came_y_ref,
    vectors_ref,
    send_y_ref,
    send_x_ref,
    left_x_ref,
    left_y_ref,
    vectors_out_ref,
):
    slots = keep_x_ref.shape[1]
    for keep, came, send, left, me in (
        (keep_x_ref, came_x_ref, send_y_ref, left_x_ref, place_ref[4]),
        (keep_y_ref, came_y_ref, send_x_ref, left_y_ref, place_ref[3]),
    ):
        for s in range(slots):
            send[s] = (keep[1 - me, s] + came[(1 - me) * slots + s].astype(F32)).astype(BF16)
            left[s] = keep[me, s] + came[me * slots + s].astype(F32)
    count = vectors_ref.shape[0]
    vectors = vectors_ref[...].astype(F32) + get_vectors(came_x_ref, came_y_ref, count)
    vectors = vectors.astype(BF16)
    vectors_out_ref[...] = vectors
    put_vectors(vectors, send_y_ref, send_x_ref)


def third_sum_kernel(left_x_ref, came_x_ref, left_y_ref, came_y_ref, vectors_ref, total_ref):
    slots = left_x_ref.shape[0]
    half = left_x_ref.shape[2]
    for s in range(slots):
        total_ref[s, :, :half] = (left_x_ref[s] + came_x_ref[s].astype(F32)).astype(BF16)
        total_ref[s, :, half:] = (left_y_ref[s] + came_y_ref[s].astype(F32)).astype(BF16)
    count = vectors_ref.shape[0]
    vectors = vectors_ref[...].astype(F32) + get_vectors(came_x_ref, came_y_ref, count)
    total_ref[slots] = jnp.zeros(total_ref.shape[1:], BF16)
    total_ref[slots, :count] = vectors.astype(BF16)


def small_call(kernel, place, operands, out_shapes, name, after=()):
    ahead = 0 if place is None else 1
    count = len(operands)

    def body(*refs):
        kernel(*refs[: ahead + count], *refs[ahead + count + len(after) :])

    fixed = lambda s: pl.BlockSpec(s.shape, lambda *_: (0,) * len(s.shape))
    size = sum(math.prod(a.shape) * a.dtype.itemsize for a in list(operands) + list(out_shapes))
    return pl.pallas_call(
        body,
        grid_spec=pltpu.PrefetchScalarGridSpec(
            num_scalar_prefetch=ahead,
            grid=(1,),
            in_specs=[fixed(a) for a in operands] + [pl.BlockSpec(memory_space=pl.ANY)] * len(after),
            out_specs=[fixed(s) for s in out_shapes],
        ),
        out_shape=out_shapes,
        compiler_params=params(),
        cost_estimate=pl.CostEstimate(flops=0, transcendentals=0, bytes_accessed=size),
        name=name,
    )(*(() if place is None else (place,)), *operands, *after)


def sum_core(place, groups, vectors, name, after=()):
    groups = [list(g) + [swap(a, "batch", 1) for a in sent] for g, sent in groups]
    vectors_other = swap(vectors, "batch", 1)
    slots = sum(g[0].shape[1] for g in groups)
    _, _, rows, width = groups[0][0].shape
    half = width // 2
    counts = tuple(len(g) for g in groups)
    message = shape_of((2 * slots + 1, rows, half), BF16)
    kept = shape_of((2, slots, rows, half), F32)
    along_x, along_y, keep_x, keep_y, vectors = small_call(
        functools.partial(first_sum_kernel, counts),
        place,
        [a for g in groups for a in g] + [vectors, vectors_other],
        [message, message, kept, kept, shape_of(vectors.shape, BF16)],
        name + "_sum_core",
        after,
    )
    came_x, came_y = swap(along_x, "batch", 2), swap(along_y, "batch", 4)
    return (keep_x, came_x, keep_y, came_y, vectors), along_x


def sum_first(place, pieces, name, after=()):
    keep_x, _, _, _, vectors = pieces
    _, slots, rows, half = keep_x.shape
    message = shape_of((slots + 1, rows, half), BF16)
    kept = shape_of((slots, rows, half), F32)
    send_y, send_x, left_x, left_y, vectors = small_call(
        second_sum_kernel,
        place,
        pieces,
        [message, message, kept, kept, shape_of(vectors.shape, BF16)],
        name + "_sum_first",
        after,
    )
    came_x, came_y = swap(send_y, "batch", 4), swap(send_x, "batch", 2)
    return (left_x, came_x, left_y, came_y, vectors), send_y


def sum_second(pieces, name, after=()):
    slots, rows, half = pieces[0].shape
    shape = shape_of((slots + 1, rows, 2 * half), BF16)
    return small_call(third_sum_kernel, None, pieces, [shape], name + "_sum_second", after)[0]


def batch_slices_any(groups, vectors):
    me = lax.axis_index("batch")
    bits = lax.axis_size("batch").bit_length() - 1
    pieces = []
    for kept, sent in groups:
        values = [a.astype(F32) for a in kept] + [swap(a, "batch", 1).astype(F32) for a in sent]
        pieces.append(functools.reduce(lambda a, b: a + b, values))
    total = jnp.concatenate(pieces, 1)
    total = total.reshape((2,) * (bits - 1) + total.shape[1:])
    for bit in range(bits - 1, 0, -1):
        mine = (me >> bit) & 1
        sent = lax.dynamic_index_in_dim(total, 1 - mine, 0, keepdims=False).astype(BF16)
        total = lax.dynamic_index_in_dim(total, mine, 0, keepdims=False)
        total = total + swap(sent, "batch", 1 << bit).astype(F32)
    total = lax.psum(total.astype(BF16), "rows").astype(F32)
    return total, lax.psum(vectors, ("batch", "rows"))


def rows_sum(total):
    for mask in (1, 2):
        total = (total.astype(F32) + swap(total, "rows", mask).astype(F32)).astype(
            BF16 if mask == 1 else F32
        )
    return total


def rows_sum_halving(total):
    me = lax.axis_index("rows")
    low_bit, high_bit = me & 1, me >> 1
    slots, rows, _ = total.shape
    half, part = slots // 2, rows // 2
    cut = lambda a, i, axis, n: lax.dynamic_slice_in_dim(a, i * n, n, axis)
    kept = cut(total, low_bit, 0, half).astype(F32)
    kept = kept + swap(cut(total, 1 - low_bit, 0, half), "rows", 1).astype(F32)
    sent = cut(kept, 1 - high_bit, 1, part).astype(BF16)
    kept = (cut(kept, high_bit, 1, part) + swap(sent, "rows", 2).astype(F32)).astype(BF16)
    other = swap(kept, "rows", 2)
    join = lambda bit, a, b, axis: jnp.concatenate(
        [jnp.where(bit == 0, a, b), jnp.where(bit == 0, b, a)], axis
    )
    kept = join(high_bit, kept, other, 1)
    other = swap(kept, "rows", 1)
    return join(low_bit, kept, other, 0).astype(F32)


def final_kernel(own_count, *refs):
    terms = refs[:own_count]
    atoms_ref, gain_ref, shift_ref, grad_middle_ref, out_ref = refs[own_count:]
    rows, width = terms[0].shape[1:]
    gain = gain_ref[...].astype(F32)
    for stage in range(own_count // 3):
        own_ref, near_ref, cross_ref = terms[3 * stage : 3 * stage + 3]
        count = own_ref.shape[0]
        grad = own_ref[...] + near_ref[0].astype(F32) + cross_ref[...].astype(F32)
        grad = grad.reshape(count * rows, width)
        at = slice(stage * count, (stage + 1) * count)
        atoms = atoms_ref[at].reshape(count * rows, width).astype(F32)
        _, normed, inverse = norm_forward(atoms, gain, shift_ref[...].astype(F32))
        middle = grad_middle_ref[at].reshape(count * rows, width)
        result = middle + norm_backward(grad, normed, inverse, gain)
        out_ref[at] = result.astype(BF16).reshape(count, rows, width)


def shards(
    atoms,
    pair_bias,
    lengths,
    first_gain,
    first_shift,
    query_weight,
    query_bias,
    key_weight,
    value_weight,
    value_bias,
    out_weight,
    out_bias,
    second_gain,
    second_shift,
    inner_weight,
    inner_bias,
    outer_weight,
    outer_bias,
    atoms_cotangent,
    pair_cotangent,
):
    molecules, rows, model_width = atoms.shape
    head_count = pair_bias.shape[1]
    head_size = model_width // head_count
    batch_count = lax.axis_size("batch")
    batch_index = lax.axis_index("batch")
    row = lax.axis_index("rows")
    place = jnp.stack(
        [batch_index, row, batch_index & 1, (batch_index >> 1) & 1, (batch_index >> 2) & 1]
    ).astype(jnp.int32)
    line = lambda v: v[None]
    count = molecules // STAGES
    stages = []
    pair_out = jnp.zeros((1,), BF16)
    for stage in range(STAGES):
        first = stage * count
        mine = atoms[first : first + count]
        pieces = [atoms] + [swap(mine, "rows", mask) for mask in (1, 2, 3)]
        pair_out, *kept = attention_forward(
            head_size,
            first,
            count,
            place,
            lengths,
            pieces,
            pair_bias,
            (
                line(first_gain),
                line(first_shift),
                query_weight,
                line(query_bias),
                key_weight,
                value_weight,
                line(value_bias),
            ),
            pair_out,
        )
        stages.append(kept)
    (
        atoms_out,
        outer_send,
        outer_keep,
        inner_send,
        inner_keep,
        out_send,
        out_keep,
        grad_middle,
        grad_mixed,
        dense_vectors,
    ) = dense(
        place,
        [s[1] for s in stages],
        atoms,
        atoms_cotangent,
        (
            out_weight,
            line(out_bias),
            line(second_gain),
            line(second_shift),
            inner_weight,
            line(inner_bias),
            outer_weight,
            line(outer_bias),
        ),
        batch_count,
    )
    pairs = batch_count // 2
    own_rows = model_width // batch_count
    slots = lambda a: a.reshape(pairs, -1, own_rows, model_width)
    dense_groups = [
        ([slots(outer_keep)], [slots(outer_send)]),
        ([inner_keep], [inner_send]),
        ([slots(out_keep)], [slots(out_send)]),
    ]
    usual = batch_count == 8
    held = pair_bias
    if usual:
        dense_pieces, held = sum_core(place, dense_groups, dense_vectors, "dense")
    else:
        dense_total, dense_vectors = batch_slices_any(dense_groups, dense_vectors)

    pair_grad = jnp.zeros((1,), BF16)
    sent, kept, vectors, terms = [], [], [], []
    for stage in range(STAGES):
        pair_grad, near, cross, own, send, keep, vector = attention_backward(
            head_size,
            stage * count,
            place,
            (stages[stage][0],) + tuple(stages[stage][1:]),
            pair_cotangent,
            grad_mixed,
            (query_weight, key_weight, value_weight),
            pair_grad,
            batch_count,
            held,
        )
        if usual and stage == 0:
            dense_pieces, held = sum_first(place, dense_pieces, "dense", (near,))
        near = swap(near, "rows", 1)
        cross = (cross.astype(F32) + near[1].astype(F32)).astype(BF16)
        terms += [own, near, swap(cross, "rows", 2)]
        sent.append(send)
        kept.append(keep)
        vectors.append(vector)
    groups = [(kept, sent)]
    tail_vectors = functools.reduce(lambda a, b: a + b, vectors)
    if usual:
        dense_total = sum_second(dense_pieces, "dense", (near,))
        dense_total = rows_sum_halving(dense_total)
        dense_vectors = dense_total[-1, : dense_vectors.shape[0]]
        pieces, _ = sum_core(place, groups, tail_vectors, "tail")
        pieces, _ = sum_first(place, pieces, "tail")
        total = rows_sum(sum_second(pieces, "tail"))
        tail_vectors = total[-1, : tail_vectors.shape[0]]
    else:
        total, tail_vectors = batch_slices_any(groups, tail_vectors)
    atoms_grad = small_call(
        functools.partial(final_kernel, len(terms)),
        None,
        terms + [atoms, line(first_gain), line(first_shift), grad_middle],
        [shape_of(atoms.shape, BF16)],
        "first_norm_backward",
    )[0]
    part = lambda v: lax.dynamic_slice_in_dim(
        v, batch_index * (v.shape[0] // batch_count), v.shape[0] // batch_count
    )
    ratio = inner_weight.shape[1] // model_width
    outer_grad = dense_total[:ratio].reshape(-1, model_width)
    inner_grad = dense_total[ratio : 2 * ratio].transpose(1, 0, 2).reshape(own_rows, -1)
    return (
        atoms_out,
        pair_out,
        atoms_grad,
        pair_grad,
        part(tail_vectors[0]),
        part(tail_vectors[1]),
        total[0],
        part(tail_vectors[2]),
        total[1],
        total[2],
        part(tail_vectors[3]),
        dense_total[2 * ratio],
        part(dense_vectors[3]),
        part(dense_vectors[1]),
        part(dense_vectors[2]),
        inner_grad,
        part(dense_vectors[4:].reshape(-1)),
        outer_grad,
        part(dense_vectors[0]),
    )


def solution(mesh):
    tokens = P("batch", "rows", None)
    pairs = P("batch", None, "rows", None)
    vector = P("batch")
    matrix = P("batch", None)
    return jax.shard_map(
        shards,
        mesh=mesh,
        in_specs=(tokens, pairs, P("batch")) + (P(),) * 15 + (tokens, pairs),
        out_specs=(
            tokens,
            pairs,
            tokens,
            pairs,
            vector,
            vector,
            matrix,
            vector,
            matrix,
            matrix,
            vector,
            matrix,
            vector,
            vector,
            vector,
            matrix,
            vector,
            matrix,
            vector,
        ),
        check_vma=False,
    )
```

time: 242 us -> 199 us (0.82)
  Pallas kernels: 38.8 us -> 91.3 us
  waiting for transfers between devices: 64.9 us -> 36 us
  matrix products: 23.9 us -> 0 us
  other arithmetic: 27.2 us -> 4.55 us
  starting transfers between devices: 51.8 us -> 37.5 us
  local copies, waits for them, and re-layouts: 31.5 us -> 26.8 us
    pallas_call x2 -> x12, Pallas kernels: 38.8 us -> 91.3 us  [the longest x2 32.6 us: attention_backward(): pl.pallas_call(functools.partial(backward_kernel, head_size, 4), grid_spe...]
    ppermute x43 -> x31, waiting for transfers between devices: 64.9 us -> 36 us  [swap(): return lax.ppermute(value, axis, [(i, i ^ mask) for i in range(size)])]
    dot_general x15 -> x0, matrix products: 23.9 us -> none  [the longest x6 10.3 us: against(): lax.dot_general(left, right, (((1,), (1,)), ((), ())), preferred_element_...]
    ppermute x43 -> x31, starting transfers between devices: 51.8 us -> 37.5 us  [swap(): return lax.ppermute(value, axis, [(i, i ^ mask) for i in range(size)])]
    add x25 -> x3, other arithmetic: 12.2 us -> 1.85 us  [the longest x1 1.06 us: rows_sum_halving(): kept = kept + swap(cut(total, 1 - low_bit, 0, half), 'rows', 1).astype(F32)]
    broadcast_in_dim x4 -> x9, local copies, waits for them, and re-layouts: 2.73 us -> 11.4 us  [shards(): line = lambda v: v[None]]
    convert_element_type x21 -> x1, local copies, waits for them, and re-layouts: 6.74 us -> 0.03 us  [rows_sum_halving(): sent = cut(kept, 1 - high_bit, 1, part).astype(BF16)]
    convert_element_type x27 -> x5, other arithmetic: 7.94 us -> 1.26 us  [the longest x2 1.06 us: shards(): cross = (cross.astype(F32) + near[1].astype(F32)).astype(BF16)]
  transfers between devices with their start and end apart: 43 -> 31, of which waited for: 19 -> 9; matrix products, arithmetic and copies ran while one was open for 18% -> 9% of each run, Pallas kernels for 0% -> 29%
where the time goes in v2:
time: 199 us; the launch traced here: 197 us
  Pallas kernels  91.3 us (46%)
  starting transfers between devices  37.5 us (19%)
  waiting for transfers between devices  36 us (18%)
  local copies, waits for them, and re-layouts  26.8 us (13%)
  other arithmetic  4.55 us (2%)
    ppermute x31, starting transfers between devices, swap(): return lax.ppermute(value, axis, [(i, i ^ mask) for i in range(size)])  37.5 us
    ppermute x31, waiting for transfers between devices, swap(): return lax.ppermute(value, axis, [(i, i ^ mask) for i in range(size)])  36 us
    pallas_call x2, Pallas kernels, attention_backward(): pl.pallas_call(functools.partial(backward_kernel, head_size, 4), grid_spe...  32.6 us
    pallas_call x2, Pallas kernels, attention_forward(): pl.pallas_call(functools.partial(forward_kernel, head_size, 4, first=firs...  25.4 us
    pallas_call x7, Pallas kernels, small_call(): pl.pallas_call(body, grid_spec=pltpu.PrefetchScalarGridSpec(num_scalar_pr...  22.6 us
    broadcast_in_dim x9, local copies, waits for them, and re-layouts, shards(): line = lambda v: v[None]  11.4 us
    pallas_call x1, Pallas kernels, dense(): pl.pallas_call(functools.partial(dense_kernel, len(mixed)), grid_spec=plt...  10.7 us
    unnamed x63, local copies, waits for them, and re-layouts  8.56 us
  transfers between devices with their start and end apart: 31, of which 9 were waited for; matrix products, arithmetic and copies ran while one was open for 9% of the time, Pallas kernels for 29%

profile of v2, /device:TPU:0, one launch (start us, length us, event | category | flops | bytes accessed | tf_op | source)
XLA Modules:
  0.0 197.3 jit_solution(9488422541086091770)
XLA Ops:
  1.6 3.1 %collective-permute-start = (bf16[2,64,512]{2,1,0:T(8,128)(2,1)S(1)}, bf16[2,64,512]{2,1,0:T(8,128)(2,1)S(1)}, u32[]{:S(2)}, u32[]{:S(2)}) collective-permute-start(bf16[2,64,512]{2,1,0:T(8,128)(2,1)S(1)} %get-tuple-element.161), channel_id=1, source_target_pairs={{0,1},{1,0},{2,3},{3,2},{4,5},{5,4},{6,7},{7,6},{8,9},{9,8},{10,11... | collective-permute-start | bytes 393224 | tf_op jit(solution)/shard_map/ppermute | solution.py:636
  4.7 2.6 %collective-permute-start.1 = (bf16[2,64,512]{2,1,0:T(8,128)(2,1)S(1)}, bf16[2,64,512]{2,1,0:T(8,128)(2,1)S(1)}, u32[]{:S(2)}, u32[]{:S(2)}) collective-permute-start(bf16[2,64,512]{2,1,0:T(8,128)(2,1)S(1)} %get-tuple-element.161), channel_id=1, source_target_pairs={{0,2},{1,3},{2,0},{3,1},{4,6},{5,7},{6,4},{7,5},{8,10},{9,11},{10,... | collective-permute-start | bytes 393224 | tf_op jit(solution)/shard_map/ppermute | solution.py:636
  8.2 3.5 %collective-permute-start.4 = (bf16[2,64,512]{2,1,0:T(8,128)(2,1)S(1)}, bf16[2,64,512]{2,1,0:T(8,128)(2,1)S(1)}, u32[]{:S(2)}, u32[]{:S(2)}) collective-permute-start(bf16[2,64,512]{2,1,0:T(8,128)(2,1)S(1)} %get-tuple-element.160), channel_id=1, source_target_pairs={{0,2},{1,3},{2,0},{3,1},{4,6},{5,7},{6,4},{7,5},{8,10},{9,11},{10,... | collective-permute-start | bytes 393224 | tf_op jit(solution)/shard_map/ppermute | solution.py:636
  25.0 12.7 %attention_forward.2 = (bf16[4,64,64,256]{3,2,1,0:T(8,128)(2,1)}, bf16[2,64,64,256]{3,2,1,0:T(8,128)(2,1)}, f32[2,64,512]{2,1,0:T(8,128)}, f32[2,64,512]{2,1,0:T...) custom-call(s32[5]{0:T(128)} %stack.23.place_ref.refs_0_, ...), custom_call_target="tpu_custom_call" | custom-call | flops 1610612736 | bytes 12582912 | tf_op jit(solution)/shard_map/attention_forward/pallas_call | solution.py:177
  38.5 12.7 %attention_forward.3 = (bf16[4,64,64,256]{3,2,1,0:T(8,128)(2,1)}, bf16[2,64,64,256]{3,2,1,0:T(8,128)(2,1)}, f32[2,64,512]{2,1,0:T(8,128)}, f32[2,64,512]{2,1,0:T...) custom-call(s32[5]{0:T(128)} %stack.23.place_ref.refs_0_, ...), custom_call_target="tpu_custom_call", output_to_operand_aliasing={{0}: (14, {})} | custom-call | flops 1610612736 | bytes 12582912 | tf_op jit(solution)/shard_map/attention_forward/pallas_call | solution.py:177
  51.2 10.7 %dense.1 = (bf16[4,64,512]{2,1,0:T(8,128)(2,1)}, bf16[4,256,512]{2,1,0:T(8,128)(2,1)}, bf16[4,256,512]{2,1,0:T(8,128)(2,1)}, bf16[4,4,64,512]{3,2,1,0:T(8,128)(2...) custom-call(s32[5]{0:T(128)} %stack.23.place_ref.refs_0_, ...), custom_call_target="tpu_custom_call" | custom-call | flops 3221225472 | bytes 12582912 | tf_op jit(solution)/shard_map/dense/pallas_call | solution.py:386
  63.0 3.7 %collective-permute-done.9.refs_8_ = f32[8,512]{1,0:T(8,128)S(1)} collective-permute-done((f32[8,512]{1,0:T(8,128)}, f32[8,512]{1,0:T(8,128)S(1)}, u32[]{:S(2)}, u32[]{:S(2)}) %collective-permute-start.9) | collective-permute-done | bytes 16416 | tf_op jit(solution)/shard_map/ppermute | solution.py:636
  68.1 5.0 %dense_sum_core.1 = (bf16[19,64,256]{2,1,0:T(8,128)(2,1)}, bf16[19,64,256]{2,1,0:T(8,128)(2,1)}, f32[2,9,64,256]{3,2,1,0:T(8,128)}, f32[2,9,64,256]{3,2,1,0:T(8,128)}, bf16[8,512]{1,0:T(8,128)(2,1)}) custom-call(s32[5]{0:T(128)} %stack.23.place_ref.refs_0_, bf16[4,4,64,512]{3,2,1,0:T(8,128)(2,1)} %bitcast.51, bf16[4,4,64,512]{3,2,1,0:T(8,128)(2,1)} %copy-done.2, ...), custom_call_target="tpu_custom_call" | custom-call | bytes 8364032 | tf_op jit(solution)/shard_map/dense_sum_core/pallas_call | solution.py:731
  73.2 1.7 collective-permute-start.12
  74.8 1.5 collective-permute-start.13
  76.4 16.3 %attention_backward.2 = (bf16[4,64,64,256]{3,2,1,0:T(8,128)(2,1)}, bf16[2,2,64,512]{3,2,1,0:T(8,128)(2,1)}, bf16[2,64,512]{2,1,0:T(8,128)(2,1)}, f32[2,64,512]{2...) custom-call(s32[5]{0:T(128)} %stack.23.place_ref.refs_0_, ...), custom_call_target="tpu_custom_call" | custom-call | flops 3221225472 | bytes 12582912 | tf_op jit(solution)/shard_map/attention_backward/pallas_call | solution.py:580
  93.8 4.1 %dense_sum_first.1 = (bf16[10,64,256]{2,1,0:T(8,128)(2,1)}, bf16[10,64,256]{2,1,0:T(8,128)(2,1)}, f32[9,64,256]{2,1,0:T(8,128)}, f32[9,64,256]{2,1,0:T(8,128)}, bf16[8,512]{1,0:T(8,128)(2,1)}) custom-call(s32[5]{0:T(128)} %stack.23.place_ref.refs_0_, f32[2,9,64,256]{3,2,1,0:T(8,128)} %get-tuple-element.112.refs_1_, bf16[19,64,256]{2,1,0:T(8,128)(2,1)} %copy-done.7, ...), custom_call_target="tpu_custom_call" | custom-call | bytes 5455872 | tf_op jit(solution)/shard_map/dense_sum_first/pallas_call | solution.py:731
  98.7 16.3 %attention_backward.3 = (bf16[4,64,64,256]{3,2,1,0:T(8,128)(2,1)}, bf16[2,2,64,512]{3,2,1,0:T(8,128)(2,1)}, bf16[2,64,512]{2,1,0:T(8,128)(2,1)}, f32[2,64,512]{2...) custom-call(s32[5]{0:T(128)} %stack.23.place_ref.refs_0_, ...), custom_call_target="tpu_custom_call", output_to_operand_aliasing={{0}: (15, {})} | custom-call | flops 3221225472 | bytes 12582912 | tf_op jit(solution)/shard_map/attention_backward/pallas_call | solution.py:580
  115.6 6.9 %collective-permute-done.14.refs_4_.refs_5_ = bf16[2,2,64,512]{3,2,1,0:T(8,128)(2,1)S(1)} collective-permute-done((bf16[2,2,64,512]{3,2,1,0:T(8,128)(2,1)}, bf16[2,2,64,512]{3,2,1,0:T(8,128)(2,1)S(1)}, u32[]{:S(2)}, u32[]{:S(2)}) %collective-permute-start.14) | collective-permute-done | bytes 262176 | tf_op jit(solution)/shard_map/ppermute | solution.py:636
  123.5 2.4 %dense_sum_second.1 = bf16[10,64,512]{2,1,0:T(8,128)(2,1)} custom-call(f32[9,64,256]{2,1,0:T(8,128)} %get-tuple-element.139.refs_0_, bf16[10,64,256]{2,1,0:T(8,128)(2,1)} %copy-done.10, f32[9,64,256]{2,1,0:T(8,128)} %get-tuple-element.140.refs_2_, bf16[10,64,256]{2,1,0:T(8,128)(2,1)} %copy-done.11, bf16[8,512]{1,0:T(8,128)(2,1)} %get-tuple-element.142.refs_4_, ...), custom_call_target="tpu_custom_call" | custom-call | bytes 2498560 | tf_op jit(solution)/shard_map/dense_sum_second/pallas_call | solution.py:731
  128.0 6.7 %collective-permute-done.27 = bf16[5,64,512]{2,1,0:T(8,128)(2,1)S(1)} collective-permute-done((bf16[5,64,512]{2,1,0:T(8,128)(2,1)S(1)}, bf16[5,64,512]{2,1,0:T(8,128)(2,1)S(1)}, u32[]{:S(2)}, u32[]{:S(2)}) %collective-permute-start.27) | collective-permute-done | bytes 327712 | tf_op jit(solution)/shard_map/ppermute | solution.py:636
  135.8 2.9 %collective-permute-start.28 = (bf16[5,32,512]{2,1,0:T(8,128)(2,1)S(1)}, bf16[5,32,512]{2,1,0:T(8,128)(2,1)S(1)}, u32[]{:S(2)}, u32[]{:S(2)}) collective-permute-start(bf16[5,32,512]{2,1,0:T(8,128)(2,1)S(1)} %dynamic-slice_convert_fusion), channel_id=1, source_target_pairs={{0,2},{1,3},{2,0},{3,1},{4,6},{5,7},{6,4},{7,5},{8,10},{9,11},{10,... | collective-permute-start | bytes 491528 | tf_op jit(solution)/shard_map/ppermute | solution.py:636
  140.9 2.5 %collective-permute-done.28 = bf16[5,32,512]{2,1,0:T(8,128)(2,1)S(1)} collective-permute-done((bf16[5,32,512]{2,1,0:T(8,128)(2,1)S(1)}, bf16[5,32,512]{2,1,0:T(8,128)(2,1)S(1)}, u32[]{:S(2)}, u32[]{:S(2)}) %collective-permute-start.28) | collective-permute-done | bytes 163872 | tf_op jit(solution)/shard_map/ppermute | solution.py:636
  143.4 3.5 %collective-permute-start.29 = (bf16[5,32,512]{2,1,0:T(8,128)(2,1)S(1)}, bf16[5,32,512]{2,1,0:T(8,128)(2,1)S(1)}, u32[]{:S(2)}, u32[]{:S(2)}) collective-permute-start(bf16[5,32,512]{2,1,0:T(8,128)(2,1)S(1)} %add_convert_fusion.1), channel_id=1, source_target_pairs={{0,2},{1,3},{2,0},{3,1},{4,6},{5,7},{6,4},{7,5},{8,10},{9,11},{10,... | collective-permute-start | bytes 491528 | tf_op jit(solution)/shard_map/ppermute | solution.py:636
  146.9 2.2 %collective-permute-done.10.refs_1_ = bf16[2,2,64,512]{3,2,1,0:T(8,128)(2,1)S(1)} collective-permute-done((bf16[2,2,64,512]{3,2,1,0:T(8,128)(2,1)S(1)}, bf16[2,2,64,512]{3,2,1,0:T(8,128)(2,1)S(1)}, u32[]{:S(2)}, u32[]{:S(2)}) %collective-permute-start.10) | collective-permute-done | bytes 262176 | tf_op jit(solution)/shard_map/ppermute | solution.py:636
  151.4 3.7 %tail_sum_core.1 = (bf16[7,64,256]{2,1,0:T(8,128)(2,1)}, bf16[7,64,256]{2,1,0:T(8,128)(2,1)}, f32[2,3,64,256]{3,2,1,0:T(8,128)}, f32[2,3,64,256]{3,2,1,0:T(8,128)}, bf16[8,512]{1,0:T(8,128)(2,1)}) custom-call(s32[5]{0:T(128)} %stack.23.place_ref.refs_0_, bf16[4,3,64,512]{3,2,1,0:T(8,128)(2,1)} %get-tuple-element.123.refs_1_, ...), custom_call_target="tpu_custom_call" | custom-call | bytes 4431872 | tf_op jit(solution)/shard_map/tail_sum_core/pallas_call | solution.py:731
  155.1 1.5 collective-permute-start.19
  156.6 1.5 collective-permute-start.20
  158.2 1.5 collective-permute-start.30
  159.8 3.0 %collective-permute-start.15 = (bf16[2,64,512]{2,1,0:T(8,128)(2,1)S(1)}, bf16[2,64,512]{2,1,0:T(8,128)(2,1)S(1)}, u32[]{:S(2)}, u32[]{:S(2)}) collective-permute-start(bf16[2,64,512]{2,1,0:T(8,128)(2,1)S(1)} %fusion), channel_id=1, source_target_pairs={{0,2},{1,3},{2,0},{3,1},{4,6},{5,7},{6,4},{7,5},{8,10},{9,11},{10,... | collective-permute-start | bytes 393224 | tf_op jit(solution)/shard_map/ppermute | solution.py:636
  163.6 2.9 %tail_sum_first.1 = (bf16[4,64,256]{2,1,0:T(8,128)(2,1)}, bf16[4,64,256]{2,1,0:T(8,128)(2,1)}, f32[3,64,256]{2,1,0:T(8,128)}, f32[3,64,256]{2,1,0:T(8,128)}, bf16[8,512]{1,0:T(8,128)(2,1)}) custom-call(s32[5]{0:T(128)} %stack.23.place_ref.refs_0_, f32[2,3,64,256]{3,2,1,0:T(8,128)} %get-tuple-element.129.refs_1_, bf16[7,64,256]{2,1,0:T(8,128)(2,1)} %copy-done.14, ...), custom_call_target="tpu_custom_call" | custom-call | bytes 1916928 | tf_op jit(solution)/shard_map/tail_sum_first/pallas_call | solution.py:731
  166.5 1.5 collective-permute-start.21
  169.2 2.6 %first_norm_backward.1 = bf16[4,64,512]{2,1,0:T(8,128)(2,1)} custom-call(f32[2,64,512]{2,1,0:T(8,128)} %get-tuple-element.102.refs_0_, bf16[2,2,64,512]{3,2,1,0:T(8,128)(2,1)} %copy-done.9, bf16[2,64,512]{2,1,0:T(8,128)(2,1)} %copy-done.23, f32[2,64,512]{2,1,0:T(8,128)} %get-tuple-element.118.refs_3_, bf16[2,2,64,512]{3,2,1,0:T(8,128)(2,1)} %copy-done, ...), custom_call_target="tpu_custom_call" | custom-call | bytes 2361344 | tf_op jit(solution)/shard_map/first_norm_backward/pallas_call | solution.py:731
  173.8 1.9 tail_sum_second.1
  175.7 1.7 collective-permute-start.23
  178.5 6.5 %collective-permute-done.23 = bf16[4,64,512]{2,1,0:T(8,128)(2,1)S(1)} collective-permute-done((bf16[4,64,512]{2,1,0:T(8,128)(2,1)}, bf16[4,64,512]{2,1,0:T(8,128)(2,1)S(1)}, u32[]{:S(2)}, u32[]{:S(2)}) %collective-permute-start.23) | collective-permute-done | bytes 262176 | tf_op jit(solution)/shard_map/ppermute | solution.py:636
  189.2 6.0 %collective-permute-done.24 = bf16[4,64,512]{2,1,0:T(8,128)(2,1)S(1)} collective-permute-done((bf16[4,64,512]{2,1,0:T(8,128)(2,1)S(1)}, bf16[4,64,512]{2,1,0:T(8,128)(2,1)S(1)}, u32[]{:S(2)}, u32[]{:S(2)}) %collective-permute-start.24) | collective-permute-done | bytes 262176 | tf_op jit(solution)/shard_map/ppermute | solution.py:636
  (139 shorter events, 40.9 us)
Async XLA Ops:
  1.6 22.0 %collective-permute-start = (bf16[2,64,512]{2,1,0:T(8,128)(2,1)S(1)}, bf16[2,64,512]{2,1,0:T(8,128)(2,1)S(1)}, u32[]{:S(2)}, u32[]{:S(2)}) collective-permute-start(bf16[2,64,512]{2,1,0:T(8,128)(2,1)S(1)} %get-tuple-element.161), channel_id=1, source_target_pairs={{0,1},{1,0},{2,3},{3,2},{4,5},{5,4},{6,7},{7,6},{8,9},{9,8},{10,11... | collective-permute-start | bytes 393224 | tf_op jit(solution)/shard_map/ppermute | solution.py:636
  4.7 18.9 %collective-permute-start.1 = (bf16[2,64,512]{2,1,0:T(8,128)(2,1)S(1)}, bf16[2,64,512]{2,1,0:T(8,128)(2,1)S(1)}, u32[]{:S(2)}, u32[]{:S(2)}) collective-permute-start(bf16[2,64,512]{2,1,0:T(8,128)(2,1)S(1)} %get-tuple-element.161), channel_id=1, source_target_pairs={{0,2},{1,3},{2,0},{3,1},{4,6},{5,7},{6,4},{7,5},{8,10},{9,11},{10,... | collective-permute-start | bytes 393224 | tf_op jit(solution)/shard_map/ppermute | solution.py:636
  7.3 16.4 %collective-permute-start.2 = (bf16[2,64,512]{2,1,0:T(8,128)(2,1)S(1)}, bf16[2,64,512]{2,1,0:T(8,128)(2,1)S(1)}, u32[]{:S(2)}, u32[]{:S(2)}) collective-permute-start(bf16[2,64,512]{2,1,0:T(8,128)(2,1)S(1)} %get-tuple-element.161), channel_id=1, source_target_pairs={{0,3},{1,2},{2,1},{3,0},{4,7},{5,6},{6,5},{7,4},{8,11},{9,10},{10,... | collective-permute-start | bytes 393224 | tf_op jit(solution)/shard_map/ppermute | solution.py:636
  7.3 30.4 %collective-permute-start.3 = (bf16[2,64,512]{2,1,0:T(8,128)(2,1)S(1)}, bf16[2,64,512]{2,1,0:T(8,128)(2,1)S(1)}, u32[]{:S(2)}, u32[]{:S(2)}) collective-permute-start(bf16[2,64,512]{2,1,0:T(8,128)(2,1)S(1)} %get-tuple-element.160), channel_id=1, source_target_pairs={{0,1},{1,0},{2,3},{3,2},{4,5},{5,4},{6,7},{7,6},{8,9},{9,8},{10,11... | collective-permute-start | bytes 393224 | tf_op jit(solution)/shard_map/ppermute | solution.py:636
  8.2 29.5 %collective-permute-start.4 = (bf16[2,64,512]{2,1,0:T(8,128)(2,1)S(1)}, bf16[2,64,512]{2,1,0:T(8,128)(2,1)S(1)}, u32[]{:S(2)}, u32[]{:S(2)}) collective-permute-start(bf16[2,64,512]{2,1,0:T(8,128)(2,1)S(1)} %get-tuple-element.160), channel_id=1, source_target_pairs={{0,2},{1,3},{2,0},{3,1},{4,6},{5,7},{6,4},{7,5},{8,10},{9,11},{10,... | collective-permute-start | bytes 393224 | tf_op jit(solution)/shard_map/ppermute | solution.py:636
  23.7 14.1 %collective-permute-start.5 = (bf16[2,64,512]{2,1,0:T(8,128)(2,1)S(1)}, bf16[2,64,512]{2,1,0:T(8,128)(2,1)S(1)}, u32[]{:S(2)}, u32[]{:S(2)}) collective-permute-start(bf16[2,64,512]{2,1,0:T(8,128)(2,1)S(1)} %get-tuple-element.160), channel_id=1, source_target_pairs={{0,3},{1,2},{2,1},{3,0},{4,7},{5,6},{6,5},{7,4},{8,11},{9,10},{10,... | collective-permute-start | bytes 393224 | tf_op jit(solution)/shard_map/ppermute | solution.py:636
  61.9 4.8 %collective-permute-start.6 = (bf16[4,4,64,512]{3,2,1,0:T(8,128)(2,1)}, bf16[4,4,64,512]{3,2,1,0:T(8,128)(2,1)S(1)}, u32[]{:S(2)}, u32[]{:S(2)}) collective-permute-start(bf16[4,4,64,512]{3,2,1,0:T(8,128)(2,1)} %bitcast.56), channel_id=1, source_target_pairs={{0,4},{4,0},{8,12},{12,8},{16,20},{20,16},{24,28},{28,24},{1,5},{5... | collective-permute-start | bytes 3145736 | tf_op jit(solution)/shard_map/ppermute | solution.py:636
  62.0 4.8 %collective-permute-start.7 = (bf16[4,4,64,512]{3,2,1,0:T(8,128)(2,1)}, bf16[4,4,64,512]{3,2,1,0:T(8,128)(2,1)S(1)}, u32[]{:S(2)}, u32[]{:S(2)}) collective-permute-start(bf16[4,4,64,512]{3,2,1,0:T(8,128)(2,1)} %get-tuple-element.97), channel_id=1, source_target_pairs={{0,4},{4,0},{8,12},{12,8},{16,20},{20,16},{24,28},{28,24},{1,5},{5... | collective-permute-start | bytes 3145736 | tf_op jit(solution)/shard_map/ppermute | solution.py:636
  62.5 4.3 %collective-permute-start.8 = (bf16[4,1,64,512]{3,2,1,0:T(8,128)(2,1)}, bf16[4,1,64,512]{3,2,1,0:T(8,128)(2,1)S(1)}, u32[]{:S(2)}, u32[]{:S(2)}) collective-permute-start(bf16[4,1,64,512]{3,2,1,0:T(8,128)(2,1)} %bitcast.57), channel_id=1, source_target_pairs={{0,4},{4,0},{8,12},{12,8},{16,20},{20,16},{24,28},{28,24},{1,5},{5... | collective-permute-start | bytes 786440 | tf_op jit(solution)/shard_map/ppermute | solution.py:636
  62.5 4.2 %collective-permute-start.9 = (f32[8,512]{1,0:T(8,128)}, f32[8,512]{1,0:T(8,128)S(1)}, u32[]{:S(2)}, u32[]{:S(2)}) collective-permute-start(f32[8,512]{1,0:T(8,128)} %get-tuple-element.100.refs_7_), channel_id=1, source_target_pairs={{0,4},{4,0},{8,12},{12,8},{16,20},{20,16},{24,28},{28,24},{1,5},{5... | collective-permute-start | bytes 49160 | tf_op jit(solution)/shard_map/ppermute | solution.py:636
  73.2 19.5 %collective-permute-start.12 = (bf16[19,64,256]{2,1,0:T(8,128)(2,1)}, bf16[19,64,256]{2,1,0:T(8,128)(2,1)S(1)}, u32[]{:S(2)}, u32[]{:S(2)}) collective-permute-start(bf16[19,64,256]{2,1,0:T(8,128)(2,1)} %get-tuple-element.101._after), channel_id=1, source_target_pairs={{0,8},{4,12},{8,0},{12,4},{16,24},{20,28},{24,16},{28,20},{1,9},{5... | collective-permute-start | bytes 1867784 | tf_op jit(solution)/shard_map/ppermute | solution.py:636
  74.8 17.8 %collective-permute-start.13 = (bf16[19,64,256]{2,1,0:T(8,128)(2,1)}, bf16[19,64,256]{2,1,0:T(8,128)(2,1)S(1)}, u32[]{:S(2)}, u32[]{:S(2)}) collective-permute-start(bf16[19,64,256]{2,1,0:T(8,128)(2,1)} %get-tuple-element.114), channel_id=1, source_target_pairs={{0,16},{4,20},{8,24},{12,28},{16,0},{20,4},{24,8},{28,12},{1,17},{... | collective-permute-start | bytes 1867784 | tf_op jit(solution)/shard_map/ppermute | solution.py:636
  97.8 24.7 %collective-permute-start.25 = (bf16[10,64,256]{2,1,0:T(8,128)(2,1)}, bf16[10,64,256]{2,1,0:T(8,128)(2,1)S(1)}, u32[]{:S(2)}, u32[]{:S(2)}) collective-permute-start(bf16[10,64,256]{2,1,0:T(8,128)(2,1)} %get-tuple-element.116._after), channel_id=1, source_target_pairs={{0,16},{4,20},{8,24},{12,28},{16,0},{20,4},{24,8},{28,12},{1,17},{... | collective-permute-start | bytes 983048 | tf_op jit(solution)/shard_map/ppermute | solution.py:636
  98.3 24.2 %collective-permute-start.26 = (bf16[10,64,256]{2,1,0:T(8,128)(2,1)}, bf16[10,64,256]{2,1,0:T(8,128)(2,1)S(1)}, u32[]{:S(2)}, u32[]{:S(2)}) collective-permute-start(bf16[10,64,256]{2,1,0:T(8,128)(2,1)} %get-tuple-element.141), channel_id=1, source_target_pairs={{0,8},{4,12},{8,0},{12,4},{16,24},{20,28},{24,16},{28,20},{1,9},{5... | collective-permute-start | bytes 983048 | tf_op jit(solution)/shard_map/ppermute | solution.py:636
  115.0 7.5 %collective-permute-start.14 = (bf16[2,2,64,512]{3,2,1,0:T(8,128)(2,1)}, bf16[2,2,64,512]{3,2,1,0:T(8,128)(2,1)S(1)}, u32[]{:S(2)}, u32[]{:S(2)}) collective-permute-start(bf16[2,2,64,512]{3,2,1,0:T(8,128)(2,1)} %get-tuple-element.119), channel_id=1, source_target_pairs={{0,1},{1,0},{2,3},{3,2},{4,5},{5,4},{6,7},{7,6},{8,9},{9,8},{10,11... | collective-permute-start | bytes 786440 | tf_op jit(solution)/shard_map/ppermute | solution.py:636
  125.9 33.8 %copy-start.22 = (bf16[2,64,512]{2,1,0:T(8,128)(2,1)S(1)}, bf16[2,64,512]{2,1,0:T(8,128)(2,1)}, u32[]{:S(2)}) copy-start(bf16[2,64,512]{2,1,0:T(8,128)(2,1)} %get-tuple-element.120) | copy-start | bytes 393220
  126.9 7.8 %collective-permute-start.27 = (bf16[5,64,512]{2,1,0:T(8,128)(2,1)S(1)}, bf16[5,64,512]{2,1,0:T(8,128)(2,1)S(1)}, u32[]{:S(2)}, u32[]{:S(2)}) collective-permute-start(bf16[5,64,512]{2,1,0:T(8,128)(2,1)S(1)} %constant_dynamic-slice_fusion.8), channel_id=1, source_target_pairs={{0,1},{1,0},{2,3},{3,2},{4,5},{5,4},{6,7},{7,6},{8,9},{9,8},{10,11... | collective-permute-start | bytes 983048 | tf_op jit(solution)/shard_map/ppermute | solution.py:636
  127.5 22.7 %collective-permute-start.16 = (bf16[4,3,64,512]{3,2,1,0:T(8,128)(2,1)}, bf16[4,3,64,512]{3,2,1,0:T(8,128)(2,1)S(1)}, u32[]{:S(2)}, u32[]{:S(2)}) collective-permute-start(bf16[4,3,64,512]{3,2,1,0:T(8,128)(2,1)} %get-tuple-element.125), channel_id=1, source_target_pairs={{0,4},{4,0},{8,12},{12,8},{16,20},{20,16},{24,28},{28,24},{1,5},{5... | collective-permute-start | bytes 2359304 | tf_op jit(solution)/shard_map/ppermute | solution.py:636
  127.5 22.7 %collective-permute-start.17 = (bf16[4,3,64,512]{3,2,1,0:T(8,128)(2,1)}, bf16[4,3,64,512]{3,2,1,0:T(8,128)(2,1)S(1)}, u32[]{:S(2)}, u32[]{:S(2)}) collective-permute-start(bf16[4,3,64,512]{3,2,1,0:T(8,128)(2,1)} %get-tuple-element.126), channel_id=1, source_target_pairs={{0,4},{4,0},{8,12},{12,8},{16,20},{20,16},{24,28},{28,24},{1,5},{5... | collective-permute-start | bytes 2359304 | tf_op jit(solution)/shard_map/ppermute | solution.py:636
  135.8 7.6 %collective-permute-start.28 = (bf16[5,32,512]{2,1,0:T(8,128)(2,1)S(1)}, bf16[5,32,512]{2,1,0:T(8,128)(2,1)S(1)}, u32[]{:S(2)}, u32[]{:S(2)}) collective-permute-start(bf16[5,32,512]{2,1,0:T(8,128)(2,1)S(1)} %dynamic-slice_convert_fusion), channel_id=1, source_target_pairs={{0,2},{1,3},{2,0},{3,1},{4,6},{5,7},{6,4},{7,5},{8,10},{9,11},{10,... | collective-permute-start | bytes 491528 | tf_op jit(solution)/shard_map/ppermute | solution.py:636
  138.7 10.3 %collective-permute-start.10 = (bf16[2,2,64,512]{3,2,1,0:T(8,128)(2,1)S(1)}, bf16[2,2,64,512]{3,2,1,0:T(8,128)(2,1)S(1)}, u32[]{:S(2)}, u32[]{:S(2)}) collective-permute-start(bf16[2,2,64,512]{3,2,1,0:T(8,128)(2,1)S(1)} %copy-done.12), channel_id=1, source_target_pairs={{0,1},{1,0},{2,3},{3,2},{4,5},{5,4},{6,7},{7,6},{8,9},{9,8},{10,11... | collective-permute-start | bytes 786440 | tf_op jit(solution)/shard_map/ppermute | solution.py:636
  140.9 9.3 %collective-permute-start.18 = (f32[8,512]{1,0:T(8,128)S(1)}, f32[8,512]{1,0:T(8,128)S(1)}, u32[]{:S(2)}, u32[]{:S(2)}) collective-permute-start(f32[8,512]{1,0:T(8,128)S(1)} %add.48.refs_5_), channel_id=1, source_target_pairs={{0,4},{4,0},{8,12},{12,8},{16,20},{20,16},{24,28},{28,24},{1,5},{5... | collective-permute-start | bytes 49160 | tf_op jit(solution)/shard_map/ppermute | solution.py:636
  143.4 14.7 %collective-permute-start.29 = (bf16[5,32,512]{2,1,0:T(8,128)(2,1)S(1)}, bf16[5,32,512]{2,1,0:T(8,128)(2,1)S(1)}, u32[]{:S(2)}, u32[]{:S(2)}) collective-permute-start(bf16[5,32,512]{2,1,0:T(8,128)(2,1)S(1)} %add_convert_fusion.1), channel_id=1, source_target_pairs={{0,2},{1,3},{2,0},{3,1},{4,6},{5,7},{6,4},{7,5},{8,10},{9,11},{10,... | collective-permute-start | bytes 491528 | tf_op jit(solution)/shard_map/ppermute | solution.py:636
  150.1 18.4 %collective-permute-start.11 = (bf16[2,64,512]{2,1,0:T(8,128)(2,1)S(1)}, bf16[2,64,512]{2,1,0:T(8,128)(2,1)S(1)}, u32[]{:S(2)}, u32[]{:S(2)}) collective-permute-start(bf16[2,64,512]{2,1,0:T(8,128)(2,1)S(1)} %fusion.1), channel_id=1, source_target_pairs={{0,2},{1,3},{2,0},{3,1},{4,6},{5,7},{6,4},{7,5},{8,10},{9,11},{10,... | collective-permute-start | bytes 393224 | tf_op jit(solution)/shard_map/ppermute | solution.py:636
  155.1 7.6 %collective-permute-start.19 = (bf16[7,64,256]{2,1,0:T(8,128)(2,1)}, bf16[7,64,256]{2,1,0:T(8,128)(2,1)S(1)}, u32[]{:S(2)}, u32[]{:S(2)}) collective-permute-start(bf16[7,64,256]{2,1,0:T(8,128)(2,1)} %get-tuple-element.130), channel_id=1, source_target_pairs={{0,8},{4,12},{8,0},{12,4},{16,24},{20,28},{24,16},{28,20},{1,9},{5... | collective-permute-start | bytes 688136 | tf_op jit(solution)/shard_map/ppermute | solution.py:636
  156.6 6.2 %collective-permute-start.20 = (bf16[7,64,256]{2,1,0:T(8,128)(2,1)}, bf16[7,64,256]{2,1,0:T(8,128)(2,1)S(1)}, u32[]{:S(2)}, u32[]{:S(2)}) collective-permute-start(bf16[7,64,256]{2,1,0:T(8,128)(2,1)} %get-tuple-element.132), channel_id=1, source_target_pairs={{0,16},{4,20},{8,24},{12,28},{16,0},{20,4},{24,8},{28,12},{1,17},{... | collective-permute-start | bytes 688136 | tf_op jit(solution)/shard_map/ppermute | solution.py:636
  158.2 19.2 %collective-permute-start.30 = (bf16[5,64,512]{2,1,0:T(8,128)(2,1)S(1)}, bf16[5,64,512]{2,1,0:T(8,128)(2,1)S(1)}, u32[]{:S(2)}, u32[]{:S(2)}) collective-permute-start(bf16[5,64,512]{2,1,0:T(8,128)(2,1)S(1)} %pad_maximum_fusion), channel_id=1, source_target_pairs={{0,1},{1,0},{2,3},{3,2},{4,5},{5,4},{6,7},{7,6},{8,9},{9,8},{10,11... | collective-permute-start | bytes 983048 | tf_op jit(solution)/shard_map/ppermute | solution.py:636
  159.8 8.8 %collective-permute-start.15 = (bf16[2,64,512]{2,1,0:T(8,128)(2,1)S(1)}, bf16[2,64,512]{2,1,0:T(8,128)(2,1)S(1)}, u32[]{:S(2)}, u32[]{:S(2)}) collective-permute-start(bf16[2,64,512]{2,1,0:T(8,128)(2,1)S(1)} %fusion), channel_id=1, source_target_pairs={{0,2},{1,3},{2,0},{3,1},{4,6},{5,7},{6,4},{7,5},{8,10},{9,11},{10,... | collective-permute-start | bytes 393224 | tf_op jit(solution)/shard_map/ppermute | solution.py:636
  166.5 5.4 %collective-permute-start.21 = (bf16[4,64,256]{2,1,0:T(8,128)(2,1)}, bf16[4,64,256]{2,1,0:T(8,128)(2,1)S(1)}, u32[]{:S(2)}, u32[]{:S(2)}) collective-permute-start(bf16[4,64,256]{2,1,0:T(8,128)(2,1)} %get-tuple-element.135), channel_id=1, source_target_pairs={{0,16},{4,20},{8,24},{12,28},{16,0},{20,4},{24,8},{28,12},{1,17},{... | collective-permute-start | bytes 393224 | tf_op jit(solution)/shard_map/ppermute | solution.py:636
  168.0 5.2 %collective-permute-start.22 = (bf16[4,64,256]{2,1,0:T(8,128)(2,1)}, bf16[4,64,256]{2,1,0:T(8,128)(2,1)S(1)}, u32[]{:S(2)}, u32[]{:S(2)}) collective-permute-start(bf16[4,64,256]{2,1,0:T(8,128)(2,1)} %get-tuple-element.137), channel_id=1, source_target_pairs={{0,8},{4,12},{8,0},{12,4},{16,24},{20,28},{24,16},{28,20},{1,9},{5... | collective-permute-start | bytes 393224 | tf_op jit(solution)/shard_map/ppermute | solution.py:636
  175.7 9.4 %collective-permute-start.23 = (bf16[4,64,512]{2,1,0:T(8,128)(2,1)}, bf16[4,64,512]{2,1,0:T(8,128)(2,1)S(1)}, u32[]{:S(2)}, u32[]{:S(2)}) collective-permute-start(bf16[4,64,512]{2,1,0:T(8,128)(2,1)} %tail_sum_second.1), channel_id=1, source_target_pairs={{0,1},{1,0},{2,3},{3,2},{4,5},{5,4},{6,7},{7,6},{8,9},{9,8},{10,11... | collective-permute-start | bytes 786440 | tf_op jit(solution)/shard_map/ppermute | solution.py:636
  185.1 10.1 %collective-permute-start.24 = (bf16[4,64,512]{2,1,0:T(8,128)(2,1)S(1)}, bf16[4,64,512]{2,1,0:T(8,128)(2,1)S(1)}, u32[]{:S(2)}, u32[]{:S(2)}) collective-permute-start(bf16[4,64,512]{2,1,0:T(8,128)(2,1)S(1)} %add_convert_fusion), channel_id=1, source_target_pairs={{0,2},{1,3},{2,0},{3,1},{4,6},{5,7},{6,4},{7,5},{8,10},{9,11},{10,... | collective-permute-start | bytes 786440 | tf_op jit(solution)/shard_map/ppermute | solution.py:636
  (30 other events, 140.4 us)

commit v3 on v2

v3 whole, which is shorter than its diff:
```python
import functools
import math

import jax
import jax.numpy as jnp
from jax import lax
from jax.experimental import pallas as pl
from jax.experimental.pallas import tpu as pltpu
from jax.sharding import PartitionSpec as P

EPSILON = 1e-05
MASKED = -1000000000.0
F32 = jnp.float32
BF16 = jnp.bfloat16
LANES = 128
STAGES = 2
VMEM_LIMIT = 18 << 20


def shape_of(shape, dtype):
    return jax.ShapeDtypeStruct(tuple(shape), dtype)


def norm_forward(values_in, gain, shift):
    centre = values_in - jnp.mean(values_in, -1, keepdims=True)
    inverse = lax.rsqrt(jnp.mean(centre * centre, -1, keepdims=True) + EPSILON)
    normed = centre * inverse
    return (normed * gain + shift, normed, inverse)


def norm_backward(upstream, normed, inverse, gain):
    scaled = upstream * gain
    return inverse * (
        scaled
        - jnp.mean(scaled, -1, keepdims=True)
        - normed * jnp.mean(scaled * normed, -1, keepdims=True)
    )


def dot(left, right):
    return jnp.dot(left, right, preferred_element_type=F32)


def across(left, right):
    return lax.dot_general(left, right, (((0,), (0,)), ((), ())), preferred_element_type=F32)


def against(left, right):
    return lax.dot_general(left, right, (((1,), (1,)), ((), ())), preferred_element_type=F32)


def column_sum(values_in):
    return jnp.sum(values_in.astype(F32), 0, keepdims=True)


def near(shape, dtype):
    return pltpu.VMEM(tuple(shape), dtype)


def near_spec():
    return pl.BlockSpec(memory_space=pltpu.VMEM)


def as_row(ref):
    return ref[...].astype(F32).reshape(1, -1)


def whole(array):
    return pl.BlockSpec(array.shape, lambda *_: (0,) * array.ndim)


def params(mib=10):
    return pltpu.CompilerParams(vmem_limit_bytes=mib << 20)


def load_kernel(count, *refs):
    sources, targets, semaphores = refs[:count], refs[count : 2 * count], refs[2 * count]
    copies = [
        pltpu.make_async_copy(source, target, semaphores.at[i])
        for i, (source, target) in enumerate(zip(sources, targets))
    ]
    for copy in copies:
        copy.start()
    for copy in copies:
        copy.wait()


def load(arrays, name):
    return pl.pallas_call(
        functools.partial(load_kernel, len(arrays)),
        in_specs=[pl.BlockSpec(memory_space=pltpu.HBM)] * len(arrays),
        out_specs=[near_spec()] * len(arrays),
        out_shape=[near(a.shape, a.dtype) for a in arrays],
        scratch_shapes=[pltpu.SemaphoreType.DMA((len(arrays),))],
        compiler_params=params(),
        name=name,
    )(*arrays)


def forward_kernel(
    head_size,
    chunk,
    first,
    place_ref,
    length_ref,
    own_ref,
    one_ref,
    two_ref,
    three_ref,
    pair_ref,
    gain_ref,
    shift_ref,
    query_weight_ref,
    query_bias_ref,
    key_weight_ref,
    value_weight_ref,
    value_bias_ref,
    _,
    pair_out_ref,
    weights_ref,
    mixed_ref,
    inverse_ref,
    hidden_ref,
    normed_ref,
    query_ref,
    key_ref,
    value_ref,
    atoms_scratch,
    pair_scratch,
    semaphores,
):
    molecule = pl.program_id(0)
    group = pl.program_id(1)
    count, groups, keys, width = key_ref.shape
    heads = width // head_size
    rows, model_width = own_ref.shape[1:]
    factor = head_size**-0.5

    def pair_copy(m, g):
        span = pl.ds(g * heads, heads)
        return pltpu.make_async_copy(
            pair_ref.at[m + first, span], pair_scratch.at[m, span], semaphores.at[m, g]
        )

    @pl.when((molecule == 0) & (group == 0))
    def _():
        for m in range(count):
            for g in range(groups):
                pair_copy(m, g).start()
        row = place_ref[1]
        gain = as_row(gain_ref)
        shift = as_row(shift_ref)
        query_bias = as_row(query_bias_ref)
        value_bias = as_row(value_bias_ref)
        ones = jnp.ones((keys, width), BF16)
        for m in range(count):
            for i, piece in enumerate((own_ref, one_ref, two_ref, three_ref)):
                start = pl.multiple_of((row ^ i) * rows, rows)
                atoms_scratch[pl.ds(start, rows)] = piece[m]
            hidden, normed, _ = norm_forward(atoms_scratch[...].astype(F32), gain, shift)
            hidden = hidden.astype(BF16)
            hidden_ref[m] = hidden
            normed_ref[m] = normed.astype(BF16)
            key_rows = dot(hidden, key_weight_ref[...]).astype(BF16)
            value_rows = (dot(hidden, value_weight_ref[...]) + value_bias).astype(BF16)
            for t in range(groups):
                lanes = slice(t * width, (t + 1) * width)
                key_ref[m, t] = key_rows[:, lanes]
                value_ref[m, t, :, :width] = value_rows[:, lanes]
                value_ref[m, t, :, width:] = ones
        own = own_ref[...].reshape(count * rows, model_width).astype(F32)
        own = norm_forward(own, gain, shift)[0].astype(BF16)
        query_rows = (dot(own, query_weight_ref[...]) + query_bias) * factor
        query_rows = query_rows.astype(BF16).reshape(count, rows, model_width)
        for t in range(groups):
            query_ref[:, t] = query_rows[:, :, t * width : (t + 1) * width]

    pair_copy(molecule, group).wait()
    query = query_ref[molecule, group]
    key = key_ref[molecule, group]
    value = value_ref[molecule, group]
    valid = lax.broadcasted_iota(jnp.int32, (1, keys), 1) < length_ref[molecule + first]
    lane = lax.broadcasted_iota(jnp.int32, (1, width), 1) // head_size
    lane_pair = lax.broadcasted_iota(jnp.int32, (1, 2 * width), 1) % width // head_size
    total = jnp.zeros((rows, 2 * width), F32)
    zero = jnp.zeros((), BF16)
    for c in range(0, heads, chunk):
        here = slice(c, c + chunk)
        there = pl.ds(group * heads + c, chunk)
        spread = jnp.concatenate([jnp.where(lane == c + t, query, zero) for t in range(chunk)], 0)
        pair = pair_scratch[molecule, there].reshape(chunk * rows, keys)
        scores = against(spread, key) + pair.astype(F32)
        pair_out_ref[0, here] = scores.astype(BF16).reshape(chunk, rows, keys)
        masked = jnp.where(valid, scores, MASKED)
        weights = jnp.exp(masked - jnp.max(masked, -1, keepdims=True)).astype(BF16)
        weights_ref[molecule, there] = weights.reshape(chunk, rows, keys)
        product = dot(weights, value)
        for t in range(chunk):
            total = jnp.where(lane_pair == c + t, product[t * rows : (t + 1) * rows], total)
    inverse = 1.0 / total[:, width:]
    inverse_ref[molecule, group] = inverse
    mixed_ref[molecule, group] = total[:, :width] * inverse


def attention_forward(head_size, first, count, place, lengths, pieces, pair_bias, parameters, held):
    _, head_count, rows, keys = pair_bias.shape
    model_width = pieces[0].shape[2]
    groups = model_width // LANES
    heads = LANES // head_size
    pair_spec = pl.BlockSpec((1, heads, rows, keys), lambda m, g, *_: (m + first, g, 0, 0))
    elements = count * head_count * rows * keys
    own_spec = pl.BlockSpec((count, rows, model_width), lambda *_: (first // count, 0, 0))
    operands = (place, lengths, *pieces, pair_bias, *parameters, held)
    return pl.pallas_call(
        functools.partial(forward_kernel, head_size, 8, first),
        grid_spec=pltpu.PrefetchScalarGridSpec(
            num_scalar_prefetch=2,
            grid=(count, groups),
            in_specs=[own_spec]
            + [near_spec()] * (len(pieces) - 1)
            + [pl.BlockSpec(memory_space=pltpu.HBM)]
            + [whole(a) for a in parameters]
            + [pl.BlockSpec(memory_space=pl.ANY)],
            out_specs=[pair_spec] + [near_spec()] * 8,
            scratch_shapes=[
                pltpu.VMEM((keys, model_width), BF16),
                pltpu.VMEM((count, head_count, rows, keys), BF16),
                pltpu.SemaphoreType.DMA((count, groups)),
            ],
        ),
        out_shape=[
            shape_of(pair_bias.shape, BF16),
            near((count, head_count, rows, keys), BF16),
            near((count, groups, rows, LANES), F32),
            near((count, groups, rows, LANES), F32),
            near((count, keys, model_width), BF16),
            near((count, keys, model_width), BF16),
            near((count, groups, rows, LANES), BF16),
            near((count, groups, keys, LANES), BF16),
            near((count, groups, keys, 2 * LANES), BF16),
        ],
        input_output_aliases={} if held.ndim == 1 else {len(operands) - 1: 0},
        compiler_params=params(16),
        cost_estimate=pl.CostEstimate(
            flops=elements * 2 * 384, transcendentals=elements, bytes_accessed=elements * 6
        ),
        name="attention_forward",
    )(*operands)


def dense_kernel(
    mixed_count,
    place_ref,
    *refs,
):
    mixed_refs = refs[:mixed_count]
    (
        atoms_ref,
        cotangent_ref,
        out_weight_ref,
        out_bias_ref,
        gain_ref,
        shift_ref,
        inner_weight_ref,
        inner_bias_ref,
        outer_weight_ref,
        outer_bias_ref,
        atoms_out_ref,
        outer_send_ref,
        outer_keep_ref,
        inner_send_ref,
        inner_keep_ref,
        out_send_ref,
        out_keep_ref,
        grad_middle_ref,
        grad_mixed_ref,
        vectors_ref,
        hidden_scratch,
        turned_scratch,
        normed_scratch,
        inverse_scratch,
        result_scratch,
        upstream_scratch,
        outer_scratch,
        inner_scratch,
    ) = refs[mixed_count:]
    step = pl.program_id(0)
    steps = pl.num_programs(0)
    core = place_ref[2]
    tokens, model_width = hidden_scratch.shape
    cotangent = cotangent_ref[...].reshape(tokens, model_width)

    def mixed_rows():
        parts = []
        for ref in mixed_refs:
            count, groups, rows, width = ref.shape
            join = [ref[:, t].reshape(count * rows, width) for t in range(groups)]
            parts.append(jnp.concatenate(join, 1))
        return jnp.concatenate(parts, 0)

    @pl.when(step == 0)
    def _():
        mixed_low = mixed_rows().astype(BF16)
        middle = (
            atoms_ref[...].reshape(tokens, model_width).astype(F32)
            + dot(mixed_low, out_weight_ref[...])
            + as_row(out_bias_ref)
        )
        hidden, normed, inverse = norm_forward(
            middle, as_row(gain_ref), as_row(shift_ref)
        )
        hidden_scratch[...] = hidden.astype(BF16)
        turned_scratch[...] = jnp.transpose(hidden).astype(BF16)
        normed_scratch[...] = normed
        inverse_scratch[...] = inverse
        result_scratch[...] = middle + as_row(outer_bias_ref)
        upstream_scratch[...] = jnp.zeros_like(upstream_scratch)
        vectors_ref[0:1] = column_sum(cotangent)

    hidden = hidden_scratch[...]
    pre = dot(hidden, inner_weight_ref[...]) + as_row(inner_bias_ref)
    slope = math.sqrt(2.0 / math.pi)
    square = pre * pre
    tanh = jnp.tanh(slope * (pre + 0.044715 * (pre * square)))
    half = 0.5 * (1.0 + tanh)
    active = (pre * half).astype(BF16)
    result_scratch[...] += dot(active, outer_weight_ref[...])
    derivative = half + (0.5 * slope) * pre * (1.0 - tanh * tanh) * (1.0 + 0.134145 * square)
    grad_pre = against(cotangent, outer_weight_ref[...]) * derivative
    vectors_ref[pl.ds(4 + step, 1)] = column_sum(grad_pre.astype(BF16))
    grad_pre = grad_pre.astype(BF16)
    outer_scratch[...] = across(active, cotangent).reshape(outer_scratch.shape)
    outer_send_ref[...] = outer_scratch[:, 1 - core].astype(BF16).reshape(outer_send_ref.shape)
    outer_keep_ref[...] = outer_scratch[:, core].astype(BF16).reshape(outer_keep_ref.shape)
    inner_scratch[...] = dot(turned_scratch[...], grad_pre).reshape(inner_scratch.shape)
    inner_send_ref[:, 0] = inner_scratch[:, 1 - core].astype(BF16)
    inner_keep_ref[:, 0] = inner_scratch[:, core].astype(BF16)
    upstream_scratch[...] += against(grad_pre, inner_weight_ref[...])

    @pl.when(step == steps - 1)
    def _():
        atoms_out_ref[...] = result_scratch[...].astype(BF16).reshape(atoms_out_ref.shape)
        upstream = upstream_scratch[...]
        normed = normed_scratch[...]
        vectors_ref[1:2] = column_sum(upstream * normed)
        vectors_ref[2:3] = column_sum(upstream)
        grad_middle = cotangent.astype(F32) + norm_backward(
            upstream, normed, inverse_scratch[...], as_row(gain_ref)
        )
        grad_middle_ref[...] = grad_middle.reshape(grad_middle_ref.shape)
        branch = grad_middle.astype(BF16)
        vectors_ref[3:4] = column_sum(branch)
        grad_mixed = against(branch, out_weight_ref[...]).astype(BF16)
        molecules, groups, rows, lanes = grad_mixed_ref.shape
        grad_mixed = grad_mixed.reshape(molecules, rows, model_width)
        for t in range(groups):
            grad_mixed_ref[:, t] = grad_mixed[:, :, t * lanes : (t + 1) * lanes]
        turned = jnp.transpose(mixed_rows()).astype(BF16)
        inner_scratch[...] = dot(turned, branch).reshape(inner_scratch.shape)
        out_send_ref[...] = inner_scratch[:, 1 - core].astype(BF16)
        out_keep_ref[...] = inner_scratch[:, core].astype(BF16)


def dense(place, mixed, atoms, cotangent, parameters, batch_count):
    (
        out_weight,
        out_bias,
        gain,
        shift,
        inner_weight,
        inner_bias,
        outer_weight,
        outer_bias,
    ) = parameters
    model_width, inner_width = inner_weight.shape
    tokens = atoms.shape[0] * atoms.shape[1]
    width = model_width
    steps = inner_width // width
    pairs = batch_count // 2
    outer_rows = inner_width // batch_count
    outer_pairs = width // (2 * outer_rows)
    own_rows = model_width // batch_count
    operands = (
        place,
        *mixed,
        atoms,
        cotangent,
        out_weight,
        out_bias,
        gain,
        shift,
        inner_weight,
        inner_bias,
        outer_weight,
        outer_bias,
    )
    outer_spec = pl.BlockSpec((outer_pairs, outer_rows, model_width), lambda s, *_: (s, 0, 0))
    inner_spec = pl.BlockSpec((pairs, 1, own_rows, width), lambda s, *_: (0, s, 0, 0))
    outer_shape = shape_of((pairs, outer_rows, model_width), BF16)
    inner_shape = shape_of((pairs, steps, own_rows, width), BF16)
    out_shape = shape_of((pairs, own_rows, model_width), BF16)
    out_shapes = [
        shape_of(atoms.shape, BF16),
        outer_shape,
        outer_shape,
        inner_shape,
        inner_shape,
        out_shape,
        out_shape,
        near(atoms.shape, F32),
        near((atoms.shape[0], model_width // LANES, atoms.shape[1], LANES), BF16),
        shape_of((4 + steps, model_width), F32),
    ]
    fixed = lambda s: pl.BlockSpec(s.shape, lambda *_: (0,) * len(s.shape))
    out_specs = [fixed(s) for s in out_shapes]
    out_specs[1:5] = [outer_spec, outer_spec, inner_spec, inner_spec]
    out_specs[7:9] = [near_spec(), near_spec()]
    in_specs = [whole(a) for a in operands[1:]]
    in_specs[: len(mixed)] = [near_spec() for _ in mixed]
    in_specs[-4] = pl.BlockSpec((model_width, width), lambda s, *_: (0, s))
    in_specs[-3] = pl.BlockSpec((width,), lambda s, *_: (s,))
    in_specs[-2] = pl.BlockSpec((width, model_width), lambda s, *_: (s, 0))
    return pl.pallas_call(
        functools.partial(dense_kernel, len(mixed)),
        grid_spec=pltpu.PrefetchScalarGridSpec(
            num_scalar_prefetch=1,
            grid=(steps,),
            in_specs=in_specs,
            out_specs=out_specs,
            scratch_shapes=[
                pltpu.VMEM((tokens, model_width), BF16),
                pltpu.VMEM((model_width, tokens), BF16),
                pltpu.VMEM((tokens, model_width), F32),
                pltpu.VMEM((tokens, 1), F32),
                pltpu.VMEM((tokens, model_width), F32),
                pltpu.VMEM((tokens, model_width), F32),
                pltpu.VMEM((outer_pairs, 2, outer_rows, model_width), F32),
                pltpu.VMEM((pairs, 2, own_rows, width), F32),
            ],
        ),
        out_shape=out_shapes,
        compiler_params=params(18),
        cost_estimate=pl.CostEstimate(
            flops=12 * tokens * model_width * inner_width,
            transcendentals=tokens * inner_width,
            bytes_accessed=12 * model_width * inner_width,
        ),
        name="dense",
    )(*operands)


def backward_kernel(
    head_size,
    chunk,
    first,
    base,
    start,
    fresh,
    place_ref,
    weights_ref,
    cotangent_ref,
    grad_mixed_ref,
    mixed_ref,
    inverse_ref,
    query_ref,
    key_ref,
    value_ref,
    normed_ref,
    query_weight_ref,
    key_weight_ref,
    value_weight_ref,
    *refs,
):
    refs = refs[start:]
    pair_grad_ref, near_ref, cross_ref, own_ref, vectors_ref = refs[:5]
    query_grad_ref, key_grad_ref, value_grad_ref = refs[5:8]
    grad_query_scratch, grad_key_scratch, grad_value_scratch, grad_scratch = refs[-4:]
    molecule = pl.program_id(0) + base
    group = pl.program_id(1)
    _, groups, rows, width = query_ref.shape
    keys = key_ref.shape[2]
    heads = width // head_size
    factor = head_size**-0.5
    query = query_ref[molecule, group]
    key = key_ref[molecule, group]
    value = value_ref[molecule, group]
    upstream = grad_mixed_ref[molecule + first, group].astype(F32) * inverse_ref[molecule, group]
    upstream = upstream.astype(BF16)
    offset = (-(upstream.astype(F32) * mixed_ref[molecule, group])).astype(BF16)
    both = jnp.concatenate([upstream, offset], 1)
    lane = lax.broadcasted_iota(jnp.int32, (1, width), 1) // head_size
    lane_pair = lax.broadcasted_iota(jnp.int32, (1, 2 * width), 1) % width // head_size
    query_turned = jnp.transpose(query.astype(F32)).astype(BF16)
    upstream_turned = jnp.transpose(upstream.astype(F32)).astype(BF16)
    query_turned = jnp.concatenate([query_turned] * chunk, 1)
    upstream_turned = jnp.concatenate([upstream_turned] * chunk, 1)
    turned_shape = (chunk * head_size, chunk * rows)
    same = (
        lax.broadcasted_iota(jnp.int32, turned_shape, 0) // head_size
        == lax.broadcasted_iota(jnp.int32, turned_shape, 1) // rows
    )
    zero = jnp.zeros((), BF16)
    total = jnp.zeros((rows, width), F32)
    key_parts = []
    value_parts = []
    for c in range(0, heads, chunk):
        here = slice(c, c + chunk)
        feature = slice(c * head_size, (c + chunk) * head_size)
        spread = jnp.concatenate([jnp.where(lane_pair == c + t, both, zero) for t in range(chunk)], 0)
        centred = against(spread, value)
        there = pl.ds(group * heads + c, chunk)
        weights = weights_ref[molecule, there].reshape(chunk * rows, keys)
        cotangent = cotangent_ref[0, here].reshape(chunk * rows, keys)
        grad = (weights.astype(F32) * centred + cotangent.astype(F32)).astype(BF16)
        pair_grad_ref[0, here] = grad.reshape(chunk, rows, keys)
        product = dot(grad, key)
        for t in range(chunk):
            total = jnp.where(lane == c + t, product[t * rows : (t + 1) * rows], total)
        key_parts.append(dot(jnp.where(same, query_turned[feature], zero), grad))
        value_parts.append(dot(jnp.where(same, upstream_turned[feature], zero), weights))
    grad_query_scratch[group] = (total * factor).astype(BF16)
    grad_key_scratch[group] = jnp.transpose(jnp.concatenate(key_parts, 0)).astype(BF16)
    grad_value_scratch[group] = jnp.transpose(jnp.concatenate(value_parts, 0)).astype(BF16)

    if fresh:

        @pl.when((pl.program_id(0) == 0) & (group == 0))
        def _():
            vectors_ref[...] = jnp.zeros_like(vectors_ref)

    @pl.when(group == groups - 1)
    def _():
        row = place_ref[1]
        mine = pl.ds(pl.multiple_of(row * rows, rows), rows)
        join = lambda ref: jnp.concatenate([ref[t] for t in range(groups)], 1)
        grad_query = join(grad_query_scratch)
        grad_key = join(grad_key_scratch)
        grad_value = join(grad_value_scratch)
        at = pl.program_id(0)
        query_grad_ref[at] = grad_query
        key_grad_ref[at] = grad_key
        value_grad_ref[at] = grad_value
        grad_scratch[...] = against(grad_key, key_weight_ref[...]) + against(
            grad_value, value_weight_ref[...]
        )
        grad_scratch[mine] += against(grad_query, query_weight_ref[...])
        grad = grad_scratch[...]
        vectors_ref[0:1] += column_sum(grad * normed_ref[molecule].astype(F32))
        vectors_ref[1:2] += column_sum(grad)
        vectors_ref[2:3] += column_sum(grad_query)
        vectors_ref[3:4] += column_sum(grad_value)
        at = lambda other: pl.ds(pl.multiple_of((row ^ other) * rows, rows), rows)
        near_ref[0, 0] = grad_scratch[at(1)].astype(BF16)
        near_ref[1, 0] = grad_scratch[at(3)].astype(BF16)
        cross_ref[0] = grad_scratch[at(2)].astype(BF16)
        own_ref[pl.program_id(0)] = grad_scratch[mine]

def attention_backward(
    head_size, first, span, place, stage, cotangent, grad_mixed, parameters, held, sums, after
):
    weights, mixed, inverse, _, normed, query, key, value = stage
    _, head_count, rows, keys = weights.shape
    base, count = span[0], span[1] - span[0]
    groups = query.shape[1]
    model_width = groups * LANES
    heads = LANES // head_size
    pair_spec = pl.BlockSpec((1, heads, rows, keys), lambda m, g, *_: (m + first + base, g, 0, 0))
    elements = count * head_count * rows * keys
    operands = [
        place,
        weights,
        cotangent,
        grad_mixed,
        mixed,
        inverse,
        query,
        key,
        value,
        normed,
        *parameters,
    ]
    in_specs = [near_spec()] * (len(operands) - 1)
    in_specs[1] = pair_spec
    in_specs[-3:] = [whole(a) for a in parameters]
    aliases = {}
    start = len(operands)
    if sums is not None:
        aliases = {start: 0, start + 1: 4}
        operands += [held, sums]
        in_specs += [pl.BlockSpec(memory_space=pl.ANY), near_spec()]
    operands += list(after)
    in_specs += [pl.BlockSpec(memory_space=pl.ANY)] * len(after)
    out_shape = [
        shape_of(cotangent.shape, BF16),
        shape_of((2, count, rows, model_width), BF16),
        shape_of((count, rows, model_width), BF16),
        near((count, rows, model_width), F32),
        near((8, model_width), F32),
        near((count, rows, model_width), BF16),
        near((count, keys, model_width), BF16),
        near((count, keys, model_width), BF16),
    ]
    out_specs = [
        pair_spec,
        pl.BlockSpec((2, 1, rows, model_width), lambda m, g, *_: (0, m, 0, 0)),
        pl.BlockSpec((1, rows, model_width), lambda m, g, *_: (m, 0, 0)),
        near_spec(),
        near_spec(),
        near_spec(),
        near_spec(),
        near_spec(),
    ]
    return pl.pallas_call(
        functools.partial(
            backward_kernel, head_size, 4, first, base, len(operands) - start, sums is None
        ),
        grid_spec=pltpu.PrefetchScalarGridSpec(
            num_scalar_prefetch=1,
            grid=(count, groups),
            in_specs=in_specs,
            out_specs=out_specs,
            scratch_shapes=[
                pltpu.VMEM((groups, rows, LANES), BF16),
                pltpu.VMEM((groups, keys, LANES), BF16),
                pltpu.VMEM((groups, keys, LANES), BF16),
                pltpu.VMEM((keys, model_width), F32),
            ],
        ),
        out_shape=out_shape,
        input_output_aliases=aliases,
        compiler_params=params(14),
        cost_estimate=pl.CostEstimate(
            flops=elements * 2 * 768, transcendentals=0, bytes_accessed=elements * 6
        ),
        name="attention_backward",
    )(*operands)


def weight_kernel(calls, stages, place_ref, *refs):
    hidden_refs = refs[:stages]
    grads = refs[stages : stages + 3 * calls]
    out_refs = refs[stages + 3 * calls : -1]
    total_ref = refs[-1]
    rows = grads[0].shape[1]
    row = place_ref[1]
    core = place_ref[2]
    mine = pl.ds(pl.multiple_of(row * rows, rows), rows)
    hidden = [(ref, m) for ref in hidden_refs for m in range(ref.shape[0])]
    width = hidden_refs[0].shape[2]
    own = jnp.concatenate([ref[m, mine] for ref, m in hidden], 0)
    every = jnp.concatenate([ref[m] for ref, m in hidden], 0)
    own = jnp.transpose(own.astype(F32)).astype(BF16)
    every = jnp.transpose(every.astype(F32)).astype(BF16)
    for j, left in enumerate((own, every, every)):
        right = jnp.concatenate([grads[3 * c + j][...].reshape(-1, width) for c in range(calls)], 0)
        total_ref[...] = dot(left, right).reshape(total_ref.shape)
        send_ref, keep_ref = out_refs[2 * j : 2 * j + 2]
        send_ref[:, 0] = total_ref[:, 1 - core].astype(BF16)
        keep_ref[:, 0] = total_ref[:, core].astype(BF16)


def swap(value, axis, mask):
    size = lax.axis_size(axis)
    return lax.ppermute(value, axis, [(i, i ^ mask) for i in range(size)])


VECTOR_ROWS = 8


def first_sum_kernel(counts, place_ref, *refs):
    terms = sum(counts)
    mine_ref, other_ref = refs[terms : terms + 2]
    along_x_ref, along_y_ref, keep_x_ref, keep_y_ref, vectors_ref = refs[terms + 2 :]
    x, y = place_ref[3], place_ref[4]
    half = along_x_ref.shape[1]
    size = keep_x_ref.shape[1]
    low, high = slice(0, half), slice(half, None)
    row = 0
    start = 0
    for count in counts:
        group = refs[start : start + count]
        start += count
        for s in range(group[0].shape[1]):
            rows = group[0].shape[2]

            def total(at, lanes):
                values = [r[at, s, :, lanes].astype(F32) for r in group]
                return functools.reduce(lambda a, b: a + b, values)

            for k in range(2):
                to = slice(k * size + row, k * size + row + rows)
                here = slice(row, row + rows)
                along_x_ref[to] = total(2 * k + (1 - x), low).astype(BF16)
                keep_x_ref[k, here] = total(2 * k + x, low)
                along_y_ref[to] = total(2 * (1 - y) + k, high).astype(BF16)
                keep_y_ref[k, here] = total(2 * y + k, high)
            row += rows
    vectors = (mine_ref[...] + other_ref[...]).astype(BF16)
    vectors_ref[...] = vectors
    put_vectors(vectors, along_x_ref, along_y_ref)


def put_vectors(vectors, low_ref, high_ref):
    half = vectors.shape[1] // 2
    low_ref[low_ref.shape[0] - VECTOR_ROWS :] = vectors[:, :half]
    high_ref[high_ref.shape[0] - VECTOR_ROWS :] = vectors[:, half:]


def get_vectors(low_ref, high_ref):
    low = low_ref[low_ref.shape[0] - VECTOR_ROWS :]
    return jnp.concatenate([low, high_ref[high_ref.shape[0] - VECTOR_ROWS :]], 1).astype(F32)


def second_sum_kernel(
    place_ref,
    keep_x_ref,
    came_x_ref,
    keep_y_ref,
    came_y_ref,
    vectors_ref,
    send_y_ref,
    send_x_ref,
    left_x_ref,
    left_y_ref,
    vectors_out_ref,
):
    size = keep_x_ref.shape[1]
    for keep, came, send, left, me in (
        (keep_x_ref, came_x_ref, send_y_ref, left_x_ref, place_ref[4]),
        (keep_y_ref, came_y_ref, send_x_ref, left_y_ref, place_ref[3]),
    ):
        at = lambda i: pl.ds(pl.multiple_of(i * size, size), size)
        send[:size] = (keep[1 - me] + came[at(1 - me)].astype(F32)).astype(BF16)
        left[...] = keep[me] + came[at(me)].astype(F32)
    vectors = vectors_ref[...].astype(F32) + get_vectors(came_x_ref, came_y_ref)
    vectors = vectors.astype(BF16)
    vectors_out_ref[...] = vectors
    put_vectors(vectors, send_y_ref, send_x_ref)


def third_sum_kernel(left_x_ref, came_x_ref, left_y_ref, came_y_ref, vectors_ref, total_ref):
    size, half = left_x_ref.shape
    total_ref[:size, :half] = (left_x_ref[...] + came_x_ref[:size].astype(F32)).astype(BF16)
    total_ref[:size, half:] = (left_y_ref[...] + came_y_ref[:size].astype(F32)).astype(BF16)
    vectors = vectors_ref[...].astype(F32) + get_vectors(came_x_ref, came_y_ref)
    total_ref[size : size + VECTOR_ROWS] = vectors.astype(BF16)


def third_cut_kernel(place_ref, *refs):
    third_sum_kernel(*refs[:-1])
    total_ref, sent_ref = refs[-2:]
    filled = refs[0].shape[0] + VECTOR_ROWS
    if filled < total_ref.shape[0]:
        total_ref[filled:] = jnp.zeros((total_ref.shape[0] - filled, total_ref.shape[1]), BF16)
    half = sent_ref.shape[0]
    away = pl.multiple_of((1 - (place_ref[1] & 1)) * half, half)
    sent_ref[...] = total_ref[pl.ds(away, half)]


def near_sum_kernel(place_ref, total_ref, came_ref, sent_ref, kept_ref):
    half, part = came_ref.shape[0], sent_ref.shape[0]
    row = place_ref[1]
    here = (row & 1) * half

    def total(other):
        start = other * part
        mine = total_ref[pl.ds(pl.multiple_of(here + start, part), part)]
        return mine.astype(F32) + came_ref[pl.ds(pl.multiple_of(start, part), part)].astype(F32)

    kept_ref[...] = total(row >> 1)
    sent_ref[...] = total(1 - (row >> 1)).astype(BF16)


def add_kernel(left_ref, right_ref, out_ref):
    out_ref[...] = (left_ref[...].astype(F32) + right_ref[...].astype(F32)).astype(out_ref.dtype)


def join_rows(place, mine_ref, other_ref, out_ref):
    part = mine_ref.shape[0]
    out_ref[pl.ds(pl.multiple_of(place * part, part), part)] = mine_ref[...]
    out_ref[pl.ds(pl.multiple_of((1 - place) * part, part), part)] = other_ref[...]


def join_kernel(place_ref, mine_ref, other_ref, out_ref):
    join_rows(place_ref[1] >> 1, mine_ref, other_ref, out_ref)


def finish_dense_kernel(
    ratio, place_ref, mine_ref, other_ref, outer_ref, inner_ref, out_ref, vectors_ref, total_scratch
):
    rows, width = out_ref.shape
    join_rows(place_ref[1] & 1, mine_ref, other_ref, total_scratch)
    outer_ref[...] = total_scratch[: ratio * rows].astype(F32)
    for s in range(ratio):
        at = (ratio + s) * rows
        inner_ref[:, s * width : (s + 1) * width] = total_scratch[at : at + rows].astype(F32)
    at = 2 * ratio * rows
    out_ref[...] = total_scratch[at : at + rows].astype(F32)
    vectors_ref[...] = total_scratch[at + rows : at + rows + VECTOR_ROWS].astype(F32)


def finish_tail_kernel(low_ref, came_ref, query_ref, key_ref, value_ref, vectors_ref):
    rows = query_ref.shape[0]
    for s, ref in enumerate((query_ref, key_ref, value_ref, vectors_ref)):
        at = slice(s * rows, s * rows + ref.shape[0])
        ref[...] = low_ref[at].astype(F32) + came_ref[at].astype(F32)


def small_call(kernel, place, operands, out_shapes, name, after=(), inside=True, scratch=(), mib=4):
    ahead = 0 if place is None else 1
    count = len(operands)

    def body(*refs):
        kernel(*refs[: ahead + count], *refs[ahead + count + len(after) :])

    size = sum(math.prod(a.shape) * a.dtype.itemsize for a in list(operands) + list(out_shapes))
    return pl.pallas_call(
        body,
        grid_spec=pltpu.PrefetchScalarGridSpec(
            num_scalar_prefetch=ahead,
            grid=(1,),
            in_specs=[near_spec() for a in operands] + [pl.BlockSpec(memory_space=pl.ANY)] * len(after),
            out_specs=[near_spec() for s in out_shapes],
            scratch_shapes=list(scratch),
        ),
        out_shape=[near(s.shape, s.dtype) if inside else s for s in out_shapes],
        compiler_params=params(mib),
        cost_estimate=pl.CostEstimate(flops=0, transcendentals=0, bytes_accessed=size),
        name=name,
    )(*(() if place is None else (place,)), *operands, *after)


def sum_core(place, groups, vectors, name, after=()):
    groups = [list(g) + [swap(a, "batch", 1) for a in sent] for g, sent in groups]
    vectors_other = swap(vectors, "batch", 1)
    _, _, rows, width = groups[0][0].shape
    size = sum(g[0].shape[1] for g in groups) * rows
    half = width // 2
    counts = tuple(len(g) for g in groups)
    message = shape_of((2 * size + VECTOR_ROWS, half), BF16)
    kept = shape_of((2, size, half), F32)
    along_x, along_y, keep_x, keep_y, vectors = small_call(
        functools.partial(first_sum_kernel, counts),
        place,
        [a for g in groups for a in g] + [vectors, vectors_other],
        [message, message, kept, kept, shape_of(vectors.shape, BF16)],
        name + "_sum_core",
        after,
    )
    came_x, came_y = swap(along_x, "batch", 2), swap(along_y, "batch", 4)
    return (keep_x, came_x, keep_y, came_y, vectors), along_x


def sum_first(place, pieces, name, after=()):
    keep_x, _, _, _, vectors = pieces
    _, size, half = keep_x.shape
    message = shape_of((size + VECTOR_ROWS, half), BF16)
    kept = shape_of((size, half), F32)
    send_y, send_x, left_x, left_y, vectors = small_call(
        second_sum_kernel,
        place,
        pieces,
        [message, message, kept, kept, shape_of(vectors.shape, BF16)],
        name + "_sum_first",
        after,
    )
    came_x, came_y = swap(send_y, "batch", 4), swap(send_x, "batch", 2)
    return (left_x, came_x, left_y, came_y, vectors), send_y


def sum_second(pieces, name, after=()):
    size, half = pieces[0].shape
    shape = shape_of((size + VECTOR_ROWS, 2 * half), BF16)
    return small_call(third_sum_kernel, None, pieces, [shape], name + "_sum_second", after)[0]


def sum_second_cut(place, pieces, name, after=()):
    size, half = pieces[0].shape
    rows = -(-(size + VECTOR_ROWS) // 32) * 32
    total, sent = small_call(
        third_cut_kernel,
        place,
        pieces,
        [shape_of((rows, 2 * half), BF16), shape_of((rows // 2, 2 * half), BF16)],
        name + "_sum_second",
        after,
    )
    return total, swap(sent, "rows", 1)


def batch_slices_any(groups, vectors):
    me = lax.axis_index("batch")
    bits = lax.axis_size("batch").bit_length() - 1
    pieces = []
    for kept, sent in groups:
        values = [a.astype(F32) for a in kept] + [swap(a, "batch", 1).astype(F32) for a in sent]
        pieces.append(functools.reduce(lambda a, b: a + b, values))
    total = jnp.concatenate(pieces, 1)
    total = total.reshape((2,) * (bits - 1) + total.shape[1:])
    for bit in range(bits - 1, 0, -1):
        mine = (me >> bit) & 1
        sent = lax.dynamic_index_in_dim(total, 1 - mine, 0, keepdims=False).astype(BF16)
        total = lax.dynamic_index_in_dim(total, mine, 0, keepdims=False)
        total = total + swap(sent, "batch", 1 << bit).astype(F32)
    total = lax.psum(total.astype(BF16), "rows").astype(F32)
    return total, lax.psum(vectors, ("batch", "rows"))


def cross_kernel(count, *refs):
    out_ref = refs[-1]
    start = 0
    for term, came in zip(refs[:count], refs[count : 2 * count]):
        end = start + term.shape[0]
        out_ref[start:end] = (term[...].astype(F32) + came[1].astype(F32)).astype(BF16)
        start = end


def cross_sum(terms, came, name, after=()):
    shape = (sum(t.shape[0] for t in terms),) + terms[0].shape[1:]
    return small_call(
        functools.partial(cross_kernel, len(terms)),
        None,
        list(terms) + list(came),
        [shape_of(shape, BF16)],
        name,
        after,
    )[0]


def final_kernel(calls, crosses, *refs):
    own_refs, near_refs = refs[:calls], refs[calls : 2 * calls]
    cross_refs = refs[2 * calls : 2 * calls + crosses]
    atoms_ref, gain_ref, shift_ref, grad_middle_ref, out_ref = refs[2 * calls + crosses :]
    rows, width = own_refs[0].shape[1:]
    gain = as_row(gain_ref)
    shift = as_row(shift_ref)
    crosses = [(ref, i) for ref in cross_refs for i in range(ref.shape[0])]
    m = 0
    for own_ref, near_ref in zip(own_refs, near_refs):
        for i in range(own_ref.shape[0]):
            cross_ref, at = crosses[m]
            grad = own_ref[i] + near_ref[0, i].astype(F32) + cross_ref[at].astype(F32)
            _, normed, inverse = norm_forward(atoms_ref[m].astype(F32), gain, shift)
            result = grad_middle_ref[m] + norm_backward(grad, normed, inverse, gain)
            out_ref[m] = result.astype(BF16)
            m += 1


def first_norm_backward(owns, nears, crosses, others, after=()):
    return small_call(
        functools.partial(final_kernel, len(owns), len(crosses)),
        None,
        owns + nears + crosses + list(others),
        [shape_of(others[0].shape, BF16)],
        "first_norm_backward",
        after,
        inside=False,
    )[0]


def shards(
    atoms,
    pair_bias,
    lengths,
    first_gain,
    first_shift,
    query_weight,
    query_bias,
    key_weight,
    value_weight,
    value_bias,
    out_weight,
    out_bias,
    second_gain,
    second_shift,
    inner_weight,
    inner_bias,
    outer_weight,
    outer_bias,
    atoms_cotangent,
    pair_cotangent,
):
    molecules, rows, model_width = atoms.shape
    head_count = pair_bias.shape[1]
    head_size = model_width // head_count
    batch_count = lax.axis_size("batch")
    batch_index = lax.axis_index("batch")
    row = lax.axis_index("rows")
    (
        atoms_far,
        pair_bias,
        first_gain,
        first_shift,
        query_weight,
        query_bias,
        key_weight,
        value_weight,
        value_bias,
        out_weight,
        out_bias,
        second_gain,
        second_shift,
        inner_weight,
        inner_bias,
        outer_weight,
        outer_bias,
        atoms_cotangent,
        pair_cotangent,
    ) = [
        pltpu.with_memory_space_constraint(a, pltpu.HBM)
        for a in (
            atoms,
            pair_bias,
            first_gain,
            first_shift,
            query_weight,
            query_bias,
            key_weight,
            value_weight,
            value_bias,
            out_weight,
            out_bias,
            second_gain,
            second_shift,
            inner_weight,
            inner_bias,
            outer_weight,
            outer_bias,
            atoms_cotangent,
            pair_cotangent,
        )
    ]
    place = jnp.stack(
        [batch_index, row, batch_index & 1, (batch_index >> 1) & 1, (batch_index >> 2) & 1]
    ).astype(jnp.int32)
    line = lambda v: v
    count = molecules // STAGES
    stages = []
    pair_out = jnp.zeros((1,), BF16)
    gathered = []
    for stage in range(STAGES):
        mine = atoms[stage * count : (stage + 1) * count]
        gathered.append([swap(mine, "rows", mask) for mask in (1, 2, 3)])
    pair_near, query_near, key_near, value_near = pair_bias, query_weight, key_weight, value_weight
    for stage in range(STAGES):
        first = stage * count
        pieces = [atoms_far] + gathered[stage]
        pair_out, *kept = attention_forward(
            head_size,
            first,
            count,
            place,
            lengths,
            pieces,
            pair_near,
            (
                line(first_gain),
                line(first_shift),
                query_near,
                line(query_bias),
                key_near,
                value_near,
                line(value_bias),
            ),
            pair_out,
        )
        stages.append(kept)
    (
        atoms_out,
        outer_send,
        outer_keep,
        inner_send,
        inner_keep,
        out_send,
        out_keep,
        grad_middle,
        grad_mixed,
        dense_vectors,
    ) = dense(
        place,
        [s[1] for s in stages],
        atoms,
        atoms_cotangent,
        (
            out_weight,
            line(out_bias),
            line(second_gain),
            line(second_shift),
            inner_weight,
            line(inner_bias),
            outer_weight,
            line(outer_bias),
        ),
        batch_count,
    )
    pairs = batch_count // 2
    own_rows = model_width // batch_count
    slots = lambda a: a.reshape(pairs, -1, own_rows, model_width)
    dense_groups = [
        ([slots(outer_keep)], [slots(outer_send)]),
        ([inner_keep], [inner_send]),
        ([slots(out_keep)], [slots(out_send)]),
    ]
    usual = batch_count == 8
    if usual:
        dense_pieces, held = sum_core(place, dense_groups, dense_vectors, "dense")
        after = [held]
    else:
        dense_total, dense_vectors = batch_slices_any(dense_groups, dense_vectors)
        after = []

    def backward(stage, span, held, sums, after):
        return attention_backward(
            head_size,
            stage * count,
            span,
            place,
            stages[stage],
            pair_cotangent,
            grad_mixed,
            (query_near, key_near, value_near),
            held,
            sums,
            after,
        )

    pair_grad, near0, cross0, own0, sums, *grads0 = backward(0, (0, count), None, None, after)
    near0 = swap(near0, "rows", 1)
    after = []
    if usual:
        dense_pieces, held = sum_first(place, dense_pieces, "dense", (own0,))
        after = [held]
    half = count // 2
    pair_grad, near1, cross1, own1, sums, *grads1 = backward(1, (0, half), pair_grad, sums, after)
    near1 = swap(near1, "rows", 1)
    after = [own1]
    came = near1
    if usual:
        dense_total, came = sum_second_cut(place, dense_pieces, "dense", after)
        after = [dense_total]
    cross0 = cross_sum([cross0], [near0], "cross_first", after)
    far0 = swap(cross0, "rows", 2)
    pair_grad, near2, cross2, own2, tail_vectors, *grads2 = backward(
        1, (half, count), pair_grad, sums, [cross0]
    )
    near2 = swap(near2, "rows", 1)
    part = shape_of((pairs, 1, own_rows, model_width), BF16)
    parts = small_call(
        functools.partial(weight_kernel, 3, STAGES),
        place,
        [s[3] for s in stages] + grads0 + grads1 + grads2,
        [part] * 6,
        "attention_weights",
        (far0, near1, came),
        scratch=[pltpu.VMEM((pairs, 2, own_rows, model_width), F32)],
        mib=14,
    )
    groups = [([parts[2 * i + 1]], [parts[2 * i]]) for i in range(3)]
    matrix = shape_of((own_rows, model_width), F32)
    ratio = inner_weight.shape[1] // model_width
    vectors_shape = shape_of((8, model_width), F32)
    finish = (atoms, line(first_gain), line(first_shift), grad_middle)
    if usual:
        pieces, held = sum_core(place, groups, tail_vectors, "tail")
        part = shape_of((came.shape[0] // 2, model_width), BF16)
        sent, kept = small_call(
            near_sum_kernel,
            place,
            [dense_total, came],
            [part, shape_of(part.shape, F32)],
            "dense_near_sum",
            (held,),
        )
        came = swap(sent, "rows", 2)
        cross1 = cross_sum([cross1, cross2], [near1, near2], "cross_second", (sent,))
        far1 = swap(cross1, "rows", 2)
        pieces, held = sum_first(place, pieces, "tail", (cross1,))
        total = sum_second(pieces, "tail", (held,))
        tail_came = swap(total, "rows", 1)
        mine = small_call(add_kernel, None, [kept, came], [part], "dense_far_sum", (total,))[0]
        came = swap(mine, "rows", 2)
        atoms_grad = first_norm_backward(
            [own0, own1, own2], [near0, near1, near2], [far0, far1], finish, (mine,)
        )
        total = small_call(
            add_kernel, None, [total, tail_came], [total], "tail_near_sum", (atoms_grad,)
        )[0]
        tail_came = swap(total, "rows", 2)
        half_shape = shape_of((2 * part.shape[0], model_width), BF16)
        mine = small_call(
            join_kernel, place, [mine, came], [half_shape], "dense_join", (total,)
        )[0]
        came = swap(mine, "rows", 1)
        outer_grad, inner_grad, out_grad, dense_vectors = small_call(
            functools.partial(finish_dense_kernel, ratio),
            place,
            [mine, came],
            [
                shape_of((ratio * own_rows, model_width), F32),
                shape_of((own_rows, ratio * model_width), F32),
                matrix,
                vectors_shape,
            ],
            "finish_dense",
            (total,),
            inside=False,
            scratch=[pltpu.VMEM((4 * part.shape[0], model_width), BF16)],
        )
        query_grad, key_grad, value_grad, tail_vectors = small_call(
            finish_tail_kernel,
            None,
            [total, tail_came],
            [matrix, matrix, matrix, vectors_shape],
            "finish_tail",
            (out_grad,),
            inside=False,
        )
    else:
        far1 = swap(cross_sum([cross1, cross2], [near1, near2], "cross_second"), "rows", 2)
        atoms_grad = first_norm_backward(
            [own0, own1, own2], [near0, near1, near2], [far0, far1], finish
        )
        total, tail_vectors = batch_slices_any(groups, tail_vectors)
        query_grad, key_grad, value_grad = total[0], total[1], total[2]
        outer_grad = dense_total[:ratio].reshape(-1, model_width)
        inner_grad = dense_total[ratio : 2 * ratio].transpose(1, 0, 2).reshape(own_rows, -1)
        out_grad = dense_total[2 * ratio]
    part = lambda v: lax.dynamic_slice_in_dim(
        v, batch_index * (v.shape[0] // batch_count), v.shape[0] // batch_count
    )
    return (
        atoms_out,
        pair_out,
        atoms_grad,
        pair_grad,
        part(tail_vectors[0]),
        part(tail_vectors[1]),
        query_grad,
        part(tail_vectors[2]),
        key_grad,
        value_grad,
        part(tail_vectors[3]),
        out_grad,
        part(dense_vectors[3]),
        part(dense_vectors[1]),
        part(dense_vectors[2]),
        inner_grad,
        part(dense_vectors[4:].reshape(-1)),
        outer_grad,
        part(dense_vectors[0]),
    )


def solution(mesh):
    tokens = P("batch", "rows", None)
    pairs = P("batch", None, "rows", None)
    vector = P("batch")
    matrix = P("batch", None)
    return jax.shard_map(
        shards,
        mesh=mesh,
        in_specs=(tokens, pairs, P("batch")) + (P(),) * 15 + (tokens, pairs),
        out_specs=(
            tokens,
            pairs,
            tokens,
            pairs,
            vector,
            vector,
            matrix,
            vector,
            matrix,
            matrix,
            vector,
            matrix,
            vector,
            vector,
            vector,
            matrix,
            vector,
            matrix,
            vector,
        ),
        check_vma=False,
    )
```

time: 199 us -> 159 us (0.80)
  Pallas kernels: 91.3 us -> 67.6 us
  local copies, waits for them, and re-layouts: 26.8 us -> 6.59 us
  starting transfers between devices: 37.5 us -> 44.6 us
  other arithmetic: 4.55 us -> 0 us
  waiting for transfers between devices: 36 us -> 38.4 us
    broadcast_in_dim x9 -> x0, local copies, waits for them, and re-layouts: 11.4 us -> none  [shards(): line = lambda v: v[None]]
    pallas_call x4 -> x5, Pallas kernels: 58 us -> 46.7 us  [the longest x3 27.8 us: attention_backward(): pl.pallas_call(functools.partial(backward_kernel, head_size, 4, first, ba...]
    pallas_call x7 -> x16, Pallas kernels: 22.6 us -> 11.6 us  [small_call(): pl.pallas_call(body, grid_spec=pltpu.PrefetchScalarGridSpec(num_scalar_pr...]
    ppermute x31 -> x33, starting transfers between devices: 37.5 us -> 44.6 us  [swap(): return lax.ppermute(value, axis, [(i, i ^ mask) for i in range(size)])]
    unnamed x63 -> x12, local copies, waits for them, and re-layouts: 8.56 us -> 2.52 us
    ppermute x31 -> x33, waiting for transfers between devices: 36 us -> 38.4 us  [swap(): return lax.ppermute(value, axis, [(i, i ^ mask) for i in range(size)])]
  transfers between devices with their start and end apart: 31 -> 33, of which waited for: 9 -> 12; matrix products, arithmetic and copies ran while one was open for 9% -> 0% of each run, Pallas kernels for 29% -> 27%
where the time goes in v3:
time: 159 us; the launch traced here: 158 us
  Pallas kernels  67.6 us (43%)
  starting transfers between devices  44.6 us (28%)
  waiting for transfers between devices  38.4 us (24%)
  local copies, waits for them, and re-layouts  6.59 us (4%)
    ppermute x33, starting transfers between devices, swap(): return lax.ppermute(value, axis, [(i, i ^ mask) for i in range(size)])  44.6 us
    ppermute x33, waiting for transfers between devices, swap(): return lax.ppermute(value, axis, [(i, i ^ mask) for i in range(size)])  38.4 us
    pallas_call x3, Pallas kernels, attention_backward(): pl.pallas_call(functools.partial(backward_kernel, head_size, 4, first, ba...  27.8 us
    pallas_call x2, Pallas kernels, attention_forward(): pl.pallas_call(functools.partial(forward_kernel, head_size, 8, first), gr...  18.8 us
    pallas_call x16, Pallas kernels, small_call(): pl.pallas_call(body, grid_spec=pltpu.PrefetchScalarGridSpec(num_scalar_pr...  11.6 us
    pallas_call x1, Pallas kernels, dense(): pl.pallas_call(functools.partial(dense_kernel, len(mixed)), grid_spec=plt...  9.27 us
  transfers between devices with their start and end apart: 33, of which 12 were waited for; matrix products, arithmetic and copies ran while one was open for 0% of the time, Pallas kernels for 27%

profile of v3, /device:TPU:0, one launch (start us, length us, event | category | flops | bytes accessed | tf_op | source)
XLA Modules:
  0.0 158.1 jit_solution(15648167176066035410)
XLA Ops:
  1.7 3.1 %collective-permute-start = (bf16[2,64,512]{2,1,0:T(8,128)(2,1)S(1)}, bf16[2,64,512]{2,1,0:T(8,128)(2,1)S(1)}, u32[]{:S(2)}, u32[]{:S(2)}) collective-permute-start(bf16[2,64,512]{2,1,0:T(8,128)(2,1)S(1)} %get-tuple-element.200), channel_id=1, source_target_pairs={{0,1},{1,0},{2,3},{3,2},{4,5},{5,4},{6,7},{7,6},{8,9},{9,8},{10,11... | collective-permute-start | bytes 393224 | tf_op jit(solution)/shard_map/ppermute | solution.py:664
  4.8 2.6 %collective-permute-start.1 = (bf16[2,64,512]{2,1,0:T(8,128)(2,1)S(1)}, bf16[2,64,512]{2,1,0:T(8,128)(2,1)S(1)}, u32[]{:S(2)}, u32[]{:S(2)}) collective-permute-start(bf16[2,64,512]{2,1,0:T(8,128)(2,1)S(1)} %get-tuple-element.200), channel_id=1, source_target_pairs={{0,2},{1,3},{2,0},{3,1},{4,6},{5,7},{6,4},{7,5},{8,10},{9,11},{10,... | collective-permute-start | bytes 393224 | tf_op jit(solution)/shard_map/ppermute | solution.py:664
  8.2 3.5 %collective-permute-start.4 = (bf16[2,64,512]{2,1,0:T(8,128)(2,1)S(1)}, bf16[2,64,512]{2,1,0:T(8,128)(2,1)S(1)}, u32[]{:S(2)}, u32[]{:S(2)}) collective-permute-start(bf16[2,64,512]{2,1,0:T(8,128)(2,1)S(1)} %get-tuple-element.199), channel_id=1, source_target_pairs={{0,2},{1,3},{2,0},{3,1},{4,6},{5,7},{6,4},{7,5},{8,10},{9,11},{10,... | collective-permute-start | bytes 393224 | tf_op jit(solution)/shard_map/ppermute | solution.py:664
  11.8 3.1 %collective-permute-start.5 = (bf16[2,64,512]{2,1,0:T(8,128)(2,1)S(1)}, bf16[2,64,512]{2,1,0:T(8,128)(2,1)S(1)}, u32[]{:S(2)}, u32[]{:S(2)}) collective-permute-start(bf16[2,64,512]{2,1,0:T(8,128)(2,1)S(1)} %get-tuple-element.199), channel_id=1, source_target_pairs={{0,3},{1,2},{2,1},{3,0},{4,7},{5,6},{6,5},{7,4},{8,11},{9,10},{10,... | collective-permute-start | bytes 393224 | tf_op jit(solution)/shard_map/ppermute | solution.py:664
  15.0 2.7 %collective-permute-done.1.two_ref = bf16[2,64,512]{2,1,0:T(8,128)(2,1)S(1)} collective-permute-done((bf16[2,64,512]{2,1,0:T(8,128)(2,1)S(1)}, bf16[2,64,512]{2,1,0:T(8,128)(2,1)S(1)}, u32[]{:S(2)}, u32[]{:S(2)}) %collective-permute-start.1) | collective-permute-done | bytes 131104 | tf_op jit(solution)/shard_map/ppermute | solution.py:664
  18.4 9.4 %attention_forward.2 = (bf16[4,64,64,256]{3,2,1,0:T(8,128)(2,1)}, bf16[2,64,64,256]{3,2,1,0:T(8,128)(2,1)S(1)}, f32[2,4,64,128]{3,2,1,0:T(8,128)S(1)}, f32[2,4,6...) custom-call(s32[5]{0:T(128)S(1)} %stack.23.place_ref.refs_0_, ...), custom_call_target="tpu_custom_call" | custom-call | flops 1610612736 | bytes 12582912 | tf_op jit(solution)/shard_map/attention_forward/pallas_call | solution.py:214
  28.9 9.4 %attention_forward.3 = (bf16[4,64,64,256]{3,2,1,0:T(8,128)(2,1)}, bf16[2,64,64,256]{3,2,1,0:T(8,128)(2,1)S(1)}, f32[2,4,64,128]{3,2,1,0:T(8,128)S(1)}, f32[2,4,6...) custom-call(s32[5]{0:T(128)S(1)} %stack.23.place_ref.refs_0_, ...), custom_call_target="tpu_custom_call", output_to_operand_aliasing={{0}: (14, {})} | custom-call | flops 1610612736 | bytes 12582912 | tf_op jit(solution)/shard_map/attention_forward/pallas_call | solution.py:214
  38.4 9.3 %dense.1 = (bf16[4,64,512]{2,1,0:T(8,128)(2,1)}, bf16[4,256,512]{2,1,0:T(8,128)(2,1)S(1)}, bf16[4,256,512]{2,1,0:T(8,128)(2,1)S(1)}, bf16[4,4,64,512]{3,2,1,0:T(...) custom-call(s32[5]{0:T(128)S(1)} %stack.23.place_ref.refs_0_, ...), custom_call_target="tpu_custom_call" | custom-call | flops 3221225472 | bytes 12582912 | tf_op jit(solution)/shard_map/dense/pallas_call | solution.py:423
  48.7 3.5 %collective-permute-done.9.refs_8_ = f32[8,512]{1,0:T(8,128)S(1)} collective-permute-done((f32[8,512]{1,0:T(8,128)S(1)}, f32[8,512]{1,0:T(8,128)S(1)}, u32[]{:S(2)}, u32[]{:S(2)}) %collective-permute-start.9) | collective-permute-done | bytes 16416 | tf_op jit(solution)/shard_map/ppermute | solution.py:664
  53.3 1.6 collective-permute-start.10
  54.8 1.5 collective-permute-start.11
  56.3 12.7 %attention_backward.3 = (bf16[4,64,64,256]{3,2,1,0:T(8,128)(2,1)}, bf16[2,2,64,512]{3,2,1,0:T(8,128)(2,1)S(1)}, bf16[2,64,512]{2,1,0:T(8,128)(2,1)S(1)}, f32[2,6...) custom-call(s32[5]{0:T(128)S(1)} %stack.23.place_ref.refs_0_, ...), custom_call_target="tpu_custom_call" | custom-call | flops 3221225472 | bytes 12582912 | tf_op jit(solution)/shard_map/attention_backward/pallas_call | solution.py:613
  70.8 1.6 %collective-permute-start.13 = (bf16[584,256]{1,0:T(8,128)(2,1)S(1)}, bf16[584,256]{1,0:T(8,128)(2,1)S(1)}, u32[]{:S(2)}, u32[]{:S(2)}) collective-permute-start(bf16[584,256]{1,0:T(8,128)(2,1)S(1)} %get-tuple-element.142.refs_2_), channel_id=1, source_target_pairs={{0,16},{4,20},{8,24},{12,28},{16,0},{20,4},{24,8},{28,12},{1,17},{... | collective-permute-start | bytes 897032 | tf_op jit(solution)/shard_map/ppermute | solution.py:664
  72.9 7.9 %collective-permute-start.12 = (bf16[2,2,64,512]{3,2,1,0:T(8,128)(2,1)S(1)}, bf16[2,2,64,512]{3,2,1,0:T(8,128)(2,1)S(1)}, u32[]{:S(2)}, u32[]{:S(2)}) collective-permute-start(bf16[2,2,64,512]{3,2,1,0:T(8,128)(2,1)S(1)} %get-tuple-element.147), channel_id=1, source_target_pairs={{0,1},{1,0},{2,3},{3,2},{4,5},{5,4},{6,7},{7,6},{8,9},{9,8},{10,11... | collective-permute-start | bytes 786440 | tf_op jit(solution)/shard_map/ppermute | solution.py:664
  80.8 7.6 %attention_backward.4 = (bf16[4,64,64,256]{3,2,1,0:T(8,128)(2,1)}, bf16[2,1,64,512]{3,2,1,0:T(8,128)(2,1)S(1)}, bf16[1,64,512]{2,1,0:T(8,128)(2,1)S(1)}, f32[1,6...) custom-call(s32[5]{0:T(128)S(1)} %stack.23.place_ref.refs_0_, ...), custom_call_target="tpu_custom_call", output_to_operand_aliasing={{0}: (13, {}), {4}: (14, {})} | custom-call | flops 1610612736 | bytes 6291456 | tf_op jit(solution)/shard_map/attention_backward/pallas_call | solution.py:613
  89.2 2.0 %collective-permute-start.15 = (bf16[2,1,64,512]{3,2,1,0:T(8,128)(2,1)S(1)}, bf16[2,1,64,512]{3,2,1,0:T(8,128)(2,1)S(1)}, u32[]{:S(2)}, u32[]{:S(2)}) collective-permute-start(bf16[2,1,64,512]{3,2,1,0:T(8,128)(2,1)S(1)} %get-tuple-element.154), channel_id=1, source_target_pairs={{0,1},{1,0},{2,3},{3,2},{4,5},{5,4},{6,7},{7,6},{8,9},{9,8},{10,11... | collective-permute-start | bytes 393224 | tf_op jit(solution)/shard_map/ppermute | solution.py:664
  92.3 7.6 %attention_backward.5 = (bf16[4,64,64,256]{3,2,1,0:T(8,128)(2,1)}, bf16[2,1,64,512]{3,2,1,0:T(8,128)(2,1)S(1)}, bf16[1,64,512]{2,1,0:T(8,128)(2,1)S(1)}, f32[1,6...) custom-call(s32[5]{0:T(128)S(1)} %stack.23.place_ref.refs_0_, ...), custom_call_target="tpu_custom_call", output_to_operand_aliasing={{0}: (13, {}), {4}: (14, {})} | custom-call | flops 1610612736 | bytes 6291456 | tf_op jit(solution)/shard_map/attention_backward/pallas_call | solution.py:613
  99.9 2.5 %collective-permute-done.15.refs_13_.refs_2_.refs_4_ = bf16[2,1,64,512]{3,2,1,0:T(8,128)(2,1)S(1)} collective-permute-done((bf16[2,1,64,512]{3,2,1,0:T(8,128)(2,1)S(1)}, bf16[2,1,64,512]{3,2,1,0:T(8,128)(2,1)S(1)}, u32[]{:S(2)}, u32[]{:S(2)}) %collective-permute-start.15) | collective-permute-done | bytes 131104 | tf_op jit(solution)/shard_map/ppermute | solution.py:664
  102.3 2.1 %attention_weights.1 = (bf16[4,1,64,512]{3,2,1,0:T(8,128)(2,1)S(1)}, bf16[4,1,64,512]{3,2,1,0:T(8,128)(2,1)S(1)}, bf16[4,1,64,512]{3,2,1,0:T(8,128)(2,1)S(1)}, b...) custom-call(s32[5]{0:T(128)S(1)} %stack.23.place_ref.refs_0_, ...), custom_call_target="tpu_custom_call" | custom-call | bytes 4980736 | tf_op jit(solution)/shard_map/attention_weights/pallas_call | solution.py:817
  105.5 1.3 collective-permute-done.22.refs_8_
  107.5 1.5 collective-permute-start.25
  109.5 1.1 collective-permute-start.16
  111.3 1.8 %collective-permute-start.24 = (bf16[152,512]{1,0:T(8,128)(2,1)S(1)}, bf16[152,512]{1,0:T(8,128)(2,1)S(1)}, u32[]{:S(2)}, u32[]{:S(2)}) collective-permute-start(bf16[152,512]{1,0:T(8,128)(2,1)S(1)} %get-tuple-element.178.refs_4_), channel_id=1, source_target_pairs={{0,2},{1,3},{2,0},{3,1},{4,6},{5,7},{6,4},{7,5},{8,10},{9,11},{10,... | collective-permute-start | bytes 466952 | tf_op jit(solution)/shard_map/ppermute | solution.py:664
  113.1 2.1 %collective-permute-done.16.refs_3_.refs_5_ = bf16[2,1,64,512]{3,2,1,0:T(8,128)(2,1)S(1)} collective-permute-done((bf16[2,1,64,512]{3,2,1,0:T(8,128)(2,1)S(1)}, bf16[2,1,64,512]{3,2,1,0:T(8,128)(2,1)S(1)}, u32[]{:S(2)}, u32[]{:S(2)}) %collective-permute-start.16) | collective-permute-done | bytes 131104 | tf_op jit(solution)/shard_map/ppermute | solution.py:664
  118.0 3.1 %collective-permute-done.27.refs_1_ = bf16[200,256]{1,0:T(8,128)(2,1)S(1)} collective-permute-done((bf16[200,256]{1,0:T(8,128)(2,1)S(1)}, bf16[200,256]{1,0:T(8,128)(2,1)S(1)}, u32[]{:S(2)}, u32[]{:S(2)}) %collective-permute-start.27) | collective-permute-done | bytes 102432 | tf_op jit(solution)/shard_map/ppermute | solution.py:664
  122.2 1.2 collective-permute-start.29
  123.4 2.9 %collective-permute-start.31 = (bf16[152,512]{1,0:T(8,128)(2,1)S(1)}, bf16[152,512]{1,0:T(8,128)(2,1)S(1)}, u32[]{:S(2)}, u32[]{:S(2)}) collective-permute-start(bf16[152,512]{1,0:T(8,128)(2,1)S(1)} %dense_far_sum.1.refs_12_.refs_1_), channel_id=1, source_target_pairs={{0,2},{1,3},{2,0},{3,1},{4,6},{5,7},{6,4},{7,5},{8,10},{9,11},{10,... | collective-permute-start | bytes 466952 | tf_op jit(solution)/shard_map/ppermute | solution.py:664
  126.4 9.7 %collective-permute-done.23.refs_7_ = bf16[2,64,512]{2,1,0:T(8,128)(2,1)S(1)} collective-permute-done((bf16[2,64,512]{2,1,0:T(8,128)(2,1)S(1)}, bf16[2,64,512]{2,1,0:T(8,128)(2,1)S(1)}, u32[]{:S(2)}, u32[]{:S(2)}) %collective-permute-start.23) | collective-permute-done | bytes 131104 | tf_op jit(solution)/shard_map/ppermute | solution.py:664
  136.1 1.8 %first_norm_backward.1.refs_2_ = bf16[4,64,512]{2,1,0:T(8,128)(2,1)} custom-call(f32[2,64,512]{2,1,0:T(8,128)S(1)} %get-tuple-element.129.refs_6_.refs_0_, f32[1,64,512]{2,1,0:T(8,128)S(1)} %get-tuple-element.143.refs_6_.refs_1_, f32[1,64,512]{2,1,0:T(8,128)S(1)} %get-tuple-element.153.refs_2_, ...), custom_call_target="tpu_custom_call" | custom-call | bytes 2361344 | tf_op jit(solution)/shard_map/first_norm_backward/pallas_call | solution.py:817
  139.6 2.3 %collective-permute-start.30 = (bf16[200,512]{1,0:T(8,128)(2,1)S(1)}, bf16[200,512]{1,0:T(8,128)(2,1)S(1)}, u32[]{:S(2)}, u32[]{:S(2)}) collective-permute-start(bf16[200,512]{1,0:T(8,128)(2,1)S(1)} %tail_near_sum.1.refs_3_.refs_0_), channel_id=1, source_target_pairs={{0,2},{1,3},{2,0},{3,1},{4,6},{5,7},{6,4},{7,5},{8,10},{9,11},{10,... | collective-permute-start | bytes 614408 | tf_op jit(solution)/shard_map/ppermute | solution.py:664
  141.9 9.8 %collective-permute-done.32.refs_2_ = bf16[304,512]{1,0:T(8,128)(2,1)S(1)} collective-permute-done((bf16[304,512]{1,0:T(8,128)(2,1)S(1)}, bf16[304,512]{1,0:T(8,128)(2,1)S(1)}, u32[]{:S(2)}, u32[]{:S(2)}) %collective-permute-start.32) | collective-permute-done | bytes 311328 | tf_op jit(solution)/shard_map/ppermute | solution.py:664
  151.7 1.6 %finish_dense.1 = (f32[256,512]{1,0:T(8,128)}, f32[64,2048]{1,0:T(8,128)}, f32[64,512]{1,0:T(8,128)}, f32[8,512]{1,0:T(8,128)S(1)}) custom-call(s32[5]{0:T(128)S(1)} %stack.23.place_ref.refs_0_, bf16[304,512]{1,0:T(8,128)(2,1)S(1)} %dense_join.1.refs_1_, bf16[304,512]{1,0:T(8,128)(2,1)S(1)} %collective-permute-done.32.refs_2_, ...), custom_call_target="tpu_custom_call" | custom-call | bytes 1818624 | tf_op jit(solution)/shard_map/finish_dense/pallas_call | solution.py:817
  (77 shorter events, 23.3 us)
Async XLA Ops:
  1.7 10.2 %collective-permute-start = (bf16[2,64,512]{2,1,0:T(8,128)(2,1)S(1)}, bf16[2,64,512]{2,1,0:T(8,128)(2,1)S(1)}, u32[]{:S(2)}, u32[]{:S(2)}) collective-permute-start(bf16[2,64,512]{2,1,0:T(8,128)(2,1)S(1)} %get-tuple-element.200), channel_id=1, source_target_pairs={{0,1},{1,0},{2,3},{3,2},{4,5},{5,4},{6,7},{7,6},{8,9},{9,8},{10,11... | collective-permute-start | bytes 393224 | tf_op jit(solution)/shard_map/ppermute | solution.py:664
  4.8 12.9 %collective-permute-start.1 = (bf16[2,64,512]{2,1,0:T(8,128)(2,1)S(1)}, bf16[2,64,512]{2,1,0:T(8,128)(2,1)S(1)}, u32[]{:S(2)}, u32[]{:S(2)}) collective-permute-start(bf16[2,64,512]{2,1,0:T(8,128)(2,1)S(1)} %get-tuple-element.200), channel_id=1, source_target_pairs={{0,2},{1,3},{2,0},{3,1},{4,6},{5,7},{6,4},{7,5},{8,10},{9,11},{10,... | collective-permute-start | bytes 393224 | tf_op jit(solution)/shard_map/ppermute | solution.py:664
  7.3 10.4 %collective-permute-start.2 = (bf16[2,64,512]{2,1,0:T(8,128)(2,1)S(1)}, bf16[2,64,512]{2,1,0:T(8,128)(2,1)S(1)}, u32[]{:S(2)}, u32[]{:S(2)}) collective-permute-start(bf16[2,64,512]{2,1,0:T(8,128)(2,1)S(1)} %get-tuple-element.200), channel_id=1, source_target_pairs={{0,3},{1,2},{2,1},{3,0},{4,7},{5,6},{6,5},{7,4},{8,11},{9,10},{10,... | collective-permute-start | bytes 393224 | tf_op jit(solution)/shard_map/ppermute | solution.py:664
  7.3 20.4 %collective-permute-start.3 = (bf16[2,64,512]{2,1,0:T(8,128)(2,1)S(1)}, bf16[2,64,512]{2,1,0:T(8,128)(2,1)S(1)}, u32[]{:S(2)}, u32[]{:S(2)}) collective-permute-start(bf16[2,64,512]{2,1,0:T(8,128)(2,1)S(1)} %get-tuple-element.199), channel_id=1, source_target_pairs={{0,1},{1,0},{2,3},{3,2},{4,5},{5,4},{6,7},{7,6},{8,9},{9,8},{10,11... | collective-permute-start | bytes 393224 | tf_op jit(solution)/shard_map/ppermute | solution.py:664
  8.2 20.7 %collective-permute-start.4 = (bf16[2,64,512]{2,1,0:T(8,128)(2,1)S(1)}, bf16[2,64,512]{2,1,0:T(8,128)(2,1)S(1)}, u32[]{:S(2)}, u32[]{:S(2)}) collective-permute-start(bf16[2,64,512]{2,1,0:T(8,128)(2,1)S(1)} %get-tuple-element.199), channel_id=1, source_target_pairs={{0,2},{1,3},{2,0},{3,1},{4,6},{5,7},{6,4},{7,5},{8,10},{9,11},{10,... | collective-permute-start | bytes 393224 | tf_op jit(solution)/shard_map/ppermute | solution.py:664
  11.8 17.1 %collective-permute-start.5 = (bf16[2,64,512]{2,1,0:T(8,128)(2,1)S(1)}, bf16[2,64,512]{2,1,0:T(8,128)(2,1)S(1)}, u32[]{:S(2)}, u32[]{:S(2)}) collective-permute-start(bf16[2,64,512]{2,1,0:T(8,128)(2,1)S(1)} %get-tuple-element.199), channel_id=1, source_target_pairs={{0,3},{1,2},{2,1},{3,0},{4,7},{5,6},{6,5},{7,4},{8,11},{9,10},{10,... | collective-permute-start | bytes 393224 | tf_op jit(solution)/shard_map/ppermute | solution.py:664
  47.6 4.6 %collective-permute-start.6 = (bf16[4,4,64,512]{3,2,1,0:T(8,128)(2,1)S(1)}, bf16[4,4,64,512]{3,2,1,0:T(8,128)(2,1)S(1)}, u32[]{:S(2)}, u32[]{:S(2)}) collective-permute-start(bf16[4,4,64,512]{3,2,1,0:T(8,128)(2,1)S(1)} %bitcast.30), channel_id=1, source_target_pairs={{0,4},{4,0},{8,12},{12,8},{16,20},{20,16},{24,28},{28,24},{1,5},{5... | collective-permute-start | bytes 3145736 | tf_op jit(solution)/shard_map/ppermute | solution.py:664
  47.6 4.6 %collective-permute-start.7 = (bf16[4,4,64,512]{3,2,1,0:T(8,128)(2,1)S(1)}, bf16[4,4,64,512]{3,2,1,0:T(8,128)(2,1)S(1)}, u32[]{:S(2)}, u32[]{:S(2)}) collective-permute-start(bf16[4,4,64,512]{3,2,1,0:T(8,128)(2,1)S(1)} %get-tuple-element.124), channel_id=1, source_target_pairs={{0,4},{4,0},{8,12},{12,8},{16,20},{20,16},{24,28},{28,24},{1,5},{5... | collective-permute-start | bytes 3145736 | tf_op jit(solution)/shard_map/ppermute | solution.py:664
  48.1 4.1 %collective-permute-start.8 = (bf16[4,1,64,512]{3,2,1,0:T(8,128)(2,1)S(1)}, bf16[4,1,64,512]{3,2,1,0:T(8,128)(2,1)S(1)}, u32[]{:S(2)}, u32[]{:S(2)}) collective-permute-start(bf16[4,1,64,512]{3,2,1,0:T(8,128)(2,1)S(1)} %bitcast.31), channel_id=1, source_target_pairs={{0,4},{4,0},{8,12},{12,8},{16,20},{20,16},{24,28},{28,24},{1,5},{5... | collective-permute-start | bytes 786440 | tf_op jit(solution)/shard_map/ppermute | solution.py:664
  48.1 4.0 %collective-permute-start.9 = (f32[8,512]{1,0:T(8,128)S(1)}, f32[8,512]{1,0:T(8,128)S(1)}, u32[]{:S(2)}, u32[]{:S(2)}) collective-permute-start(f32[8,512]{1,0:T(8,128)S(1)} %get-tuple-element.127.refs_7_), channel_id=1, source_target_pairs={{0,4},{4,0},{8,12},{12,8},{16,20},{20,16},{24,28},{28,24},{1,5},{5... | collective-permute-start | bytes 49160 | tf_op jit(solution)/shard_map/ppermute | solution.py:664
  53.3 15.7 %collective-permute-start.10 = (bf16[1160,256]{1,0:T(8,128)(2,1)S(1)}, bf16[1160,256]{1,0:T(8,128)(2,1)S(1)}, u32[]{:S(2)}, u32[]{:S(2)}) collective-permute-start(bf16[1160,256]{1,0:T(8,128)(2,1)S(1)} %get-tuple-element.128.refs_0_), channel_id=1, source_target_pairs={{0,8},{4,12},{8,0},{12,4},{16,24},{20,28},{24,16},{28,20},{1,9},{5... | collective-permute-start | bytes 1781768 | tf_op jit(solution)/shard_map/ppermute | solution.py:664
  54.8 15.2 %collective-permute-start.11 = (bf16[1160,256]{1,0:T(8,128)(2,1)S(1)}, bf16[1160,256]{1,0:T(8,128)(2,1)S(1)}, u32[]{:S(2)}, u32[]{:S(2)}) collective-permute-start(bf16[1160,256]{1,0:T(8,128)(2,1)S(1)} %get-tuple-element.140), channel_id=1, source_target_pairs={{0,16},{4,20},{8,24},{12,28},{16,0},{20,4},{24,8},{28,12},{1,17},{... | collective-permute-start | bytes 1781768 | tf_op jit(solution)/shard_map/ppermute | solution.py:664
  70.8 17.6 %collective-permute-start.13 = (bf16[584,256]{1,0:T(8,128)(2,1)S(1)}, bf16[584,256]{1,0:T(8,128)(2,1)S(1)}, u32[]{:S(2)}, u32[]{:S(2)}) collective-permute-start(bf16[584,256]{1,0:T(8,128)(2,1)S(1)} %get-tuple-element.142.refs_2_), channel_id=1, source_target_pairs={{0,16},{4,20},{8,24},{12,28},{16,0},{20,4},{24,8},{28,12},{1,17},{... | collective-permute-start | bytes 897032 | tf_op jit(solution)/shard_map/ppermute | solution.py:664
  72.4 16.0 %collective-permute-start.14 = (bf16[584,256]{1,0:T(8,128)(2,1)S(1)}, bf16[584,256]{1,0:T(8,128)(2,1)S(1)}, u32[]{:S(2)}, u32[]{:S(2)}) collective-permute-start(bf16[584,256]{1,0:T(8,128)(2,1)S(1)} %get-tuple-element.150), channel_id=1, source_target_pairs={{0,8},{4,12},{8,0},{12,4},{16,24},{20,28},{24,16},{28,20},{1,9},{5... | collective-permute-start | bytes 897032 | tf_op jit(solution)/shard_map/ppermute | solution.py:664
  72.9 18.4 %collective-permute-start.12 = (bf16[2,2,64,512]{3,2,1,0:T(8,128)(2,1)S(1)}, bf16[2,2,64,512]{3,2,1,0:T(8,128)(2,1)S(1)}, u32[]{:S(2)}, u32[]{:S(2)}) collective-permute-start(bf16[2,2,64,512]{3,2,1,0:T(8,128)(2,1)S(1)} %get-tuple-element.147), channel_id=1, source_target_pairs={{0,1},{1,0},{2,3},{3,2},{4,5},{5,4},{6,7},{7,6},{8,9},{9,8},{10,11... | collective-permute-start | bytes 786440 | tf_op jit(solution)/shard_map/ppermute | solution.py:664
  89.2 13.2 %collective-permute-start.18 = (bf16[304,512]{1,0:T(8,128)(2,1)S(1)}, bf16[304,512]{1,0:T(8,128)(2,1)S(1)}, u32[]{:S(2)}, u32[]{:S(2)}) collective-permute-start(bf16[304,512]{1,0:T(8,128)(2,1)S(1)} %get-tuple-element.158), channel_id=1, source_target_pairs={{0,1},{1,0},{2,3},{3,2},{4,5},{5,4},{6,7},{7,6},{8,9},{9,8},{10,11... | collective-permute-start | bytes 933896 | tf_op jit(solution)/shard_map/ppermute | solution.py:664
  89.2 13.1 %collective-permute-start.15 = (bf16[2,1,64,512]{3,2,1,0:T(8,128)(2,1)S(1)}, bf16[2,1,64,512]{3,2,1,0:T(8,128)(2,1)S(1)}, u32[]{:S(2)}, u32[]{:S(2)}) collective-permute-start(bf16[2,1,64,512]{3,2,1,0:T(8,128)(2,1)S(1)} %get-tuple-element.154), channel_id=1, source_target_pairs={{0,1},{1,0},{2,3},{3,2},{4,5},{5,4},{6,7},{7,6},{8,9},{9,8},{10,11... | collective-permute-start | bytes 393224 | tf_op jit(solution)/shard_map/ppermute | solution.py:664
  91.3 11.0 %collective-permute-start.17 = (bf16[2,64,512]{2,1,0:T(8,128)(2,1)S(1)}, bf16[2,64,512]{2,1,0:T(8,128)(2,1)S(1)}, u32[]{:S(2)}, u32[]{:S(2)}) collective-permute-start(bf16[2,64,512]{2,1,0:T(8,128)(2,1)S(1)} %cross_first.1.refs_2_), channel_id=1, source_target_pairs={{0,2},{1,3},{2,0},{3,1},{4,6},{5,7},{6,4},{7,5},{8,10},{9,11},{10,... | collective-permute-start | bytes 393224 | tf_op jit(solution)/shard_map/ppermute | solution.py:664
  104.4 2.4 %collective-permute-start.19 = (bf16[4,1,64,512]{3,2,1,0:T(8,128)(2,1)S(1)}, bf16[4,1,64,512]{3,2,1,0:T(8,128)(2,1)S(1)}, u32[]{:S(2)}, u32[]{:S(2)}) collective-permute-start(bf16[4,1,64,512]{3,2,1,0:T(8,128)(2,1)S(1)} %get-tuple-element.171), channel_id=1, source_target_pairs={{0,4},{4,0},{8,12},{12,8},{16,20},{20,16},{24,28},{28,24},{1,5},{5... | collective-permute-start | bytes 786440 | tf_op jit(solution)/shard_map/ppermute | solution.py:664
  104.5 2.3 %collective-permute-start.20 = (bf16[4,1,64,512]{3,2,1,0:T(8,128)(2,1)S(1)}, bf16[4,1,64,512]{3,2,1,0:T(8,128)(2,1)S(1)}, u32[]{:S(2)}, u32[]{:S(2)}) collective-permute-start(bf16[4,1,64,512]{3,2,1,0:T(8,128)(2,1)S(1)} %get-tuple-element.173), channel_id=1, source_target_pairs={{0,4},{4,0},{8,12},{12,8},{16,20},{20,16},{24,28},{28,24},{1,5},{5... | collective-permute-start | bytes 786440 | tf_op jit(solution)/shard_map/ppermute | solution.py:664
  105.0 1.8 %collective-permute-start.21 = (bf16[4,1,64,512]{3,2,1,0:T(8,128)(2,1)S(1)}, bf16[4,1,64,512]{3,2,1,0:T(8,128)(2,1)S(1)}, u32[]{:S(2)}, u32[]{:S(2)}) collective-permute-start(bf16[4,1,64,512]{3,2,1,0:T(8,128)(2,1)S(1)} %get-tuple-element.175), channel_id=1, source_target_pairs={{0,4},{4,0},{8,12},{12,8},{16,20},{20,16},{24,28},{28,24},{1,5},{5... | collective-permute-start | bytes 786440 | tf_op jit(solution)/shard_map/ppermute | solution.py:664
  107.5 7.7 %collective-permute-start.25 = (bf16[392,256]{1,0:T(8,128)(2,1)S(1)}, bf16[392,256]{1,0:T(8,128)(2,1)S(1)}, u32[]{:S(2)}, u32[]{:S(2)}) collective-permute-start(bf16[392,256]{1,0:T(8,128)(2,1)S(1)} %get-tuple-element.177.refs_3_), channel_id=1, source_target_pairs={{0,8},{4,12},{8,0},{12,4},{16,24},{20,28},{24,16},{28,20},{1,9},{5... | collective-permute-start | bytes 602120 | tf_op jit(solution)/shard_map/ppermute | solution.py:664
  109.0 6.8 %collective-permute-start.26 = (bf16[392,256]{1,0:T(8,128)(2,1)S(1)}, bf16[392,256]{1,0:T(8,128)(2,1)S(1)}, u32[]{:S(2)}, u32[]{:S(2)}) collective-permute-start(bf16[392,256]{1,0:T(8,128)(2,1)S(1)} %get-tuple-element.183), channel_id=1, source_target_pairs={{0,16},{4,20},{8,24},{12,28},{16,0},{20,4},{24,8},{28,12},{1,17},{... | collective-permute-start | bytes 602120 | tf_op jit(solution)/shard_map/ppermute | solution.py:664
  109.5 5.6 %collective-permute-start.16 = (bf16[2,1,64,512]{3,2,1,0:T(8,128)(2,1)S(1)}, bf16[2,1,64,512]{3,2,1,0:T(8,128)(2,1)S(1)}, u32[]{:S(2)}, u32[]{:S(2)}) collective-permute-start(bf16[2,1,64,512]{3,2,1,0:T(8,128)(2,1)S(1)} %get-tuple-element.155), channel_id=1, source_target_pairs={{0,1},{1,0},{2,3},{3,2},{4,5},{5,4},{6,7},{7,6},{8,9},{9,8},{10,11... | collective-permute-start | bytes 393224 | tf_op jit(solution)/shard_map/ppermute | solution.py:664
  111.3 12.1 %collective-permute-start.24 = (bf16[152,512]{1,0:T(8,128)(2,1)S(1)}, bf16[152,512]{1,0:T(8,128)(2,1)S(1)}, u32[]{:S(2)}, u32[]{:S(2)}) collective-permute-start(bf16[152,512]{1,0:T(8,128)(2,1)S(1)} %get-tuple-element.178.refs_4_), channel_id=1, source_target_pairs={{0,2},{1,3},{2,0},{3,1},{4,6},{5,7},{6,4},{7,5},{8,10},{9,11},{10,... | collective-permute-start | bytes 466952 | tf_op jit(solution)/shard_map/ppermute | solution.py:664
  116.4 4.7 %collective-permute-start.27 = (bf16[200,256]{1,0:T(8,128)(2,1)S(1)}, bf16[200,256]{1,0:T(8,128)(2,1)S(1)}, u32[]{:S(2)}, u32[]{:S(2)}) collective-permute-start(bf16[200,256]{1,0:T(8,128)(2,1)S(1)} %get-tuple-element.186.refs_5_), channel_id=1, source_target_pairs={{0,16},{4,20},{8,24},{12,28},{16,0},{20,4},{24,8},{28,12},{1,17},{... | collective-permute-start | bytes 307208 | tf_op jit(solution)/shard_map/ppermute | solution.py:664
  117.5 4.7 %collective-permute-start.28 = (bf16[200,256]{1,0:T(8,128)(2,1)S(1)}, bf16[200,256]{1,0:T(8,128)(2,1)S(1)}, u32[]{:S(2)}, u32[]{:S(2)}) collective-permute-start(bf16[200,256]{1,0:T(8,128)(2,1)S(1)} %get-tuple-element.188), channel_id=1, source_target_pairs={{0,8},{4,12},{8,0},{12,4},{16,24},{20,28},{24,16},{28,20},{1,9},{5... | collective-permute-start | bytes 307208 | tf_op jit(solution)/shard_map/ppermute | solution.py:664
  122.2 15.8 %collective-permute-start.29 = (bf16[200,512]{1,0:T(8,128)(2,1)S(1)}, bf16[200,512]{1,0:T(8,128)(2,1)S(1)}, u32[]{:S(2)}, u32[]{:S(2)}) collective-permute-start(bf16[200,512]{1,0:T(8,128)(2,1)S(1)} %tail_sum_second.1.refs_2_.refs_0_), channel_id=1, source_target_pairs={{0,1},{1,0},{2,3},{3,2},{4,5},{5,4},{6,7},{7,6},{8,9},{9,8},{10,11... | collective-permute-start | bytes 614408 | tf_op jit(solution)/shard_map/ppermute | solution.py:664
  123.4 15.5 %collective-permute-start.31 = (bf16[152,512]{1,0:T(8,128)(2,1)S(1)}, bf16[152,512]{1,0:T(8,128)(2,1)S(1)}, u32[]{:S(2)}, u32[]{:S(2)}) collective-permute-start(bf16[152,512]{1,0:T(8,128)(2,1)S(1)} %dense_far_sum.1.refs_12_.refs_1_), channel_id=1, source_target_pairs={{0,2},{1,3},{2,0},{3,1},{4,6},{5,7},{6,4},{7,5},{8,10},{9,11},{10,... | collective-permute-start | bytes 466952 | tf_op jit(solution)/shard_map/ppermute | solution.py:664
  126.3 9.8 %collective-permute-start.23 = (bf16[2,64,512]{2,1,0:T(8,128)(2,1)S(1)}, bf16[2,64,512]{2,1,0:T(8,128)(2,1)S(1)}, u32[]{:S(2)}, u32[]{:S(2)}) collective-permute-start(bf16[2,64,512]{2,1,0:T(8,128)(2,1)S(1)} %cross_second.1.refs_6_), channel_id=1, source_target_pairs={{0,2},{1,3},{2,0},{3,1},{4,6},{5,7},{6,4},{7,5},{8,10},{9,11},{10,... | collective-permute-start | bytes 393224 | tf_op jit(solution)/shard_map/ppermute | solution.py:664
  139.5 12.2 %collective-permute-start.32 = (bf16[304,512]{1,0:T(8,128)(2,1)S(1)}, bf16[304,512]{1,0:T(8,128)(2,1)S(1)}, u32[]{:S(2)}, u32[]{:S(2)}) collective-permute-start(bf16[304,512]{1,0:T(8,128)(2,1)S(1)} %dense_join.1.refs_1_), channel_id=1, source_target_pairs={{0,1},{1,0},{2,3},{3,2},{4,5},{5,4},{6,7},{7,6},{8,9},{9,8},{10,11... | collective-permute-start | bytes 933896 | tf_op jit(solution)/shard_map/ppermute | solution.py:664
  139.6 13.8 %collective-permute-start.30 = (bf16[200,512]{1,0:T(8,128)(2,1)S(1)}, bf16[200,512]{1,0:T(8,128)(2,1)S(1)}, u32[]{:S(2)}, u32[]{:S(2)}) collective-permute-start(bf16[200,512]{1,0:T(8,128)(2,1)S(1)} %tail_near_sum.1.refs_3_.refs_0_), channel_id=1, source_target_pairs={{0,2},{1,3},{2,0},{3,1},{4,6},{5,7},{6,4},{7,5},{8,10},{9,11},{10,... | collective-permute-start | bytes 614408 | tf_op jit(solution)/shard_map/ppermute | solution.py:664
  (6 other events, 41.9 us)

commit v4 on v3

--- a/solution.py
+++ b/solution.py
@@ -73,11 +73,11 @@
     return pltpu.CompilerParams(vmem_limit_bytes=mib << 20)
 
 
-def load_kernel(count, *refs):
-    sources, targets, semaphores = refs[:count], refs[count : 2 * count], refs[2 * count]
+def load_kernel(count, starts, *refs):
+    sources, targets, semaphores = refs[:count], refs[-count - 1 : -1], refs[-1]
     copies = [
-        pltpu.make_async_copy(source, target, semaphores.at[i])
-        for i, (source, target) in enumerate(zip(sources, targets))
+        pltpu.make_async_copy(source.at[pl.ds(start, target.shape[0])], target, semaphores.at[i])
+        for i, (source, target, start) in enumerate(zip(sources, targets, starts))
     ]
     for copy in copies:
         copy.start()
@@ -85,29 +85,80 @@
         copy.wait()
 
 
-def load(arrays, name):
+def copies_beside(sources, targets, semaphores):
+    return [
+        pltpu.make_async_copy(source, target, semaphores.at[i])
+        for i, (source, target) in enumerate(zip(sources, targets))
+    ]
+
+
+def load(arrays, name, starts=None, after=()):
+    count = len(arrays)
+    starts = starts or (0,) * count
     return pl.pallas_call(
-        functools.partial(load_kernel, len(arrays)),
-        in_specs=[pl.BlockSpec(memory_space=pltpu.HBM)] * len(arrays),
-        out_specs=[near_spec()] * len(arrays),
-        out_shape=[near(a.shape, a.dtype) for a in arrays],
-        scratch_shapes=[pltpu.SemaphoreType.DMA((len(arrays),))],
+        functools.partial(load_kernel, count, starts),
+        in_specs=[pl.BlockSpec(memory_space=pltpu.HBM)] * count
+        + [pl.BlockSpec(memory_space=pl.ANY)] * len(after),
+        out_specs=[near_spec()] * count,
+        out_shape=[
+            near((a.shape[0] - start,) + a.shape[1:], a.dtype) for a, start in zip(arrays, starts)
+        ],
+        scratch_shapes=[pltpu.SemaphoreType.DMA((count,))],
         compiler_params=params(),
         name=name,
-    )(*arrays)
-
-
-def forward_kernel(
+    )(*arrays, *after)
+
+
+def project(pieces, first, parameters, row, refs, atoms_scratch):
+    gain_ref, shift_ref, key_weight_ref, value_weight_ref, value_bias_ref = parameters
+    hidden_ref, normed_ref, key_ref, value_ref = refs
+    count = hidden_ref.shape[0]
+    _, groups, keys, width = key_ref.shape
+    rows = keys // 4
+    half = 2 * rows
+    model_width = hidden_ref.shape[2]
+    for m in range(count):
+        for i, piece in enumerate(pieces):
+            start = pl.multiple_of(m * half + ((row ^ i) & 1) * rows, rows)
+            atoms_scratch[pl.ds(start, rows)] = piece[m + first]
+    hidden, normed, _ = norm_forward(
+        atoms_scratch[...].astype(F32), as_row(gain_ref), as_row(shift_ref)
+    )
+    hidden = hidden.astype(BF16)
+    normed = normed.astype(BF16)
+    key_rows = dot(hidden, key_weight_ref[...]).astype(BF16)
+    value_rows = (dot(hidden, value_weight_ref[...]) + as_row(value_bias_ref)).astype(BF16)
+    return [a.reshape(count, half, model_width) for a in (hidden, normed, key_rows, value_rows)]
+
+
+def put_half(values, at, refs):
+    hidden, normed, key_rows, value_rows = values
+    hidden_ref, normed_ref, key_ref, value_ref = refs
+    count, groups, _, width = key_ref.shape
+    half = hidden.shape[1]
+    ones = jnp.ones((count, half, width), BF16)
+    hidden_ref[:, at] = hidden
+    normed_ref[:, at] = normed
+    for t in range(groups):
+        lanes = slice(t * width, (t + 1) * width)
+        key_ref[:, t, at] = key_rows[:, :, lanes]
+        value_ref[:, t, at, :width] = value_rows[:, :, lanes]
+        value_ref[:, t, at, width:] = ones
+
+
+def half_rows(row, other, rows):
+    which = row >> 1
+    which = 1 - which if other else which
+    return pl.ds(pl.multiple_of(which * 2 * rows, 2 * rows), 2 * rows)
+
+
+def near_half_kernel(
     head_size,
-    chunk,
-    first,
+    stages,
+    ahead,
     place_ref,
-    length_ref,
     own_ref,
     one_ref,
-    two_ref,
-    three_ref,
-    pair_ref,
     gain_ref,
     shift_ref,
     query_weight_ref,
@@ -115,67 +166,104 @@
     key_weight_ref,
     value_weight_ref,
     value_bias_ref,
-    _,
-    pair_out_ref,
-    weights_ref,
-    mixed_ref,
-    inverse_ref,
-    hidden_ref,
-    normed_ref,
+    *refs,
+):
+    refs = refs[ahead:]
+    atoms_scratch = refs[-1]
+    row = place_ref[1]
+    rows, model_width = own_ref.shape[1:]
+    factor = head_size**-0.5
+    parameters = (gain_ref, shift_ref, key_weight_ref, value_weight_ref, value_bias_ref)
+    for stage in range(stages):
+        hidden_ref, normed_ref, key_ref, value_ref, query_ref = refs[5 * stage : 5 * stage + 5]
+        outs = (hidden_ref, normed_ref, key_ref, value_ref)
+        count, groups, _, width = key_ref.shape
+        values = project((own_ref, one_ref), stage * count, parameters, row, outs, atoms_scratch)
+        put_half(values, half_rows(row, False, rows), outs)
+        mine = pl.ds(pl.multiple_of(row * rows, rows), rows)
+        own = jnp.concatenate([hidden_ref[m, mine] for m in range(count)], 0)
+        query_rows = (dot(own, query_weight_ref[...]) + as_row(query_bias_ref)) * factor
+        query_rows = query_rows.astype(BF16).reshape(count, rows, model_width)
+        for t in range(groups):
+            query_ref[:, t] = query_rows[:, :, t * width : (t + 1) * width]
+
+
+def near_half(head_size, stages, place, atoms, one, parameters, after):
+    molecules, rows, model_width = atoms.shape
+    keys = 4 * rows
+    count = molecules // stages
+    groups = model_width // LANES
+    operands = (place, atoms, one, *parameters, *after)
+    return pl.pallas_call(
+        functools.partial(near_half_kernel, head_size, stages, len(after)),
+        grid_spec=pltpu.PrefetchScalarGridSpec(
+            num_scalar_prefetch=1,
+            grid=(1,),
+            in_specs=[whole(atoms), near_spec()]
+            + [near_spec() if a.ndim > 1 else whole(a) for a in parameters]
+            + [pl.BlockSpec(memory_space=pl.ANY)] * len(after),
+            out_specs=[near_spec()] * (5 * stages),
+            scratch_shapes=[pltpu.VMEM((count * 2 * rows, model_width), BF16)],
+        ),
+        out_shape=[
+            near((count, keys, model_width), BF16),
+            near((count, keys, model_width), BF16),
+            near((count, groups, keys, LANES), BF16),
+            near((count, groups, keys, 2 * LANES), BF16),
+            near((count, groups, rows, LANES), BF16),
+        ]
+        * stages,
+        compiler_params=params(10),
+        name="near_half",
+    )(*operands)
+
+
+def forward_kernel(
+    head_size,
+    chunk,
+    first,
+    extra,
+    place_ref,
+    length_ref,
+    two_ref,
+    three_ref,
+    pair_ref,
     query_ref,
-    key_ref,
-    value_ref,
-    atoms_scratch,
-    pair_scratch,
-    semaphores,
+    gain_ref,
+    shift_ref,
+    key_weight_ref,
+    value_weight_ref,
+    value_bias_ref,
+    *refs,
 ):
+    (
+        pair_out_ref,
+        weights_ref,
+        mixed_ref,
+        inverse_ref,
+        hidden_ref,
+        normed_ref,
+        key_ref,
+        value_ref,
+    ) = refs[5 + extra : 13 + extra]
+    atoms_scratch, semaphores = refs[-2:]
+    copies = copies_beside(refs[5 : 5 + extra], refs[13 + extra : 13 + 2 * extra], semaphores)
     molecule = pl.program_id(0)
     group = pl.program_id(1)
     count, groups, keys, width = key_ref.shape
     heads = width // head_size
-    rows, model_width = own_ref.shape[1:]
-    factor = head_size**-0.5
-
-    def pair_copy(m, g):
-        span = pl.ds(g * heads, heads)
-        return pltpu.make_async_copy(
-            pair_ref.at[m + first, span], pair_scratch.at[m, span], semaphores.at[m, g]
-        )
+    rows = query_ref.shape[2]
 
     @pl.when((molecule == 0) & (group == 0))
     def _():
-        for m in range(count):
-            for g in range(groups):
-                pair_copy(m, g).start()
+        for copy in copies:
+            copy.start()
         row = place_ref[1]
-        gain = as_row(gain_ref)
-        shift = as_row(shift_ref)
-        query_bias = as_row(query_bias_ref)
-        value_bias = as_row(value_bias_ref)
-        ones = jnp.ones((keys, width), BF16)
-        for m in range(count):
-            for i, piece in enumerate((own_ref, one_ref, two_ref, three_ref)):
-                start = pl.multiple_of((row ^ i) * rows, rows)
-                atoms_scratch[pl.ds(start, rows)] = piece[m]
-            hidden, normed, _ = norm_forward(atoms_scratch[...].astype(F32), gain, shift)
-            hidden = hidden.astype(BF16)
-            hidden_ref[m] = hidden
-            normed_ref[m] = normed.astype(BF16)
-            key_rows = dot(hidden, key_weight_ref[...]).astype(BF16)
-            value_rows = (dot(hidden, value_weight_ref[...]) + value_bias).astype(BF16)
-            for t in range(groups):
-                lanes = slice(t * width, (t + 1) * width)
-                key_ref[m, t] = key_rows[:, lanes]
-                value_ref[m, t, :, :width] = value_rows[:, lanes]
-                value_ref[m, t, :, width:] = ones
-        own = own_ref[...].reshape(count * rows, model_width).astype(F32)
-        own = norm_forward(own, gain, shift)[0].astype(BF16)
-        query_rows = (dot(own, query_weight_ref[...]) + query_bias) * factor
-        query_rows = query_rows.astype(BF16).reshape(count, rows, model_width)
-        for t in range(groups):
-            query_ref[:, t] = query_rows[:, :, t * width : (t + 1) * width]
-
-    pair_copy(molecule, group).wait()
+        outs = (hidden_ref, normed_ref, key_ref, value_ref)
+        parameters = (gain_ref, shift_ref, key_weight_ref, value_weight_ref, value_bias_ref)
+        values = project((two_ref, three_ref), 0, parameters, row, outs, atoms_scratch)
+        put_half(values, half_rows(row, True, rows), outs)
+
     query = query_ref[molecule, group]
     key = key_ref[molecule, group]
     value = value_ref[molecule, group]
@@ -188,7 +276,7 @@
         here = slice(c, c + chunk)
         there = pl.ds(group * heads + c, chunk)
         spread = jnp.concatenate([jnp.where(lane == c + t, query, zero) for t in range(chunk)], 0)
-        pair = pair_scratch[molecule, there].reshape(chunk * rows, keys)
+        pair = pair_ref[molecule + first, there].reshape(chunk * rows, keys)
         scores = against(spread, key) + pair.astype(F32)
         pair_out_ref[0, here] = scores.astype(BF16).reshape(chunk, rows, keys)
         masked = jnp.where(valid, scores, MASKED)
@@ -201,31 +289,43 @@
     inverse_ref[molecule, group] = inverse
     mixed_ref[molecule, group] = total[:, :width] * inverse
 
-
-def attention_forward(head_size, first, count, place, lengths, pieces, pair_bias, parameters, held):
+    @pl.when((molecule == count - 1) & (group == groups - 1))
+    def _():
+        for copy in copies:
+            copy.wait()
+
+
+def attention_forward(
+    head_size, first, place, lengths, pieces, pair_bias, parameters, projected, held, extra
+):
     _, head_count, rows, keys = pair_bias.shape
-    model_width = pieces[0].shape[2]
-    groups = model_width // LANES
+    hidden, normed, key, value, query = projected
+    count, groups = key.shape[:2]
+    model_width = groups * LANES
     heads = LANES // head_size
     pair_spec = pl.BlockSpec((1, heads, rows, keys), lambda m, g, *_: (m + first, g, 0, 0))
     elements = count * head_count * rows * keys
-    own_spec = pl.BlockSpec((count, rows, model_width), lambda *_: (first // count, 0, 0))
-    operands = (place, lengths, *pieces, pair_bias, *parameters, held)
-    return pl.pallas_call(
-        functools.partial(forward_kernel, head_size, 8, first),
+    operands = [place, lengths, *pieces, pair_bias, query, *parameters]
+    in_specs = [near_spec()] * (len(pieces) + 2)
+    in_specs += [near_spec() if a.ndim > 1 else whole(a) for a in parameters]
+    start = len(operands)
+    operands += [hidden, normed, key, value, held]
+    in_specs += [near_spec()] * 4 + [pl.BlockSpec(memory_space=pl.ANY)]
+    aliases = {start + i: 4 + i for i in range(4)}
+    if held.ndim > 1:
+        aliases[start + 4] = 0
+    operands += extra
+    in_specs += [pl.BlockSpec(memory_space=pltpu.HBM)] * len(extra)
+    outs = pl.pallas_call(
+        functools.partial(forward_kernel, head_size, 8, first, len(extra)),
         grid_spec=pltpu.PrefetchScalarGridSpec(
             num_scalar_prefetch=2,
             grid=(count, groups),
-            in_specs=[own_spec]
-            + [near_spec()] * (len(pieces) - 1)
-            + [pl.BlockSpec(memory_space=pltpu.HBM)]
-            + [whole(a) for a in parameters]
-            + [pl.BlockSpec(memory_space=pl.ANY)],
-            out_specs=[pair_spec] + [near_spec()] * 8,
+            in_specs=in_specs,
+            out_specs=[pair_spec] + [near_spec()] * (7 + len(extra)),
             scratch_shapes=[
-                pltpu.VMEM((keys, model_width), BF16),
-                pltpu.VMEM((count, head_count, rows, keys), BF16),
-                pltpu.SemaphoreType.DMA((count, groups)),
+                pltpu.VMEM((count * 2 * rows, model_width), BF16),
+                pltpu.SemaphoreType.DMA((max(len(extra), 1),)),
             ],
         ),
         out_shape=[
@@ -233,19 +333,21 @@
             near((count, head_count, rows, keys), BF16),
             near((count, groups, rows, LANES), F32),
             near((count, groups, rows, LANES), F32),
-            near((count, keys, model_width), BF16),
-            near((count, keys, model_width), BF16),
-            near((count, groups, rows, LANES), BF16),
-            near((count, groups, keys, LANES), BF16),
-            near((count, groups, keys, 2 * LANES), BF16),
-        ],
-        input_output_aliases={} if held.ndim == 1 else {len(operands) - 1: 0},
-        compiler_params=params(16),
+            near(hidden.shape, BF16),
+            near(normed.shape, BF16),
+            near(key.shape, BF16),
+            near(value.shape, BF16),
+        ]
+        + [near(a.shape, a.dtype) for a in extra],
+        input_output_aliases=aliases,
+        compiler_params=params(10),
         cost_estimate=pl.CostEstimate(
             flops=elements * 2 * 384, transcendentals=elements, bytes_accessed=elements * 6
         ),
         name="attention_forward",
     )(*operands)
+    pair_out, weights, mixed, inverse, hidden, normed, key, value = outs[:8]
+    return pair_out, (weights, mixed, inverse, hidden, normed, query, key, value), outs[8:]
 
 
 def dense_kernel(
@@ -265,6 +367,7 @@
         inner_bias_ref,
         outer_weight_ref,
         outer_bias_ref,
+        far_ref,
         atoms_out_ref,
         outer_send_ref,
         outer_keep_ref,
@@ -275,6 +378,7 @@
         grad_middle_ref,
         grad_mixed_ref,
         vectors_ref,
+        copied_ref,
         hidden_scratch,
         turned_scratch,
         normed_scratch,
@@ -283,7 +387,9 @@
         upstream_scratch,
         outer_scratch,
         inner_scratch,
+        semaphores,
     ) = refs[mixed_count:]
+    (copy,) = copies_beside([far_ref], [copied_ref], semaphores)
     step = pl.program_id(0)
     steps = pl.num_programs(0)
     core = place_ref[2]
@@ -300,6 +406,7 @@
 
     @pl.when(step == 0)
     def _():
+        copy.start()
         mixed_low = mixed_rows().astype(BF16)
         middle = (
             atoms_ref[...].reshape(tokens, model_width).astype(F32)
@@ -318,15 +425,19 @@
         vectors_ref[0:1] = column_sum(cotangent)
 
     hidden = hidden_scratch[...]
-    pre = dot(hidden, inner_weight_ref[...]) + as_row(inner_bias_ref)
+    width = outer_weight_ref.shape[1]
+    at = pl.ds(pl.multiple_of(step * width, width), width)
+    inner_weight = inner_weight_ref[:, at]
+    outer_weight = outer_weight_ref[at]
+    pre = dot(hidden, inner_weight) + as_row(inner_bias_ref)
     slope = math.sqrt(2.0 / math.pi)
     square = pre * pre
     tanh = jnp.tanh(slope * (pre + 0.044715 * (pre * square)))
     half = 0.5 * (1.0 + tanh)
     active = (pre * half).astype(BF16)
-    result_scratch[...] += dot(active, outer_weight_ref[...])
+    result_scratch[...] += dot(active, outer_weight)
     derivative = half + (0.5 * slope) * pre * (1.0 - tanh * tanh) * (1.0 + 0.134145 * square)
-    grad_pre = against(cotangent, outer_weight_ref[...]) * derivative
+    grad_pre = against(cotangent, outer_weight) * derivative
     vectors_ref[pl.ds(4 + step, 1)] = column_sum(grad_pre.astype(BF16))
     grad_pre = grad_pre.astype(BF16)
     outer_scratch[...] = across(active, cotangent).reshape(outer_scratch.shape)
@@ -335,7 +446,7 @@
     inner_scratch[...] = dot(turned_scratch[...], grad_pre).reshape(inner_scratch.shape)
     inner_send_ref[:, 0] = inner_scratch[:, 1 - core].astype(BF16)
     inner_keep_ref[:, 0] = inner_scratch[:, core].astype(BF16)
-    upstream_scratch[...] += against(grad_pre, inner_weight_ref[...])
+    upstream_scratch[...] += against(grad_pre, inner_weight)
 
     @pl.when(step == steps - 1)
     def _():
@@ -359,9 +470,10 @@
         inner_scratch[...] = dot(turned, branch).reshape(inner_scratch.shape)
         out_send_ref[...] = inner_scratch[:, 1 - core].astype(BF16)
         out_keep_ref[...] = inner_scratch[:, core].astype(BF16)
-
-
-def dense(place, mixed, atoms, cotangent, parameters, batch_count):
+        copy.wait()
+
+
+def dense(place, mixed, atoms, cotangent, parameters, batch_count, extra):
     (
         out_weight,
         out_bias,
@@ -393,6 +505,7 @@
         inner_bias,
         outer_weight,
         outer_bias,
+        extra,
     )
     outer_spec = pl.BlockSpec((outer_pairs, outer_rows, model_width), lambda s, *_: (s, 0, 0))
     inner_spec = pl.BlockSpec((pairs, 1, own_rows, width), lambda s, *_: (0, s, 0, 0))
@@ -410,16 +523,19 @@
         near(atoms.shape, F32),
         near((atoms.shape[0], model_width // LANES, atoms.shape[1], LANES), BF16),
         shape_of((4 + steps, model_width), F32),
+        near(extra.shape, extra.dtype),
     ]
     fixed = lambda s: pl.BlockSpec(s.shape, lambda *_: (0,) * len(s.shape))
     out_specs = [fixed(s) for s in out_shapes]
     out_specs[1:5] = [outer_spec, outer_spec, inner_spec, inner_spec]
     out_specs[7:9] = [near_spec(), near_spec()]
+    out_specs[10] = near_spec()
     in_specs = [whole(a) for a in operands[1:]]
-    in_specs[: len(mixed)] = [near_spec() for _ in mixed]
-    in_specs[-4] = pl.BlockSpec((model_width, width), lambda s, *_: (0, s))
-    in_specs[-3] = pl.BlockSpec((width,), lambda s, *_: (s,))
-    in_specs[-2] = pl.BlockSpec((width, model_width), lambda s, *_: (s, 0))
+    for i, a in enumerate(operands[1:]):
+        if a.ndim > 1 and i != len(mixed):
+            in_specs[i] = near_spec()
+    in_specs[-4] = pl.BlockSpec((width,), lambda s, *_: (s,))
+    in_specs[-1] = pl.BlockSpec(memory_space=pltpu.HBM)
     return pl.pallas_call(
         functools.partial(dense_kernel, len(mixed)),
         grid_spec=pltpu.PrefetchScalarGridSpec(
@@ -436,10 +552,11 @@
                 pltpu.VMEM((tokens, model_width), F32),
                 pltpu.VMEM((outer_pairs, 2, outer_rows, model_width), F32),
                 pltpu.VMEM((pairs, 2, own_rows, width), F32),
+                pltpu.SemaphoreType.DMA((1,)),
             ],
         ),
         out_shape=out_shapes,
-        compiler_params=params(18),
+        compiler_params=params(14),
         cost_estimate=pl.CostEstimate(
             flops=12 * tokens * model_width * inner_width,
             transcendentals=tokens * inner_width,
@@ -456,6 +573,7 @@
     base,
     start,
     fresh,
+    joined,
     place_ref,
     weights_ref,
     cotangent_ref,
@@ -471,6 +589,7 @@
     value_weight_ref,
     *refs,
 ):
+    before_ref = refs[start - 1] if joined else None
     refs = refs[start:]
     pair_grad_ref, near_ref, cross_ref, own_ref, vectors_ref = refs[:5]
     query_grad_ref, key_grad_ref, value_grad_ref = refs[5:8]
@@ -510,7 +629,7 @@
         centred = against(spread, value)
         there = pl.ds(group * heads + c, chunk)
         weights = weights_ref[molecule, there].reshape(chunk * rows, keys)
-        cotangent = cotangent_ref[0, here].reshape(chunk * rows, keys)
+        cotangent = cotangent_ref[molecule + first, there].reshape(chunk * rows, keys)
         grad = (weights.astype(F32) * centred + cotangent.astype(F32)).astype(BF16)
         pair_grad_ref[0, here] = grad.reshape(chunk, rows, keys)
         product = dot(grad, key)
@@ -536,10 +655,9 @@
         grad_query = join(grad_query_scratch)
         grad_key = join(grad_key_scratch)
         grad_value = join(grad_value_scratch)
-        at = pl.program_id(0)
-        query_grad_ref[at] = grad_query
-        key_grad_ref[at] = grad_key
-        value_grad_ref[at] = grad_value
+        query_grad_ref[0] = grad_query
+        key_grad_ref[0] = grad_key
+        value_grad_ref[0] = grad_value
         grad_scratch[...] = against(grad_key, key_weight_ref[...]) + against(
             grad_value, value_weight_ref[...]
         )
@@ -550,17 +668,21 @@
         vectors_ref[2:3] += column_sum(grad_query)
         vectors_ref[3:4] += column_sum(grad_value)
         at = lambda other: pl.ds(pl.multiple_of((row ^ other) * rows, rows), rows)
-        near_ref[0, 0] = grad_scratch[at(1)].astype(BF16)
-        near_ref[1, 0] = grad_scratch[at(3)].astype(BF16)
+        slot = near_ref.shape[1] - 1
+        near_ref[0, slot] = grad_scratch[at(1)].astype(BF16)
+        near_ref[1, slot] = grad_scratch[at(3)].astype(BF16)
+        if joined:
+            near_ref[:, 0] = before_ref[:, 0]
         cross_ref[0] = grad_scratch[at(2)].astype(BF16)
-        own_ref[pl.program_id(0)] = grad_scratch[mine]
+        own_ref[0] = grad_scratch[mine]
+
 
 def attention_backward(
-    head_size, first, span, place, stage, cotangent, grad_mixed, parameters, held, sums, after
+    head_size, first, base, place, stage, cotangent, grad_mixed, parameters, held, sums, after, before
 ):
     weights, mixed, inverse, _, normed, query, key, value = stage
     _, head_count, rows, keys = weights.shape
-    base, count = span[0], span[1] - span[0]
+    count = 1
     groups = query.shape[1]
     model_width = groups * LANES
     heads = LANES // head_size
@@ -580,8 +702,6 @@
         *parameters,
     ]
     in_specs = [near_spec()] * (len(operands) - 1)
-    in_specs[1] = pair_spec
-    in_specs[-3:] = [whole(a) for a in parameters]
     aliases = {}
     start = len(operands)
     if sums is not None:
@@ -590,10 +710,14 @@
         in_specs += [pl.BlockSpec(memory_space=pl.ANY), near_spec()]
     operands += list(after)
     in_specs += [pl.BlockSpec(memory_space=pl.ANY)] * len(after)
+    joined = before is not None
+    if joined:
+        operands.append(before)
+        in_specs.append(near_spec())
     out_shape = [
         shape_of(cotangent.shape, BF16),
-        shape_of((2, count, rows, model_width), BF16),
-        shape_of((count, rows, model_width), BF16),
+        near((2, 1 + joined, rows, model_width), BF16),
+        near((count, rows, model_width), BF16),
         near((count, rows, model_width), F32),
         near((8, model_width), F32),
         near((count, rows, model_width), BF16),
@@ -602,8 +726,8 @@
     ]
     out_specs = [
         pair_spec,
-        pl.BlockSpec((2, 1, rows, model_width), lambda m, g, *_: (0, m, 0, 0)),
-        pl.BlockSpec((1, rows, model_width), lambda m, g, *_: (m, 0, 0)),
+        near_spec(),
+        near_spec(),
         near_spec(),
         near_spec(),
         near_spec(),
@@ -612,7 +736,7 @@
     ]
     return pl.pallas_call(
         functools.partial(
-            backward_kernel, head_size, 4, first, base, len(operands) - start, sums is None
+            backward_kernel, head_size, 4, first, base, len(operands) - start, sums is None, joined
         ),
         grid_spec=pltpu.PrefetchScalarGridSpec(
             num_scalar_prefetch=1,
@@ -628,7 +752,7 @@
         ),
         out_shape=out_shape,
         input_output_aliases=aliases,
-        compiler_params=params(14),
+        compiler_params=params(8),
         cost_estimate=pl.CostEstimate(
             flops=elements * 2 * 768, transcendentals=0, bytes_accessed=elements * 6
         ),
@@ -757,18 +881,10 @@
     sent_ref[...] = total_ref[pl.ds(away, half)]
 
 
-def near_sum_kernel(place_ref, total_ref, came_ref, sent_ref, kept_ref):
-    half, part = came_ref.shape[0], sent_ref.shape[0]
-    row = place_ref[1]
-    here = (row & 1) * half
-
-    def total(other):
-        start = other * part
-        mine = total_ref[pl.ds(pl.multiple_of(here + start, part), part)]
-        return mine.astype(F32) + came_ref[pl.ds(pl.multiple_of(start, part), part)].astype(F32)
-
-    kept_ref[...] = total(row >> 1)
-    sent_ref[...] = total(1 - (row >> 1)).astype(BF16)
+def near_sum_kernel(place_ref, total_ref, came_ref, out_ref):
+    half = came_ref.shape[0]
+    mine = total_ref[pl.ds(pl.multiple_of((place_ref[1] & 1) * half, half), half)]
+    out_ref[...] = (mine.astype(F32) + came_ref[...].astype(F32)).astype(BF16)
 
 
 def add_kernel(left_ref, right_ref, out_ref):
@@ -781,13 +897,10 @@
     out_ref[pl.ds(pl.multiple_of((1 - place) * part, part), part)] = other_ref[...]
 
 
-def join_kernel(place_ref, mine_ref, other_ref, out_ref):
-    join_rows(place_ref[1] >> 1, mine_ref, other_ref, out_ref)
-
-
 def finish_dense_kernel(
-    ratio, place_ref, mine_ref, other_ref, outer_ref, inner_ref, out_ref, vectors_ref, total_scratch
+    ratio, place_ref, mine_ref, other_ref, outer_ref, inner_ref, out_ref, *refs
 ):
+    vector_refs, wide_ref, total_scratch, row_scratch = refs[:4], refs[4], refs[5], refs[6]
     rows, width = out_ref.shape
     join_rows(place_ref[1] & 1, mine_ref, other_ref, total_scratch)
     outer_ref[...] = total_scratch[: ratio * rows].astype(F32)
@@ -796,14 +909,28 @@
         inner_ref[:, s * width : (s + 1) * width] = total_scratch[at : at + rows].astype(F32)
     at = 2 * ratio * rows
     out_ref[...] = total_scratch[at : at + rows].astype(F32)
-    vectors_ref[...] = total_scratch[at + rows : at + rows + VECTOR_ROWS].astype(F32)
-
-
-def finish_tail_kernel(low_ref, came_ref, query_ref, key_ref, value_ref, vectors_ref):
+    vectors = total_scratch[at + rows : at + rows + VECTOR_ROWS].astype(F32)
+    put_slices(vectors, place_ref[0], vector_refs)
+    row_scratch[...] = vectors
+    size = wide_ref.shape[0]
+    start = place_ref[0] * size
+    row = row_scratch[pl.ds(len(vector_refs) + start // width, 1)]
+    wide_ref[...] = pltpu.roll(row, lax.rem(width - lax.rem(start, width), width), 1)[0, :size]
+
+
+def put_slices(vectors, index, refs):
+    width, size = vectors.shape[1], refs[0].shape[0]
+    turned = pltpu.roll(vectors, lax.rem(width - index * size, width), 1)
+    for i, ref in enumerate(refs):
+        ref[...] = turned[i, :size]
+
+
+def finish_tail_kernel(place_ref, low_ref, came_ref, query_ref, key_ref, value_ref, *vector_refs):
     rows = query_ref.shape[0]
-    for s, ref in enumerate((query_ref, key_ref, value_ref, vectors_ref)):
-        at = slice(s * rows, s * rows + ref.shape[0])
-        ref[...] = low_ref[at].astype(F32) + came_ref[at].astype(F32)
+    total = lambda at: low_ref[at].astype(F32) + came_ref[at].astype(F32)
+    for s, ref in enumerate((query_ref, key_ref, value_ref)):
+        ref[...] = total(slice(s * rows, (s + 1) * rows))
+    put_slices(total(slice(3 * rows, 3 * rows + VECTOR_ROWS)), place_ref[0], vector_refs)
 
 
 def small_call(kernel, place, operands, out_shapes, name, after=(), inside=True, scratch=(), mib=4):
@@ -908,15 +1035,13 @@
 
 def cross_kernel(count, *refs):
     out_ref = refs[-1]
-    start = 0
-    for term, came in zip(refs[:count], refs[count : 2 * count]):
-        end = start + term.shape[0]
-        out_ref[start:end] = (term[...].astype(F32) + came[1].astype(F32)).astype(BF16)
-        start = end
+    came = [(ref, i) for ref in refs[count:-1] for i in range(ref.shape[1])]
+    for m, (term, (ref, i)) in enumerate(zip(refs[:count], came)):
+        out_ref[m] = (term[0].astype(F32) + ref[1, i].astype(F32)).astype(BF16)
 
 
 def cross_sum(terms, came, name, after=()):
-    shape = (sum(t.shape[0] for t in terms),) + terms[0].shape[1:]
+    shape = (len(terms),) + terms[0].shape[1:]
     return small_call(
         functools.partial(cross_kernel, len(terms)),
         None,
@@ -927,28 +1052,25 @@
     )[0]
 
 
-def final_kernel(calls, crosses, *refs):
-    own_refs, near_refs = refs[:calls], refs[calls : 2 * calls]
-    cross_refs = refs[2 * calls : 2 * calls + crosses]
-    atoms_ref, gain_ref, shift_ref, grad_middle_ref, out_ref = refs[2 * calls + crosses :]
-    rows, width = own_refs[0].shape[1:]
+def final_kernel(counts, *refs):
+    owns, nears, crosses = [refs[sum(counts[:i]) : sum(counts[: i + 1])] for i in range(3)]
+    atoms_ref, gain_ref, shift_ref, grad_middle_ref, out_ref = refs[sum(counts) :]
     gain = as_row(gain_ref)
     shift = as_row(shift_ref)
-    crosses = [(ref, i) for ref in cross_refs for i in range(ref.shape[0])]
-    m = 0
-    for own_ref, near_ref in zip(own_refs, near_refs):
-        for i in range(own_ref.shape[0]):
-            cross_ref, at = crosses[m]
-            grad = own_ref[i] + near_ref[0, i].astype(F32) + cross_ref[at].astype(F32)
-            _, normed, inverse = norm_forward(atoms_ref[m].astype(F32), gain, shift)
-            result = grad_middle_ref[m] + norm_backward(grad, normed, inverse, gain)
-            out_ref[m] = result.astype(BF16)
-            m += 1
+    nears = [(ref, i) for ref in nears for i in range(ref.shape[1])]
+    crosses = [(ref, i) for ref in crosses for i in range(ref.shape[0])]
+    for m, own_ref in enumerate(owns):
+        near_ref, i = nears[m]
+        cross_ref, at = crosses[m]
+        grad = own_ref[0] + near_ref[0, i].astype(F32) + cross_ref[at].astype(F32)
+        _, normed, inverse = norm_forward(atoms_ref[m].astype(F32), gain, shift)
+        result = grad_middle_ref[m] + norm_backward(grad, normed, inverse, gain)
+        out_ref[m] = result.astype(BF16)
 
 
 def first_norm_backward(owns, nears, crosses, others, after=()):
     return small_call(
-        functools.partial(final_kernel, len(owns), len(crosses)),
+        functools.partial(final_kernel, (len(owns), len(nears), len(crosses))),
         None,
         owns + nears + crosses + list(others),
         [shape_of(others[0].shape, BF16)],
@@ -1037,34 +1159,48 @@
     count = molecules // STAGES
     stages = []
     pair_out = jnp.zeros((1,), BF16)
-    gathered = []
+    one = swap(atoms, "rows", 1)
+    mine = [atoms[:count]]
+    pair_near, query_near, key_near, value_near, later = load(
+        [pair_bias, query_weight, key_weight, value_weight, atoms_far],
+        "load_first",
+        (0, 0, 0, 0, count),
+        (place,),
+    )
+    mine.append(later)
+    gathered = [[swap(a, "rows", mask) for mask in (2, 3)] for a in mine]
+    projected = near_half(
+        head_size,
+        STAGES,
+        place,
+        atoms_far,
+        one,
+        (
+            first_gain,
+            first_shift,
+            query_near,
+            query_bias,
+            key_near,
+            value_near,
+            value_bias,
+        ),
+        (),
+    )
     for stage in range(STAGES):
-        mine = atoms[stage * count : (stage + 1) * count]
-        gathered.append([swap(mine, "rows", mask) for mask in (1, 2, 3)])
-    pair_near, query_near, key_near, value_near = pair_bias, query_weight, key_weight, value_weight
-    for stage in range(STAGES):
-        first = stage * count
-        pieces = [atoms_far] + gathered[stage]
-        pair_out, *kept = attention_forward(
+        pair_out, kept, loaded = attention_forward(
             head_size,
-            first,
-            count,
+            stage * count,
             place,
             lengths,
-            pieces,
+            gathered[stage],
             pair_near,
-            (
-                line(first_gain),
-                line(first_shift),
-                query_near,
-                line(query_bias),
-                key_near,
-                value_near,
-                line(value_bias),
-            ),
+            (first_gain, first_shift, key_near, value_near, value_bias),
+            projected[5 * stage : 5 * stage + 5],
             pair_out,
+            [out_weight, inner_weight, outer_weight, atoms_cotangent] if stage else [],
         )
         stages.append(kept)
+    out_weight, inner_weight, outer_weight, atoms_cotangent = loaded
     (
         atoms_out,
         outer_send,
@@ -1076,6 +1212,7 @@
         grad_middle,
         grad_mixed,
         dense_vectors,
+        pair_cotangent,
     ) = dense(
         place,
         [s[1] for s in stages],
@@ -1092,6 +1229,7 @@
             line(outer_bias),
         ),
         batch_count,
+        pair_cotangent,
     )
     pairs = batch_count // 2
     own_rows = model_width // batch_count
@@ -1102,18 +1240,13 @@
         ([slots(out_keep)], [slots(out_send)]),
     ]
     usual = batch_count == 8
-    if usual:
-        dense_pieces, held = sum_core(place, dense_groups, dense_vectors, "dense")
-        after = [held]
-    else:
-        dense_total, dense_vectors = batch_slices_any(dense_groups, dense_vectors)
-        after = []
-
-    def backward(stage, span, held, sums, after):
+
+    def backward(molecule, held, sums, after, before=None):
+        stage = molecule // count
         return attention_backward(
             head_size,
             stage * count,
-            span,
+            molecule % count,
             place,
             stages[stage],
             pair_cotangent,
@@ -1122,76 +1255,73 @@
             held,
             sums,
             after,
+            before,
         )
 
-    pair_grad, near0, cross0, own0, sums, *grads0 = backward(0, (0, count), None, None, after)
-    near0 = swap(near0, "rows", 1)
+    pair_grad, near0, cross0, own0, sums, *grads0 = backward(0, None, None, [])
     after = []
     if usual:
-        dense_pieces, held = sum_first(place, dense_pieces, "dense", (own0,))
+        dense_pieces, held = sum_core(place, dense_groups, dense_vectors, "dense", (own0,))
         after = [held]
-    half = count // 2
-    pair_grad, near1, cross1, own1, sums, *grads1 = backward(1, (0, half), pair_grad, sums, after)
+    else:
+        dense_total, dense_vectors = batch_slices_any(dense_groups, dense_vectors)
+    pair_grad, near1, cross1, own1, sums, *grads1 = backward(1, pair_grad, sums, after, near0)
     near1 = swap(near1, "rows", 1)
-    after = [own1]
-    came = near1
+    pair_grad, near2, cross2, own2, sums, *grads2 = backward(2, pair_grad, sums, [own1])
+    near2 = swap(near2, "rows", 1)
+    after = [own2]
+    if usual:
+        dense_pieces, held = sum_first(place, dense_pieces, "dense", after)
+        after = [held]
+    cross0 = cross_sum([cross0, cross1], [near1], "cross_first", after)
+    far0 = swap(cross0, "rows", 2)
+    pair_grad, near3, cross3, own3, tail_vectors, *grads3 = backward(3, pair_grad, sums, [cross0])
+    near3 = swap(near3, "rows", 1)
+    after = [own3]
     if usual:
         dense_total, came = sum_second_cut(place, dense_pieces, "dense", after)
         after = [dense_total]
-    cross0 = cross_sum([cross0], [near0], "cross_first", after)
-    far0 = swap(cross0, "rows", 2)
-    pair_grad, near2, cross2, own2, tail_vectors, *grads2 = backward(
-        1, (half, count), pair_grad, sums, [cross0]
-    )
-    near2 = swap(near2, "rows", 1)
+    cross2 = cross_sum([cross2], [near2], "cross_second", after)
+    far2 = swap(cross2, "rows", 2)
+    after = [far0, cross2]
     part = shape_of((pairs, 1, own_rows, model_width), BF16)
     parts = small_call(
-        functools.partial(weight_kernel, 3, STAGES),
+        functools.partial(weight_kernel, 4, STAGES),
         place,
-        [s[3] for s in stages] + grads0 + grads1 + grads2,
+        [s[3] for s in stages] + grads0 + grads1 + grads2 + grads3,
         [part] * 6,
         "attention_weights",
-        (far0, near1, came),
+        after,
         scratch=[pltpu.VMEM((pairs, 2, own_rows, model_width), F32)],
         mib=14,
     )
     groups = [([parts[2 * i + 1]], [parts[2 * i]]) for i in range(3)]
     matrix = shape_of((own_rows, model_width), F32)
     ratio = inner_weight.shape[1] // model_width
-    vectors_shape = shape_of((8, model_width), F32)
+    vector = shape_of((own_rows,), F32)
     finish = (atoms, line(first_gain), line(first_shift), grad_middle)
     if usual:
-        pieces, held = sum_core(place, groups, tail_vectors, "tail")
-        part = shape_of((came.shape[0] // 2, model_width), BF16)
-        sent, kept = small_call(
-            near_sum_kernel,
-            place,
-            [dense_total, came],
-            [part, shape_of(part.shape, F32)],
-            "dense_near_sum",
-            (held,),
-        )
-        came = swap(sent, "rows", 2)
-        cross1 = cross_sum([cross1, cross2], [near1, near2], "cross_second", (sent,))
-        far1 = swap(cross1, "rows", 2)
-        pieces, held = sum_first(place, pieces, "tail", (cross1,))
-        total = sum_second(pieces, "tail", (held,))
+        pieces, _ = sum_core(place, groups, tail_vectors, "tail")
+        pieces, held = sum_first(place, pieces, "tail")
+        part = shape_of(came.shape, BF16)
+        mine = small_call(
+            near_sum_kernel, place, [dense_total, came], [part], "dense_near_sum", (held, far2)
+        )[0]
+        came = swap(mine, "rows", 2)
+        cross3 = cross_sum([cross3], [near3], "cross_third", (mine,))
+        far3 = swap(cross3, "rows", 2)
+        total = sum_second(pieces, "tail", (cross3,))
         tail_came = swap(total, "rows", 1)
-        mine = small_call(add_kernel, None, [kept, came], [part], "dense_far_sum", (total,))[0]
-        came = swap(mine, "rows", 2)
-        atoms_grad = first_norm_backward(
-            [own0, own1, own2], [near0, near1, near2], [far0, far1], finish, (mine,)
-        )
+        mine = small_call(add_kernel, None, [mine, came], [part], "dense_far_sum", (total,))[0]
+        came = swap(mine, "rows", 1)
         total = small_call(
-            add_kernel, None, [total, tail_came], [total], "tail_near_sum", (atoms_grad,)
+            add_kernel, None, [total, tail_came], [total], "tail_near_sum", (mine, far3)
         )[0]
         tail_came = swap(total, "rows", 2)
-        half_shape = shape_of((2 * part.shape[0], model_width), BF16)
-        mine = small_call(
-            join_kernel, place, [mine, came], [half_shape], "dense_join", (total,)
-        )[0]
-        came = swap(mine, "rows", 1)
-        outer_grad, inner_grad, out_grad, dense_vectors = small_call(
+        atoms_grad = first_norm_backward(
+            [own0, own1, own2, own3], [near1, near2, near3], [far0, far2, far3], finish, (total,)
+        )
+        outer_grad, inner_grad, out_grad, *dense_parts = small_call(
             functools.partial(finish_dense_kernel, ratio),
             place,
             [mine, came],
@@ -1199,55 +1329,64 @@
                 shape_of((ratio * own_rows, model_width), F32),
                 shape_of((own_rows, ratio * model_width), F32),
                 matrix,
-                vectors_shape,
+                vector,
+                vector,
+                vector,
+                vector,
+                shape_of((ratio * own_rows,), F32),
             ],
             "finish_dense",
-            (total,),
+            (atoms_grad,),
             inside=False,
-            scratch=[pltpu.VMEM((4 * part.shape[0], model_width), BF16)],
+            scratch=[
+                pltpu.VMEM((2 * part.shape[0], model_width), BF16),
+                pltpu.VMEM((VECTOR_ROWS, model_width), F32),
+            ],
         )
-        query_grad, key_grad, value_grad, tail_vectors = small_call(
+        query_grad, key_grad, value_grad, *tail_parts = small_call(
             finish_tail_kernel,
-            None,
+            place,
             [total, tail_came],
-            [matrix, matrix, matrix, vectors_shape],
+            [matrix, matrix, matrix, vector, vector, vector, vector],
             "finish_tail",
             (out_grad,),
             inside=False,
         )
     else:
-        far1 = swap(cross_sum([cross1, cross2], [near1, near2], "cross_second"), "rows", 2)
+        far3 = swap(cross_sum([cross3], [near3], "cross_third"), "rows", 2)
         atoms_grad = first_norm_backward(
-            [own0, own1, own2], [near0, near1, near2], [far0, far1], finish
+            [own0, own1, own2, own3], [near1, near2, near3], [far0, far2, far3], finish
         )
         total, tail_vectors = batch_slices_any(groups, tail_vectors)
         query_grad, key_grad, value_grad = total[0], total[1], total[2]
         outer_grad = dense_total[:ratio].reshape(-1, model_width)
         inner_grad = dense_total[ratio : 2 * ratio].transpose(1, 0, 2).reshape(own_rows, -1)
         out_grad = dense_total[2 * ratio]
-    part = lambda v: lax.dynamic_slice_in_dim(
-        v, batch_index * (v.shape[0] // batch_count), v.shape[0] // batch_count
-    )
+        part = lambda v: lax.dynamic_slice_in_dim(
+            v, batch_index * (v.shape[0] // batch_count), v.shape[0] // batch_count
+        )
+        tail_parts = [part(v) for v in tail_vectors[:4]]
+        dense_parts = [part(v) for v in dense_vectors[:4]] + [part(dense_vectors[4:].reshape(-1))]
     return (
         atoms_out,
         pair_out,
         atoms_grad,
         pair_grad,
-        part(tail_vectors[0]),
-        part(tail_vectors[1]),
+        tail_parts[0],
+        tail_parts[1],
         query_grad,
-        part(tail_vectors[2]),
+        tail_parts[2],
         key_grad,
         value_grad,
-        part(tail_vectors[3]),
+        tail_parts[3],
         out_grad,
-        part(dense_vectors[3]),
-        part(dense_vectors[1]),
-        part(dense_vectors[2]),
+        dense_parts[3],
+        dense_parts[1],
+        dense_parts[2],
         inner_grad,
-        part(dense_vectors[4:].reshape(-1)),
+        dense_parts[4],
         outer_grad,
-        part(dense_vectors[0]),
+        dense_parts[0],
     )
 
 

time: 159 us -> 143 us (0.90)
  starting transfers between devices: 44.6 us -> 35.7 us
  local copies, waits for them, and re-layouts: 6.59 us -> 2.9 us
    ppermute x33 -> x32, starting transfers between devices: 44.6 us -> 35.7 us  [swap(): return lax.ppermute(value, axis, [(i, i ^ mask) for i in range(size)])]
    pallas_call x3 -> x4, Pallas kernels: 27.8 us -> 22.9 us  [attention_backward(): pl.pallas_call(functools.partial(backward_kernel, head_size, 4, first, ba...]
    pallas_call x2 -> x4, Pallas kernels: 18.8 us -> 23.3 us  [the longest x2 16.7 us: attention_forward(): pl.pallas_call(functools.partial(forward_kernel, head_size, 8, first, len...]
    dynamic_slice x5 -> x0, local copies, waits for them, and re-layouts: 2.98 us -> none  [shards(): lax.dynamic_slice_in_dim(v, batch_index * (v.shape[0] // batch_count), v....]
    ppermute x33 -> x32, waiting for transfers between devices: 38.4 us -> 37.2 us  [swap(): return lax.ppermute(value, axis, [(i, i ^ mask) for i in range(size)])]
  transfers between devices with their start and end apart: 33 -> 32, of which waited for: 12 -> 11; matrix products, arithmetic and copies ran while one was open for 0% -> 1% of each run, Pallas kernels for 27% -> 31%
where the time goes in v4:
time: 143 us
  Pallas kernels  66.4 us (46%)
  waiting for transfers between devices  37.2 us (26%)
  starting transfers between devices  35.7 us (25%)
  local copies, waits for them, and re-layouts  2.9 us (2%)
    ppermute x32, waiting for transfers between devices, swap(): return lax.ppermute(value, axis, [(i, i ^ mask) for i in range(size)])  37.2 us
    ppermute x32, starting transfers between devices, swap(): return lax.ppermute(value, axis, [(i, i ^ mask) for i in range(size)])  35.7 us
    pallas_call x4, Pallas kernels, attention_backward(): pl.pallas_call(functools.partial(backward_kernel, head_size, 4, first, ba...  22.9 us
    pallas_call x2, Pallas kernels, attention_forward(): pl.pallas_call(functools.partial(forward_kernel, head_size, 8, first, len...  16.7 us
    pallas_call x16, Pallas kernels, small_call(): pl.pallas_call(body, grid_spec=pltpu.PrefetchScalarGridSpec(num_scalar_pr...  11.6 us
    pallas_call x1, Pallas kernels, dense(): pl.pallas_call(functools.partial(dense_kernel, len(mixed)), grid_spec=plt...  8.61 us
    pallas_call x1, Pallas kernels, load(): pl.pallas_call(functools.partial(load_kernel, count, starts), in_specs=[p...  3.78 us
  transfers between devices with their start and end apart: 32, of which 11 were waited for; matrix products, arithmetic and copies ran while one was open for 1% of the time, Pallas kernels for 31%

profile of v4, /device:TPU:0, one launch (start us, length us, event | category | flops | bytes accessed | tf_op | source)
XLA Modules:
  0.0 143.0 jit_solution(2620466909112955513)
XLA Ops:
  0.7 3.1 %collective-permute-start.2 = (bf16[4,64,512]{2,1,0:T(8,128)(2,1)}, bf16[4,64,512]{2,1,0:T(8,128)(2,1)S(1)}, u32[]{:S(2)}, u32[]{:S(2)}) collective-permute-start(bf16[4,64,512]{2,1,0:T(8,128)(2,1)} %refs_10_.1), channel_id=1, source_target_pairs={{0,1},{1,0},{2,3},{3,2},{4,5},{5,4},{6,7},{7,6},{8,9},{9,8},{10,11... | collective-permute-start | bytes 786440 | tf_op jit(solution)/shard_map/ppermute | solution.py:788
  4.7 2.5 %collective-permute-start.1 = (bf16[2,64,512]{2,1,0:T(8,128)(2,1)S(1)}, bf16[2,64,512]{2,1,0:T(8,128)(2,1)S(1)}, u32[]{:S(2)}, u32[]{:S(2)}) collective-permute-start(bf16[2,64,512]{2,1,0:T(8,128)(2,1)S(1)} %slice.3), channel_id=1, source_target_pairs={{0,3},{1,2},{2,1},{3,0},{4,7},{5,6},{6,5},{7,4},{8,11},{9,10},{10,... | collective-permute-start | bytes 393224 | tf_op jit(solution)/shard_map/ppermute | solution.py:788
  7.5 3.8 %load_first.1 = (bf16[4,64,64,256]{3,2,1,0:T(8,128)(2,1)S(1)}, bf16[512,512]{1,0:T(8,128)(2,1)S(1)}, bf16[512,512]{1,0:T(8,128)(2,1)S(1)}, bf16[512,512]{1,0:T(8,128)(2,1)S(1)}, bf16[2,64,512]{2,1,0:T(8,128)(2,1)S(1)}) custom-call(bf16[4,64,64,256]{3,2,1,0:T(8,128)(2,1)} %refs_0_.1, bf16[512,512]{1,0:T(8,128)(2,1)} %refs_1_.1, bf16[512,512]{1,0:T(8,128)(2,1)} %refs_2_.2, ...), custom_call_target="tpu_custom_call" | custom-call | tf_op jit(solution)/shard_map/load_first/pallas_call | solution.py:98
  11.3 2.9 %collective-permute-start.4 = (bf16[2,64,512]{2,1,0:T(8,128)(2,1)S(1)}, bf16[2,64,512]{2,1,0:T(8,128)(2,1)S(1)}, u32[]{:S(2)}, u32[]{:S(2)}) collective-permute-start(bf16[2,64,512]{2,1,0:T(8,128)(2,1)S(1)} %get-tuple-element.150), channel_id=1, source_target_pairs={{0,3},{1,2},{2,1},{3,0},{4,7},{5,6},{6,5},{7,4},{8,11},{9,10},{10,... | collective-permute-start | bytes 393224 | tf_op jit(solution)/shard_map/ppermute | solution.py:788
  14.6 2.8 %near_half.1 = (bf16[2,256,512]{2,1,0:T(8,128)(2,1)S(1)}, bf16[2,256,512]{2,1,0:T(8,128)(2,1)S(1)}, bf16[2,4,256,128]{3,2,1,0:T(8,128)(2,1)S(1)}, bf16[2,4,256,2...) custom-call(s32[5]{0:T(128)S(1)} %stack.23.refs_5_.place_ref.refs_0_, ...), custom_call_target="tpu_custom_call" | custom-call | tf_op jit(solution)/shard_map/near_half/pallas_call | solution.py:197
  17.3 8.0 %collective-permute-done.two_ref = bf16[2,64,512]{2,1,0:T(8,128)(2,1)S(1)} collective-permute-done((bf16[2,64,512]{2,1,0:T(8,128)(2,1)S(1)}, bf16[2,64,512]{2,1,0:T(8,128)(2,1)S(1)}, u32[]{:S(2)}, u32[]{:S(2)}) %collective-permute-start) | collective-permute-done | bytes 131104 | tf_op jit(solution)/shard_map/ppermute | solution.py:788
  25.4 8.1 %attention_forward.2 = (bf16[4,64,64,256]{3,2,1,0:T(8,128)(2,1)}, bf16[2,64,64,256]{3,2,1,0:T(8,128)(2,1)S(1)}, f32[2,4,64,128]{3,2,1,0:T(8,128)S(1)}, f32[2,4,6...) custom-call(s32[5]{0:T(128)S(1)} %stack.23.refs_5_.place_ref.refs_0_, ...), custom_call_target="tpu_custom_call", output_to_operand_aliasing={{4}: (11, {}), {5}: (12, {}), {6}: (13, {}), {7}: (14, {})} | custom-call | flops 1610612736 | bytes 12582912 | tf_op jit(solution)/shard_map/attention_forward/pallas_call | solution.py:319
  33.5 8.6 %attention_forward.3 = (bf16[4,64,64,256]{3,2,1,0:T(8,128)(2,1)}, bf16[2,64,64,256]{3,2,1,0:T(8,128)(2,1)S(1)}, f32[2,4,64,128]{3,2,1,0:T(8,128)S(1)}, f32[2,4,6...) custom-call(s32[5]{0:T(128)S(1)} %stack.23.refs_5_.place_ref.refs_0_, ...), custom_call_target="tpu_custom_call", output_to_operand_aliasing={{4}: (11, {}), {5}: (12, {}), {6}: (13, {}), {7}: (14, {}),... | custom-call | flops 1610612736 | bytes 12582912 | tf_op jit(solution)/shard_map/attention_forward/pallas_call | solution.py:319
  42.2 8.6 %dense.1 = (bf16[4,64,512]{2,1,0:T(8,128)(2,1)}, bf16[4,256,512]{2,1,0:T(8,128)(2,1)S(1)}, bf16[4,256,512]{2,1,0:T(8,128)(2,1)S(1)}, bf16[4,4,64,512]{3,2,1,0:T(...) custom-call(s32[5]{0:T(128)S(1)} %stack.23.refs_5_.place_ref.refs_0_, ...), custom_call_target="tpu_custom_call" | custom-call | flops 3221225472 | bytes 12582912 | tf_op jit(solution)/shard_map/dense/pallas_call | solution.py:539
  51.9 5.7 %attention_backward.4 = (bf16[4,64,64,256]{3,2,1,0:T(8,128)(2,1)}, bf16[2,1,64,512]{3,2,1,0:T(8,128)(2,1)S(1)}, bf16[1,64,512]{2,1,0:T(8,128)(2,1)S(1)}, f32[1,6...) custom-call(s32[5]{0:T(128)S(1)} %stack.23.refs_5_.place_ref.refs_0_, ...), custom_call_target="tpu_custom_call" | custom-call | flops 1610612736 | bytes 6291456 | tf_op jit(solution)/shard_map/attention_backward/pallas_call | solution.py:737
  58.7 1.6 %collective-permute-start.11 = (bf16[1160,256]{1,0:T(8,128)(2,1)S(1)}, bf16[1160,256]{1,0:T(8,128)(2,1)S(1)}, u32[]{:S(2)}, u32[]{:S(2)}) collective-permute-start(bf16[1160,256]{1,0:T(8,128)(2,1)S(1)} %get-tuple-element.199), channel_id=1, source_target_pairs={{0,16},{4,20},{8,24},{12,28},{16,0},{20,4},{24,8},{28,12},{1,17},{... | collective-permute-start | bytes 1781768 | tf_op jit(solution)/shard_map/ppermute | solution.py:788
  60.3 1.5 %collective-permute-start.10 = (bf16[1160,256]{1,0:T(8,128)(2,1)S(1)}, bf16[1160,256]{1,0:T(8,128)(2,1)S(1)}, u32[]{:S(2)}, u32[]{:S(2)}) collective-permute-start(bf16[1160,256]{1,0:T(8,128)(2,1)S(1)} %get-tuple-element.181.refs_2_), channel_id=1, source_target_pairs={{0,8},{4,12},{8,0},{12,4},{16,24},{20,28},{24,16},{28,20},{1,9},{5... | collective-permute-start | bytes 1781768 | tf_op jit(solution)/shard_map/ppermute | solution.py:788
  61.8 5.7 %attention_backward.5 = (bf16[4,64,64,256]{3,2,1,0:T(8,128)(2,1)}, bf16[2,2,64,512]{3,2,1,0:T(8,128)(2,1)S(1)}, bf16[1,64,512]{2,1,0:T(8,128)(2,1)S(1)}, f32[1,6...) custom-call(s32[5]{0:T(128)S(1)} %stack.23.refs_5_.place_ref.refs_0_, ...), custom_call_target="tpu_custom_call", output_to_operand_aliasing={{0}: (13, {}), {4}: (14, {})} | custom-call | flops 1610612736 | bytes 6291456 | tf_op jit(solution)/shard_map/attention_backward/pallas_call | solution.py:737
  68.0 5.7 %attention_backward.6 = (bf16[4,64,64,256]{3,2,1,0:T(8,128)(2,1)}, bf16[2,1,64,512]{3,2,1,0:T(8,128)(2,1)S(1)}, bf16[1,64,512]{2,1,0:T(8,128)(2,1)S(1)}, f32[1,6...) custom-call(s32[5]{0:T(128)S(1)} %stack.23.refs_5_.place_ref.refs_0_, ...), custom_call_target="tpu_custom_call", output_to_operand_aliasing={{0}: (13, {}), {4}: (14, {})} | custom-call | flops 1610612736 | bytes 6291456 | tf_op jit(solution)/shard_map/attention_backward/pallas_call | solution.py:737
  76.2 1.6 %collective-permute-start.16 = (bf16[584,256]{1,0:T(8,128)(2,1)S(1)}, bf16[584,256]{1,0:T(8,128)(2,1)S(1)}, u32[]{:S(2)}, u32[]{:S(2)}) collective-permute-start(bf16[584,256]{1,0:T(8,128)(2,1)S(1)} %get-tuple-element.208), channel_id=1, source_target_pairs={{0,8},{4,12},{8,0},{12,4},{16,24},{20,28},{24,16},{28,20},{1,9},{5... | collective-permute-start | bytes 897032 | tf_op jit(solution)/shard_map/ppermute | solution.py:788
  78.8 3.4 %collective-permute-start.14 = (bf16[2,64,512]{2,1,0:T(8,128)(2,1)S(1)}, bf16[2,64,512]{2,1,0:T(8,128)(2,1)S(1)}, u32[]{:S(2)}, u32[]{:S(2)}) collective-permute-start(bf16[2,64,512]{2,1,0:T(8,128)(2,1)S(1)} %cross_first.1.refs_2_), channel_id=1, source_target_pairs={{0,2},{1,3},{2,0},{3,1},{4,6},{5,7},{6,4},{7,5},{8,10},{9,11},{10,... | collective-permute-start | bytes 393224 | tf_op jit(solution)/shard_map/ppermute | solution.py:788
  82.2 5.7 %attention_backward.7 = (bf16[4,64,64,256]{3,2,1,0:T(8,128)(2,1)}, bf16[2,1,64,512]{3,2,1,0:T(8,128)(2,1)S(1)}, bf16[1,64,512]{2,1,0:T(8,128)(2,1)S(1)}, f32[1,6...) custom-call(s32[5]{0:T(128)S(1)} %stack.23.refs_5_.place_ref.refs_0_, ...), custom_call_target="tpu_custom_call", output_to_operand_aliasing={{0}: (13, {}), {4}: (14, {})} | custom-call | flops 1610612736 | bytes 6291456 | tf_op jit(solution)/shard_map/attention_backward/pallas_call | solution.py:737
  88.8 2.1 %attention_weights.1 = (bf16[4,1,64,512]{3,2,1,0:T(8,128)(2,1)S(1)}, bf16[4,1,64,512]{3,2,1,0:T(8,128)(2,1)S(1)}, bf16[4,1,64,512]{3,2,1,0:T(8,128)(2,1)S(1)}, b...) custom-call(s32[5]{0:T(128)S(1)} %stack.23.refs_5_.place_ref.refs_0_, ...), custom_call_target="tpu_custom_call" | custom-call | bytes 4980736 | tf_op jit(solution)/shard_map/attention_weights/pallas_call | solution.py:944
  92.0 1.3 collective-permute-done.22.refs_8_
  94.6 1.5 %collective-permute-start.24 = (bf16[392,256]{1,0:T(8,128)(2,1)S(1)}, bf16[392,256]{1,0:T(8,128)(2,1)S(1)}, u32[]{:S(2)}, u32[]{:S(2)}) collective-permute-start(bf16[392,256]{1,0:T(8,128)(2,1)S(1)} %get-tuple-element.237), channel_id=1, source_target_pairs={{0,16},{4,20},{8,24},{12,28},{16,0},{20,4},{24,8},{28,12},{1,17},{... | collective-permute-start | bytes 602120 | tf_op jit(solution)/shard_map/ppermute | solution.py:788
  97.0 4.1 %collective-permute-done.23.refs_2_ = bf16[392,256]{1,0:T(8,128)(2,1)S(1)} collective-permute-done((bf16[392,256]{1,0:T(8,128)(2,1)S(1)}, bf16[392,256]{1,0:T(8,128)(2,1)S(1)}, u32[]{:S(2)}, u32[]{:S(2)}) %collective-permute-start.23) | collective-permute-done | bytes 200736 | tf_op jit(solution)/shard_map/ppermute | solution.py:788
  105.8 1.5 %collective-permute-start.26 = (bf16[200,256]{1,0:T(8,128)(2,1)S(1)}, bf16[200,256]{1,0:T(8,128)(2,1)S(1)}, u32[]{:S(2)}, u32[]{:S(2)}) collective-permute-start(bf16[200,256]{1,0:T(8,128)(2,1)S(1)} %get-tuple-element.239.refs_3_), channel_id=1, source_target_pairs={{0,16},{4,20},{8,24},{12,28},{16,0},{20,4},{24,8},{28,12},{1,17},{... | collective-permute-start | bytes 307208 | tf_op jit(solution)/shard_map/ppermute | solution.py:788
  107.3 6.7 %collective-permute-done.13.refs_1_.refs_6_ = bf16[2,1,64,512]{3,2,1,0:T(8,128)(2,1)S(1)} collective-permute-done((bf16[2,1,64,512]{3,2,1,0:T(8,128)(2,1)S(1)}, bf16[2,1,64,512]{3,2,1,0:T(8,128)(2,1)S(1)}, u32[]{:S(2)}, u32[]{:S(2)}) %collective-permute-start.13) | collective-permute-done | bytes 131104 | tf_op jit(solution)/shard_map/ppermute | solution.py:788
  114.1 2.5 %collective-permute-start.28 = (bf16[200,512]{1,0:T(8,128)(2,1)S(1)}, bf16[200,512]{1,0:T(8,128)(2,1)S(1)}, u32[]{:S(2)}, u32[]{:S(2)}) collective-permute-start(bf16[200,512]{1,0:T(8,128)(2,1)S(1)} %tail_sum_second.1.refs_2_.refs_0_), channel_id=1, source_target_pairs={{0,1},{1,0},{2,3},{3,2},{4,5},{5,4},{6,7},{7,6},{8,9},{9,8},{10,11... | collective-permute-start | bytes 614408 | tf_op jit(solution)/shard_map/ppermute | solution.py:788
  116.6 3.0 %collective-permute-done.29.refs_1_ = bf16[304,512]{1,0:T(8,128)(2,1)S(1)} collective-permute-done((bf16[304,512]{1,0:T(8,128)(2,1)S(1)}, bf16[304,512]{1,0:T(8,128)(2,1)S(1)}, u32[]{:S(2)}, u32[]{:S(2)}) %collective-permute-start.29) | collective-permute-done | bytes 311328 | tf_op jit(solution)/shard_map/ppermute | solution.py:788
  119.8 1.7 %collective-permute-start.25 = (bf16[1,64,512]{2,1,0:T(8,128)(2,1)S(1)}, bf16[1,64,512]{2,1,0:T(8,128)(2,1)S(1)}, u32[]{:S(2)}, u32[]{:S(2)}) collective-permute-start(bf16[1,64,512]{2,1,0:T(8,128)(2,1)S(1)} %cross_third.1.refs_5_), channel_id=1, source_target_pairs={{0,2},{1,3},{2,0},{3,1},{4,6},{5,7},{6,4},{7,5},{8,10},{9,11},{10,... | collective-permute-start | bytes 196616 | tf_op jit(solution)/shard_map/ppermute | solution.py:788
  121.5 6.7 %collective-permute-done.25.refs_3_.refs_9_ = bf16[1,64,512]{2,1,0:T(8,128)(2,1)S(1)} collective-permute-done((bf16[1,64,512]{2,1,0:T(8,128)(2,1)S(1)}, bf16[1,64,512]{2,1,0:T(8,128)(2,1)S(1)}, u32[]{:S(2)}, u32[]{:S(2)}) %collective-permute-start.25) | collective-permute-done | bytes 65568 | tf_op jit(solution)/shard_map/ppermute | solution.py:788
  128.3 3.4 %collective-permute-start.30 = (bf16[200,512]{1,0:T(8,128)(2,1)S(1)}, bf16[200,512]{1,0:T(8,128)(2,1)S(1)}, u32[]{:S(2)}, u32[]{:S(2)}) collective-permute-start(bf16[200,512]{1,0:T(8,128)(2,1)S(1)} %tail_near_sum.1.refs_14_.refs_1_), channel_id=1, source_target_pairs={{0,2},{1,3},{2,0},{3,1},{4,6},{5,7},{6,4},{7,5},{8,10},{9,11},{10,... | collective-permute-start | bytes 614408 | tf_op jit(solution)/shard_map/ppermute | solution.py:788
  131.7 1.8 %first_norm_backward.1.refs_3_ = bf16[4,64,512]{2,1,0:T(8,128)(2,1)} custom-call(f32[1,64,512]{2,1,0:T(8,128)S(1)} %get-tuple-element.171.refs_9_.refs_0_, f32[1,64,512]{2,1,0:T(8,128)S(1)} %get-tuple-element.183.refs_2_.refs_1_, f32[1,64,512]{2,1,0:T(8,128)S(1)} %get-tuple-element.191.refs_6_.refs_2_, f32[1,64,512]{2,1,0:T(8,128)S(1)} %get-tuple-element.202.refs_6_.refs_3_, ...), custom_call_target="tpu_custom_call" | custom-call | bytes 2361344 | tf_op jit(solution)/shard_map/first_norm_backward/pallas_call | solution.py:944
  134.5 1.6 %finish_dense.1 = (f32[256,512]{1,0:T(8,128)}, f32[64,2048]{1,0:T(8,128)}, f32[64,512]{1,0:T(8,128)}, f32[64]{0:T(128)}, f32[64]{0:T(128)}, /*index=5*/f32[64]{0:T(128)}, f32[64]{0:T(128)}, f32[256]{0:T(256)}) custom-call(s32[5]{0:T(128)S(1)} %stack.23.refs_5_.place_ref.refs_0_, bf16[304,512]{1,0:T(8,128)(2,1)S(1)} %dense_far_sum.1.refs_2_.refs_1_, ...), custom_call_target="tpu_custom_call" | custom-call | bytes 1804288 | tf_op jit(solution)/shard_map/finish_dense/pallas_call | solution.py:944
  136.1 4.7 %collective-permute-done.30.refs_2_ = bf16[200,512]{1,0:T(8,128)(2,1)S(1)} collective-permute-done((bf16[200,512]{1,0:T(8,128)(2,1)S(1)}, bf16[200,512]{1,0:T(8,128)(2,1)S(1)}, u32[]{:S(2)}, u32[]{:S(2)}) %collective-permute-start.30) | collective-permute-done | bytes 204832 | tf_op jit(solution)/shard_map/ppermute | solution.py:788
  141.7 1.3 finish_tail.1
  (67 shorter events, 18.6 us)
Async XLA Ops:
  0.7 13.9 %collective-permute-start.2 = (bf16[4,64,512]{2,1,0:T(8,128)(2,1)}, bf16[4,64,512]{2,1,0:T(8,128)(2,1)S(1)}, u32[]{:S(2)}, u32[]{:S(2)}) collective-permute-start(bf16[4,64,512]{2,1,0:T(8,128)(2,1)} %refs_10_.1), channel_id=1, source_target_pairs={{0,1},{1,0},{2,3},{3,2},{4,5},{5,4},{6,7},{7,6},{8,9},{9,8},{10,11... | collective-permute-start | bytes 786440 | tf_op jit(solution)/shard_map/ppermute | solution.py:788
  4.7 12.6 %collective-permute-start.1 = (bf16[2,64,512]{2,1,0:T(8,128)(2,1)S(1)}, bf16[2,64,512]{2,1,0:T(8,128)(2,1)S(1)}, u32[]{:S(2)}, u32[]{:S(2)}) collective-permute-start(bf16[2,64,512]{2,1,0:T(8,128)(2,1)S(1)} %slice.3), channel_id=1, source_target_pairs={{0,3},{1,2},{2,1},{3,0},{4,7},{5,6},{6,5},{7,4},{8,11},{9,10},{10,... | collective-permute-start | bytes 393224 | tf_op jit(solution)/shard_map/ppermute | solution.py:788
  7.2 18.1 %collective-permute-start = (bf16[2,64,512]{2,1,0:T(8,128)(2,1)S(1)}, bf16[2,64,512]{2,1,0:T(8,128)(2,1)S(1)}, u32[]{:S(2)}, u32[]{:S(2)}) collective-permute-start(bf16[2,64,512]{2,1,0:T(8,128)(2,1)S(1)} %slice.3), channel_id=1, source_target_pairs={{0,2},{1,3},{2,0},{3,1},{4,6},{5,7},{6,4},{7,5},{8,10},{9,11},{10,... | collective-permute-start | bytes 393224 | tf_op jit(solution)/shard_map/ppermute | solution.py:788
  11.3 22.2 %collective-permute-start.4 = (bf16[2,64,512]{2,1,0:T(8,128)(2,1)S(1)}, bf16[2,64,512]{2,1,0:T(8,128)(2,1)S(1)}, u32[]{:S(2)}, u32[]{:S(2)}) collective-permute-start(bf16[2,64,512]{2,1,0:T(8,128)(2,1)S(1)} %get-tuple-element.150), channel_id=1, source_target_pairs={{0,3},{1,2},{2,1},{3,0},{4,7},{5,6},{6,5},{7,4},{8,11},{9,10},{10,... | collective-permute-start | bytes 393224 | tf_op jit(solution)/shard_map/ppermute | solution.py:788
  14.2 19.3 %collective-permute-start.3 = (bf16[2,64,512]{2,1,0:T(8,128)(2,1)S(1)}, bf16[2,64,512]{2,1,0:T(8,128)(2,1)S(1)}, u32[]{:S(2)}, u32[]{:S(2)}) collective-permute-start(bf16[2,64,512]{2,1,0:T(8,128)(2,1)S(1)} %get-tuple-element.150), channel_id=1, source_target_pairs={{0,2},{1,3},{2,0},{3,1},{4,6},{5,7},{6,4},{7,5},{8,10},{9,11},{10,... | collective-permute-start | bytes 393224 | tf_op jit(solution)/shard_map/ppermute | solution.py:788
  50.8 6.8 %collective-permute-start.5 = (bf16[4,4,64,512]{3,2,1,0:T(8,128)(2,1)S(1)}, bf16[4,4,64,512]{3,2,1,0:T(8,128)(2,1)S(1)}, u32[]{:S(2)}, u32[]{:S(2)}) collective-permute-start(bf16[4,4,64,512]{3,2,1,0:T(8,128)(2,1)S(1)} %bitcast.11), channel_id=1, source_target_pairs={{0,4},{4,0},{8,12},{12,8},{16,20},{20,16},{24,28},{28,24},{1,5},{5... | collective-permute-start | bytes 3145736 | tf_op jit(solution)/shard_map/ppermute | solution.py:788
  50.9 6.8 %collective-permute-start.6 = (bf16[4,4,64,512]{3,2,1,0:T(8,128)(2,1)S(1)}, bf16[4,4,64,512]{3,2,1,0:T(8,128)(2,1)S(1)}, u32[]{:S(2)}, u32[]{:S(2)}) collective-permute-start(bf16[4,4,64,512]{3,2,1,0:T(8,128)(2,1)S(1)} %get-tuple-element.177), channel_id=1, source_target_pairs={{0,4},{4,0},{8,12},{12,8},{16,20},{20,16},{24,28},{28,24},{1,5},{5... | collective-permute-start | bytes 3145736 | tf_op jit(solution)/shard_map/ppermute | solution.py:788
  51.4 6.3 %collective-permute-start.7 = (bf16[4,1,64,512]{3,2,1,0:T(8,128)(2,1)S(1)}, bf16[4,1,64,512]{3,2,1,0:T(8,128)(2,1)S(1)}, u32[]{:S(2)}, u32[]{:S(2)}) collective-permute-start(bf16[4,1,64,512]{3,2,1,0:T(8,128)(2,1)S(1)} %bitcast.12), channel_id=1, source_target_pairs={{0,4},{4,0},{8,12},{12,8},{16,20},{20,16},{24,28},{28,24},{1,5},{5... | collective-permute-start | bytes 786440 | tf_op jit(solution)/shard_map/ppermute | solution.py:788
  51.4 6.2 %collective-permute-start.8 = (f32[8,512]{1,0:T(8,128)S(1)}, f32[8,512]{1,0:T(8,128)S(1)}, u32[]{:S(2)}, u32[]{:S(2)}) collective-permute-start(f32[8,512]{1,0:T(8,128)S(1)} %get-tuple-element.180.refs_7_), channel_id=1, source_target_pairs={{0,4},{4,0},{8,12},{12,8},{16,20},{20,16},{24,28},{28,24},{1,5},{5... | collective-permute-start | bytes 49160 | tf_op jit(solution)/shard_map/ppermute | solution.py:788
  58.7 15.5 %collective-permute-start.11 = (bf16[1160,256]{1,0:T(8,128)(2,1)S(1)}, bf16[1160,256]{1,0:T(8,128)(2,1)S(1)}, u32[]{:S(2)}, u32[]{:S(2)}) collective-permute-start(bf16[1160,256]{1,0:T(8,128)(2,1)S(1)} %get-tuple-element.199), channel_id=1, source_target_pairs={{0,16},{4,20},{8,24},{12,28},{16,0},{20,4},{24,8},{28,12},{1,17},{... | collective-permute-start | bytes 1781768 | tf_op jit(solution)/shard_map/ppermute | solution.py:788
  60.3 15.1 %collective-permute-start.10 = (bf16[1160,256]{1,0:T(8,128)(2,1)S(1)}, bf16[1160,256]{1,0:T(8,128)(2,1)S(1)}, u32[]{:S(2)}, u32[]{:S(2)}) collective-permute-start(bf16[1160,256]{1,0:T(8,128)(2,1)S(1)} %get-tuple-element.181.refs_2_), channel_id=1, source_target_pairs={{0,8},{4,12},{8,0},{12,4},{16,24},{20,28},{24,16},{28,20},{1,9},{5... | collective-permute-start | bytes 1781768 | tf_op jit(solution)/shard_map/ppermute | solution.py:788
  67.5 11.3 %collective-permute-start.9 = (bf16[2,2,64,512]{3,2,1,0:T(8,128)(2,1)S(1)}, bf16[2,2,64,512]{3,2,1,0:T(8,128)(2,1)S(1)}, u32[]{:S(2)}, u32[]{:S(2)}) collective-permute-start(bf16[2,2,64,512]{3,2,1,0:T(8,128)(2,1)S(1)} %get-tuple-element.196), channel_id=1, source_target_pairs={{0,1},{1,0},{2,3},{3,2},{4,5},{5,4},{6,7},{7,6},{8,9},{9,8},{10,11... | collective-permute-start | bytes 786440 | tf_op jit(solution)/shard_map/ppermute | solution.py:788
  76.2 11.8 %collective-permute-start.16 = (bf16[584,256]{1,0:T(8,128)(2,1)S(1)}, bf16[584,256]{1,0:T(8,128)(2,1)S(1)}, u32[]{:S(2)}, u32[]{:S(2)}) collective-permute-start(bf16[584,256]{1,0:T(8,128)(2,1)S(1)} %get-tuple-element.208), channel_id=1, source_target_pairs={{0,8},{4,12},{8,0},{12,4},{16,24},{20,28},{24,16},{28,20},{1,9},{5... | collective-permute-start | bytes 897032 | tf_op jit(solution)/shard_map/ppermute | solution.py:788
  77.7 10.2 %collective-permute-start.15 = (bf16[584,256]{1,0:T(8,128)(2,1)S(1)}, bf16[584,256]{1,0:T(8,128)(2,1)S(1)}, u32[]{:S(2)}, u32[]{:S(2)}) collective-permute-start(bf16[584,256]{1,0:T(8,128)(2,1)S(1)} %get-tuple-element.201.refs_3_), channel_id=1, source_target_pairs={{0,16},{4,20},{8,24},{12,28},{16,0},{20,4},{24,8},{28,12},{1,17},{... | collective-permute-start | bytes 897032 | tf_op jit(solution)/shard_map/ppermute | solution.py:788
  78.2 10.5 %collective-permute-start.12 = (bf16[2,1,64,512]{3,2,1,0:T(8,128)(2,1)S(1)}, bf16[2,1,64,512]{3,2,1,0:T(8,128)(2,1)S(1)}, u32[]{:S(2)}, u32[]{:S(2)}) collective-permute-start(bf16[2,1,64,512]{3,2,1,0:T(8,128)(2,1)S(1)} %get-tuple-element.203), channel_id=1, source_target_pairs={{0,1},{1,0},{2,3},{3,2},{4,5},{5,4},{6,7},{7,6},{8,9},{9,8},{10,11... | collective-permute-start | bytes 393224 | tf_op jit(solution)/shard_map/ppermute | solution.py:788
  78.8 10.0 %collective-permute-start.14 = (bf16[2,64,512]{2,1,0:T(8,128)(2,1)S(1)}, bf16[2,64,512]{2,1,0:T(8,128)(2,1)S(1)}, u32[]{:S(2)}, u32[]{:S(2)}) collective-permute-start(bf16[2,64,512]{2,1,0:T(8,128)(2,1)S(1)} %cross_first.1.refs_2_), channel_id=1, source_target_pairs={{0,2},{1,3},{2,0},{3,1},{4,6},{5,7},{6,4},{7,5},{8,10},{9,11},{10,... | collective-permute-start | bytes 393224 | tf_op jit(solution)/shard_map/ppermute | solution.py:788
  90.9 2.4 %collective-permute-start.19 = (bf16[4,1,64,512]{3,2,1,0:T(8,128)(2,1)S(1)}, bf16[4,1,64,512]{3,2,1,0:T(8,128)(2,1)S(1)}, u32[]{:S(2)}, u32[]{:S(2)}) collective-permute-start(bf16[4,1,64,512]{3,2,1,0:T(8,128)(2,1)S(1)} %get-tuple-element.228), channel_id=1, source_target_pairs={{0,4},{4,0},{8,12},{12,8},{16,20},{20,16},{24,28},{28,24},{1,5},{5... | collective-permute-start | bytes 786440 | tf_op jit(solution)/shard_map/ppermute | solution.py:788
  91.0 2.3 %collective-permute-start.20 = (bf16[4,1,64,512]{3,2,1,0:T(8,128)(2,1)S(1)}, bf16[4,1,64,512]{3,2,1,0:T(8,128)(2,1)S(1)}, u32[]{:S(2)}, u32[]{:S(2)}) collective-permute-start(bf16[4,1,64,512]{3,2,1,0:T(8,128)(2,1)S(1)} %get-tuple-element.230), channel_id=1, source_target_pairs={{0,4},{4,0},{8,12},{12,8},{16,20},{20,16},{24,28},{28,24},{1,5},{5... | collective-permute-start | bytes 786440 | tf_op jit(solution)/shard_map/ppermute | solution.py:788
  91.4 1.8 %collective-permute-start.21 = (bf16[4,1,64,512]{3,2,1,0:T(8,128)(2,1)S(1)}, bf16[4,1,64,512]{3,2,1,0:T(8,128)(2,1)S(1)}, u32[]{:S(2)}, u32[]{:S(2)}) collective-permute-start(bf16[4,1,64,512]{3,2,1,0:T(8,128)(2,1)S(1)} %get-tuple-element.232), channel_id=1, source_target_pairs={{0,4},{4,0},{8,12},{12,8},{16,20},{20,16},{24,28},{28,24},{1,5},{5... | collective-permute-start | bytes 786440 | tf_op jit(solution)/shard_map/ppermute | solution.py:788
  91.5 11.1 %collective-permute-start.18 = (bf16[304,512]{1,0:T(8,128)(2,1)S(1)}, bf16[304,512]{1,0:T(8,128)(2,1)S(1)}, u32[]{:S(2)}, u32[]{:S(2)}) collective-permute-start(bf16[304,512]{1,0:T(8,128)(2,1)S(1)} %get-tuple-element.212), channel_id=1, source_target_pairs={{0,1},{1,0},{2,3},{3,2},{4,5},{5,4},{6,7},{7,6},{8,9},{9,8},{10,11... | collective-permute-start | bytes 933896 | tf_op jit(solution)/shard_map/ppermute | solution.py:788
  91.5 1.7 %collective-permute-start.22 = (f32[8,512]{1,0:T(8,128)S(1)}, f32[8,512]{1,0:T(8,128)S(1)}, u32[]{:S(2)}, u32[]{:S(2)}) collective-permute-start(f32[8,512]{1,0:T(8,128)S(1)} %get-tuple-element.233.refs_7_), channel_id=1, source_target_pairs={{0,4},{4,0},{8,12},{12,8},{16,20},{20,16},{24,28},{28,24},{1,5},{5... | collective-permute-start | bytes 49160 | tf_op jit(solution)/shard_map/ppermute | solution.py:788
  94.0 7.1 %collective-permute-start.23 = (bf16[392,256]{1,0:T(8,128)(2,1)S(1)}, bf16[392,256]{1,0:T(8,128)(2,1)S(1)}, u32[]{:S(2)}, u32[]{:S(2)}) collective-permute-start(bf16[392,256]{1,0:T(8,128)(2,1)S(1)} %get-tuple-element.235), channel_id=1, source_target_pairs={{0,8},{4,12},{8,0},{12,4},{16,24},{20,28},{24,16},{28,20},{1,9},{5... | collective-permute-start | bytes 602120 | tf_op jit(solution)/shard_map/ppermute | solution.py:788
  94.6 6.8 %collective-permute-start.24 = (bf16[392,256]{1,0:T(8,128)(2,1)S(1)}, bf16[392,256]{1,0:T(8,128)(2,1)S(1)}, u32[]{:S(2)}, u32[]{:S(2)}) collective-permute-start(bf16[392,256]{1,0:T(8,128)(2,1)S(1)} %get-tuple-element.237), channel_id=1, source_target_pairs={{0,16},{4,20},{8,24},{12,28},{16,0},{20,4},{24,8},{28,12},{1,17},{... | collective-permute-start | bytes 602120 | tf_op jit(solution)/shard_map/ppermute | solution.py:788
  96.1 6.5 %collective-permute-start.17 = (bf16[1,64,512]{2,1,0:T(8,128)(2,1)S(1)}, bf16[1,64,512]{2,1,0:T(8,128)(2,1)S(1)}, u32[]{:S(2)}, u32[]{:S(2)}) collective-permute-start(bf16[1,64,512]{2,1,0:T(8,128)(2,1)S(1)} %cross_second.1.refs_16_), channel_id=1, source_target_pairs={{0,2},{1,3},{2,0},{3,1},{4,6},{5,7},{6,4},{7,5},{8,10},{9,11},{10,... | collective-permute-start | bytes 196616 | tf_op jit(solution)/shard_map/ppermute | solution.py:788
  103.3 16.4 %collective-permute-start.29 = (bf16[304,512]{1,0:T(8,128)(2,1)S(1)}, bf16[304,512]{1,0:T(8,128)(2,1)S(1)}, u32[]{:S(2)}, u32[]{:S(2)}) collective-permute-start(bf16[304,512]{1,0:T(8,128)(2,1)S(1)} %dense_near_sum.1.refs_2_.refs_0_), channel_id=1, source_target_pairs={{0,2},{1,3},{2,0},{3,1},{4,6},{5,7},{6,4},{7,5},{8,10},{9,11},{10,... | collective-permute-start | bytes 933896 | tf_op jit(solution)/shard_map/ppermute | solution.py:788
  104.5 9.5 %collective-permute-start.13 = (bf16[2,1,64,512]{3,2,1,0:T(8,128)(2,1)S(1)}, bf16[2,1,64,512]{3,2,1,0:T(8,128)(2,1)S(1)}, u32[]{:S(2)}, u32[]{:S(2)}) collective-permute-start(bf16[2,1,64,512]{3,2,1,0:T(8,128)(2,1)S(1)} %get-tuple-element.204), channel_id=1, source_target_pairs={{0,1},{1,0},{2,3},{3,2},{4,5},{5,4},{6,7},{7,6},{8,9},{9,8},{10,11... | collective-permute-start | bytes 393224 | tf_op jit(solution)/shard_map/ppermute | solution.py:788
  104.8 9.2 %collective-permute-start.27 = (bf16[200,256]{1,0:T(8,128)(2,1)S(1)}, bf16[200,256]{1,0:T(8,128)(2,1)S(1)}, u32[]{:S(2)}, u32[]{:S(2)}) collective-permute-start(bf16[200,256]{1,0:T(8,128)(2,1)S(1)} %get-tuple-element.243), channel_id=1, source_target_pairs={{0,8},{4,12},{8,0},{12,4},{16,24},{20,28},{24,16},{28,20},{1,9},{5... | collective-permute-start | bytes 307208 | tf_op jit(solution)/shard_map/ppermute | solution.py:788
  105.8 8.3 %collective-permute-start.26 = (bf16[200,256]{1,0:T(8,128)(2,1)S(1)}, bf16[200,256]{1,0:T(8,128)(2,1)S(1)}, u32[]{:S(2)}, u32[]{:S(2)}) collective-permute-start(bf16[200,256]{1,0:T(8,128)(2,1)S(1)} %get-tuple-element.239.refs_3_), channel_id=1, source_target_pairs={{0,16},{4,20},{8,24},{12,28},{16,0},{20,4},{24,8},{28,12},{1,17},{... | collective-permute-start | bytes 307208 | tf_op jit(solution)/shard_map/ppermute | solution.py:788
  114.1 14.1 %collective-permute-start.28 = (bf16[200,512]{1,0:T(8,128)(2,1)S(1)}, bf16[200,512]{1,0:T(8,128)(2,1)S(1)}, u32[]{:S(2)}, u32[]{:S(2)}) collective-permute-start(bf16[200,512]{1,0:T(8,128)(2,1)S(1)} %tail_sum_second.1.refs_2_.refs_0_), channel_id=1, source_target_pairs={{0,1},{1,0},{2,3},{3,2},{4,5},{5,4},{6,7},{7,6},{8,9},{9,8},{10,11... | collective-permute-start | bytes 614408 | tf_op jit(solution)/shard_map/ppermute | solution.py:788
  119.7 13.9 %collective-permute-start.31 = (bf16[304,512]{1,0:T(8,128)(2,1)S(1)}, bf16[304,512]{1,0:T(8,128)(2,1)S(1)}, u32[]{:S(2)}, u32[]{:S(2)}) collective-permute-start(bf16[304,512]{1,0:T(8,128)(2,1)S(1)} %dense_far_sum.1.refs_2_.refs_1_), channel_id=1, source_target_pairs={{0,1},{1,0},{2,3},{3,2},{4,5},{5,4},{6,7},{7,6},{8,9},{9,8},{10,11... | collective-permute-start | bytes 933896 | tf_op jit(solution)/shard_map/ppermute | solution.py:788
  119.8 8.5 %collective-permute-start.25 = (bf16[1,64,512]{2,1,0:T(8,128)(2,1)S(1)}, bf16[1,64,512]{2,1,0:T(8,128)(2,1)S(1)}, u32[]{:S(2)}, u32[]{:S(2)}) collective-permute-start(bf16[1,64,512]{2,1,0:T(8,128)(2,1)S(1)} %cross_third.1.refs_5_), channel_id=1, source_target_pairs={{0,2},{1,3},{2,0},{3,1},{4,6},{5,7},{6,4},{7,5},{8,10},{9,11},{10,... | collective-permute-start | bytes 196616 | tf_op jit(solution)/shard_map/ppermute | solution.py:788
  128.3 12.5 %collective-permute-start.30 = (bf16[200,512]{1,0:T(8,128)(2,1)S(1)}, bf16[200,512]{1,0:T(8,128)(2,1)S(1)}, u32[]{:S(2)}, u32[]{:S(2)}) collective-permute-start(bf16[200,512]{1,0:T(8,128)(2,1)S(1)} %tail_near_sum.1.refs_14_.refs_1_), channel_id=1, source_target_pairs={{0,2},{1,3},{2,0},{3,1},{4,6},{5,7},{6,4},{7,5},{8,10},{9,11},{10,... | collective-permute-start | bytes 614408 | tf_op jit(solution)/shard_map/ppermute | solution.py:788
  (4 other events, 35.2 us)

commit v5 on v4

--- a/solution.py
+++ b/solution.py
@@ -200,7 +200,7 @@
             num_scalar_prefetch=1,
             grid=(1,),
             in_specs=[whole(atoms), near_spec()]
-            + [near_spec() if a.ndim > 1 else whole(a) for a in parameters]
+            + [near_spec() for a in parameters]
             + [pl.BlockSpec(memory_space=pl.ANY)] * len(after),
             out_specs=[near_spec()] * (5 * stages),
             scratch_shapes=[pltpu.VMEM((count * 2 * rows, model_width), BF16)],
@@ -307,7 +307,7 @@
     elements = count * head_count * rows * keys
     operands = [place, lengths, *pieces, pair_bias, query, *parameters]
     in_specs = [near_spec()] * (len(pieces) + 2)
-    in_specs += [near_spec() if a.ndim > 1 else whole(a) for a in parameters]
+    in_specs += [near_spec() for a in parameters]
     start = len(operands)
     operands += [hidden, normed, key, value, held]
     in_specs += [near_spec()] * 4 + [pl.BlockSpec(memory_space=pl.ANY)]
@@ -429,7 +429,7 @@
     at = pl.ds(pl.multiple_of(step * width, width), width)
     inner_weight = inner_weight_ref[:, at]
     outer_weight = outer_weight_ref[at]
-    pre = dot(hidden, inner_weight) + as_row(inner_bias_ref)
+    pre = dot(hidden, inner_weight) + inner_bias_ref[at].astype(F32).reshape(1, -1)
     slope = math.sqrt(2.0 / math.pi)
     square = pre * pre
     tanh = jnp.tanh(slope * (pre + 0.044715 * (pre * square)))
@@ -532,9 +532,8 @@
     out_specs[10] = near_spec()
     in_specs = [whole(a) for a in operands[1:]]
     for i, a in enumerate(operands[1:]):
-        if a.ndim > 1 and i != len(mixed):
+        if i != len(mixed):
             in_specs[i] = near_spec()
-    in_specs[-4] = pl.BlockSpec((width,), lambda s, *_: (s,))
     in_specs[-1] = pl.BlockSpec(memory_space=pltpu.HBM)
     return pl.pallas_call(
         functools.partial(dense_kernel, len(mixed)),
@@ -870,21 +869,32 @@
     total_ref[size : size + VECTOR_ROWS] = vectors.astype(BF16)
 
 
-def third_cut_kernel(place_ref, *refs):
-    third_sum_kernel(*refs[:-1])
-    total_ref, sent_ref = refs[-2:]
-    filled = refs[0].shape[0] + VECTOR_ROWS
+def third_cut_kernel(place_ref, left_x_ref, came_x_ref, left_y_ref, came_y_ref, vectors_ref, *refs):
+    more_ref, total_ref, sent_ref = refs
+    third_sum_kernel(left_x_ref, came_x_ref, left_y_ref, came_y_ref, vectors_ref, total_ref)
+    filled = left_x_ref.shape[0] + VECTOR_ROWS
     if filled < total_ref.shape[0]:
         total_ref[filled:] = jnp.zeros((total_ref.shape[0] - filled, total_ref.shape[1]), BF16)
-    half = sent_ref.shape[0]
+    half = total_ref.shape[0] // 2
+    rows = more_ref.shape[2]
     away = pl.multiple_of((1 - (place_ref[1] & 1)) * half, half)
-    sent_ref[...] = total_ref[pl.ds(away, half)]
-
-
-def near_sum_kernel(place_ref, total_ref, came_ref, out_ref):
-    half = came_ref.shape[0]
+    sent_ref[:half] = total_ref[pl.ds(away, half)]
+    for i in range(2):
+        sent_ref[half + i * rows : half + (i + 1) * rows] = more_ref[i, 0]
+
+
+def near_sum_kernel(place_ref, total_ref, came_ref, second_ref, out_ref):
+    half = total_ref.shape[0] // 2
+    rows = second_ref.shape[1]
     mine = total_ref[pl.ds(pl.multiple_of((place_ref[1] & 1) * half, half), half)]
-    out_ref[...] = (mine.astype(F32) + came_ref[...].astype(F32)).astype(BF16)
+    out_ref[:half] = (mine.astype(F32) + came_ref[:half].astype(F32)).astype(BF16)
+    second = second_ref[0].astype(F32) + came_ref[half + rows : half + 2 * rows].astype(F32)
+    out_ref[half : half + rows] = second.astype(BF16)
+
+
+def far_sum_kernel(left_ref, right_ref, out_ref):
+    at = slice(0, out_ref.shape[0])
+    out_ref[...] = (left_ref[at].astype(F32) + right_ref[at].astype(F32)).astype(BF16)
 
 
 def add_kernel(left_ref, right_ref, out_ref):
@@ -897,11 +907,14 @@
     out_ref[pl.ds(pl.multiple_of((1 - place) * part, part), part)] = other_ref[...]
 
 
-def finish_dense_kernel(
-    ratio, place_ref, mine_ref, other_ref, outer_ref, inner_ref, out_ref, *refs
-):
-    vector_refs, wide_ref, total_scratch, row_scratch = refs[:4], refs[4], refs[5], refs[6]
+def finish_kernel(ratio, place_ref, low_ref, came_ref, mine_ref, other_ref, *refs):
+    query_ref, key_ref, value_ref, outer_ref, inner_ref, out_ref = refs[:6]
+    tail_refs, dense_refs, wide_ref, total_scratch, row_scratch = refs[6:10], refs[10:14], *refs[14:]
     rows, width = out_ref.shape
+    total = lambda at: low_ref[at].astype(F32) + came_ref[at].astype(F32)
+    for s, ref in enumerate((query_ref, key_ref, value_ref)):
+        ref[...] = total(slice(s * rows, (s + 1) * rows))
+    put_slices(total(slice(3 * rows, 3 * rows + VECTOR_ROWS)), place_ref[0], tail_refs)
     join_rows(place_ref[1] & 1, mine_ref, other_ref, total_scratch)
     outer_ref[...] = total_scratch[: ratio * rows].astype(F32)
     for s in range(ratio):
@@ -910,11 +923,11 @@
     at = 2 * ratio * rows
     out_ref[...] = total_scratch[at : at + rows].astype(F32)
     vectors = total_scratch[at + rows : at + rows + VECTOR_ROWS].astype(F32)
-    put_slices(vectors, place_ref[0], vector_refs)
+    put_slices(vectors, place_ref[0], dense_refs)
     row_scratch[...] = vectors
     size = wide_ref.shape[0]
     start = place_ref[0] * size
-    row = row_scratch[pl.ds(len(vector_refs) + start // width, 1)]
+    row = row_scratch[pl.ds(len(dense_refs) + start // width, 1)]
     wide_ref[...] = pltpu.roll(row, lax.rem(width - lax.rem(start, width), width), 1)[0, :size]
 
 
@@ -925,22 +938,15 @@
         ref[...] = turned[i, :size]
 
 
-def finish_tail_kernel(place_ref, low_ref, came_ref, query_ref, key_ref, value_ref, *vector_refs):
-    rows = query_ref.shape[0]
-    total = lambda at: low_ref[at].astype(F32) + came_ref[at].astype(F32)
-    for s, ref in enumerate((query_ref, key_ref, value_ref)):
-        ref[...] = total(slice(s * rows, (s + 1) * rows))
-    put_slices(total(slice(3 * rows, 3 * rows + VECTOR_ROWS)), place_ref[0], vector_refs)
-
-
-def small_call(kernel, place, operands, out_shapes, name, after=(), inside=True, scratch=(), mib=4):
+def small_call(kernel, place, operands, out_shapes, name, after=(), inside=True, scratch=(), mib=4, size=None):
     ahead = 0 if place is None else 1
     count = len(operands)
 
     def body(*refs):
         kernel(*refs[: ahead + count], *refs[ahead + count + len(after) :])
 
-    size = sum(math.prod(a.shape) * a.dtype.itemsize for a in list(operands) + list(out_shapes))
+    if size is None:
+        size = sum(math.prod(a.shape) * a.dtype.itemsize for a in list(operands) + list(out_shapes))
     return pl.pallas_call(
         body,
         grid_spec=pltpu.PrefetchScalarGridSpec(
@@ -1001,14 +1007,17 @@
     return small_call(third_sum_kernel, None, pieces, [shape], name + "_sum_second", after)[0]
 
 
-def sum_second_cut(place, pieces, name, after=()):
+def sum_second_cut(place, pieces, more, name, after=()):
     size, half = pieces[0].shape
     rows = -(-(size + VECTOR_ROWS) // 32) * 32
     total, sent = small_call(
         third_cut_kernel,
         place,
-        pieces,
-        [shape_of((rows, 2 * half), BF16), shape_of((rows // 2, 2 * half), BF16)],
+        list(pieces) + [more],
+        [
+            shape_of((rows, 2 * half), BF16),
+            shape_of((rows // 2 + 2 * more.shape[2], 2 * half), BF16),
+        ],
         name + "_sum_second",
         after,
     )
@@ -1052,27 +1061,31 @@
     )[0]
 
 
-def final_kernel(counts, *refs):
-    owns, nears, crosses = [refs[sum(counts[:i]) : sum(counts[: i + 1])] for i in range(3)]
-    atoms_ref, gain_ref, shift_ref, grad_middle_ref, out_ref = refs[sum(counts) :]
+def final_kernel(count, *refs):
+    owns, nears, crosses = refs[:count], refs[count : 2 * count], refs[2 * count : 3 * count]
+    atoms_ref, gain_ref, shift_ref, grad_middle_ref, out_ref = refs[3 * count :]
     gain = as_row(gain_ref)
     shift = as_row(shift_ref)
-    nears = [(ref, i) for ref in nears for i in range(ref.shape[1])]
-    crosses = [(ref, i) for ref in crosses for i in range(ref.shape[0])]
-    for m, own_ref in enumerate(owns):
-        near_ref, i = nears[m]
-        cross_ref, at = crosses[m]
-        grad = own_ref[0] + near_ref[0, i].astype(F32) + cross_ref[at].astype(F32)
+    for m in range(count):
+        grad = owns[m][0] + nears[m][...].astype(F32) + crosses[m][...].astype(F32)
         _, normed, inverse = norm_forward(atoms_ref[m].astype(F32), gain, shift)
         result = grad_middle_ref[m] + norm_backward(grad, normed, inverse, gain)
         out_ref[m] = result.astype(BF16)
 
 
 def first_norm_backward(owns, nears, crosses, others, after=()):
+    count = len(owns)
+    arrays = [a for a, _ in nears + crosses]
+    spots = [at for _, at in nears + crosses]
+
+    def kernel(*refs):
+        picked = [r.at[at] for r, at in zip(refs[count : 3 * count], spots)]
+        final_kernel(count, *refs[:count], *picked, *refs[3 * count :])
+
     return small_call(
-        functools.partial(final_kernel, (len(owns), len(nears), len(crosses))),
+        kernel,
         None,
-        owns + nears + crosses + list(others),
+        list(owns) + arrays + list(others),
         [shape_of(others[0].shape, BF16)],
         "first_norm_backward",
         after,
@@ -1161,10 +1174,40 @@
     pair_out = jnp.zeros((1,), BF16)
     one = swap(atoms, "rows", 1)
     mine = [atoms[:count]]
-    pair_near, query_near, key_near, value_near, later = load(
-        [pair_bias, query_weight, key_weight, value_weight, atoms_far],
+    (
+        pair_near,
+        query_near,
+        key_near,
+        value_near,
+        later,
+        first_gain,
+        first_shift,
+        query_bias,
+        value_bias,
+        out_bias,
+        second_gain,
+        second_shift,
+        inner_bias,
+        outer_bias,
+    ) = load(
+        [
+            pair_bias,
+            query_weight,
+            key_weight,
+            value_weight,
+            atoms_far,
+            first_gain,
+            first_shift,
+            query_bias,
+            value_bias,
+            out_bias,
+            second_gain,
+            second_shift,
+            inner_bias,
+            outer_bias,
+        ],
         "load_first",
-        (0, 0, 0, 0, count),
+        (0, 0, 0, 0, count) + (0,) * 9,
         (place,),
     )
     mine.append(later)
@@ -1276,12 +1319,12 @@
     cross0 = cross_sum([cross0, cross1], [near1], "cross_first", after)
     far0 = swap(cross0, "rows", 2)
     pair_grad, near3, cross3, own3, tail_vectors, *grads3 = backward(3, pair_grad, sums, [cross0])
-    near3 = swap(near3, "rows", 1)
-    after = [own3]
+    owns = [own0, own1, own2, own3]
+    after = [far0, near2]
     if usual:
-        dense_total, came = sum_second_cut(place, dense_pieces, "dense", after)
-        after = [dense_total]
-    cross2 = cross_sum([cross2], [near2], "cross_second", after)
+        dense_total, came = sum_second_cut(place, dense_pieces, near3, "dense", (own3,))
+        after.append(dense_total)
+    cross2 = cross_sum([cross2], [near2], "cross_second", after[-1:])
     far2 = swap(cross2, "rows", 2)
     after = [far0, cross2]
     part = shape_of((pairs, 1, own_rows, model_width), BF16)
@@ -1303,59 +1346,60 @@
     if usual:
         pieces, _ = sum_core(place, groups, tail_vectors, "tail")
         pieces, held = sum_first(place, pieces, "tail")
-        part = shape_of(came.shape, BF16)
+        start = dense_total.shape[0] // 2
+        first_rows = slice(start, start + rows)
         mine = small_call(
-            near_sum_kernel, place, [dense_total, came], [part], "dense_near_sum", (held, far2)
+            near_sum_kernel,
+            place,
+            [dense_total, came, cross3],
+            [shape_of((start + rows, model_width), BF16)],
+            "dense_near_sum",
+            (held, far2),
         )[0]
-        came = swap(mine, "rows", 2)
-        cross3 = cross_sum([cross3], [near3], "cross_third", (mine,))
-        far3 = swap(cross3, "rows", 2)
-        total = sum_second(pieces, "tail", (cross3,))
+        far = swap(mine, "rows", 2)
+        total = sum_second(pieces, "tail", (mine,))
         tail_came = swap(total, "rows", 1)
-        mine = small_call(add_kernel, None, [mine, came], [part], "dense_far_sum", (total,))[0]
-        came = swap(mine, "rows", 1)
-        total = small_call(
-            add_kernel, None, [total, tail_came], [total], "tail_near_sum", (mine, far3)
-        )[0]
+        total = small_call(add_kernel, None, [total, tail_came], [total], "tail_near_sum")[0]
         tail_came = swap(total, "rows", 2)
+        part = shape_of((start, model_width), BF16)
+        mine = small_call(far_sum_kernel, None, [mine, far], [part], "dense_far_sum", (total,))[0]
+        other = swap(mine, "rows", 1)
         atoms_grad = first_norm_backward(
-            [own0, own1, own2, own3], [near1, near2, near3], [far0, far2, far3], finish, (total,)
+            owns,
+            [(near1, (0, 0)), (near1, (0, 1)), (near2, (0, 0)), (came, first_rows)],
+            [(far0, 0), (far0, 1), (far2, 0), (far, first_rows)],
+            finish,
+            (mine,),
         )
-        outer_grad, inner_grad, out_grad, *dense_parts = small_call(
-            functools.partial(finish_dense_kernel, ratio),
+        outs = small_call(
+            functools.partial(finish_kernel, ratio),
             place,
-            [mine, came],
-            [
+            [total, tail_came, mine, other],
+            [matrix] * 3
+            + [
                 shape_of((ratio * own_rows, model_width), F32),
                 shape_of((own_rows, ratio * model_width), F32),
                 matrix,
-                vector,
-                vector,
-                vector,
-                vector,
-                shape_of((ratio * own_rows,), F32),
-            ],
-            "finish_dense",
-            (atoms_grad,),
+            ]
+            + [vector] * 8
+            + [shape_of((ratio * own_rows,), F32)],
+            "finish",
             inside=False,
             scratch=[
                 pltpu.VMEM((2 * part.shape[0], model_width), BF16),
                 pltpu.VMEM((VECTOR_ROWS, model_width), F32),
             ],
         )
-        query_grad, key_grad, value_grad, *tail_parts = small_call(
-            finish_tail_kernel,
-            place,
-            [total, tail_came],
-            [matrix, matrix, matrix, vector, vector, vector, vector],
-            "finish_tail",
-            (out_grad,),
-            inside=False,
-        )
+        query_grad, key_grad, value_grad, outer_grad, inner_grad, out_grad = outs[:6]
+        tail_parts, dense_parts = outs[6:10], outs[10:]
     else:
+        near3 = swap(near3, "rows", 1)
         far3 = swap(cross_sum([cross3], [near3], "cross_third"), "rows", 2)
         atoms_grad = first_norm_backward(
-            [own0, own1, own2, own3], [near1, near2, near3], [far0, far2, far3], finish
+            owns,
+            [(near1, (0, 0)), (near1, (0, 1)), (near2, (0, 0)), (near3, (0, 0))],
+            [(far0, 0), (far0, 1), (far2, 0), (far3, 0)],
+            finish,
         )
         total, tail_vectors = batch_slices_any(groups, tail_vectors)
         query_grad, key_grad, value_grad = total[0], total[1], total[2]

time: 143 us -> 139 us (0.972)
  waiting for transfers between devices: 37.2 us -> 45.8 us
  starting transfers between devices: 35.7 us -> 28.1 us
  Pallas kernels: 66.4 us -> 62.5 us
  local copies, waits for them, and re-layouts: 2.9 us -> 1.04 us
    ppermute x32 -> x30, waiting for transfers between devices: 37.2 us -> 45.8 us  [swap(): return lax.ppermute(value, axis, [(i, i ^ mask) for i in range(size)])]
    ppermute x32 -> x30, starting transfers between devices: 35.7 us -> 28.1 us  [swap(): return lax.ppermute(value, axis, [(i, i ^ mask) for i in range(size)])]
    unnamed x8 -> x4, local copies, waits for them, and re-layouts: 1.87 us -> 0.01 us
    pallas_call x16 -> x14, Pallas kernels: 11.6 us -> 9.81 us  [small_call(): pl.pallas_call(body, grid_spec=pltpu.PrefetchScalarGridSpec(num_scalar_pr...]
    pallas_call x2, Pallas kernels: 16.7 us -> 15.2 us  [attention_forward(): pl.pallas_call(functools.partial(forward_kernel, head_size, 8, first, len...]
  transfers between devices with their start and end apart: 32 -> 30, of which waited for: 11 -> 13; matrix products, arithmetic and copies ran while one was open for 1% -> 1% of each run, Pallas kernels for 31% -> 30%
where the time goes in v5:
time: 139 us
  Pallas kernels  62.5 us (45%)
  waiting for transfers between devices  45.8 us (33%)
  starting transfers between devices  28.1 us (20%)
    ppermute x30, waiting for transfers between devices, swap(): return lax.ppermute(value, axis, [(i, i ^ mask) for i in range(size)])  45.8 us
    ppermute x30, starting transfers between devices, swap(): return lax.ppermute(value, axis, [(i, i ^ mask) for i in range(size)])  28.1 us
    pallas_call x4, Pallas kernels, attention_backward(): pl.pallas_call(functools.partial(backward_kernel, head_size, 4, first, ba...  23.1 us
    pallas_call x2, Pallas kernels, attention_forward(): pl.pallas_call(functools.partial(forward_kernel, head_size, 8, first, len...  15.2 us
    pallas_call x14, Pallas kernels, small_call(): pl.pallas_call(body, grid_spec=pltpu.PrefetchScalarGridSpec(num_scalar_pr...  9.81 us
    pallas_call x1, Pallas kernels, dense(): pl.pallas_call(functools.partial(dense_kernel, len(mixed)), grid_spec=plt...  7.78 us
    pallas_call x1, Pallas kernels, load(): pl.pallas_call(functools.partial(load_kernel, count, starts), in_specs=[p...  3.88 us
  transfers between devices with their start and end apart: 30, of which 13 were waited for; matrix products, arithmetic and copies ran while one was open for 1% of the time, Pallas kernels for 30%

profile of v5, /device:TPU:0, one launch (start us, length us, event | category | flops | bytes accessed | tf_op | source)
XLA Modules:
  0.0 138.5 jit_solution(945276410031368805)
XLA Ops:
  0.7 3.1 %collective-permute-start.2 = (bf16[4,64,512]{2,1,0:T(8,128)(2,1)}, bf16[4,64,512]{2,1,0:T(8,128)(2,1)S(1)}, u32[]{:S(2)}, u32[]{:S(2)}) collective-permute-start(bf16[4,64,512]{2,1,0:T(8,128)(2,1)} %refs_12_.5), channel_id=1, source_target_pairs={{0,1},{1,0},{2,3},{3,2},{4,5},{5,4},{6,7},{7,6},{8,9},{9,8},{10,11... | collective-permute-start | bytes 786440 | tf_op jit(solution)/shard_map/ppermute | solution.py:787
  4.7 2.5 %collective-permute-start.1 = (bf16[2,64,512]{2,1,0:T(8,128)(2,1)S(1)}, bf16[2,64,512]{2,1,0:T(8,128)(2,1)S(1)}, u32[]{:S(2)}, u32[]{:S(2)}) collective-permute-start(bf16[2,64,512]{2,1,0:T(8,128)(2,1)S(1)} %slice.3), channel_id=1, source_target_pairs={{0,3},{1,2},{2,1},{3,0},{4,7},{5,6},{6,5},{7,4},{8,11},{9,10},{10,... | collective-permute-start | bytes 393224 | tf_op jit(solution)/shard_map/ppermute | solution.py:787
  7.5 3.9 %load_first.1 = (bf16[4,64,64,256]{3,2,1,0:T(8,128)(2,1)S(1)}, bf16[512,512]{1,0:T(8,128)(2,1)S(1)}, bf16[512,512]{1,0:T(8,128)(2,1)S(1)}, bf16[512,512]{1,0:T(8...) custom-call(bf16[4,64,64,256]{3,2,1,0:T(8,128)(2,1)} %refs_0_.1, ...), custom_call_target="tpu_custom_call" | custom-call | tf_op jit(solution)/shard_map/load_first/pallas_call | solution.py:98
  11.4 2.9 %collective-permute-start.4 = (bf16[2,64,512]{2,1,0:T(8,128)(2,1)S(1)}, bf16[2,64,512]{2,1,0:T(8,128)(2,1)S(1)}, u32[]{:S(2)}, u32[]{:S(2)}) collective-permute-start(bf16[2,64,512]{2,1,0:T(8,128)(2,1)S(1)} %get-tuple-element.163), channel_id=1, source_target_pairs={{0,3},{1,2},{2,1},{3,0},{4,7},{5,6},{6,5},{7,4},{8,11},{9,10},{10,... | collective-permute-start | bytes 393224 | tf_op jit(solution)/shard_map/ppermute | solution.py:787
  14.7 2.7 %near_half.1 = (bf16[2,256,512]{2,1,0:T(8,128)(2,1)S(1)}, bf16[2,256,512]{2,1,0:T(8,128)(2,1)S(1)}, bf16[2,4,256,128]{3,2,1,0:T(8,128)(2,1)S(1)}, bf16[2,4,256,2...) custom-call(s32[5]{0:T(128)S(1)} %stack.23.refs_14_.place_ref.refs_0, ...), custom_call_target="tpu_custom_call" | custom-call | tf_op jit(solution)/shard_map/near_half/pallas_call | solution.py:197
  17.4 8.0 %collective-permute-done.two_ref = bf16[2,64,512]{2,1,0:T(8,128)(2,1)S(1)} collective-permute-done((bf16[2,64,512]{2,1,0:T(8,128)(2,1)S(1)}, bf16[2,64,512]{2,1,0:T(8,128)(2,1)S(1)}, u32[]{:S(2)}, u32[]{:S(2)}) %collective-permute-start) | collective-permute-done | bytes 131104 | tf_op jit(solution)/shard_map/ppermute | solution.py:787
  25.4 7.3 %attention_forward.2 = (bf16[4,64,64,256]{3,2,1,0:T(8,128)(2,1)}, bf16[2,64,64,256]{3,2,1,0:T(8,128)(2,1)S(1)}, f32[2,4,64,128]{3,2,1,0:T(8,128)S(1)}, f32[2,4,6...) custom-call(s32[5]{0:T(128)S(1)} %stack.23.refs_14_.place_ref.refs_0, ...), custom_call_target="tpu_custom_call", output_to_operand_aliasing={{4}: (11, {}), {5}: (12, {}), {6}: (13, {}), {7}: (14, {})} | custom-call | flops 1610612736 | bytes 12582912 | tf_op jit(solution)/shard_map/attention_forward/pallas_call | solution.py:319
  32.7 7.9 %attention_forward.3 = (bf16[4,64,64,256]{3,2,1,0:T(8,128)(2,1)}, bf16[2,64,64,256]{3,2,1,0:T(8,128)(2,1)S(1)}, f32[2,4,64,128]{3,2,1,0:T(8,128)S(1)}, f32[2,4,6...) custom-call(s32[5]{0:T(128)S(1)} %stack.23.refs_14_.place_ref.refs_0, ...), custom_call_target="tpu_custom_call", output_to_operand_aliasing={{4}: (11, {}), {5}: (12, {}), {6}: (13, {}), {7}: (14, {}),... | custom-call | flops 1610612736 | bytes 12582912 | tf_op jit(solution)/shard_map/attention_forward/pallas_call | solution.py:319
  40.6 7.8 %dense.1 = (bf16[4,64,512]{2,1,0:T(8,128)(2,1)}, bf16[4,256,512]{2,1,0:T(8,128)(2,1)S(1)}, bf16[4,256,512]{2,1,0:T(8,128)(2,1)S(1)}, bf16[4,4,64,512]{3,2,1,0:T(...) custom-call(s32[5]{0:T(128)S(1)} %stack.23.refs_14_.place_ref.refs_0, ...), custom_call_target="tpu_custom_call" | custom-call | flops 3221225472 | bytes 12582912 | tf_op jit(solution)/shard_map/dense/pallas_call | solution.py:538
  49.5 5.8 %attention_backward.4 = (bf16[4,64,64,256]{3,2,1,0:T(8,128)(2,1)}, bf16[2,1,64,512]{3,2,1,0:T(8,128)(2,1)S(1)}, bf16[1,64,512]{2,1,0:T(8,128)(2,1)S(1)}, f32[1,6...) custom-call(s32[5]{0:T(128)S(1)} %stack.23.refs_14_.place_ref.refs_0, ...), custom_call_target="tpu_custom_call" | custom-call | flops 1610612736 | bytes 6291456 | tf_op jit(solution)/shard_map/attention_backward/pallas_call | solution.py:736
  56.4 1.6 %collective-permute-start.11 = (bf16[1160,256]{1,0:T(8,128)(2,1)S(1)}, bf16[1160,256]{1,0:T(8,128)(2,1)S(1)}, u32[]{:S(2)}, u32[]{:S(2)}) collective-permute-start(bf16[1160,256]{1,0:T(8,128)(2,1)S(1)} %get-tuple-element.217), channel_id=1, source_target_pairs={{0,16},{4,20},{8,24},{12,28},{16,0},{20,4},{24,8},{28,12},{1,17},{... | collective-permute-start | bytes 1781768 | tf_op jit(solution)/shard_map/ppermute | solution.py:787
  58.0 1.5 %collective-permute-start.10 = (bf16[1160,256]{1,0:T(8,128)(2,1)S(1)}, bf16[1160,256]{1,0:T(8,128)(2,1)S(1)}, u32[]{:S(2)}, u32[]{:S(2)}) collective-permute-start(bf16[1160,256]{1,0:T(8,128)(2,1)S(1)} %get-tuple-element.199.refs_2_), channel_id=1, source_target_pairs={{0,8},{4,12},{8,0},{12,4},{16,24},{20,28},{24,16},{28,20},{1,9},{5... | collective-permute-start | bytes 1781768 | tf_op jit(solution)/shard_map/ppermute | solution.py:787
  59.5 5.8 %attention_backward.5 = (bf16[4,64,64,256]{3,2,1,0:T(8,128)(2,1)}, bf16[2,2,64,512]{3,2,1,0:T(8,128)(2,1)S(1)}, bf16[1,64,512]{2,1,0:T(8,128)(2,1)S(1)}, f32[1,6...) custom-call(s32[5]{0:T(128)S(1)} %stack.23.refs_14_.place_ref.refs_0, ...), custom_call_target="tpu_custom_call", output_to_operand_aliasing={{0}: (13, {}), {4}: (14, {})} | custom-call | flops 1610612736 | bytes 6291456 | tf_op jit(solution)/shard_map/attention_backward/pallas_call | solution.py:736
  65.8 5.8 %attention_backward.6 = (bf16[4,64,64,256]{3,2,1,0:T(8,128)(2,1)}, bf16[2,1,64,512]{3,2,1,0:T(8,128)(2,1)S(1)}, bf16[1,64,512]{2,1,0:T(8,128)(2,1)S(1)}, f32[1,6...) custom-call(s32[5]{0:T(128)S(1)} %stack.23.refs_14_.place_ref.refs_0, ...), custom_call_target="tpu_custom_call", output_to_operand_aliasing={{0}: (13, {}), {4}: (14, {})} | custom-call | flops 1610612736 | bytes 6291456 | tf_op jit(solution)/shard_map/attention_backward/pallas_call | solution.py:736
  71.8 1.2 collective-permute-done.10.refs_2_
  73.9 1.6 %collective-permute-start.14 = (bf16[584,256]{1,0:T(8,128)(2,1)S(1)}, bf16[584,256]{1,0:T(8,128)(2,1)S(1)}, u32[]{:S(2)}, u32[]{:S(2)}) collective-permute-start(bf16[584,256]{1,0:T(8,128)(2,1)S(1)} %get-tuple-element.224), channel_id=1, source_target_pairs={{0,8},{4,12},{8,0},{12,4},{16,24},{20,28},{24,16},{28,20},{1,9},{5... | collective-permute-start | bytes 897032 | tf_op jit(solution)/shard_map/ppermute | solution.py:787
  76.5 3.4 %collective-permute-start.16 = (bf16[2,64,512]{2,1,0:T(8,128)(2,1)S(1)}, bf16[2,64,512]{2,1,0:T(8,128)(2,1)S(1)}, u32[]{:S(2)}, u32[]{:S(2)}) collective-permute-start(bf16[2,64,512]{2,1,0:T(8,128)(2,1)S(1)} %cross_first.1.refs_2_), channel_id=1, source_target_pairs={{0,2},{1,3},{2,0},{3,1},{4,6},{5,7},{6,4},{7,5},{8,10},{9,11},{10,... | collective-permute-start | bytes 393224 | tf_op jit(solution)/shard_map/ppermute | solution.py:787
  80.0 5.8 %attention_backward.7 = (bf16[4,64,64,256]{3,2,1,0:T(8,128)(2,1)}, bf16[2,1,64,512]{3,2,1,0:T(8,128)(2,1)S(1)}, bf16[1,64,512]{2,1,0:T(8,128)(2,1)S(1)}, f32[1,6...) custom-call(s32[5]{0:T(128)S(1)} %stack.23.refs_14_.place_ref.refs_0, ...), custom_call_target="tpu_custom_call", output_to_operand_aliasing={{0}: (13, {}), {4}: (14, {})} | custom-call | flops 1610612736 | bytes 6291456 | tf_op jit(solution)/shard_map/attention_backward/pallas_call | solution.py:736
  86.6 2.1 %attention_weights.1 = (bf16[4,1,64,512]{3,2,1,0:T(8,128)(2,1)S(1)}, bf16[4,1,64,512]{3,2,1,0:T(8,128)(2,1)S(1)}, bf16[4,1,64,512]{3,2,1,0:T(8,128)(2,1)S(1)}, b...) custom-call(s32[5]{0:T(128)S(1)} %stack.23.refs_14_.place_ref.refs_0_, ...), custom_call_target="tpu_custom_call" | custom-call | bytes 4980736 | tf_op jit(solution)/shard_map/attention_weights/pallas_call | solution.py:950
  89.8 1.3 collective-permute-done.21.refs_8_
  92.4 1.5 %collective-permute-start.23 = (bf16[392,256]{1,0:T(8,128)(2,1)S(1)}, bf16[392,256]{1,0:T(8,128)(2,1)S(1)}, u32[]{:S(2)}, u32[]{:S(2)}) collective-permute-start(bf16[392,256]{1,0:T(8,128)(2,1)S(1)} %get-tuple-element.255), channel_id=1, source_target_pairs={{0,16},{4,20},{8,24},{12,28},{16,0},{20,4},{24,8},{28,12},{1,17},{... | collective-permute-start | bytes 602120 | tf_op jit(solution)/shard_map/ppermute | solution.py:787
  94.7 4.2 %collective-permute-done.22.refs_2_ = bf16[392,256]{1,0:T(8,128)(2,1)S(1)} collective-permute-done((bf16[392,256]{1,0:T(8,128)(2,1)S(1)}, bf16[392,256]{1,0:T(8,128)(2,1)S(1)}, u32[]{:S(2)}, u32[]{:S(2)}) %collective-permute-start.22) | collective-permute-done | bytes 200736 | tf_op jit(solution)/shard_map/ppermute | solution.py:787
  99.8 1.3 collective-permute-done.17.refs_5_.refs_10_
  101.0 2.2 %collective-permute-done.15.refs_2_.refs_7_ = bf16[432,512]{1,0:T(8,128)(2,1)S(1)} collective-permute-done((bf16[432,512]{1,0:T(8,128)(2,1)S(1)}, bf16[432,512]{1,0:T(8,128)(2,1)S(1)}, u32[]{:S(2)}, u32[]{:S(2)}) %collective-permute-start.15) | collective-permute-done | bytes 442400 | tf_op jit(solution)/shard_map/ppermute | solution.py:787
  103.9 1.2 collective-permute-start.24
  105.7 1.5 %collective-permute-start.25 = (bf16[200,256]{1,0:T(8,128)(2,1)S(1)}, bf16[200,256]{1,0:T(8,128)(2,1)S(1)}, u32[]{:S(2)}, u32[]{:S(2)}) collective-permute-start(bf16[200,256]{1,0:T(8,128)(2,1)S(1)} %get-tuple-element.257.refs_4_), channel_id=1, source_target_pairs={{0,16},{4,20},{8,24},{12,28},{16,0},{20,4},{24,8},{28,12},{1,17},{... | collective-permute-start | bytes 307208 | tf_op jit(solution)/shard_map/ppermute | solution.py:787
  107.2 2.6 %collective-permute-done.26.refs_3_ = bf16[200,256]{1,0:T(8,128)(2,1)S(1)} collective-permute-done((bf16[200,256]{1,0:T(8,128)(2,1)S(1)}, bf16[200,256]{1,0:T(8,128)(2,1)S(1)}, u32[]{:S(2)}, u32[]{:S(2)}) %collective-permute-start.26) | collective-permute-done | bytes 102432 | tf_op jit(solution)/shard_map/ppermute | solution.py:787
  110.7 13.2 %collective-permute-done.27.refs_1_ = bf16[200,512]{1,0:T(8,128)(2,1)S(1)} collective-permute-done((bf16[200,512]{1,0:T(8,128)(2,1)S(1)}, bf16[200,512]{1,0:T(8,128)(2,1)S(1)}, u32[]{:S(2)}, u32[]{:S(2)}) %collective-permute-start.27) | collective-permute-done | bytes 204832 | tf_op jit(solution)/shard_map/ppermute | solution.py:787
  124.8 1.1 first_norm_backward.1
  125.9 8.5 %collective-permute-done.28.refs_2_ = bf16[200,512]{1,0:T(8,128)(2,1)S(1)} collective-permute-done((bf16[200,512]{1,0:T(8,128)(2,1)S(1)}, bf16[200,512]{1,0:T(8,128)(2,1)S(1)}, u32[]{:S(2)}, u32[]{:S(2)}) %collective-permute-start.28) | collective-permute-done | bytes 204832 | tf_op jit(solution)/shard_map/ppermute | solution.py:787
  134.4 2.2 %collective-permute-done.29.refs_4_ = bf16[304,512]{1,0:T(8,128)(2,1)S(1)} collective-permute-done((bf16[304,512]{1,0:T(8,128)(2,1)S(1)}, bf16[304,512]{1,0:T(8,128)(2,1)S(1)}, u32[]{:S(2)}, u32[]{:S(2)}) %collective-permute-start.29) | collective-permute-done | bytes 311328 | tf_op jit(solution)/shard_map/ppermute | solution.py:787
  136.6 1.8 %finish.1 = (f32[64,512]{1,0:T(8,128)}, f32[64,512]{1,0:T(8,128)}, f32[64,512]{1,0:T(8,128)}, f32[256,512]{1,0:T(8,128)}, f32[64,2048]{1,0:T(8,128)}, /*index=5*...) custom-call(s32[5]{0:T(128)S(1)} %stack.23.refs_14_.place_ref.refs_0, ...), custom_call_target="tpu_custom_call" | custom-call | bytes 2608128 | tf_op jit(solution)/shard_map/finish/pallas_call | solution.py:950
  (57 shorter events, 14.2 us)
Async XLA Ops:
  0.7 24.7 %copy-start.1 = (s32[4]{0:T(128)S(1)}, s32[4]{0:T(128)}, u32[]{:S(2)}) copy-start(s32[4]{0:T(128)} %length_ref.3) | copy-start | bytes 52
  0.7 14.0 %collective-permute-start.2 = (bf16[4,64,512]{2,1,0:T(8,128)(2,1)}, bf16[4,64,512]{2,1,0:T(8,128)(2,1)S(1)}, u32[]{:S(2)}, u32[]{:S(2)}) collective-permute-start(bf16[4,64,512]{2,1,0:T(8,128)(2,1)} %refs_12_.5), channel_id=1, source_target_pairs={{0,1},{1,0},{2,3},{3,2},{4,5},{5,4},{6,7},{7,6},{8,9},{9,8},{10,11... | collective-permute-start | bytes 786440 | tf_op jit(solution)/shard_map/ppermute | solution.py:787
  4.7 12.7 %collective-permute-start.1 = (bf16[2,64,512]{2,1,0:T(8,128)(2,1)S(1)}, bf16[2,64,512]{2,1,0:T(8,128)(2,1)S(1)}, u32[]{:S(2)}, u32[]{:S(2)}) collective-permute-start(bf16[2,64,512]{2,1,0:T(8,128)(2,1)S(1)} %slice.3), channel_id=1, source_target_pairs={{0,3},{1,2},{2,1},{3,0},{4,7},{5,6},{6,5},{7,4},{8,11},{9,10},{10,... | collective-permute-start | bytes 393224 | tf_op jit(solution)/shard_map/ppermute | solution.py:787
  7.2 18.1 %collective-permute-start = (bf16[2,64,512]{2,1,0:T(8,128)(2,1)S(1)}, bf16[2,64,512]{2,1,0:T(8,128)(2,1)S(1)}, u32[]{:S(2)}, u32[]{:S(2)}) collective-permute-start(bf16[2,64,512]{2,1,0:T(8,128)(2,1)S(1)} %slice.3), channel_id=1, source_target_pairs={{0,2},{1,3},{2,0},{3,1},{4,6},{5,7},{6,4},{7,5},{8,10},{9,11},{10,... | collective-permute-start | bytes 393224 | tf_op jit(solution)/shard_map/ppermute | solution.py:787
  11.4 21.3 %collective-permute-start.4 = (bf16[2,64,512]{2,1,0:T(8,128)(2,1)S(1)}, bf16[2,64,512]{2,1,0:T(8,128)(2,1)S(1)}, u32[]{:S(2)}, u32[]{:S(2)}) collective-permute-start(bf16[2,64,512]{2,1,0:T(8,128)(2,1)S(1)} %get-tuple-element.163), channel_id=1, source_target_pairs={{0,3},{1,2},{2,1},{3,0},{4,7},{5,6},{6,5},{7,4},{8,11},{9,10},{10,... | collective-permute-start | bytes 393224 | tf_op jit(solution)/shard_map/ppermute | solution.py:787
  14.3 18.4 %collective-permute-start.3 = (bf16[2,64,512]{2,1,0:T(8,128)(2,1)S(1)}, bf16[2,64,512]{2,1,0:T(8,128)(2,1)S(1)}, u32[]{:S(2)}, u32[]{:S(2)}) collective-permute-start(bf16[2,64,512]{2,1,0:T(8,128)(2,1)S(1)} %get-tuple-element.163), channel_id=1, source_target_pairs={{0,2},{1,3},{2,0},{3,1},{4,6},{5,7},{6,4},{7,5},{8,10},{9,11},{10,... | collective-permute-start | bytes 393224 | tf_op jit(solution)/shard_map/ppermute | solution.py:787
  32.7 7.9 %copy-start = (bf16[4,64,512]{2,1,0:T(8,128)(2,1)S(1)}, bf16[4,64,512]{2,1,0:T(8,128)(2,1)}, u32[]{:S(2)}) copy-start(bf16[4,64,512]{2,1,0:T(8,128)(2,1)} %refs_12_.5) | copy-start | bytes 786436
  48.4 6.9 %collective-permute-start.5 = (bf16[4,4,64,512]{3,2,1,0:T(8,128)(2,1)S(1)}, bf16[4,4,64,512]{3,2,1,0:T(8,128)(2,1)S(1)}, u32[]{:S(2)}, u32[]{:S(2)}) collective-permute-start(bf16[4,4,64,512]{3,2,1,0:T(8,128)(2,1)S(1)} %bitcast.11), channel_id=1, source_target_pairs={{0,4},{4,0},{8,12},{12,8},{16,20},{20,16},{24,28},{28,24},{1,5},{5... | collective-permute-start | bytes 3145736 | tf_op jit(solution)/shard_map/ppermute | solution.py:787
  48.5 6.8 %collective-permute-start.6 = (bf16[4,4,64,512]{3,2,1,0:T(8,128)(2,1)S(1)}, bf16[4,4,64,512]{3,2,1,0:T(8,128)(2,1)S(1)}, u32[]{:S(2)}, u32[]{:S(2)}) collective-permute-start(bf16[4,4,64,512]{3,2,1,0:T(8,128)(2,1)S(1)} %get-tuple-element.195), channel_id=1, source_target_pairs={{0,4},{4,0},{8,12},{12,8},{16,20},{20,16},{24,28},{28,24},{1,5},{5... | collective-permute-start | bytes 3145736 | tf_op jit(solution)/shard_map/ppermute | solution.py:787
  49.0 6.3 %collective-permute-start.7 = (bf16[4,1,64,512]{3,2,1,0:T(8,128)(2,1)S(1)}, bf16[4,1,64,512]{3,2,1,0:T(8,128)(2,1)S(1)}, u32[]{:S(2)}, u32[]{:S(2)}) collective-permute-start(bf16[4,1,64,512]{3,2,1,0:T(8,128)(2,1)S(1)} %bitcast.12), channel_id=1, source_target_pairs={{0,4},{4,0},{8,12},{12,8},{16,20},{20,16},{24,28},{28,24},{1,5},{5... | collective-permute-start | bytes 786440 | tf_op jit(solution)/shard_map/ppermute | solution.py:787
  49.1 6.2 %collective-permute-start.8 = (f32[8,512]{1,0:T(8,128)S(1)}, f32[8,512]{1,0:T(8,128)S(1)}, u32[]{:S(2)}, u32[]{:S(2)}) collective-permute-start(f32[8,512]{1,0:T(8,128)S(1)} %get-tuple-element.198.refs_7_), channel_id=1, source_target_pairs={{0,4},{4,0},{8,12},{12,8},{16,20},{20,16},{24,28},{28,24},{1,5},{5... | collective-permute-start | bytes 49160 | tf_op jit(solution)/shard_map/ppermute | solution.py:787
  56.4 15.5 %collective-permute-start.11 = (bf16[1160,256]{1,0:T(8,128)(2,1)S(1)}, bf16[1160,256]{1,0:T(8,128)(2,1)S(1)}, u32[]{:S(2)}, u32[]{:S(2)}) collective-permute-start(bf16[1160,256]{1,0:T(8,128)(2,1)S(1)} %get-tuple-element.217), channel_id=1, source_target_pairs={{0,16},{4,20},{8,24},{12,28},{16,0},{20,4},{24,8},{28,12},{1,17},{... | collective-permute-start | bytes 1781768 | tf_op jit(solution)/shard_map/ppermute | solution.py:787
  58.0 15.1 %collective-permute-start.10 = (bf16[1160,256]{1,0:T(8,128)(2,1)S(1)}, bf16[1160,256]{1,0:T(8,128)(2,1)S(1)}, u32[]{:S(2)}, u32[]{:S(2)}) collective-permute-start(bf16[1160,256]{1,0:T(8,128)(2,1)S(1)} %get-tuple-element.199.refs_2_), channel_id=1, source_target_pairs={{0,8},{4,12},{8,0},{12,4},{16,24},{20,28},{24,16},{28,20},{1,9},{5... | collective-permute-start | bytes 1781768 | tf_op jit(solution)/shard_map/ppermute | solution.py:787
  65.2 11.3 %collective-permute-start.9 = (bf16[2,2,64,512]{3,2,1,0:T(8,128)(2,1)S(1)}, bf16[2,2,64,512]{3,2,1,0:T(8,128)(2,1)S(1)}, u32[]{:S(2)}, u32[]{:S(2)}) collective-permute-start(bf16[2,2,64,512]{3,2,1,0:T(8,128)(2,1)S(1)} %get-tuple-element.214), channel_id=1, source_target_pairs={{0,1},{1,0},{2,3},{3,2},{4,5},{5,4},{6,7},{7,6},{8,9},{9,8},{10,11... | collective-permute-start | bytes 786440 | tf_op jit(solution)/shard_map/ppermute | solution.py:787
  73.9 11.8 %collective-permute-start.14 = (bf16[584,256]{1,0:T(8,128)(2,1)S(1)}, bf16[584,256]{1,0:T(8,128)(2,1)S(1)}, u32[]{:S(2)}, u32[]{:S(2)}) collective-permute-start(bf16[584,256]{1,0:T(8,128)(2,1)S(1)} %get-tuple-element.224), channel_id=1, source_target_pairs={{0,8},{4,12},{8,0},{12,4},{16,24},{20,28},{24,16},{28,20},{1,9},{5... | collective-permute-start | bytes 897032 | tf_op jit(solution)/shard_map/ppermute | solution.py:787
  75.5 10.3 %collective-permute-start.13 = (bf16[584,256]{1,0:T(8,128)(2,1)S(1)}, bf16[584,256]{1,0:T(8,128)(2,1)S(1)}, u32[]{:S(2)}, u32[]{:S(2)}) collective-permute-start(bf16[584,256]{1,0:T(8,128)(2,1)S(1)} %get-tuple-element.219.refs_3_), channel_id=1, source_target_pairs={{0,16},{4,20},{8,24},{12,28},{16,0},{20,4},{24,8},{28,12},{1,17},{... | collective-permute-start | bytes 897032 | tf_op jit(solution)/shard_map/ppermute | solution.py:787
  76.0 10.6 %collective-permute-start.12 = (bf16[2,1,64,512]{3,2,1,0:T(8,128)(2,1)S(1)}, bf16[2,1,64,512]{3,2,1,0:T(8,128)(2,1)S(1)}, u32[]{:S(2)}, u32[]{:S(2)}) collective-permute-start(bf16[2,1,64,512]{3,2,1,0:T(8,128)(2,1)S(1)} %get-tuple-element.221), channel_id=1, source_target_pairs={{0,1},{1,0},{2,3},{3,2},{4,5},{5,4},{6,7},{7,6},{8,9},{9,8},{10,11... | collective-permute-start | bytes 393224 | tf_op jit(solution)/shard_map/ppermute | solution.py:787
  76.5 10.0 %collective-permute-start.16 = (bf16[2,64,512]{2,1,0:T(8,128)(2,1)S(1)}, bf16[2,64,512]{2,1,0:T(8,128)(2,1)S(1)}, u32[]{:S(2)}, u32[]{:S(2)}) collective-permute-start(bf16[2,64,512]{2,1,0:T(8,128)(2,1)S(1)} %cross_first.1.refs_2_), channel_id=1, source_target_pairs={{0,2},{1,3},{2,0},{3,1},{4,6},{5,7},{6,4},{7,5},{8,10},{9,11},{10,... | collective-permute-start | bytes 393224 | tf_op jit(solution)/shard_map/ppermute | solution.py:787
  88.7 2.4 %collective-permute-start.18 = (bf16[4,1,64,512]{3,2,1,0:T(8,128)(2,1)S(1)}, bf16[4,1,64,512]{3,2,1,0:T(8,128)(2,1)S(1)}, u32[]{:S(2)}, u32[]{:S(2)}) collective-permute-start(bf16[4,1,64,512]{3,2,1,0:T(8,128)(2,1)S(1)} %get-tuple-element.246), channel_id=1, source_target_pairs={{0,4},{4,0},{8,12},{12,8},{16,20},{20,16},{24,28},{28,24},{1,5},{5... | collective-permute-start | bytes 786440 | tf_op jit(solution)/shard_map/ppermute | solution.py:787
  88.8 2.3 %collective-permute-start.19 = (bf16[4,1,64,512]{3,2,1,0:T(8,128)(2,1)S(1)}, bf16[4,1,64,512]{3,2,1,0:T(8,128)(2,1)S(1)}, u32[]{:S(2)}, u32[]{:S(2)}) collective-permute-start(bf16[4,1,64,512]{3,2,1,0:T(8,128)(2,1)S(1)} %get-tuple-element.248), channel_id=1, source_target_pairs={{0,4},{4,0},{8,12},{12,8},{16,20},{20,16},{24,28},{28,24},{1,5},{5... | collective-permute-start | bytes 786440 | tf_op jit(solution)/shard_map/ppermute | solution.py:787
  89.3 1.8 %collective-permute-start.20 = (bf16[4,1,64,512]{3,2,1,0:T(8,128)(2,1)S(1)}, bf16[4,1,64,512]{3,2,1,0:T(8,128)(2,1)S(1)}, u32[]{:S(2)}, u32[]{:S(2)}) collective-permute-start(bf16[4,1,64,512]{3,2,1,0:T(8,128)(2,1)S(1)} %get-tuple-element.250), channel_id=1, source_target_pairs={{0,4},{4,0},{8,12},{12,8},{16,20},{20,16},{24,28},{28,24},{1,5},{5... | collective-permute-start | bytes 786440 | tf_op jit(solution)/shard_map/ppermute | solution.py:787
  89.3 13.9 %collective-permute-start.15 = (bf16[432,512]{1,0:T(8,128)(2,1)S(1)}, bf16[432,512]{1,0:T(8,128)(2,1)S(1)}, u32[]{:S(2)}, u32[]{:S(2)}) collective-permute-start(bf16[432,512]{1,0:T(8,128)(2,1)S(1)} %get-tuple-element.227), channel_id=1, source_target_pairs={{0,1},{1,0},{2,3},{3,2},{4,5},{5,4},{6,7},{7,6},{8,9},{9,8},{10,11... | collective-permute-start | bytes 1327112 | tf_op jit(solution)/shard_map/ppermute | solution.py:787
  89.3 1.7 %collective-permute-start.21 = (f32[8,512]{1,0:T(8,128)S(1)}, f32[8,512]{1,0:T(8,128)S(1)}, u32[]{:S(2)}, u32[]{:S(2)}) collective-permute-start(f32[8,512]{1,0:T(8,128)S(1)} %get-tuple-element.251.refs_7_), channel_id=1, source_target_pairs={{0,4},{4,0},{8,12},{12,8},{16,20},{20,16},{24,28},{28,24},{1,5},{5... | collective-permute-start | bytes 49160 | tf_op jit(solution)/shard_map/ppermute | solution.py:787
  91.8 7.1 %collective-permute-start.22 = (bf16[392,256]{1,0:T(8,128)(2,1)S(1)}, bf16[392,256]{1,0:T(8,128)(2,1)S(1)}, u32[]{:S(2)}, u32[]{:S(2)}) collective-permute-start(bf16[392,256]{1,0:T(8,128)(2,1)S(1)} %get-tuple-element.253), channel_id=1, source_target_pairs={{0,8},{4,12},{8,0},{12,4},{16,24},{20,28},{24,16},{28,20},{1,9},{5... | collective-permute-start | bytes 602120 | tf_op jit(solution)/shard_map/ppermute | solution.py:787
  92.4 6.8 %collective-permute-start.23 = (bf16[392,256]{1,0:T(8,128)(2,1)S(1)}, bf16[392,256]{1,0:T(8,128)(2,1)S(1)}, u32[]{:S(2)}, u32[]{:S(2)}) collective-permute-start(bf16[392,256]{1,0:T(8,128)(2,1)S(1)} %get-tuple-element.255), channel_id=1, source_target_pairs={{0,16},{4,20},{8,24},{12,28},{16,0},{20,4},{24,8},{28,12},{1,17},{... | collective-permute-start | bytes 602120 | tf_op jit(solution)/shard_map/ppermute | solution.py:787
  93.9 7.1 %collective-permute-start.17 = (bf16[1,64,512]{2,1,0:T(8,128)(2,1)S(1)}, bf16[1,64,512]{2,1,0:T(8,128)(2,1)S(1)}, u32[]{:S(2)}, u32[]{:S(2)}) collective-permute-start(bf16[1,64,512]{2,1,0:T(8,128)(2,1)S(1)} %cross_second.1.refs_16_), channel_id=1, source_target_pairs={{0,2},{1,3},{2,0},{3,1},{4,6},{5,7},{6,4},{7,5},{8,10},{9,11},{10,... | collective-permute-start | bytes 196616 | tf_op jit(solution)/shard_map/ppermute | solution.py:787
  103.9 20.1 %collective-permute-start.24 = (bf16[368,512]{1,0:T(8,128)(2,1)S(1)}, bf16[368,512]{1,0:T(8,128)(2,1)S(1)}, u32[]{:S(2)}, u32[]{:S(2)}) collective-permute-start(bf16[368,512]{1,0:T(8,128)(2,1)S(1)} %dense_near_sum.1.refs_5_.refs_0_), channel_id=1, source_target_pairs={{0,2},{1,3},{2,0},{3,1},{4,6},{5,7},{6,4},{7,5},{8,10},{9,11},{10,... | collective-permute-start | bytes 1130504 | tf_op jit(solution)/shard_map/ppermute | solution.py:787
  105.1 4.7 %collective-permute-start.26 = (bf16[200,256]{1,0:T(8,128)(2,1)S(1)}, bf16[200,256]{1,0:T(8,128)(2,1)S(1)}, u32[]{:S(2)}, u32[]{:S(2)}) collective-permute-start(bf16[200,256]{1,0:T(8,128)(2,1)S(1)} %get-tuple-element.261), channel_id=1, source_target_pairs={{0,8},{4,12},{8,0},{12,4},{16,24},{20,28},{24,16},{28,20},{1,9},{5... | collective-permute-start | bytes 307208 | tf_op jit(solution)/shard_map/ppermute | solution.py:787
  105.7 4.7 %collective-permute-start.25 = (bf16[200,256]{1,0:T(8,128)(2,1)S(1)}, bf16[200,256]{1,0:T(8,128)(2,1)S(1)}, u32[]{:S(2)}, u32[]{:S(2)}) collective-permute-start(bf16[200,256]{1,0:T(8,128)(2,1)S(1)} %get-tuple-element.257.refs_4_), channel_id=1, source_target_pairs={{0,16},{4,20},{8,24},{12,28},{16,0},{20,4},{24,8},{28,12},{1,17},{... | collective-permute-start | bytes 307208 | tf_op jit(solution)/shard_map/ppermute | solution.py:787
  110.4 13.5 %collective-permute-start.27 = (bf16[200,512]{1,0:T(8,128)(2,1)S(1)}, bf16[200,512]{1,0:T(8,128)(2,1)S(1)}, u32[]{:S(2)}, u32[]{:S(2)}) collective-permute-start(bf16[200,512]{1,0:T(8,128)(2,1)S(1)} %tail_sum_second.1.refs_0_), channel_id=1, source_target_pairs={{0,1},{1,0},{2,3},{3,2},{4,5},{5,4},{6,7},{7,6},{8,9},{9,8},{10,11... | collective-permute-start | bytes 614408 | tf_op jit(solution)/shard_map/ppermute | solution.py:787
  124.1 12.5 %collective-permute-start.29 = (bf16[304,512]{1,0:T(8,128)(2,1)S(1)}, bf16[304,512]{1,0:T(8,128)(2,1)S(1)}, u32[]{:S(2)}, u32[]{:S(2)}) collective-permute-start(bf16[304,512]{1,0:T(8,128)(2,1)S(1)} %dense_far_sum.1.refs_16_.refs_3_), channel_id=1, source_target_pairs={{0,1},{1,0},{2,3},{3,2},{4,5},{5,4},{6,7},{7,6},{8,9},{9,8},{10,11... | collective-permute-start | bytes 933896 | tf_op jit(solution)/shard_map/ppermute | solution.py:787
  124.1 10.3 %collective-permute-start.28 = (bf16[200,512]{1,0:T(8,128)(2,1)S(1)}, bf16[200,512]{1,0:T(8,128)(2,1)S(1)}, u32[]{:S(2)}, u32[]{:S(2)}) collective-permute-start(bf16[200,512]{1,0:T(8,128)(2,1)S(1)} %tail_near_sum.1.refs_2_.refs_1_), channel_id=1, source_target_pairs={{0,2},{1,3},{2,0},{3,1},{4,6},{5,7},{6,4},{7,5},{8,10},{9,11},{10,... | collective-permute-start | bytes 614408 | tf_op jit(solution)/shard_map/ppermute | solution.py:787

commit v6 on v5

--- a/solution.py
+++ b/solution.py
@@ -169,7 +169,8 @@
     *refs,
 ):
     refs = refs[ahead:]
-    atoms_scratch = refs[-1]
+    later_ref, atoms_scratch = refs[-2:]
+    later_ref[...] = own_ref[own_ref.shape[0] - later_ref.shape[0] :]
     row = place_ref[1]
     rows, model_width = own_ref.shape[1:]
     factor = head_size**-0.5
@@ -202,7 +203,7 @@
             in_specs=[whole(atoms), near_spec()]
             + [near_spec() for a in parameters]
             + [pl.BlockSpec(memory_space=pl.ANY)] * len(after),
-            out_specs=[near_spec()] * (5 * stages),
+            out_specs=[near_spec()] * (5 * stages + 1),
             scratch_shapes=[pltpu.VMEM((count * 2 * rows, model_width), BF16)],
         ),
         out_shape=[
@@ -212,7 +213,8 @@
             near((count, groups, keys, 2 * LANES), BF16),
             near((count, groups, rows, LANES), BF16),
         ]
-        * stages,
+        * stages
+        + [near((molecules - count, rows, model_width), BF16)],
         compiler_params=params(10),
         name="near_half",
     )(*operands)
@@ -1173,13 +1175,11 @@
     stages = []
     pair_out = jnp.zeros((1,), BF16)
     one = swap(atoms, "rows", 1)
-    mine = [atoms[:count]]
     (
         pair_near,
         query_near,
         key_near,
         value_near,
-        later,
         first_gain,
         first_shift,
         query_bias,
@@ -1195,7 +1195,6 @@
             query_weight,
             key_weight,
             value_weight,
-            atoms_far,
             first_gain,
             first_shift,
             query_bias,
@@ -1207,11 +1206,9 @@
             outer_bias,
         ],
         "load_first",
-        (0, 0, 0, 0, count) + (0,) * 9,
+        None,
         (place,),
     )
-    mine.append(later)
-    gathered = [[swap(a, "rows", mask) for mask in (2, 3)] for a in mine]
     projected = near_half(
         head_size,
         STAGES,
@@ -1229,6 +1226,8 @@
         ),
         (),
     )
+    mine = [atoms[:count], projected[-1]]
+    gathered = [[swap(a, "rows", mask) for mask in (2, 3)] for a in mine]
     for stage in range(STAGES):
         pair_out, kept, loaded = attention_forward(
             head_size,

time: 139 us -> 135 us (0.971)
  waiting for transfers between devices: 45.8 us -> 33.7 us
  starting transfers between devices: 28.1 us -> 36.8 us
    ppermute x30, waiting for transfers between devices: 45.8 us -> 33.7 us  [swap(): return lax.ppermute(value, axis, [(i, i ^ mask) for i in range(size)])]
    ppermute x30, starting transfers between devices: 28.1 us -> 36.8 us  [swap(): return lax.ppermute(value, axis, [(i, i ^ mask) for i in range(size)])]
  transfers between devices with their start and end apart: 30 -> 30, of which waited for: 13 -> 15; matrix products, arithmetic and copies ran while one was open for 1% -> 1% of each run, Pallas kernels for 30% -> 31%
where the time goes in v6:
time: 135 us
  Pallas kernels  62.6 us (46%)
  starting transfers between devices  36.8 us (27%)
  waiting for transfers between devices  33.7 us (25%)
    ppermute x30, starting transfers between devices, swap(): return lax.ppermute(value, axis, [(i, i ^ mask) for i in range(size)])  36.8 us
    ppermute x30, waiting for transfers between devices, swap(): return lax.ppermute(value, axis, [(i, i ^ mask) for i in range(size)])  33.7 us
    pallas_call x4, Pallas kernels, attention_backward(): pl.pallas_call(functools.partial(backward_kernel, head_size, 4, first, ba...  23.1 us
    pallas_call x2, Pallas kernels, attention_forward(): pl.pallas_call(functools.partial(forward_kernel, head_size, 8, first, len...  15.2 us
    pallas_call x14, Pallas kernels, small_call(): pl.pallas_call(body, grid_spec=pltpu.PrefetchScalarGridSpec(num_scalar_pr...  9.85 us
    pallas_call x1, Pallas kernels, dense(): pl.pallas_call(functools.partial(dense_kernel, len(mixed)), grid_spec=plt...  7.78 us
    pallas_call x1, Pallas kernels, load(): pl.pallas_call(functools.partial(load_kernel, count, starts), in_specs=[p...  3.86 us
    pallas_call x1, Pallas kernels, near_half(): pl.pallas_call(functools.partial(near_half_kernel, head_size, stages, len...  2.78 us
  transfers between devices with their start and end apart: 30, of which 15 were waited for; matrix products, arithmetic and copies ran while one was open for 1% of the time, Pallas kernels for 31%

profile of v6, /device:TPU:0, one launch (start us, length us, event | category | flops | bytes accessed | tf_op | source)
XLA Modules:
  0.0 135.1 jit_solution(3949464345061062273)
XLA Ops:
  0.7 3.1 %collective-permute-start.2 = (bf16[4,64,512]{2,1,0:T(8,128)(2,1)}, bf16[4,64,512]{2,1,0:T(8,128)(2,1)S(1)}, u32[]{:S(2)}, u32[]{:S(2)}) collective-permute-start(bf16[4,64,512]{2,1,0:T(8,128)(2,1)} %refs_12_.5), channel_id=1, source_target_pairs={{0,1},{1,0},{2,3},{3,2},{4,5},{5,4},{6,7},{7,6},{8,9},{9,8},{10,11... | collective-permute-start | bytes 786440 | tf_op jit(solution)/shard_map/ppermute | solution.py:789
  4.7 2.5 %collective-permute-start.1 = (bf16[2,64,512]{2,1,0:T(8,128)(2,1)S(1)}, bf16[2,64,512]{2,1,0:T(8,128)(2,1)S(1)}, u32[]{:S(2)}, u32[]{:S(2)}) collective-permute-start(bf16[2,64,512]{2,1,0:T(8,128)(2,1)S(1)} %slice.3), channel_id=1, source_target_pairs={{0,3},{1,2},{2,1},{3,0},{4,7},{5,6},{6,5},{7,4},{8,11},{9,10},{10,... | collective-permute-start | bytes 393224 | tf_op jit(solution)/shard_map/ppermute | solution.py:789
  7.5 3.9 %load_first.1 = (bf16[4,64,64,256]{3,2,1,0:T(8,128)(2,1)S(1)}, bf16[512,512]{1,0:T(8,128)(2,1)S(1)}, bf16[512,512]{1,0:T(8,128)(2,1)S(1)}, bf16[512,512]{1,0:T(8...) custom-call(bf16[4,64,64,256]{3,2,1,0:T(8,128)(2,1)} %refs_0_.1, ...), custom_call_target="tpu_custom_call" | custom-call | tf_op jit(solution)/shard_map/load_first/pallas_call | solution.py:98
  11.4 2.8 %near_half.1 = (bf16[2,256,512]{2,1,0:T(8,128)(2,1)S(1)}, bf16[2,256,512]{2,1,0:T(8,128)(2,1)S(1)}, bf16[2,4,256,128]{3,2,1,0:T(8,128)(2,1)S(1)}, bf16[2,4,256,2...) custom-call(s32[5]{0:T(128)S(1)} %stack.23.refs_13_.place_ref.refs_0, ...), custom_call_target="tpu_custom_call" | custom-call | tf_op jit(solution)/shard_map/near_half/pallas_call | solution.py:198
  14.2 6.6 %collective-permute-start.4 = (bf16[2,64,512]{2,1,0:T(8,128)(2,1)S(1)}, bf16[2,64,512]{2,1,0:T(8,128)(2,1)S(1)}, u32[]{:S(2)}, u32[]{:S(2)}) collective-permute-start(bf16[2,64,512]{2,1,0:T(8,128)(2,1)S(1)} %get-tuple-element.163), channel_id=1, source_target_pairs={{0,3},{1,2},{2,1},{3,0},{4,7},{5,6},{6,5},{7,4},{8,11},{9,10},{10,... | collective-permute-start | bytes 393224 | tf_op jit(solution)/shard_map/ppermute | solution.py:789
  20.8 4.6 %collective-permute-done.two_ref = bf16[2,64,512]{2,1,0:T(8,128)(2,1)S(1)} collective-permute-done((bf16[2,64,512]{2,1,0:T(8,128)(2,1)S(1)}, bf16[2,64,512]{2,1,0:T(8,128)(2,1)S(1)}, u32[]{:S(2)}, u32[]{:S(2)}) %collective-permute-start) | collective-permute-done | bytes 131104 | tf_op jit(solution)/shard_map/ppermute | solution.py:789
  25.4 7.3 %attention_forward.2 = (bf16[4,64,64,256]{3,2,1,0:T(8,128)(2,1)}, bf16[2,64,64,256]{3,2,1,0:T(8,128)(2,1)S(1)}, f32[2,4,64,128]{3,2,1,0:T(8,128)S(1)}, f32[2,4,6...) custom-call(s32[5]{0:T(128)S(1)} %stack.23.refs_13_.place_ref.refs_0, ...), custom_call_target="tpu_custom_call", output_to_operand_aliasing={{4}: (11, {}), {5}: (12, {}), {6}: (13, {}), {7}: (14, {})} | custom-call | flops 1610612736 | bytes 12582912 | tf_op jit(solution)/shard_map/attention_forward/pallas_call | solution.py:321
  32.7 7.9 %attention_forward.3 = (bf16[4,64,64,256]{3,2,1,0:T(8,128)(2,1)}, bf16[2,64,64,256]{3,2,1,0:T(8,128)(2,1)S(1)}, f32[2,4,64,128]{3,2,1,0:T(8,128)S(1)}, f32[2,4,6...) custom-call(s32[5]{0:T(128)S(1)} %stack.23.refs_13_.place_ref.refs_0, ...), custom_call_target="tpu_custom_call", output_to_operand_aliasing={{4}: (11, {}), {5}: (12, {}), {6}: (13, {}), {7}: (14, {}),... | custom-call | flops 1610612736 | bytes 12582912 | tf_op jit(solution)/shard_map/attention_forward/pallas_call | solution.py:321
  40.6 7.8 %dense.1 = (bf16[4,64,512]{2,1,0:T(8,128)(2,1)}, bf16[4,256,512]{2,1,0:T(8,128)(2,1)S(1)}, bf16[4,256,512]{2,1,0:T(8,128)(2,1)S(1)}, bf16[4,4,64,512]{3,2,1,0:T(...) custom-call(s32[5]{0:T(128)S(1)} %stack.23.refs_13_.place_ref.refs_0, ...), custom_call_target="tpu_custom_call" | custom-call | flops 3221225472 | bytes 12582912 | tf_op jit(solution)/shard_map/dense/pallas_call | solution.py:540
  49.5 5.8 %attention_backward.4 = (bf16[4,64,64,256]{3,2,1,0:T(8,128)(2,1)}, bf16[2,1,64,512]{3,2,1,0:T(8,128)(2,1)S(1)}, bf16[1,64,512]{2,1,0:T(8,128)(2,1)S(1)}, f32[1,6...) custom-call(s32[5]{0:T(128)S(1)} %stack.23.refs_13_.place_ref.refs_0, ...), custom_call_target="tpu_custom_call" | custom-call | flops 1610612736 | bytes 6291456 | tf_op jit(solution)/shard_map/attention_backward/pallas_call | solution.py:738
  56.4 1.6 %collective-permute-start.11 = (bf16[1160,256]{1,0:T(8,128)(2,1)S(1)}, bf16[1160,256]{1,0:T(8,128)(2,1)S(1)}, u32[]{:S(2)}, u32[]{:S(2)}) collective-permute-start(bf16[1160,256]{1,0:T(8,128)(2,1)S(1)} %get-tuple-element.217), channel_id=1, source_target_pairs={{0,16},{4,20},{8,24},{12,28},{16,0},{20,4},{24,8},{28,12},{1,17},{... | collective-permute-start | bytes 1781768 | tf_op jit(solution)/shard_map/ppermute | solution.py:789
  58.0 1.5 %collective-permute-start.10 = (bf16[1160,256]{1,0:T(8,128)(2,1)S(1)}, bf16[1160,256]{1,0:T(8,128)(2,1)S(1)}, u32[]{:S(2)}, u32[]{:S(2)}) collective-permute-start(bf16[1160,256]{1,0:T(8,128)(2,1)S(1)} %get-tuple-element.199.refs_2_), channel_id=1, source_target_pairs={{0,8},{4,12},{8,0},{12,4},{16,24},{20,28},{24,16},{28,20},{1,9},{5... | collective-permute-start | bytes 1781768 | tf_op jit(solution)/shard_map/ppermute | solution.py:789
  59.5 5.8 %attention_backward.5 = (bf16[4,64,64,256]{3,2,1,0:T(8,128)(2,1)}, bf16[2,2,64,512]{3,2,1,0:T(8,128)(2,1)S(1)}, bf16[1,64,512]{2,1,0:T(8,128)(2,1)S(1)}, f32[1,6...) custom-call(s32[5]{0:T(128)S(1)} %stack.23.refs_13_.place_ref.refs_0, ...), custom_call_target="tpu_custom_call", output_to_operand_aliasing={{0}: (13, {}), {4}: (14, {})} | custom-call | flops 1610612736 | bytes 6291456 | tf_op jit(solution)/shard_map/attention_backward/pallas_call | solution.py:738
  65.3 5.8 %attention_backward.6 = (bf16[4,64,64,256]{3,2,1,0:T(8,128)(2,1)}, bf16[2,1,64,512]{3,2,1,0:T(8,128)(2,1)S(1)}, bf16[1,64,512]{2,1,0:T(8,128)(2,1)S(1)}, f32[1,6...) custom-call(s32[5]{0:T(128)S(1)} %stack.23.refs_13_.place_ref.refs_0, ...), custom_call_target="tpu_custom_call", output_to_operand_aliasing={{0}: (13, {}), {4}: (14, {})} | custom-call | flops 1610612736 | bytes 6291456 | tf_op jit(solution)/shard_map/attention_backward/pallas_call | solution.py:738
  74.0 1.6 %collective-permute-start.14 = (bf16[584,256]{1,0:T(8,128)(2,1)S(1)}, bf16[584,256]{1,0:T(8,128)(2,1)S(1)}, u32[]{:S(2)}, u32[]{:S(2)}) collective-permute-start(bf16[584,256]{1,0:T(8,128)(2,1)S(1)} %get-tuple-element.224), channel_id=1, source_target_pairs={{0,8},{4,12},{8,0},{12,4},{16,24},{20,28},{24,16},{28,20},{1,9},{5... | collective-permute-start | bytes 897032 | tf_op jit(solution)/shard_map/ppermute | solution.py:789
  77.2 5.8 %attention_backward.7 = (bf16[4,64,64,256]{3,2,1,0:T(8,128)(2,1)}, bf16[2,1,64,512]{3,2,1,0:T(8,128)(2,1)S(1)}, bf16[1,64,512]{2,1,0:T(8,128)(2,1)S(1)}, f32[1,6...) custom-call(s32[5]{0:T(128)S(1)} %stack.23.refs_13_.place_ref.refs_0, ...), custom_call_target="tpu_custom_call", output_to_operand_aliasing={{0}: (13, {}), {4}: (14, {})} | custom-call | flops 1610612736 | bytes 6291456 | tf_op jit(solution)/shard_map/attention_backward/pallas_call | solution.py:738
  84.0 2.1 %attention_weights.1 = (bf16[4,1,64,512]{3,2,1,0:T(8,128)(2,1)S(1)}, bf16[4,1,64,512]{3,2,1,0:T(8,128)(2,1)S(1)}, bf16[4,1,64,512]{3,2,1,0:T(8,128)(2,1)S(1)}, b...) custom-call(s32[5]{0:T(128)S(1)} %stack.23.refs_13_.place_ref.refs_0_, ...), custom_call_target="tpu_custom_call" | custom-call | bytes 4980736 | tf_op jit(solution)/shard_map/attention_weights/pallas_call | solution.py:952
  90.1 1.5 %collective-permute-start.23 = (bf16[392,256]{1,0:T(8,128)(2,1)S(1)}, bf16[392,256]{1,0:T(8,128)(2,1)S(1)}, u32[]{:S(2)}, u32[]{:S(2)}) collective-permute-start(bf16[392,256]{1,0:T(8,128)(2,1)S(1)} %get-tuple-element.255), channel_id=1, source_target_pairs={{0,16},{4,20},{8,24},{12,28},{16,0},{20,4},{24,8},{28,12},{1,17},{... | collective-permute-start | bytes 602120 | tf_op jit(solution)/shard_map/ppermute | solution.py:789
  91.6 2.9 %collective-permute-start.17 = (bf16[1,64,512]{2,1,0:T(8,128)(2,1)S(1)}, bf16[1,64,512]{2,1,0:T(8,128)(2,1)S(1)}, u32[]{:S(2)}, u32[]{:S(2)}) collective-permute-start(bf16[1,64,512]{2,1,0:T(8,128)(2,1)S(1)} %cross_second.1.refs_16_), channel_id=1, source_target_pairs={{0,2},{1,3},{2,0},{3,1},{4,6},{5,7},{6,4},{7,5},{8,10},{9,11},{10,... | collective-permute-start | bytes 196616 | tf_op jit(solution)/shard_map/ppermute | solution.py:789
  94.5 2.1 %collective-permute-done.22.refs_2_ = bf16[392,256]{1,0:T(8,128)(2,1)S(1)} collective-permute-done((bf16[392,256]{1,0:T(8,128)(2,1)S(1)}, bf16[392,256]{1,0:T(8,128)(2,1)S(1)}, u32[]{:S(2)}, u32[]{:S(2)}) %collective-permute-start.22) | collective-permute-done | bytes 200736 | tf_op jit(solution)/shard_map/ppermute | solution.py:789
  97.5 1.5 %collective-permute-done.17.refs_5_.refs_10_ = bf16[1,64,512]{2,1,0:T(8,128)(2,1)S(1)} collective-permute-done((bf16[1,64,512]{2,1,0:T(8,128)(2,1)S(1)}, bf16[1,64,512]{2,1,0:T(8,128)(2,1)S(1)}, u32[]{:S(2)}, u32[]{:S(2)}) %collective-permute-start.17) | collective-permute-done | bytes 65568 | tf_op jit(solution)/shard_map/ppermute | solution.py:789
  99.0 1.7 %collective-permute-done.15.refs_2_.refs_7_ = bf16[432,512]{1,0:T(8,128)(2,1)S(1)} collective-permute-done((bf16[432,512]{1,0:T(8,128)(2,1)S(1)}, bf16[432,512]{1,0:T(8,128)(2,1)S(1)}, u32[]{:S(2)}, u32[]{:S(2)}) %collective-permute-start.15) | collective-permute-done | bytes 442400 | tf_op jit(solution)/shard_map/ppermute | solution.py:789
  101.3 1.8 %collective-permute-start.24 = (bf16[368,512]{1,0:T(8,128)(2,1)S(1)}, bf16[368,512]{1,0:T(8,128)(2,1)S(1)}, u32[]{:S(2)}, u32[]{:S(2)}) collective-permute-start(bf16[368,512]{1,0:T(8,128)(2,1)S(1)} %dense_near_sum.1.refs_5_.refs_0_), channel_id=1, source_target_pairs={{0,2},{1,3},{2,0},{3,1},{4,6},{5,7},{6,4},{7,5},{8,10},{9,11},{10,... | collective-permute-start | bytes 1130504 | tf_op jit(solution)/shard_map/ppermute | solution.py:789
  103.6 1.5 %collective-permute-start.25 = (bf16[200,256]{1,0:T(8,128)(2,1)S(1)}, bf16[200,256]{1,0:T(8,128)(2,1)S(1)}, u32[]{:S(2)}, u32[]{:S(2)}) collective-permute-start(bf16[200,256]{1,0:T(8,128)(2,1)S(1)} %get-tuple-element.257.refs_4_), channel_id=1, source_target_pairs={{0,16},{4,20},{8,24},{12,28},{16,0},{20,4},{24,8},{28,12},{1,17},{... | collective-permute-start | bytes 307208 | tf_op jit(solution)/shard_map/ppermute | solution.py:789
  105.1 2.6 %collective-permute-done.26.refs_3_ = bf16[200,256]{1,0:T(8,128)(2,1)S(1)} collective-permute-done((bf16[200,256]{1,0:T(8,128)(2,1)S(1)}, bf16[200,256]{1,0:T(8,128)(2,1)S(1)}, u32[]{:S(2)}, u32[]{:S(2)}) %collective-permute-start.26) | collective-permute-done | bytes 102432 | tf_op jit(solution)/shard_map/ppermute | solution.py:789
  108.3 2.1 %collective-permute-start.27 = (bf16[200,512]{1,0:T(8,128)(2,1)S(1)}, bf16[200,512]{1,0:T(8,128)(2,1)S(1)}, u32[]{:S(2)}, u32[]{:S(2)}) collective-permute-start(bf16[200,512]{1,0:T(8,128)(2,1)S(1)} %tail_sum_second.1.refs_0_), channel_id=1, source_target_pairs={{0,1},{1,0},{2,3},{3,2},{4,5},{5,4},{6,7},{7,6},{8,9},{9,8},{10,11... | collective-permute-start | bytes 614408 | tf_op jit(solution)/shard_map/ppermute | solution.py:789
  110.4 5.0 %collective-permute-done.27.refs_1_ = bf16[200,512]{1,0:T(8,128)(2,1)S(1)} collective-permute-done((bf16[200,512]{1,0:T(8,128)(2,1)S(1)}, bf16[200,512]{1,0:T(8,128)(2,1)S(1)}, u32[]{:S(2)}, u32[]{:S(2)}) %collective-permute-start.27) | collective-permute-done | bytes 204832 | tf_op jit(solution)/shard_map/ppermute | solution.py:789
  115.4 5.3 %collective-permute-done.24.refs_1_.refs_11_ = bf16[368,512]{1,0:T(8,128)(2,1)S(1)} collective-permute-done((bf16[368,512]{1,0:T(8,128)(2,1)S(1)}, bf16[368,512]{1,0:T(8,128)(2,1)S(1)}, u32[]{:S(2)}, u32[]{:S(2)}) %collective-permute-start.24) | collective-permute-done | bytes 376864 | tf_op jit(solution)/shard_map/ppermute | solution.py:789
  120.8 4.4 %collective-permute-start.28 = (bf16[200,512]{1,0:T(8,128)(2,1)S(1)}, bf16[200,512]{1,0:T(8,128)(2,1)S(1)}, u32[]{:S(2)}, u32[]{:S(2)}) collective-permute-start(bf16[200,512]{1,0:T(8,128)(2,1)S(1)} %tail_near_sum.1.refs_2_.refs_1_), channel_id=1, source_target_pairs={{0,2},{1,3},{2,0},{3,1},{4,6},{5,7},{6,4},{7,5},{8,10},{9,11},{10,... | collective-permute-start | bytes 614408 | tf_op jit(solution)/shard_map/ppermute | solution.py:789
  126.3 5.5 %collective-permute-done.28.refs_2_ = bf16[200,512]{1,0:T(8,128)(2,1)S(1)} collective-permute-done((bf16[200,512]{1,0:T(8,128)(2,1)S(1)}, bf16[200,512]{1,0:T(8,128)(2,1)S(1)}, u32[]{:S(2)}, u32[]{:S(2)}) %collective-permute-start.28) | collective-permute-done | bytes 204832 | tf_op jit(solution)/shard_map/ppermute | solution.py:789
  131.8 1.4 %collective-permute-done.29.refs_4_ = bf16[304,512]{1,0:T(8,128)(2,1)S(1)} collective-permute-done((bf16[304,512]{1,0:T(8,128)(2,1)S(1)}, bf16[304,512]{1,0:T(8,128)(2,1)S(1)}, u32[]{:S(2)}, u32[]{:S(2)}) %collective-permute-start.29) | collective-permute-done | bytes 311328 | tf_op jit(solution)/shard_map/ppermute | solution.py:789
  133.2 1.8 %finish.1 = (f32[64,512]{1,0:T(8,128)}, f32[64,512]{1,0:T(8,128)}, f32[64,512]{1,0:T(8,128)}, f32[256,512]{1,0:T(8,128)}, f32[64,2048]{1,0:T(8,128)}, /*index=5*...) custom-call(s32[5]{0:T(128)S(1)} %stack.23.refs_13_.place_ref.refs_0, ...), custom_call_target="tpu_custom_call" | custom-call | bytes 2608128 | tf_op jit(solution)/shard_map/finish/pallas_call | solution.py:952
  (57 shorter events, 16.8 us)
Async XLA Ops:
  0.7 24.7 %copy-start.1 = (s32[4]{0:T(128)S(1)}, s32[4]{0:T(128)}, u32[]{:S(2)}) copy-start(s32[4]{0:T(128)} %length_ref.3) | copy-start | bytes 52
  0.7 10.7 %collective-permute-start.2 = (bf16[4,64,512]{2,1,0:T(8,128)(2,1)}, bf16[4,64,512]{2,1,0:T(8,128)(2,1)S(1)}, u32[]{:S(2)}, u32[]{:S(2)}) collective-permute-start(bf16[4,64,512]{2,1,0:T(8,128)(2,1)} %refs_12_.5), channel_id=1, source_target_pairs={{0,1},{1,0},{2,3},{3,2},{4,5},{5,4},{6,7},{7,6},{8,9},{9,8},{10,11... | collective-permute-start | bytes 786440 | tf_op jit(solution)/shard_map/ppermute | solution.py:789
  4.7 16.1 %collective-permute-start.1 = (bf16[2,64,512]{2,1,0:T(8,128)(2,1)S(1)}, bf16[2,64,512]{2,1,0:T(8,128)(2,1)S(1)}, u32[]{:S(2)}, u32[]{:S(2)}) collective-permute-start(bf16[2,64,512]{2,1,0:T(8,128)(2,1)S(1)} %slice.3), channel_id=1, source_target_pairs={{0,3},{1,2},{2,1},{3,0},{4,7},{5,6},{6,5},{7,4},{8,11},{9,10},{10,... | collective-permute-start | bytes 393224 | tf_op jit(solution)/shard_map/ppermute | solution.py:789
  7.2 18.1 %collective-permute-start = (bf16[2,64,512]{2,1,0:T(8,128)(2,1)S(1)}, bf16[2,64,512]{2,1,0:T(8,128)(2,1)S(1)}, u32[]{:S(2)}, u32[]{:S(2)}) collective-permute-start(bf16[2,64,512]{2,1,0:T(8,128)(2,1)S(1)} %slice.3), channel_id=1, source_target_pairs={{0,2},{1,3},{2,0},{3,1},{4,6},{5,7},{6,4},{7,5},{8,10},{9,11},{10,... | collective-permute-start | bytes 393224 | tf_op jit(solution)/shard_map/ppermute | solution.py:789
  14.2 18.5 %collective-permute-start.4 = (bf16[2,64,512]{2,1,0:T(8,128)(2,1)S(1)}, bf16[2,64,512]{2,1,0:T(8,128)(2,1)S(1)}, u32[]{:S(2)}, u32[]{:S(2)}) collective-permute-start(bf16[2,64,512]{2,1,0:T(8,128)(2,1)S(1)} %get-tuple-element.163), channel_id=1, source_target_pairs={{0,3},{1,2},{2,1},{3,0},{4,7},{5,6},{6,5},{7,4},{8,11},{9,10},{10,... | collective-permute-start | bytes 393224 | tf_op jit(solution)/shard_map/ppermute | solution.py:789
  20.8 11.9 %collective-permute-start.3 = (bf16[2,64,512]{2,1,0:T(8,128)(2,1)S(1)}, bf16[2,64,512]{2,1,0:T(8,128)(2,1)S(1)}, u32[]{:S(2)}, u32[]{:S(2)}) collective-permute-start(bf16[2,64,512]{2,1,0:T(8,128)(2,1)S(1)} %get-tuple-element.163), channel_id=1, source_target_pairs={{0,2},{1,3},{2,0},{3,1},{4,6},{5,7},{6,4},{7,5},{8,10},{9,11},{10,... | collective-permute-start | bytes 393224 | tf_op jit(solution)/shard_map/ppermute | solution.py:789
  32.7 7.9 %copy-start = (bf16[4,64,512]{2,1,0:T(8,128)(2,1)S(1)}, bf16[4,64,512]{2,1,0:T(8,128)(2,1)}, u32[]{:S(2)}) copy-start(bf16[4,64,512]{2,1,0:T(8,128)(2,1)} %refs_12_.5) | copy-start | bytes 786436
  48.4 6.9 %collective-permute-start.5 = (bf16[4,4,64,512]{3,2,1,0:T(8,128)(2,1)S(1)}, bf16[4,4,64,512]{3,2,1,0:T(8,128)(2,1)S(1)}, u32[]{:S(2)}, u32[]{:S(2)}) collective-permute-start(bf16[4,4,64,512]{3,2,1,0:T(8,128)(2,1)S(1)} %bitcast.11), channel_id=1, source_target_pairs={{0,4},{4,0},{8,12},{12,8},{16,20},{20,16},{24,28},{28,24},{1,5},{5... | collective-permute-start | bytes 3145736 | tf_op jit(solution)/shard_map/ppermute | solution.py:789
  48.5 6.8 %collective-permute-start.6 = (bf16[4,4,64,512]{3,2,1,0:T(8,128)(2,1)S(1)}, bf16[4,4,64,512]{3,2,1,0:T(8,128)(2,1)S(1)}, u32[]{:S(2)}, u32[]{:S(2)}) collective-permute-start(bf16[4,4,64,512]{3,2,1,0:T(8,128)(2,1)S(1)} %get-tuple-element.195), channel_id=1, source_target_pairs={{0,4},{4,0},{8,12},{12,8},{16,20},{20,16},{24,28},{28,24},{1,5},{5... | collective-permute-start | bytes 3145736 | tf_op jit(solution)/shard_map/ppermute | solution.py:789
  49.0 6.3 %collective-permute-start.7 = (bf16[4,1,64,512]{3,2,1,0:T(8,128)(2,1)S(1)}, bf16[4,1,64,512]{3,2,1,0:T(8,128)(2,1)S(1)}, u32[]{:S(2)}, u32[]{:S(2)}) collective-permute-start(bf16[4,1,64,512]{3,2,1,0:T(8,128)(2,1)S(1)} %bitcast.12), channel_id=1, source_target_pairs={{0,4},{4,0},{8,12},{12,8},{16,20},{20,16},{24,28},{28,24},{1,5},{5... | collective-permute-start | bytes 786440 | tf_op jit(solution)/shard_map/ppermute | solution.py:789
  49.1 6.2 %collective-permute-start.8 = (f32[8,512]{1,0:T(8,128)S(1)}, f32[8,512]{1,0:T(8,128)S(1)}, u32[]{:S(2)}, u32[]{:S(2)}) collective-permute-start(f32[8,512]{1,0:T(8,128)S(1)} %get-tuple-element.198.refs_7_), channel_id=1, source_target_pairs={{0,4},{4,0},{8,12},{12,8},{16,20},{20,16},{24,28},{28,24},{1,5},{5... | collective-permute-start | bytes 49160 | tf_op jit(solution)/shard_map/ppermute | solution.py:789
  56.4 15.5 %collective-permute-start.11 = (bf16[1160,256]{1,0:T(8,128)(2,1)S(1)}, bf16[1160,256]{1,0:T(8,128)(2,1)S(1)}, u32[]{:S(2)}, u32[]{:S(2)}) collective-permute-start(bf16[1160,256]{1,0:T(8,128)(2,1)S(1)} %get-tuple-element.217), channel_id=1, source_target_pairs={{0,16},{4,20},{8,24},{12,28},{16,0},{20,4},{24,8},{28,12},{1,17},{... | collective-permute-start | bytes 1781768 | tf_op jit(solution)/shard_map/ppermute | solution.py:789
  58.0 15.1 %collective-permute-start.10 = (bf16[1160,256]{1,0:T(8,128)(2,1)S(1)}, bf16[1160,256]{1,0:T(8,128)(2,1)S(1)}, u32[]{:S(2)}, u32[]{:S(2)}) collective-permute-start(bf16[1160,256]{1,0:T(8,128)(2,1)S(1)} %get-tuple-element.199.refs_2_), channel_id=1, source_target_pairs={{0,8},{4,12},{8,0},{12,4},{16,24},{20,28},{24,16},{28,20},{1,9},{5... | collective-permute-start | bytes 1781768 | tf_op jit(solution)/shard_map/ppermute | solution.py:789
  65.3 10.7 %collective-permute-start.9 = (bf16[2,2,64,512]{3,2,1,0:T(8,128)(2,1)S(1)}, bf16[2,2,64,512]{3,2,1,0:T(8,128)(2,1)S(1)}, u32[]{:S(2)}, u32[]{:S(2)}) collective-permute-start(bf16[2,2,64,512]{3,2,1,0:T(8,128)(2,1)S(1)} %get-tuple-element.214), channel_id=1, source_target_pairs={{0,1},{1,0},{2,3},{3,2},{4,5},{5,4},{6,7},{7,6},{8,9},{9,8},{10,11... | collective-permute-start | bytes 786440 | tf_op jit(solution)/shard_map/ppermute | solution.py:789
  74.0 9.0 %collective-permute-start.14 = (bf16[584,256]{1,0:T(8,128)(2,1)S(1)}, bf16[584,256]{1,0:T(8,128)(2,1)S(1)}, u32[]{:S(2)}, u32[]{:S(2)}) collective-permute-start(bf16[584,256]{1,0:T(8,128)(2,1)S(1)} %get-tuple-element.224), channel_id=1, source_target_pairs={{0,8},{4,12},{8,0},{12,4},{16,24},{20,28},{24,16},{28,20},{1,9},{5... | collective-permute-start | bytes 897032 | tf_op jit(solution)/shard_map/ppermute | solution.py:789
  75.5 7.6 %collective-permute-start.13 = (bf16[584,256]{1,0:T(8,128)(2,1)S(1)}, bf16[584,256]{1,0:T(8,128)(2,1)S(1)}, u32[]{:S(2)}, u32[]{:S(2)}) collective-permute-start(bf16[584,256]{1,0:T(8,128)(2,1)S(1)} %get-tuple-element.219.refs_3_), channel_id=1, source_target_pairs={{0,16},{4,20},{8,24},{12,28},{16,0},{20,4},{24,8},{28,12},{1,17},{... | collective-permute-start | bytes 897032 | tf_op jit(solution)/shard_map/ppermute | solution.py:789
  76.0 7.9 %collective-permute-start.12 = (bf16[2,1,64,512]{3,2,1,0:T(8,128)(2,1)S(1)}, bf16[2,1,64,512]{3,2,1,0:T(8,128)(2,1)S(1)}, u32[]{:S(2)}, u32[]{:S(2)}) collective-permute-start(bf16[2,1,64,512]{3,2,1,0:T(8,128)(2,1)S(1)} %get-tuple-element.221), channel_id=1, source_target_pairs={{0,1},{1,0},{2,3},{3,2},{4,5},{5,4},{6,7},{7,6},{8,9},{9,8},{10,11... | collective-permute-start | bytes 393224 | tf_op jit(solution)/shard_map/ppermute | solution.py:789
  76.1 7.9 %collective-permute-start.16 = (bf16[2,64,512]{2,1,0:T(8,128)(2,1)S(1)}, bf16[2,64,512]{2,1,0:T(8,128)(2,1)S(1)}, u32[]{:S(2)}, u32[]{:S(2)}) collective-permute-start(bf16[2,64,512]{2,1,0:T(8,128)(2,1)S(1)} %cross_first.1.refs_2_), channel_id=1, source_target_pairs={{0,2},{1,3},{2,0},{3,1},{4,6},{5,7},{6,4},{7,5},{8,10},{9,11},{10,... | collective-permute-start | bytes 393224 | tf_op jit(solution)/shard_map/ppermute | solution.py:789
  86.1 2.7 %collective-permute-start.18 = (bf16[4,1,64,512]{3,2,1,0:T(8,128)(2,1)S(1)}, bf16[4,1,64,512]{3,2,1,0:T(8,128)(2,1)S(1)}, u32[]{:S(2)}, u32[]{:S(2)}) collective-permute-start(bf16[4,1,64,512]{3,2,1,0:T(8,128)(2,1)S(1)} %get-tuple-element.246), channel_id=1, source_target_pairs={{0,4},{4,0},{8,12},{12,8},{16,20},{20,16},{24,28},{28,24},{1,5},{5... | collective-permute-start | bytes 786440 | tf_op jit(solution)/shard_map/ppermute | solution.py:789
  86.2 2.6 %collective-permute-start.19 = (bf16[4,1,64,512]{3,2,1,0:T(8,128)(2,1)S(1)}, bf16[4,1,64,512]{3,2,1,0:T(8,128)(2,1)S(1)}, u32[]{:S(2)}, u32[]{:S(2)}) collective-permute-start(bf16[4,1,64,512]{3,2,1,0:T(8,128)(2,1)S(1)} %get-tuple-element.248), channel_id=1, source_target_pairs={{0,4},{4,0},{8,12},{12,8},{16,20},{20,16},{24,28},{28,24},{1,5},{5... | collective-permute-start | bytes 786440 | tf_op jit(solution)/shard_map/ppermute | solution.py:789
  86.7 2.1 %collective-permute-start.20 = (bf16[4,1,64,512]{3,2,1,0:T(8,128)(2,1)S(1)}, bf16[4,1,64,512]{3,2,1,0:T(8,128)(2,1)S(1)}, u32[]{:S(2)}, u32[]{:S(2)}) collective-permute-start(bf16[4,1,64,512]{3,2,1,0:T(8,128)(2,1)S(1)} %get-tuple-element.250), channel_id=1, source_target_pairs={{0,4},{4,0},{8,12},{12,8},{16,20},{20,16},{24,28},{28,24},{1,5},{5... | collective-permute-start | bytes 786440 | tf_op jit(solution)/shard_map/ppermute | solution.py:789
  86.7 13.9 %collective-permute-start.15 = (bf16[432,512]{1,0:T(8,128)(2,1)S(1)}, bf16[432,512]{1,0:T(8,128)(2,1)S(1)}, u32[]{:S(2)}, u32[]{:S(2)}) collective-permute-start(bf16[432,512]{1,0:T(8,128)(2,1)S(1)} %get-tuple-element.227), channel_id=1, source_target_pairs={{0,1},{1,0},{2,3},{3,2},{4,5},{5,4},{6,7},{7,6},{8,9},{9,8},{10,11... | collective-permute-start | bytes 1327112 | tf_op jit(solution)/shard_map/ppermute | solution.py:789
  87.5 1.2 collective-permute-start.21
  89.5 7.1 %collective-permute-start.22 = (bf16[392,256]{1,0:T(8,128)(2,1)S(1)}, bf16[392,256]{1,0:T(8,128)(2,1)S(1)}, u32[]{:S(2)}, u32[]{:S(2)}) collective-permute-start(bf16[392,256]{1,0:T(8,128)(2,1)S(1)} %get-tuple-element.253), channel_id=1, source_target_pairs={{0,8},{4,12},{8,0},{12,4},{16,24},{20,28},{24,16},{28,20},{1,9},{5... | collective-permute-start | bytes 602120 | tf_op jit(solution)/shard_map/ppermute | solution.py:789
  90.1 6.8 %collective-permute-start.23 = (bf16[392,256]{1,0:T(8,128)(2,1)S(1)}, bf16[392,256]{1,0:T(8,128)(2,1)S(1)}, u32[]{:S(2)}, u32[]{:S(2)}) collective-permute-start(bf16[392,256]{1,0:T(8,128)(2,1)S(1)} %get-tuple-element.255), channel_id=1, source_target_pairs={{0,16},{4,20},{8,24},{12,28},{16,0},{20,4},{24,8},{28,12},{1,17},{... | collective-permute-start | bytes 602120 | tf_op jit(solution)/shard_map/ppermute | solution.py:789
  91.6 7.4 %collective-permute-start.17 = (bf16[1,64,512]{2,1,0:T(8,128)(2,1)S(1)}, bf16[1,64,512]{2,1,0:T(8,128)(2,1)S(1)}, u32[]{:S(2)}, u32[]{:S(2)}) collective-permute-start(bf16[1,64,512]{2,1,0:T(8,128)(2,1)S(1)} %cross_second.1.refs_16_), channel_id=1, source_target_pairs={{0,2},{1,3},{2,0},{3,1},{4,6},{5,7},{6,4},{7,5},{8,10},{9,11},{10,... | collective-permute-start | bytes 196616 | tf_op jit(solution)/shard_map/ppermute | solution.py:789
  101.3 19.4 %collective-permute-start.24 = (bf16[368,512]{1,0:T(8,128)(2,1)S(1)}, bf16[368,512]{1,0:T(8,128)(2,1)S(1)}, u32[]{:S(2)}, u32[]{:S(2)}) collective-permute-start(bf16[368,512]{1,0:T(8,128)(2,1)S(1)} %dense_near_sum.1.refs_5_.refs_0_), channel_id=1, source_target_pairs={{0,2},{1,3},{2,0},{3,1},{4,6},{5,7},{6,4},{7,5},{8,10},{9,11},{10,... | collective-permute-start | bytes 1130504 | tf_op jit(solution)/shard_map/ppermute | solution.py:789
  103.1 4.7 %collective-permute-start.26 = (bf16[200,256]{1,0:T(8,128)(2,1)S(1)}, bf16[200,256]{1,0:T(8,128)(2,1)S(1)}, u32[]{:S(2)}, u32[]{:S(2)}) collective-permute-start(bf16[200,256]{1,0:T(8,128)(2,1)S(1)} %get-tuple-element.261), channel_id=1, source_target_pairs={{0,8},{4,12},{8,0},{12,4},{16,24},{20,28},{24,16},{28,20},{1,9},{5... | collective-permute-start | bytes 307208 | tf_op jit(solution)/shard_map/ppermute | solution.py:789
  103.6 4.7 %collective-permute-start.25 = (bf16[200,256]{1,0:T(8,128)(2,1)S(1)}, bf16[200,256]{1,0:T(8,128)(2,1)S(1)}, u32[]{:S(2)}, u32[]{:S(2)}) collective-permute-start(bf16[200,256]{1,0:T(8,128)(2,1)S(1)} %get-tuple-element.257.refs_4_), channel_id=1, source_target_pairs={{0,16},{4,20},{8,24},{12,28},{16,0},{20,4},{24,8},{28,12},{1,17},{... | collective-permute-start | bytes 307208 | tf_op jit(solution)/shard_map/ppermute | solution.py:789
  108.3 7.0 %collective-permute-start.27 = (bf16[200,512]{1,0:T(8,128)(2,1)S(1)}, bf16[200,512]{1,0:T(8,128)(2,1)S(1)}, u32[]{:S(2)}, u32[]{:S(2)}) collective-permute-start(bf16[200,512]{1,0:T(8,128)(2,1)S(1)} %tail_sum_second.1.refs_0_), channel_id=1, source_target_pairs={{0,1},{1,0},{2,3},{3,2},{4,5},{5,4},{6,7},{7,6},{8,9},{9,8},{10,11... | collective-permute-start | bytes 614408 | tf_op jit(solution)/shard_map/ppermute | solution.py:789
  120.7 12.5 %collective-permute-start.29 = (bf16[304,512]{1,0:T(8,128)(2,1)S(1)}, bf16[304,512]{1,0:T(8,128)(2,1)S(1)}, u32[]{:S(2)}, u32[]{:S(2)}) collective-permute-start(bf16[304,512]{1,0:T(8,128)(2,1)S(1)} %dense_far_sum.1.refs_16_.refs_3_), channel_id=1, source_target_pairs={{0,1},{1,0},{2,3},{3,2},{4,5},{5,4},{6,7},{7,6},{8,9},{9,8},{10,11... | collective-permute-start | bytes 933896 | tf_op jit(solution)/shard_map/ppermute | solution.py:789
  120.8 11.0 %collective-permute-start.28 = (bf16[200,512]{1,0:T(8,128)(2,1)S(1)}, bf16[200,512]{1,0:T(8,128)(2,1)S(1)}, u32[]{:S(2)}, u32[]{:S(2)}) collective-permute-start(bf16[200,512]{1,0:T(8,128)(2,1)S(1)} %tail_near_sum.1.refs_2_.refs_1_), channel_id=1, source_target_pairs={{0,2},{1,3},{2,0},{3,1},{4,6},{5,7},{6,4},{7,5},{8,10},{9,11},{10,... | collective-permute-start | bytes 614408 | tf_op jit(solution)/shard_map/ppermute | solution.py:789

commit v7 on v6

--- a/solution.py
+++ b/solution.py
@@ -371,12 +371,8 @@
         outer_bias_ref,
         far_ref,
         atoms_out_ref,
-        outer_send_ref,
-        outer_keep_ref,
-        inner_send_ref,
-        inner_keep_ref,
-        out_send_ref,
-        out_keep_ref,
+        send_ref,
+        keep_ref,
         grad_middle_ref,
         grad_mixed_ref,
         vectors_ref,
@@ -443,11 +439,15 @@
     vectors_ref[pl.ds(4 + step, 1)] = column_sum(grad_pre.astype(BF16))
     grad_pre = grad_pre.astype(BF16)
     outer_scratch[...] = across(active, cotangent).reshape(outer_scratch.shape)
-    outer_send_ref[...] = outer_scratch[:, 1 - core].astype(BF16).reshape(outer_send_ref.shape)
-    outer_keep_ref[...] = outer_scratch[:, core].astype(BF16).reshape(outer_keep_ref.shape)
+    ratio = send_ref.shape[1] // 2
+    outer_pairs = outer_scratch.shape[0]
+    outer_shape = (outer_pairs, ratio) + send_ref.shape[2:]
+    outer_at = (pl.ds(step * outer_pairs, outer_pairs), slice(0, ratio))
+    send_ref[outer_at] = outer_scratch[:, 1 - core].reshape(outer_shape).astype(BF16)
+    keep_ref[outer_at] = outer_scratch[:, core].reshape(outer_shape).astype(BF16)
     inner_scratch[...] = dot(turned_scratch[...], grad_pre).reshape(inner_scratch.shape)
-    inner_send_ref[:, 0] = inner_scratch[:, 1 - core].astype(BF16)
-    inner_keep_ref[:, 0] = inner_scratch[:, core].astype(BF16)
+    send_ref[:, ratio + step] = inner_scratch[:, 1 - core].astype(BF16)
+    keep_ref[:, ratio + step] = inner_scratch[:, core].astype(BF16)
     upstream_scratch[...] += against(grad_pre, inner_weight)
 
     @pl.when(step == steps - 1)
@@ -470,8 +470,8 @@
             grad_mixed_ref[:, t] = grad_mixed[:, :, t * lanes : (t + 1) * lanes]
         turned = jnp.transpose(mixed_rows()).astype(BF16)
         inner_scratch[...] = dot(turned, branch).reshape(inner_scratch.shape)
-        out_send_ref[...] = inner_scratch[:, 1 - core].astype(BF16)
-        out_keep_ref[...] = inner_scratch[:, core].astype(BF16)
+        send_ref[:, 2 * ratio] = inner_scratch[:, 1 - core].astype(BF16)
+        keep_ref[:, 2 * ratio] = inner_scratch[:, core].astype(BF16)
         copy.wait()
 
 
@@ -509,19 +509,11 @@
         outer_bias,
         extra,
     )
-    outer_spec = pl.BlockSpec((outer_pairs, outer_rows, model_width), lambda s, *_: (s, 0, 0))
-    inner_spec = pl.BlockSpec((pairs, 1, own_rows, width), lambda s, *_: (0, s, 0, 0))
-    outer_shape = shape_of((pairs, outer_rows, model_width), BF16)
-    inner_shape = shape_of((pairs, steps, own_rows, width), BF16)
-    out_shape = shape_of((pairs, own_rows, model_width), BF16)
+    part = near((pairs, 2 * steps + 1, own_rows, model_width), BF16)
     out_shapes = [
         shape_of(atoms.shape, BF16),
-        outer_shape,
-        outer_shape,
-        inner_shape,
-        inner_shape,
-        out_shape,
-        out_shape,
+        part,
+        part,
         near(atoms.shape, F32),
         near((atoms.shape[0], model_width // LANES, atoms.shape[1], LANES), BF16),
         shape_of((4 + steps, model_width), F32),
@@ -529,9 +521,8 @@
     ]
     fixed = lambda s: pl.BlockSpec(s.shape, lambda *_: (0,) * len(s.shape))
     out_specs = [fixed(s) for s in out_shapes]
-    out_specs[1:5] = [outer_spec, outer_spec, inner_spec, inner_spec]
-    out_specs[7:9] = [near_spec(), near_spec()]
-    out_specs[10] = near_spec()
+    out_specs[1:5] = [near_spec()] * 4
+    out_specs[6] = near_spec()
     in_specs = [whole(a) for a in operands[1:]]
     for i, a in enumerate(operands[1:]):
         if i != len(mixed):
@@ -779,9 +770,9 @@
     for j, left in enumerate((own, every, every)):
         right = jnp.concatenate([grads[3 * c + j][...].reshape(-1, width) for c in range(calls)], 0)
         total_ref[...] = dot(left, right).reshape(total_ref.shape)
-        send_ref, keep_ref = out_refs[2 * j : 2 * j + 2]
-        send_ref[:, 0] = total_ref[:, 1 - core].astype(BF16)
-        keep_ref[:, 0] = total_ref[:, core].astype(BF16)
+        send_ref, keep_ref = out_refs
+        send_ref[:, j] = total_ref[:, 1 - core].astype(BF16)
+        keep_ref[:, j] = total_ref[:, core].astype(BF16)
 
 
 def swap(value, axis, mask):
@@ -1189,6 +1180,10 @@
         second_shift,
         inner_bias,
         outer_bias,
+        out_weight,
+        inner_weight,
+        outer_weight,
+        atoms_cotangent,
     ) = load(
         [
             pair_bias,
@@ -1204,6 +1199,10 @@
             second_shift,
             inner_bias,
             outer_bias,
+            out_weight,
+            inner_weight,
+            outer_weight,
+            atoms_cotangent,
         ],
         "load_first",
         None,
@@ -1229,7 +1228,7 @@
     mine = [atoms[:count], projected[-1]]
     gathered = [[swap(a, "rows", mask) for mask in (2, 3)] for a in mine]
     for stage in range(STAGES):
-        pair_out, kept, loaded = attention_forward(
+        pair_out, kept, _ = attention_forward(
             head_size,
             stage * count,
             place,
@@ -1239,18 +1238,13 @@
             (first_gain, first_shift, key_near, value_near, value_bias),
             projected[5 * stage : 5 * stage + 5],
             pair_out,
-            [out_weight, inner_weight, outer_weight, atoms_cotangent] if stage else [],
+            [],
         )
         stages.append(kept)
-    out_weight, inner_weight, outer_weight, atoms_cotangent = loaded
     (
         atoms_out,
-        outer_send,
-        outer_keep,
-        inner_send,
-        inner_keep,
-        out_send,
-        out_keep,
+        send,
+        keep,
         grad_middle,
         grad_mixed,
         dense_vectors,
@@ -1275,12 +1269,7 @@
     )
     pairs = batch_count // 2
     own_rows = model_width // batch_count
-    slots = lambda a: a.reshape(pairs, -1, own_rows, model_width)
-    dense_groups = [
-        ([slots(outer_keep)], [slots(outer_send)]),
-        ([inner_keep], [inner_send]),
-        ([slots(out_keep)], [slots(out_send)]),
-    ]
+    dense_groups = [([keep], [send])]
     usual = batch_count == 8
 
     def backward(molecule, held, sums, after, before=None):
@@ -1326,18 +1315,18 @@
     cross2 = cross_sum([cross2], [near2], "cross_second", after[-1:])
     far2 = swap(cross2, "rows", 2)
     after = [far0, cross2]
-    part = shape_of((pairs, 1, own_rows, model_width), BF16)
-    parts = small_call(
+    part = shape_of((pairs, 3, own_rows, model_width), BF16)
+    send, keep = small_call(
         functools.partial(weight_kernel, 4, STAGES),
         place,
         [s[3] for s in stages] + grads0 + grads1 + grads2 + grads3,
-        [part] * 6,
+        [part] * 2,
         "attention_weights",
         after,
         scratch=[pltpu.VMEM((pairs, 2, own_rows, model_width), F32)],
         mib=14,
     )
-    groups = [([parts[2 * i + 1]], [parts[2 * i]]) for i in range(3)]
+    groups = [([keep], [send])]
     matrix = shape_of((own_rows, model_width), F32)
     ratio = inner_weight.shape[1] // model_width
     vector = shape_of((own_rows,), F32)

time: 135 us -> 134 us (level)
  starting transfers between devices: 36.8 us -> 28.2 us
  waiting for transfers between devices: 33.7 us -> 40 us
    ppermute x30 -> x26, starting transfers between devices: 36.8 us -> 28.2 us  [swap(): return lax.ppermute(value, axis, [(i, i ^ mask) for i in range(size)])]
    ppermute x30 -> x26, waiting for transfers between devices: 33.7 us -> 40 us  [swap(): return lax.ppermute(value, axis, [(i, i ^ mask) for i in range(size)])]
    pallas_call x1, Pallas kernels: 3.86 us -> 5.43 us  [load(): pl.pallas_call(functools.partial(load_kernel, count, starts), in_specs=[p...]
  transfers between devices with their start and end apart: 30 -> 26, of which waited for: 15 -> 13; matrix products, arithmetic and copies ran while one was open for 1% -> 1% of each run, Pallas kernels for 31% -> 32%
where the time goes in v7:
time: 134 us; the launch traced here: 133 us
  Pallas kernels  63.1 us (47%)
  waiting for transfers between devices  40 us (30%)
  starting transfers between devices  28.2 us (21%)
    ppermute x26, waiting for transfers between devices, swap(): return lax.ppermute(value, axis, [(i, i ^ mask) for i in range(size)])  40 us
    ppermute x26, starting transfers between devices, swap(): return lax.ppermute(value, axis, [(i, i ^ mask) for i in range(size)])  28.2 us
    pallas_call x4, Pallas kernels, attention_backward(): pl.pallas_call(functools.partial(backward_kernel, head_size, 4, first, ba...  22.9 us
    pallas_call x2, Pallas kernels, attention_forward(): pl.pallas_call(functools.partial(forward_kernel, head_size, 8, first, len...  14.7 us
    pallas_call x14, Pallas kernels, small_call(): pl.pallas_call(body, grid_spec=pltpu.PrefetchScalarGridSpec(num_scalar_pr...  9.78 us
    pallas_call x1, Pallas kernels, dense(): pl.pallas_call(functools.partial(dense_kernel, len(mixed)), grid_spec=plt...  7.61 us
    pallas_call x1, Pallas kernels, load(): pl.pallas_call(functools.partial(load_kernel, count, starts), in_specs=[p...  5.43 us
    pallas_call x1, Pallas kernels, near_half(): pl.pallas_call(functools.partial(near_half_kernel, head_size, stages, len...  2.71 us
  transfers between devices with their start and end apart: 26, of which 13 were waited for; matrix products, arithmetic and copies ran while one was open for 1% of the time, Pallas kernels for 32%

profile of v7, /device:TPU:0, one launch (start us, length us, event | category | flops | bytes accessed | tf_op | source)
XLA Modules:
  0.0 133.4 jit_solution(13003692965421430245)
XLA Ops:
  0.7 3.1 %collective-permute-start.2 = (bf16[4,64,512]{2,1,0:T(8,128)(2,1)}, bf16[4,64,512]{2,1,0:T(8,128)(2,1)S(1)}, u32[]{:S(2)}, u32[]{:S(2)}) collective-permute-start(bf16[4,64,512]{2,1,0:T(8,128)(2,1)} %refs_12_.5), channel_id=1, source_target_pairs={{0,1},{1,0},{2,3},{3,2},{4,5},{5,4},{6,7},{7,6},{8,9},{9,8},{10,11... | collective-permute-start | bytes 786440 | tf_op jit(solution)/shard_map/ppermute | solution.py:780
  4.7 2.5 %collective-permute-start.1 = (bf16[2,64,512]{2,1,0:T(8,128)(2,1)S(1)}, bf16[2,64,512]{2,1,0:T(8,128)(2,1)S(1)}, u32[]{:S(2)}, u32[]{:S(2)}) collective-permute-start(bf16[2,64,512]{2,1,0:T(8,128)(2,1)S(1)} %slice.3), channel_id=1, source_target_pairs={{0,3},{1,2},{2,1},{3,0},{4,7},{5,6},{6,5},{7,4},{8,11},{9,10},{10,... | collective-permute-start | bytes 393224 | tf_op jit(solution)/shard_map/ppermute | solution.py:780
  7.5 5.4 %load_first.1 = (bf16[4,64,64,256]{3,2,1,0:T(8,128)(2,1)S(1)}, bf16[512,512]{1,0:T(8,128)(2,1)S(1)}, bf16[512,512]{1,0:T(8,128)(2,1)S(1)}, bf16[512,512]{1,0:T(8...) custom-call(bf16[4,64,64,256]{3,2,1,0:T(8,128)(2,1)} %refs_0_.1, ...), custom_call_target="tpu_custom_call" | custom-call | tf_op jit(solution)/shard_map/load_first/pallas_call | solution.py:98
  13.0 2.7 %near_half.1 = (bf16[2,256,512]{2,1,0:T(8,128)(2,1)S(1)}, bf16[2,256,512]{2,1,0:T(8,128)(2,1)S(1)}, bf16[2,4,256,128]{3,2,1,0:T(8,128)(2,1)S(1)}, bf16[2,4,256,2...) custom-call(s32[5]{0:T(128)S(1)} %stack.23.refs_17_.place_ref.refs_0, ...), custom_call_target="tpu_custom_call" | custom-call | tf_op jit(solution)/shard_map/near_half/pallas_call | solution.py:198
  15.7 5.0 %collective-permute-start.4 = (bf16[2,64,512]{2,1,0:T(8,128)(2,1)S(1)}, bf16[2,64,512]{2,1,0:T(8,128)(2,1)S(1)}, u32[]{:S(2)}, u32[]{:S(2)}) collective-permute-start(bf16[2,64,512]{2,1,0:T(8,128)(2,1)S(1)} %get-tuple-element.155), channel_id=1, source_target_pairs={{0,3},{1,2},{2,1},{3,0},{4,7},{5,6},{6,5},{7,4},{8,11},{9,10},{10,... | collective-permute-start | bytes 393224 | tf_op jit(solution)/shard_map/ppermute | solution.py:780
  20.7 7.3 %attention_forward.2 = (bf16[4,64,64,256]{3,2,1,0:T(8,128)(2,1)}, bf16[2,64,64,256]{3,2,1,0:T(8,128)(2,1)S(1)}, f32[2,4,64,128]{3,2,1,0:T(8,128)S(1)}, f32[2,4,6...) custom-call(s32[5]{0:T(128)S(1)} %stack.23.refs_17_.place_ref.refs_0, ...), custom_call_target="tpu_custom_call", output_to_operand_aliasing={{4}: (11, {}), {5}: (12, {}), {6}: (13, {}), {7}: (14, {})} | custom-call | flops 1610612736 | bytes 12582912 | tf_op jit(solution)/shard_map/attention_forward/pallas_call | solution.py:321
  28.1 2.2 %collective-permute-done.3.two_ref = bf16[2,64,512]{2,1,0:T(8,128)(2,1)S(1)} collective-permute-done((bf16[2,64,512]{2,1,0:T(8,128)(2,1)S(1)}, bf16[2,64,512]{2,1,0:T(8,128)(2,1)S(1)}, u32[]{:S(2)}, u32[]{:S(2)}) %collective-permute-start.3) | collective-permute-done | bytes 131104 | tf_op jit(solution)/shard_map/ppermute | solution.py:780
  30.2 7.3 %attention_forward.3 = (bf16[4,64,64,256]{3,2,1,0:T(8,128)(2,1)}, bf16[2,64,64,256]{3,2,1,0:T(8,128)(2,1)S(1)}, f32[2,4,64,128]{3,2,1,0:T(8,128)S(1)}, f32[2,4,6...) custom-call(s32[5]{0:T(128)S(1)} %stack.23.refs_17_.place_ref.refs_0, ...), custom_call_target="tpu_custom_call", output_to_operand_aliasing={{4}: (11, {}), {5}: (12, {}), {6}: (13, {}), {7}: (14, {}),... | custom-call | flops 1610612736 | bytes 12582912 | tf_op jit(solution)/shard_map/attention_forward/pallas_call | solution.py:321
  37.6 7.6 %dense.1 = (bf16[4,64,512]{2,1,0:T(8,128)(2,1)}, bf16[4,9,64,512]{3,2,1,0:T(8,128)(2,1)S(1)}, bf16[4,9,64,512]{3,2,1,0:T(8,128)(2,1)S(1)}, f32[4,64,512]{2,1,0:T...) custom-call(s32[5]{0:T(128)S(1)} %stack.23.refs_17_.place_ref.refs_0_, ...), custom_call_target="tpu_custom_call" | custom-call | flops 3221225472 | bytes 12582912 | tf_op jit(solution)/shard_map/dense/pallas_call | solution.py:531
  45.8 5.7 %attention_backward.4 = (bf16[4,64,64,256]{3,2,1,0:T(8,128)(2,1)}, bf16[2,1,64,512]{3,2,1,0:T(8,128)(2,1)S(1)}, bf16[1,64,512]{2,1,0:T(8,128)(2,1)S(1)}, f32[1,6...) custom-call(s32[5]{0:T(128)S(1)} %stack.23.refs_17_.place_ref.refs_0, ...), custom_call_target="tpu_custom_call" | custom-call | flops 1610612736 | bytes 6291456 | tf_op jit(solution)/shard_map/attention_backward/pallas_call | solution.py:729
  51.5 1.0 dense_sum_core.1
  52.6 1.6 %collective-permute-start.9 = (bf16[1160,256]{1,0:T(8,128)(2,1)S(1)}, bf16[1160,256]{1,0:T(8,128)(2,1)S(1)}, u32[]{:S(2)}, u32[]{:S(2)}) collective-permute-start(bf16[1160,256]{1,0:T(8,128)(2,1)S(1)} %get-tuple-element.205), channel_id=1, source_target_pairs={{0,16},{4,20},{8,24},{12,28},{16,0},{20,4},{24,8},{28,12},{1,17},{... | collective-permute-start | bytes 1781768 | tf_op jit(solution)/shard_map/ppermute | solution.py:780
  54.1 1.5 %collective-permute-start.8 = (bf16[1160,256]{1,0:T(8,128)(2,1)S(1)}, bf16[1160,256]{1,0:T(8,128)(2,1)S(1)}, u32[]{:S(2)}, u32[]{:S(2)}) collective-permute-start(bf16[1160,256]{1,0:T(8,128)(2,1)S(1)} %get-tuple-element.187.refs_2_), channel_id=1, source_target_pairs={{0,8},{4,12},{8,0},{12,4},{16,24},{20,28},{24,16},{28,20},{1,9},{5... | collective-permute-start | bytes 1781768 | tf_op jit(solution)/shard_map/ppermute | solution.py:780
  55.6 5.7 %attention_backward.5 = (bf16[4,64,64,256]{3,2,1,0:T(8,128)(2,1)}, bf16[2,2,64,512]{3,2,1,0:T(8,128)(2,1)S(1)}, bf16[1,64,512]{2,1,0:T(8,128)(2,1)S(1)}, f32[1,6...) custom-call(s32[5]{0:T(128)S(1)} %stack.23.refs_17_.place_ref.refs_0, ...), custom_call_target="tpu_custom_call", output_to_operand_aliasing={{0}: (13, {}), {4}: (14, {})} | custom-call | flops 1610612736 | bytes 6291456 | tf_op jit(solution)/shard_map/attention_backward/pallas_call | solution.py:729
  61.4 5.7 %attention_backward.6 = (bf16[4,64,64,256]{3,2,1,0:T(8,128)(2,1)}, bf16[2,1,64,512]{3,2,1,0:T(8,128)(2,1)S(1)}, bf16[1,64,512]{2,1,0:T(8,128)(2,1)S(1)}, f32[1,6...) custom-call(s32[5]{0:T(128)S(1)} %stack.23.refs_17_.place_ref.refs_0, ...), custom_call_target="tpu_custom_call", output_to_operand_aliasing={{0}: (13, {}), {4}: (14, {})} | custom-call | flops 1610612736 | bytes 6291456 | tf_op jit(solution)/shard_map/attention_backward/pallas_call | solution.py:729
  68.0 1.2 collective-permute-done.8.refs_2_
  70.1 1.5 %collective-permute-start.12 = (bf16[584,256]{1,0:T(8,128)(2,1)S(1)}, bf16[584,256]{1,0:T(8,128)(2,1)S(1)}, u32[]{:S(2)}, u32[]{:S(2)}) collective-permute-start(bf16[584,256]{1,0:T(8,128)(2,1)S(1)} %get-tuple-element.212), channel_id=1, source_target_pairs={{0,8},{4,12},{8,0},{12,4},{16,24},{20,28},{24,16},{28,20},{1,9},{5... | collective-permute-start | bytes 897032 | tf_op jit(solution)/shard_map/ppermute | solution.py:780
  72.2 3.3 %collective-permute-start.14 = (bf16[2,64,512]{2,1,0:T(8,128)(2,1)S(1)}, bf16[2,64,512]{2,1,0:T(8,128)(2,1)S(1)}, u32[]{:S(2)}, u32[]{:S(2)}) collective-permute-start(bf16[2,64,512]{2,1,0:T(8,128)(2,1)S(1)} %cross_first.1.refs_2_), channel_id=1, source_target_pairs={{0,2},{1,3},{2,0},{3,1},{4,6},{5,7},{6,4},{7,5},{8,10},{9,11},{10,... | collective-permute-start | bytes 393224 | tf_op jit(solution)/shard_map/ppermute | solution.py:780
  75.4 5.7 %attention_backward.7 = (bf16[4,64,64,256]{3,2,1,0:T(8,128)(2,1)}, bf16[2,1,64,512]{3,2,1,0:T(8,128)(2,1)S(1)}, bf16[1,64,512]{2,1,0:T(8,128)(2,1)S(1)}, f32[1,6...) custom-call(s32[5]{0:T(128)S(1)} %stack.23.refs_17_.place_ref.refs_0, ...), custom_call_target="tpu_custom_call", output_to_operand_aliasing={{0}: (13, {}), {4}: (14, {})} | custom-call | flops 1610612736 | bytes 6291456 | tf_op jit(solution)/shard_map/attention_backward/pallas_call | solution.py:729
  82.0 2.1 %attention_weights.1 = (bf16[4,3,64,512]{3,2,1,0:T(8,128)(2,1)S(1)}, bf16[4,3,64,512]{3,2,1,0:T(8,128)(2,1)S(1)}) custom-call(s32[5]{0:T(128)S(1)} %stack.23.refs_17_.place_ref.refs_0_, bf16[2,256,512]{2,1,0:T(8,128)(2,1)S(1)} %get-tuple-element.219.refs_1_, bf16[2,256,512]{2,1,0:T(8,128)(2,1)S(1)} %get-tuple-element.220.refs_2_, ...), custom_call_target="tpu_custom_call" | custom-call | bytes 4980736 | tf_op jit(solution)/shard_map/attention_weights/pallas_call | solution.py:943
  84.6 1.8 %collective-permute-done.17.refs_4_ = f32[8,512]{1,0:T(8,128)S(1)} collective-permute-done((f32[8,512]{1,0:T(8,128)S(1)}, f32[8,512]{1,0:T(8,128)S(1)}, u32[]{:S(2)}, u32[]{:S(2)}) %collective-permute-start.17) | collective-permute-done | bytes 16416 | tf_op jit(solution)/shard_map/ppermute | solution.py:780
  87.8 1.5 %collective-permute-start.19 = (bf16[392,256]{1,0:T(8,128)(2,1)S(1)}, bf16[392,256]{1,0:T(8,128)(2,1)S(1)}, u32[]{:S(2)}, u32[]{:S(2)}) collective-permute-start(bf16[392,256]{1,0:T(8,128)(2,1)S(1)} %get-tuple-element.239), channel_id=1, source_target_pairs={{0,16},{4,20},{8,24},{12,28},{16,0},{20,4},{24,8},{28,12},{1,17},{... | collective-permute-start | bytes 602120 | tf_op jit(solution)/shard_map/ppermute | solution.py:780
  90.0 4.3 %collective-permute-done.18.refs_2_ = bf16[392,256]{1,0:T(8,128)(2,1)S(1)} collective-permute-done((bf16[392,256]{1,0:T(8,128)(2,1)S(1)}, bf16[392,256]{1,0:T(8,128)(2,1)S(1)}, u32[]{:S(2)}, u32[]{:S(2)}) %collective-permute-start.18) | collective-permute-done | bytes 200736 | tf_op jit(solution)/shard_map/ppermute | solution.py:780
  95.9 2.2 %collective-permute-done.13.refs_2_.refs_7_ = bf16[432,512]{1,0:T(8,128)(2,1)S(1)} collective-permute-done((bf16[432,512]{1,0:T(8,128)(2,1)S(1)}, bf16[432,512]{1,0:T(8,128)(2,1)S(1)}, u32[]{:S(2)}, u32[]{:S(2)}) %collective-permute-start.13) | collective-permute-done | bytes 442400 | tf_op jit(solution)/shard_map/ppermute | solution.py:780
  98.8 1.2 collective-permute-start.20
  100.5 1.5 %collective-permute-start.21 = (bf16[200,256]{1,0:T(8,128)(2,1)S(1)}, bf16[200,256]{1,0:T(8,128)(2,1)S(1)}, u32[]{:S(2)}, u32[]{:S(2)}) collective-permute-start(bf16[200,256]{1,0:T(8,128)(2,1)S(1)} %get-tuple-element.241.refs_4_), channel_id=1, source_target_pairs={{0,16},{4,20},{8,24},{12,28},{16,0},{20,4},{24,8},{28,12},{1,17},{... | collective-permute-start | bytes 307208 | tf_op jit(solution)/shard_map/ppermute | solution.py:780
  102.1 2.6 %collective-permute-done.22.refs_3_ = bf16[200,256]{1,0:T(8,128)(2,1)S(1)} collective-permute-done((bf16[200,256]{1,0:T(8,128)(2,1)S(1)}, bf16[200,256]{1,0:T(8,128)(2,1)S(1)}, u32[]{:S(2)}, u32[]{:S(2)}) %collective-permute-start.22) | collective-permute-done | bytes 102432 | tf_op jit(solution)/shard_map/ppermute | solution.py:780
  105.9 12.9 %collective-permute-done.23.refs_1_ = bf16[200,512]{1,0:T(8,128)(2,1)S(1)} collective-permute-done((bf16[200,512]{1,0:T(8,128)(2,1)S(1)}, bf16[200,512]{1,0:T(8,128)(2,1)S(1)}, u32[]{:S(2)}, u32[]{:S(2)}) %collective-permute-start.23) | collective-permute-done | bytes 204832 | tf_op jit(solution)/shard_map/ppermute | solution.py:780
  120.0 1.1 first_norm_backward.1
  121.2 8.1 %collective-permute-done.24.refs_2_ = bf16[200,512]{1,0:T(8,128)(2,1)S(1)} collective-permute-done((bf16[200,512]{1,0:T(8,128)(2,1)S(1)}, bf16[200,512]{1,0:T(8,128)(2,1)S(1)}, u32[]{:S(2)}, u32[]{:S(2)}) %collective-permute-start.24) | collective-permute-done | bytes 204832 | tf_op jit(solution)/shard_map/ppermute | solution.py:780
  129.3 2.2 %collective-permute-done.25.refs_4_ = bf16[304,512]{1,0:T(8,128)(2,1)S(1)} collective-permute-done((bf16[304,512]{1,0:T(8,128)(2,1)S(1)}, bf16[304,512]{1,0:T(8,128)(2,1)S(1)}, u32[]{:S(2)}, u32[]{:S(2)}) %collective-permute-start.25) | collective-permute-done | bytes 311328 | tf_op jit(solution)/shard_map/ppermute | solution.py:780
  131.5 1.8 %finish.1 = (f32[64,512]{1,0:T(8,128)}, f32[64,512]{1,0:T(8,128)}, f32[64,512]{1,0:T(8,128)}, f32[256,512]{1,0:T(8,128)}, f32[64,2048]{1,0:T(8,128)}, /*index=5*...) custom-call(s32[5]{0:T(128)S(1)} %stack.23.refs_17_.place_ref.refs_0, ...), custom_call_target="tpu_custom_call" | custom-call | bytes 2608128 | tf_op jit(solution)/shard_map/finish/pallas_call | solution.py:943
  (49 shorter events, 12.8 us)
Async XLA Ops:
  0.7 12.3 %collective-permute-start.2 = (bf16[4,64,512]{2,1,0:T(8,128)(2,1)}, bf16[4,64,512]{2,1,0:T(8,128)(2,1)S(1)}, u32[]{:S(2)}, u32[]{:S(2)}) collective-permute-start(bf16[4,64,512]{2,1,0:T(8,128)(2,1)} %refs_12_.5), channel_id=1, source_target_pairs={{0,1},{1,0},{2,3},{3,2},{4,5},{5,4},{6,7},{7,6},{8,9},{9,8},{10,11... | collective-permute-start | bytes 786440 | tf_op jit(solution)/shard_map/ppermute | solution.py:780
  4.7 16.0 %collective-permute-start.1 = (bf16[2,64,512]{2,1,0:T(8,128)(2,1)S(1)}, bf16[2,64,512]{2,1,0:T(8,128)(2,1)S(1)}, u32[]{:S(2)}, u32[]{:S(2)}) collective-permute-start(bf16[2,64,512]{2,1,0:T(8,128)(2,1)S(1)} %slice.3), channel_id=1, source_target_pairs={{0,3},{1,2},{2,1},{3,0},{4,7},{5,6},{6,5},{7,4},{8,11},{9,10},{10,... | collective-permute-start | bytes 393224 | tf_op jit(solution)/shard_map/ppermute | solution.py:780
  7.2 13.5 %collective-permute-start = (bf16[2,64,512]{2,1,0:T(8,128)(2,1)S(1)}, bf16[2,64,512]{2,1,0:T(8,128)(2,1)S(1)}, u32[]{:S(2)}, u32[]{:S(2)}) collective-permute-start(bf16[2,64,512]{2,1,0:T(8,128)(2,1)S(1)} %slice.3), channel_id=1, source_target_pairs={{0,2},{1,3},{2,0},{3,1},{4,6},{5,7},{6,4},{7,5},{8,10},{9,11},{10,... | collective-permute-start | bytes 393224 | tf_op jit(solution)/shard_map/ppermute | solution.py:780
  7.5 13.2 %copy-start.1 = (s32[4]{0:T(128)S(1)}, s32[4]{0:T(128)}, u32[]{:S(2)}) copy-start(s32[4]{0:T(128)} %length_ref.3) | copy-start | bytes 52
  15.7 12.4 %collective-permute-start.4 = (bf16[2,64,512]{2,1,0:T(8,128)(2,1)S(1)}, bf16[2,64,512]{2,1,0:T(8,128)(2,1)S(1)}, u32[]{:S(2)}, u32[]{:S(2)}) collective-permute-start(bf16[2,64,512]{2,1,0:T(8,128)(2,1)S(1)} %get-tuple-element.155), channel_id=1, source_target_pairs={{0,3},{1,2},{2,1},{3,0},{4,7},{5,6},{6,5},{7,4},{8,11},{9,10},{10,... | collective-permute-start | bytes 393224 | tf_op jit(solution)/shard_map/ppermute | solution.py:780
  20.7 9.5 %collective-permute-start.3 = (bf16[2,64,512]{2,1,0:T(8,128)(2,1)S(1)}, bf16[2,64,512]{2,1,0:T(8,128)(2,1)S(1)}, u32[]{:S(2)}, u32[]{:S(2)}) collective-permute-start(bf16[2,64,512]{2,1,0:T(8,128)(2,1)S(1)} %get-tuple-element.155), channel_id=1, source_target_pairs={{0,2},{1,3},{2,0},{3,1},{4,6},{5,7},{6,4},{7,5},{8,10},{9,11},{10,... | collective-permute-start | bytes 393224 | tf_op jit(solution)/shard_map/ppermute | solution.py:780
  30.2 7.3 %copy-start = (bf16[4,64,512]{2,1,0:T(8,128)(2,1)S(1)}, bf16[4,64,512]{2,1,0:T(8,128)(2,1)}, u32[]{:S(2)}) copy-start(bf16[4,64,512]{2,1,0:T(8,128)(2,1)} %refs_12_.5) | copy-start | bytes 786436
  45.2 6.3 %collective-permute-start.5 = (bf16[4,9,64,512]{3,2,1,0:T(8,128)(2,1)S(1)}, bf16[4,9,64,512]{3,2,1,0:T(8,128)(2,1)S(1)}, u32[]{:S(2)}, u32[]{:S(2)}) collective-permute-start(bf16[4,9,64,512]{3,2,1,0:T(8,128)(2,1)S(1)} %get-tuple-element.185), channel_id=1, source_target_pairs={{0,4},{4,0},{8,12},{12,8},{16,20},{20,16},{24,28},{28,24},{1,5},{5... | collective-permute-start | bytes 7077896 | tf_op jit(solution)/shard_map/ppermute | solution.py:780
  45.3 6.2 %collective-permute-start.6 = (f32[8,512]{1,0:T(8,128)S(1)}, f32[8,512]{1,0:T(8,128)S(1)}, u32[]{:S(2)}, u32[]{:S(2)}) collective-permute-start(f32[8,512]{1,0:T(8,128)S(1)} %get-tuple-element.186.refs_3_), channel_id=1, source_target_pairs={{0,4},{4,0},{8,12},{12,8},{16,20},{20,16},{24,28},{28,24},{1,5},{5... | collective-permute-start | bytes 49160 | tf_op jit(solution)/shard_map/ppermute | solution.py:780
  52.6 15.5 %collective-permute-start.9 = (bf16[1160,256]{1,0:T(8,128)(2,1)S(1)}, bf16[1160,256]{1,0:T(8,128)(2,1)S(1)}, u32[]{:S(2)}, u32[]{:S(2)}) collective-permute-start(bf16[1160,256]{1,0:T(8,128)(2,1)S(1)} %get-tuple-element.205), channel_id=1, source_target_pairs={{0,16},{4,20},{8,24},{12,28},{16,0},{20,4},{24,8},{28,12},{1,17},{... | collective-permute-start | bytes 1781768 | tf_op jit(solution)/shard_map/ppermute | solution.py:780
  54.1 15.1 %collective-permute-start.8 = (bf16[1160,256]{1,0:T(8,128)(2,1)S(1)}, bf16[1160,256]{1,0:T(8,128)(2,1)S(1)}, u32[]{:S(2)}, u32[]{:S(2)}) collective-permute-start(bf16[1160,256]{1,0:T(8,128)(2,1)S(1)} %get-tuple-element.187.refs_2_), channel_id=1, source_target_pairs={{0,8},{4,12},{8,0},{12,4},{16,24},{20,28},{24,16},{28,20},{1,9},{5... | collective-permute-start | bytes 1781768 | tf_op jit(solution)/shard_map/ppermute | solution.py:780
  61.4 10.8 %collective-permute-start.7 = (bf16[2,2,64,512]{3,2,1,0:T(8,128)(2,1)S(1)}, bf16[2,2,64,512]{3,2,1,0:T(8,128)(2,1)S(1)}, u32[]{:S(2)}, u32[]{:S(2)}) collective-permute-start(bf16[2,2,64,512]{3,2,1,0:T(8,128)(2,1)S(1)} %get-tuple-element.202), channel_id=1, source_target_pairs={{0,1},{1,0},{2,3},{3,2},{4,5},{5,4},{6,7},{7,6},{8,9},{9,8},{10,11... | collective-permute-start | bytes 786440 | tf_op jit(solution)/shard_map/ppermute | solution.py:780
  70.1 11.1 %collective-permute-start.12 = (bf16[584,256]{1,0:T(8,128)(2,1)S(1)}, bf16[584,256]{1,0:T(8,128)(2,1)S(1)}, u32[]{:S(2)}, u32[]{:S(2)}) collective-permute-start(bf16[584,256]{1,0:T(8,128)(2,1)S(1)} %get-tuple-element.212), channel_id=1, source_target_pairs={{0,8},{4,12},{8,0},{12,4},{16,24},{20,28},{24,16},{28,20},{1,9},{5... | collective-permute-start | bytes 897032 | tf_op jit(solution)/shard_map/ppermute | solution.py:780
  71.6 9.5 %collective-permute-start.11 = (bf16[584,256]{1,0:T(8,128)(2,1)S(1)}, bf16[584,256]{1,0:T(8,128)(2,1)S(1)}, u32[]{:S(2)}, u32[]{:S(2)}) collective-permute-start(bf16[584,256]{1,0:T(8,128)(2,1)S(1)} %get-tuple-element.207.refs_3_), channel_id=1, source_target_pairs={{0,16},{4,20},{8,24},{12,28},{16,0},{20,4},{24,8},{28,12},{1,17},{... | collective-permute-start | bytes 897032 | tf_op jit(solution)/shard_map/ppermute | solution.py:780
  72.1 9.8 %collective-permute-start.10 = (bf16[2,1,64,512]{3,2,1,0:T(8,128)(2,1)S(1)}, bf16[2,1,64,512]{3,2,1,0:T(8,128)(2,1)S(1)}, u32[]{:S(2)}, u32[]{:S(2)}) collective-permute-start(bf16[2,1,64,512]{3,2,1,0:T(8,128)(2,1)S(1)} %get-tuple-element.209), channel_id=1, source_target_pairs={{0,1},{1,0},{2,3},{3,2},{4,5},{5,4},{6,7},{7,6},{8,9},{9,8},{10,11... | collective-permute-start | bytes 393224 | tf_op jit(solution)/shard_map/ppermute | solution.py:780
  72.2 9.8 %collective-permute-start.14 = (bf16[2,64,512]{2,1,0:T(8,128)(2,1)S(1)}, bf16[2,64,512]{2,1,0:T(8,128)(2,1)S(1)}, u32[]{:S(2)}, u32[]{:S(2)}) collective-permute-start(bf16[2,64,512]{2,1,0:T(8,128)(2,1)S(1)} %cross_first.1.refs_2_), channel_id=1, source_target_pairs={{0,2},{1,3},{2,0},{3,1},{4,6},{5,7},{6,4},{7,5},{8,10},{9,11},{10,... | collective-permute-start | bytes 393224 | tf_op jit(solution)/shard_map/ppermute | solution.py:780
  84.1 2.4 %collective-permute-start.16 = (bf16[4,3,64,512]{3,2,1,0:T(8,128)(2,1)S(1)}, bf16[4,3,64,512]{3,2,1,0:T(8,128)(2,1)S(1)}, u32[]{:S(2)}, u32[]{:S(2)}) collective-permute-start(bf16[4,3,64,512]{3,2,1,0:T(8,128)(2,1)S(1)} %get-tuple-element.234), channel_id=1, source_target_pairs={{0,4},{4,0},{8,12},{12,8},{16,20},{20,16},{24,28},{28,24},{1,5},{5... | collective-permute-start | bytes 2359304 | tf_op jit(solution)/shard_map/ppermute | solution.py:780
  84.1 14.0 %collective-permute-start.13 = (bf16[432,512]{1,0:T(8,128)(2,1)S(1)}, bf16[432,512]{1,0:T(8,128)(2,1)S(1)}, u32[]{:S(2)}, u32[]{:S(2)}) collective-permute-start(bf16[432,512]{1,0:T(8,128)(2,1)S(1)} %get-tuple-element.215), channel_id=1, source_target_pairs={{0,1},{1,0},{2,3},{3,2},{4,5},{5,4},{6,7},{7,6},{8,9},{9,8},{10,11... | collective-permute-start | bytes 1327112 | tf_op jit(solution)/shard_map/ppermute | solution.py:780
  84.2 2.2 %collective-permute-start.17 = (f32[8,512]{1,0:T(8,128)S(1)}, f32[8,512]{1,0:T(8,128)S(1)}, u32[]{:S(2)}, u32[]{:S(2)}) collective-permute-start(f32[8,512]{1,0:T(8,128)S(1)} %get-tuple-element.235.refs_3_), channel_id=1, source_target_pairs={{0,4},{4,0},{8,12},{12,8},{16,20},{20,16},{24,28},{28,24},{1,5},{5... | collective-permute-start | bytes 49160 | tf_op jit(solution)/shard_map/ppermute | solution.py:780
  87.2 7.1 %collective-permute-start.18 = (bf16[392,256]{1,0:T(8,128)(2,1)S(1)}, bf16[392,256]{1,0:T(8,128)(2,1)S(1)}, u32[]{:S(2)}, u32[]{:S(2)}) collective-permute-start(bf16[392,256]{1,0:T(8,128)(2,1)S(1)} %get-tuple-element.237), channel_id=1, source_target_pairs={{0,8},{4,12},{8,0},{12,4},{16,24},{20,28},{24,16},{28,20},{1,9},{5... | collective-permute-start | bytes 602120 | tf_op jit(solution)/shard_map/ppermute | solution.py:780
  87.8 6.8 %collective-permute-start.19 = (bf16[392,256]{1,0:T(8,128)(2,1)S(1)}, bf16[392,256]{1,0:T(8,128)(2,1)S(1)}, u32[]{:S(2)}, u32[]{:S(2)}) collective-permute-start(bf16[392,256]{1,0:T(8,128)(2,1)S(1)} %get-tuple-element.239), channel_id=1, source_target_pairs={{0,16},{4,20},{8,24},{12,28},{16,0},{20,4},{24,8},{28,12},{1,17},{... | collective-permute-start | bytes 602120 | tf_op jit(solution)/shard_map/ppermute | solution.py:780
  89.3 6.6 %collective-permute-start.15 = (bf16[1,64,512]{2,1,0:T(8,128)(2,1)S(1)}, bf16[1,64,512]{2,1,0:T(8,128)(2,1)S(1)}, u32[]{:S(2)}, u32[]{:S(2)}) collective-permute-start(bf16[1,64,512]{2,1,0:T(8,128)(2,1)S(1)} %cross_second.1.refs_16_), channel_id=1, source_target_pairs={{0,2},{1,3},{2,0},{3,1},{4,6},{5,7},{6,4},{7,5},{8,10},{9,11},{10,... | collective-permute-start | bytes 196616 | tf_op jit(solution)/shard_map/ppermute | solution.py:780
  98.8 20.1 %collective-permute-start.20 = (bf16[368,512]{1,0:T(8,128)(2,1)S(1)}, bf16[368,512]{1,0:T(8,128)(2,1)S(1)}, u32[]{:S(2)}, u32[]{:S(2)}) collective-permute-start(bf16[368,512]{1,0:T(8,128)(2,1)S(1)} %dense_near_sum.1.refs_5_.refs_0_), channel_id=1, source_target_pairs={{0,2},{1,3},{2,0},{3,1},{4,6},{5,7},{6,4},{7,5},{8,10},{9,11},{10,... | collective-permute-start | bytes 1130504 | tf_op jit(solution)/shard_map/ppermute | solution.py:780
  100.0 4.7 %collective-permute-start.22 = (bf16[200,256]{1,0:T(8,128)(2,1)S(1)}, bf16[200,256]{1,0:T(8,128)(2,1)S(1)}, u32[]{:S(2)}, u32[]{:S(2)}) collective-permute-start(bf16[200,256]{1,0:T(8,128)(2,1)S(1)} %get-tuple-element.245), channel_id=1, source_target_pairs={{0,8},{4,12},{8,0},{12,4},{16,24},{20,28},{24,16},{28,20},{1,9},{5... | collective-permute-start | bytes 307208 | tf_op jit(solution)/shard_map/ppermute | solution.py:780
  100.5 4.7 %collective-permute-start.21 = (bf16[200,256]{1,0:T(8,128)(2,1)S(1)}, bf16[200,256]{1,0:T(8,128)(2,1)S(1)}, u32[]{:S(2)}, u32[]{:S(2)}) collective-permute-start(bf16[200,256]{1,0:T(8,128)(2,1)S(1)} %get-tuple-element.241.refs_4_), channel_id=1, source_target_pairs={{0,16},{4,20},{8,24},{12,28},{16,0},{20,4},{24,8},{28,12},{1,17},{... | collective-permute-start | bytes 307208 | tf_op jit(solution)/shard_map/ppermute | solution.py:780
  105.3 13.5 %collective-permute-start.23 = (bf16[200,512]{1,0:T(8,128)(2,1)S(1)}, bf16[200,512]{1,0:T(8,128)(2,1)S(1)}, u32[]{:S(2)}, u32[]{:S(2)}) collective-permute-start(bf16[200,512]{1,0:T(8,128)(2,1)S(1)} %tail_sum_second.1.refs_0_), channel_id=1, source_target_pairs={{0,1},{1,0},{2,3},{3,2},{4,5},{5,4},{6,7},{7,6},{8,9},{9,8},{10,11... | collective-permute-start | bytes 614408 | tf_op jit(solution)/shard_map/ppermute | solution.py:780
  118.9 12.5 %collective-permute-start.25 = (bf16[304,512]{1,0:T(8,128)(2,1)S(1)}, bf16[304,512]{1,0:T(8,128)(2,1)S(1)}, u32[]{:S(2)}, u32[]{:S(2)}) collective-permute-start(bf16[304,512]{1,0:T(8,128)(2,1)S(1)} %dense_far_sum.1.refs_16_.refs_3_), channel_id=1, source_target_pairs={{0,1},{1,0},{2,3},{3,2},{4,5},{5,4},{6,7},{7,6},{8,9},{9,8},{10,11... | collective-permute-start | bytes 933896 | tf_op jit(solution)/shard_map/ppermute | solution.py:780
  119.0 10.3 %collective-permute-start.24 = (bf16[200,512]{1,0:T(8,128)(2,1)S(1)}, bf16[200,512]{1,0:T(8,128)(2,1)S(1)}, u32[]{:S(2)}, u32[]{:S(2)}) collective-permute-start(bf16[200,512]{1,0:T(8,128)(2,1)S(1)} %tail_near_sum.1.refs_2_.refs_1_), channel_id=1, source_target_pairs={{0,2},{1,3},{2,0},{3,1},{4,6},{5,7},{6,4},{7,5},{8,10},{9,11},{10,... | collective-permute-start | bytes 614408 | tf_op jit(solution)/shard_map/ppermute | solution.py:780

commit v8 on v7

--- a/solution.py
+++ b/solution.py
@@ -319,7 +319,7 @@
     operands += extra
     in_specs += [pl.BlockSpec(memory_space=pltpu.HBM)] * len(extra)
     outs = pl.pallas_call(
-        functools.partial(forward_kernel, head_size, 8, first, len(extra)),
+        functools.partial(forward_kernel, head_size, 4, first, len(extra)),
         grid_spec=pltpu.PrefetchScalarGridSpec(
             num_scalar_prefetch=2,
             grid=(count, groups),
@@ -623,7 +623,7 @@
         weights = weights_ref[molecule, there].reshape(chunk * rows, keys)
         cotangent = cotangent_ref[molecule + first, there].reshape(chunk * rows, keys)
         grad = (weights.astype(F32) * centred + cotangent.astype(F32)).astype(BF16)
-        pair_grad_ref[0, here] = grad.reshape(chunk, rows, keys)
+        pair_grad_ref[molecule + first, there] = grad.reshape(chunk, rows, keys)
         product = dot(grad, key)
         for t in range(chunk):
             total = jnp.where(lane == c + t, product[t * rows : (t + 1) * rows], total)
@@ -677,8 +677,6 @@
     count = 1
     groups = query.shape[1]
     model_width = groups * LANES
-    heads = LANES // head_size
-    pair_spec = pl.BlockSpec((1, heads, rows, keys), lambda m, g, *_: (m + first + base, g, 0, 0))
     elements = count * head_count * rows * keys
     operands = [
         place,
@@ -699,7 +697,7 @@
     if sums is not None:
         aliases = {start: 0, start + 1: 4}
         operands += [held, sums]
-        in_specs += [pl.BlockSpec(memory_space=pl.ANY), near_spec()]
+        in_specs += [near_spec(), near_spec()]
     operands += list(after)
     in_specs += [pl.BlockSpec(memory_space=pl.ANY)] * len(after)
     joined = before is not None
@@ -707,7 +705,7 @@
         operands.append(before)
         in_specs.append(near_spec())
     out_shape = [
-        shape_of(cotangent.shape, BF16),
+        near(cotangent.shape, BF16),
         near((2, 1 + joined, rows, model_width), BF16),
         near((count, rows, model_width), BF16),
         near((count, rows, model_width), F32),
@@ -717,7 +715,7 @@
         near((count, keys, model_width), BF16),
     ]
     out_specs = [
-        pair_spec,
+        near_spec(),
         near_spec(),
         near_spec(),
         near_spec(),
@@ -775,6 +773,25 @@
         keep_ref[:, j] = total_ref[:, core].astype(BF16)
 
 
+def store_kernel(source_ref, *refs):
+    target_ref, semaphore = refs[-2:]
+    copy = pltpu.make_async_copy(source_ref, target_ref, semaphore)
+    copy.start()
+    copy.wait()
+
+
+def store(array, after):
+    return pl.pallas_call(
+        store_kernel,
+        in_specs=[near_spec()] + [pl.BlockSpec(memory_space=pl.ANY)] * len(after),
+        out_specs=pl.BlockSpec(memory_space=pltpu.HBM),
+        out_shape=pltpu.HBM(array.shape, array.dtype),
+        scratch_shapes=[pltpu.SemaphoreType.DMA],
+        compiler_params=params(),
+        name="store",
+    )(array, *after)
+
+
 def swap(value, axis, mask):
     size = lax.axis_size(axis)
     return lax.ppermute(value, axis, [(i, i ^ mask) for i in range(size)])
@@ -862,27 +879,21 @@
     total_ref[size : size + VECTOR_ROWS] = vectors.astype(BF16)
 
 
-def third_cut_kernel(place_ref, left_x_ref, came_x_ref, left_y_ref, came_y_ref, vectors_ref, *refs):
-    more_ref, total_ref, sent_ref = refs
-    third_sum_kernel(left_x_ref, came_x_ref, left_y_ref, came_y_ref, vectors_ref, total_ref)
-    filled = left_x_ref.shape[0] + VECTOR_ROWS
+def third_cut_kernel(place_ref, *refs):
+    third_sum_kernel(*refs[:-1])
+    total_ref, sent_ref = refs[-2:]
+    filled = refs[0].shape[0] + VECTOR_ROWS
     if filled < total_ref.shape[0]:
         total_ref[filled:] = jnp.zeros((total_ref.shape[0] - filled, total_ref.shape[1]), BF16)
-    half = total_ref.shape[0] // 2
-    rows = more_ref.shape[2]
+    half = sent_ref.shape[0]
     away = pl.multiple_of((1 - (place_ref[1] & 1)) * half, half)
-    sent_ref[:half] = total_ref[pl.ds(away, half)]
-    for i in range(2):
-        sent_ref[half + i * rows : half + (i + 1) * rows] = more_ref[i, 0]
-
-
-def near_sum_kernel(place_ref, total_ref, came_ref, second_ref, out_ref):
-    half = total_ref.shape[0] // 2
-    rows = second_ref.shape[1]
+    sent_ref[...] = total_ref[pl.ds(away, half)]
+
+
+def near_sum_kernel(place_ref, total_ref, came_ref, out_ref):
+    half = came_ref.shape[0]
     mine = total_ref[pl.ds(pl.multiple_of((place_ref[1] & 1) * half, half), half)]
-    out_ref[:half] = (mine.astype(F32) + came_ref[:half].astype(F32)).astype(BF16)
-    second = second_ref[0].astype(F32) + came_ref[half + rows : half + 2 * rows].astype(F32)
-    out_ref[half : half + rows] = second.astype(BF16)
+    out_ref[...] = (mine.astype(F32) + came_ref[...].astype(F32)).astype(BF16)
 
 
 def far_sum_kernel(left_ref, right_ref, out_ref):
@@ -1000,17 +1011,14 @@
     return small_call(third_sum_kernel, None, pieces, [shape], name + "_sum_second", after)[0]
 
 
-def sum_second_cut(place, pieces, more, name, after=()):
+def sum_second_cut(place, pieces, name, after=()):
     size, half = pieces[0].shape
     rows = -(-(size + VECTOR_ROWS) // 32) * 32
     total, sent = small_call(
         third_cut_kernel,
         place,
-        list(pieces) + [more],
-        [
-            shape_of((rows, 2 * half), BF16),
-            shape_of((rows // 2 + 2 * more.shape[2], 2 * half), BF16),
-        ],
+        pieces,
+        [shape_of((rows, 2 * half), BF16), shape_of((rows // 2, 2 * half), BF16)],
         name + "_sum_second",
         after,
     )
@@ -1300,21 +1308,15 @@
     near1 = swap(near1, "rows", 1)
     pair_grad, near2, cross2, own2, sums, *grads2 = backward(2, pair_grad, sums, [own1])
     near2 = swap(near2, "rows", 1)
-    after = [own2]
-    if usual:
-        dense_pieces, held = sum_first(place, dense_pieces, "dense", after)
-        after = [held]
-    cross0 = cross_sum([cross0, cross1], [near1], "cross_first", after)
+    cross0 = cross_sum([cross0, cross1], [near1], "cross_first", (own2,))
     far0 = swap(cross0, "rows", 2)
     pair_grad, near3, cross3, own3, tail_vectors, *grads3 = backward(3, pair_grad, sums, [cross0])
+    near3 = swap(near3, "rows", 1)
     owns = [own0, own1, own2, own3]
-    after = [far0, near2]
+    after = [far0]
     if usual:
-        dense_total, came = sum_second_cut(place, dense_pieces, near3, "dense", (own3,))
-        after.append(dense_total)
-    cross2 = cross_sum([cross2], [near2], "cross_second", after[-1:])
-    far2 = swap(cross2, "rows", 2)
-    after = [far0, cross2]
+        dense_pieces, held = sum_first(place, dense_pieces, "dense", (own3,))
+        after.append(held)
     part = shape_of((pairs, 3, own_rows, model_width), BF16)
     send, keep = small_call(
         functools.partial(weight_kernel, 4, STAGES),
@@ -1332,17 +1334,14 @@
     vector = shape_of((own_rows,), F32)
     finish = (atoms, line(first_gain), line(first_shift), grad_middle)
     if usual:
-        pieces, _ = sum_core(place, groups, tail_vectors, "tail")
-        pieces, held = sum_first(place, pieces, "tail")
+        pieces, held = sum_core(place, groups, tail_vectors, "tail")
+        cross2 = cross_sum([cross2, cross3], [near2, near3], "cross_second", (held,))
+        far2 = swap(cross2, "rows", 2)
+        dense_total, came = sum_second_cut(place, dense_pieces, "dense", (cross2,))
+        pieces, held = sum_first(place, pieces, "tail", (dense_total,))
         start = dense_total.shape[0] // 2
-        first_rows = slice(start, start + rows)
         mine = small_call(
-            near_sum_kernel,
-            place,
-            [dense_total, came, cross3],
-            [shape_of((start + rows, model_width), BF16)],
-            "dense_near_sum",
-            (held, far2),
+            near_sum_kernel, place, [dense_total, came], [came], "dense_near_sum", (held, far2)
         )[0]
         far = swap(mine, "rows", 2)
         total = sum_second(pieces, "tail", (mine,))
@@ -1352,10 +1351,11 @@
         part = shape_of((start, model_width), BF16)
         mine = small_call(far_sum_kernel, None, [mine, far], [part], "dense_far_sum", (total,))[0]
         other = swap(mine, "rows", 1)
+        pair_grad = store(pair_grad, (mine,))
         atoms_grad = first_norm_backward(
             owns,
-            [(near1, (0, 0)), (near1, (0, 1)), (near2, (0, 0)), (came, first_rows)],
-            [(far0, 0), (far0, 1), (far2, 0), (far, first_rows)],
+            [(near1, (0, 0)), (near1, (0, 1)), (near2, (0, 0)), (near3, (0, 0))],
+            [(far0, 0), (far0, 1), (far2, 0), (far2, 1)],
             finish,
             (mine,),
         )
@@ -1381,12 +1381,12 @@
         query_grad, key_grad, value_grad, outer_grad, inner_grad, out_grad = outs[:6]
         tail_parts, dense_parts = outs[6:10], outs[10:]
     else:
-        near3 = swap(near3, "rows", 1)
-        far3 = swap(cross_sum([cross3], [near3], "cross_third"), "rows", 2)
+        pair_grad = store(pair_grad, ())
+        far2 = swap(cross_sum([cross2, cross3], [near2, near3], "cross_second"), "rows", 2)
         atoms_grad = first_norm_backward(
             owns,
             [(near1, (0, 0)), (near1, (0, 1)), (near2, (0, 0)), (near3, (0, 0))],
-            [(far0, 0), (far0, 1), (far2, 0), (far3, 0)],
+            [(far0, 0), (far0, 1), (far2, 0), (far2, 1)],
             finish,
         )
         total, tail_vectors = batch_slices_any(groups, tail_vectors)

time: 134 us -> 132 us (0.985)
  waiting for transfers between devices: 40 us -> 31.6 us
  starting transfers between devices: 28.2 us -> 34.1 us
    ppermute x26 -> x27, waiting for transfers between devices: 40 us -> 31.6 us  [swap(): return lax.ppermute(value, axis, [(i, i ^ mask) for i in range(size)])]
    ppermute x26 -> x27, starting transfers between devices: 28.2 us -> 34.1 us  [swap(): return lax.ppermute(value, axis, [(i, i ^ mask) for i in range(size)])]
    pallas_call x2 -> x3, Pallas kernels: 14.7 us -> 18.2 us  [the longest x2 14.8 us: attention_forward(): pl.pallas_call(functools.partial(forward_kernel, head_size, 4, first, len...]
    pallas_call x4, Pallas kernels: 22.9 us -> 19.7 us  [attention_backward(): pl.pallas_call(functools.partial(backward_kernel, head_size, 4, first, ba...]
  transfers between devices with their start and end apart: 26 -> 27, of which waited for: 13 -> 13; matrix products, arithmetic and copies ran while one was open for 1% -> 1% of each run, Pallas kernels for 32% -> 32%
where the time goes in v8:
time: 132 us; the launch traced here: 131 us
  Pallas kernels  63.3 us (48%)
  starting transfers between devices  34.1 us (26%)
  waiting for transfers between devices  31.6 us (24%)
    ppermute x27, starting transfers between devices, swap(): return lax.ppermute(value, axis, [(i, i ^ mask) for i in range(size)])  34.1 us
    ppermute x27, waiting for transfers between devices, swap(): return lax.ppermute(value, axis, [(i, i ^ mask) for i in range(size)])  31.6 us
    pallas_call x4, Pallas kernels, attention_backward(): pl.pallas_call(functools.partial(backward_kernel, head_size, 4, first, ba...  19.7 us
    pallas_call x2, Pallas kernels, attention_forward(): pl.pallas_call(functools.partial(forward_kernel, head_size, 4, first, len...  14.8 us
    pallas_call x14, Pallas kernels, small_call(): pl.pallas_call(body, grid_spec=pltpu.PrefetchScalarGridSpec(num_scalar_pr...  9.79 us
    pallas_call x1, Pallas kernels, dense(): pl.pallas_call(functools.partial(dense_kernel, len(mixed)), grid_spec=plt...  7.5 us
    pallas_call x1, Pallas kernels, load(): pl.pallas_call(functools.partial(load_kernel, count, starts), in_specs=[p...  5.43 us
    pallas_call x1, Pallas kernels, store(): pl.pallas_call(store_kernel, in_specs=[near_spec()] + [pl.BlockSpec(memor...  3.4 us
  transfers between devices with their start and end apart: 27, of which 13 were waited for; matrix products, arithmetic and copies ran while one was open for 1% of the time, Pallas kernels for 32%

profile of v8, /device:TPU:0, one launch (start us, length us, event | category | flops | bytes accessed | tf_op | source)
XLA Modules:
  0.0 131.2 jit_solution(12459801741710284066)
XLA Ops:
  0.7 3.1 %collective-permute-start.2 = (bf16[4,64,512]{2,1,0:T(8,128)(2,1)}, bf16[4,64,512]{2,1,0:T(8,128)(2,1)S(1)}, u32[]{:S(2)}, u32[]{:S(2)}) collective-permute-start(bf16[4,64,512]{2,1,0:T(8,128)(2,1)} %refs_12_.5), channel_id=1, source_target_pairs={{0,1},{1,0},{2,3},{3,2},{4,5},{5,4},{6,7},{7,6},{8,9},{9,8},{10,11... | collective-permute-start | bytes 786440 | tf_op jit(solution)/shard_map/ppermute | solution.py:797
  4.7 2.5 %collective-permute-start.1 = (bf16[2,64,512]{2,1,0:T(8,128)(2,1)S(1)}, bf16[2,64,512]{2,1,0:T(8,128)(2,1)S(1)}, u32[]{:S(2)}, u32[]{:S(2)}) collective-permute-start(bf16[2,64,512]{2,1,0:T(8,128)(2,1)S(1)} %slice.3), channel_id=1, source_target_pairs={{0,3},{1,2},{2,1},{3,0},{4,7},{5,6},{6,5},{7,4},{8,11},{9,10},{10,... | collective-permute-start | bytes 393224 | tf_op jit(solution)/shard_map/ppermute | solution.py:797
  7.5 5.4 %load_first.1 = (bf16[4,64,64,256]{3,2,1,0:T(8,128)(2,1)S(1)}, bf16[512,512]{1,0:T(8,128)(2,1)S(1)}, bf16[512,512]{1,0:T(8,128)(2,1)S(1)}, bf16[512,512]{1,0:T(8...) custom-call(bf16[4,64,64,256]{3,2,1,0:T(8,128)(2,1)} %refs_0_.1, ...), custom_call_target="tpu_custom_call" | custom-call | tf_op jit(solution)/shard_map/load_first/pallas_call | solution.py:98
  13.0 2.7 %near_half.1 = (bf16[2,256,512]{2,1,0:T(8,128)(2,1)S(1)}, bf16[2,256,512]{2,1,0:T(8,128)(2,1)S(1)}, bf16[2,4,256,128]{3,2,1,0:T(8,128)(2,1)S(1)}, bf16[2,4,256,2...) custom-call(s32[5]{0:T(128)S(1)} %stack.23.refs_17_.place_ref.refs_0, ...), custom_call_target="tpu_custom_call" | custom-call | tf_op jit(solution)/shard_map/near_half/pallas_call | solution.py:198
  15.7 5.0 %collective-permute-start.4 = (bf16[2,64,512]{2,1,0:T(8,128)(2,1)S(1)}, bf16[2,64,512]{2,1,0:T(8,128)(2,1)S(1)}, u32[]{:S(2)}, u32[]{:S(2)}) collective-permute-start(bf16[2,64,512]{2,1,0:T(8,128)(2,1)S(1)} %get-tuple-element.155), channel_id=1, source_target_pairs={{0,3},{1,2},{2,1},{3,0},{4,7},{5,6},{6,5},{7,4},{8,11},{9,10},{10,... | collective-permute-start | bytes 393224 | tf_op jit(solution)/shard_map/ppermute | solution.py:797
  20.7 7.4 %attention_forward.2 = (bf16[4,64,64,256]{3,2,1,0:T(8,128)(2,1)}, bf16[2,64,64,256]{3,2,1,0:T(8,128)(2,1)S(1)}, f32[2,4,64,128]{3,2,1,0:T(8,128)S(1)}, f32[2,4,6...) custom-call(s32[5]{0:T(128)S(1)} %stack.23.refs_17_.place_ref.refs_0, ...), custom_call_target="tpu_custom_call", output_to_operand_aliasing={{4}: (11, {}), {5}: (12, {}), {6}: (13, {}), {7}: (14, {})} | custom-call | flops 1610612736 | bytes 12582912 | tf_op jit(solution)/shard_map/attention_forward/pallas_call | solution.py:321
  28.1 2.1 %collective-permute-done.3.two_ref = bf16[2,64,512]{2,1,0:T(8,128)(2,1)S(1)} collective-permute-done((bf16[2,64,512]{2,1,0:T(8,128)(2,1)S(1)}, bf16[2,64,512]{2,1,0:T(8,128)(2,1)S(1)}, u32[]{:S(2)}, u32[]{:S(2)}) %collective-permute-start.3) | collective-permute-done | bytes 131104 | tf_op jit(solution)/shard_map/ppermute | solution.py:797
  30.2 7.4 %attention_forward.3 = (bf16[4,64,64,256]{3,2,1,0:T(8,128)(2,1)}, bf16[2,64,64,256]{3,2,1,0:T(8,128)(2,1)S(1)}, f32[2,4,64,128]{3,2,1,0:T(8,128)S(1)}, f32[2,4,6...) custom-call(s32[5]{0:T(128)S(1)} %stack.23.refs_17_.place_ref.refs_0, ...), custom_call_target="tpu_custom_call", output_to_operand_aliasing={{4}: (11, {}), {5}: (12, {}), {6}: (13, {}), {7}: (14, {}),... | custom-call | flops 1610612736 | bytes 12582912 | tf_op jit(solution)/shard_map/attention_forward/pallas_call | solution.py:321
  37.6 7.5 %dense.1 = (bf16[4,64,512]{2,1,0:T(8,128)(2,1)}, bf16[4,9,64,512]{3,2,1,0:T(8,128)(2,1)S(1)}, bf16[4,9,64,512]{3,2,1,0:T(8,128)(2,1)S(1)}, f32[4,64,512]{2,1,0:T...) custom-call(s32[5]{0:T(128)S(1)} %stack.23.refs_17_.place_ref.refs_0_, ...), custom_call_target="tpu_custom_call" | custom-call | flops 3221225472 | bytes 12582912 | tf_op jit(solution)/shard_map/dense/pallas_call | solution.py:531
  45.7 4.9 %attention_backward.4 = (bf16[4,64,64,256]{3,2,1,0:T(8,128)(2,1)S(1)}, bf16[2,1,64,512]{3,2,1,0:T(8,128)(2,1)S(1)}, bf16[1,64,512]{2,1,0:T(8,128)(2,1)S(1)}, f32...) custom-call(s32[5]{0:T(128)S(1)} %stack.23.refs_17_.place_ref.refs_0, ...), custom_call_target="tpu_custom_call" | custom-call | flops 1610612736 | bytes 6291456 | tf_op jit(solution)/shard_map/attention_backward/pallas_call | solution.py:727
  51.7 1.6 %collective-permute-start.12 = (bf16[1160,256]{1,0:T(8,128)(2,1)S(1)}, bf16[1160,256]{1,0:T(8,128)(2,1)S(1)}, u32[]{:S(2)}, u32[]{:S(2)}) collective-permute-start(bf16[1160,256]{1,0:T(8,128)(2,1)S(1)} %get-tuple-element.224), channel_id=1, source_target_pairs={{0,16},{4,20},{8,24},{12,28},{16,0},{20,4},{24,8},{28,12},{1,17},{... | collective-permute-start | bytes 1781768 | tf_op jit(solution)/shard_map/ppermute | solution.py:797
  53.3 1.5 %collective-permute-start.11 = (bf16[1160,256]{1,0:T(8,128)(2,1)S(1)}, bf16[1160,256]{1,0:T(8,128)(2,1)S(1)}, u32[]{:S(2)}, u32[]{:S(2)}) collective-permute-start(bf16[1160,256]{1,0:T(8,128)(2,1)S(1)} %get-tuple-element.187.refs_2_), channel_id=1, source_target_pairs={{0,8},{4,12},{8,0},{12,4},{16,24},{20,28},{24,16},{28,20},{1,9},{5... | collective-permute-start | bytes 1781768 | tf_op jit(solution)/shard_map/ppermute | solution.py:797
  54.8 4.9 %attention_backward.5 = (bf16[4,64,64,256]{3,2,1,0:T(8,128)(2,1)S(1)}, bf16[2,2,64,512]{3,2,1,0:T(8,128)(2,1)S(1)}, bf16[1,64,512]{2,1,0:T(8,128)(2,1)S(1)}, f32...) custom-call(s32[5]{0:T(128)S(1)} %stack.23.refs_17_.place_ref.refs_0, ...), custom_call_target="tpu_custom_call", output_to_operand_aliasing={{0}: (13, {}), {4}: (14, {})} | custom-call | flops 1610612736 | bytes 6291456 | tf_op jit(solution)/shard_map/attention_backward/pallas_call | solution.py:727
  59.7 4.9 %attention_backward.6 = (bf16[4,64,64,256]{3,2,1,0:T(8,128)(2,1)S(1)}, bf16[2,1,64,512]{3,2,1,0:T(8,128)(2,1)S(1)}, bf16[1,64,512]{2,1,0:T(8,128)(2,1)S(1)}, f32...) custom-call(s32[5]{0:T(128)S(1)} %stack.23.refs_17_.place_ref.refs_0, ...), custom_call_target="tpu_custom_call", output_to_operand_aliasing={{0}: (13, {}), {4}: (14, {})} | custom-call | flops 1610612736 | bytes 6291456 | tf_op jit(solution)/shard_map/attention_backward/pallas_call | solution.py:727
  64.6 2.8 %collective-permute-done.7.refs_2_.refs_4_.refs_5_ = bf16[2,2,64,512]{3,2,1,0:T(8,128)(2,1)S(1)} collective-permute-done((bf16[2,2,64,512]{3,2,1,0:T(8,128)(2,1)S(1)}, bf16[2,2,64,512]{3,2,1,0:T(8,128)(2,1)S(1)}, u32[]{:S(2)}, u32[]{:S(2)}) %collective-permute-start.7) | collective-permute-done | bytes 262176 | tf_op jit(solution)/shard_map/ppermute | solution.py:797
  67.5 1.5 %collective-permute-start.10 = (bf16[2,64,512]{2,1,0:T(8,128)(2,1)S(1)}, bf16[2,64,512]{2,1,0:T(8,128)(2,1)S(1)}, u32[]{:S(2)}, u32[]{:S(2)}) collective-permute-start(bf16[2,64,512]{2,1,0:T(8,128)(2,1)S(1)} %cross_first.1.refs_2_), channel_id=1, source_target_pairs={{0,2},{1,3},{2,0},{3,1},{4,6},{5,7},{6,4},{7,5},{8,10},{9,11},{10,... | collective-permute-start | bytes 393224 | tf_op jit(solution)/shard_map/ppermute | solution.py:797
  69.0 5.1 %attention_backward.7 = (bf16[4,64,64,256]{3,2,1,0:T(8,128)(2,1)S(1)}, bf16[2,1,64,512]{3,2,1,0:T(8,128)(2,1)S(1)}, bf16[1,64,512]{2,1,0:T(8,128)(2,1)S(1)}, f32...) custom-call(s32[5]{0:T(128)S(1)} %stack.23.refs_17_.place_ref.refs_0, ...), custom_call_target="tpu_custom_call", output_to_operand_aliasing={{0}: (13, {}), {4}: (14, {})} | custom-call | flops 1610612736 | bytes 6291456 | tf_op jit(solution)/shard_map/attention_backward/pallas_call | solution.py:727
  75.3 2.1 %attention_weights.1 = (bf16[4,3,64,512]{3,2,1,0:T(8,128)(2,1)S(1)}, bf16[4,3,64,512]{3,2,1,0:T(8,128)(2,1)S(1)}) custom-call(s32[5]{0:T(128)S(1)} %stack.23.refs_17_.place_ref.refs_0_, bf16[2,256,512]{2,1,0:T(8,128)(2,1)S(1)} %copy-done.2, bf16[2,256,512]{2,1,0:T(8,128)(2,1)S(1)} %get-tuple-element.209.refs_2_, ...), custom_call_target="tpu_custom_call" | custom-call | bytes 4980736 | tf_op jit(solution)/shard_map/attention_weights/pallas_call | solution.py:954
  81.9 3.0 %collective-permute-done.8.refs_2_.refs_6_ = bf16[2,1,64,512]{3,2,1,0:T(8,128)(2,1)S(1)} collective-permute-done((bf16[2,1,64,512]{3,2,1,0:T(8,128)(2,1)S(1)}, bf16[2,1,64,512]{3,2,1,0:T(8,128)(2,1)S(1)}, u32[]{:S(2)}, u32[]{:S(2)}) %collective-permute-start.8) | collective-permute-done | bytes 131104 | tf_op jit(solution)/shard_map/ppermute | solution.py:797
  84.9 2.4 %collective-permute-done.9.refs_3_.refs_7_ = bf16[2,1,64,512]{3,2,1,0:T(8,128)(2,1)S(1)} collective-permute-done((bf16[2,1,64,512]{3,2,1,0:T(8,128)(2,1)S(1)}, bf16[2,1,64,512]{3,2,1,0:T(8,128)(2,1)S(1)}, u32[]{:S(2)}, u32[]{:S(2)}) %collective-permute-start.9) | collective-permute-done | bytes 131104 | tf_op jit(solution)/shard_map/ppermute | solution.py:797
  89.6 1.5 %collective-permute-start.20 = (bf16[392,256]{1,0:T(8,128)(2,1)S(1)}, bf16[392,256]{1,0:T(8,128)(2,1)S(1)}, u32[]{:S(2)}, u32[]{:S(2)}) collective-permute-start(bf16[392,256]{1,0:T(8,128)(2,1)S(1)} %get-tuple-element.240), channel_id=1, source_target_pairs={{0,16},{4,20},{8,24},{12,28},{16,0},{20,4},{24,8},{28,12},{1,17},{... | collective-permute-start | bytes 602120 | tf_op jit(solution)/shard_map/ppermute | solution.py:797
  92.6 1.8 %collective-permute-start.15 = (bf16[2,64,512]{2,1,0:T(8,128)(2,1)S(1)}, bf16[2,64,512]{2,1,0:T(8,128)(2,1)S(1)}, u32[]{:S(2)}, u32[]{:S(2)}) collective-permute-start(bf16[2,64,512]{2,1,0:T(8,128)(2,1)S(1)} %cross_second.1.refs_6_), channel_id=1, source_target_pairs={{0,2},{1,3},{2,0},{3,1},{4,6},{5,7},{6,4},{7,5},{8,10},{9,11},{10,... | collective-permute-start | bytes 393224 | tf_op jit(solution)/shard_map/ppermute | solution.py:797
  94.4 1.5 %collective-permute-done.20.refs_4_ = bf16[392,256]{1,0:T(8,128)(2,1)S(1)} collective-permute-done((bf16[392,256]{1,0:T(8,128)(2,1)S(1)}, bf16[392,256]{1,0:T(8,128)(2,1)S(1)}, u32[]{:S(2)}, u32[]{:S(2)}) %collective-permute-start.20) | collective-permute-done | bytes 200736 | tf_op jit(solution)/shard_map/ppermute | solution.py:797
  97.8 3.5 %collective-permute-done.15.refs_4_.refs_10_.refs_11_ = bf16[2,64,512]{2,1,0:T(8,128)(2,1)S(1)} collective-permute-done((bf16[2,64,512]{2,1,0:T(8,128)(2,1)S(1)}, bf16[2,64,512]{2,1,0:T(8,128)(2,1)S(1)}, u32[]{:S(2)}, u32[]{:S(2)}) %collective-permute-start.15) | collective-permute-done | bytes 131104 | tf_op jit(solution)/shard_map/ppermute | solution.py:797
  103.0 1.5 %collective-permute-start.23 = (bf16[200,256]{1,0:T(8,128)(2,1)S(1)}, bf16[200,256]{1,0:T(8,128)(2,1)S(1)}, u32[]{:S(2)}, u32[]{:S(2)}) collective-permute-start(bf16[200,256]{1,0:T(8,128)(2,1)S(1)} %get-tuple-element.245), channel_id=1, source_target_pairs={{0,8},{4,12},{8,0},{12,4},{16,24},{20,28},{24,16},{28,20},{1,9},{5... | collective-permute-start | bytes 307208 | tf_op jit(solution)/shard_map/ppermute | solution.py:797
  104.4 1.5 %collective-permute-start.22 = (bf16[200,256]{1,0:T(8,128)(2,1)S(1)}, bf16[200,256]{1,0:T(8,128)(2,1)S(1)}, u32[]{:S(2)}, u32[]{:S(2)}) collective-permute-start(bf16[200,256]{1,0:T(8,128)(2,1)S(1)} %get-tuple-element.242.refs_3_), channel_id=1, source_target_pairs={{0,16},{4,20},{8,24},{12,28},{16,0},{20,4},{24,8},{28,12},{1,17},{... | collective-permute-start | bytes 307208 | tf_op jit(solution)/shard_map/ppermute | solution.py:797
  106.0 1.6 %collective-permute-done.23.refs_3_ = bf16[200,256]{1,0:T(8,128)(2,1)S(1)} collective-permute-done((bf16[200,256]{1,0:T(8,128)(2,1)S(1)}, bf16[200,256]{1,0:T(8,128)(2,1)S(1)}, u32[]{:S(2)}, u32[]{:S(2)}) %collective-permute-start.23) | collective-permute-done | bytes 102432 | tf_op jit(solution)/shard_map/ppermute | solution.py:797
  107.6 1.5 %collective-permute-done.22.refs_1_ = bf16[200,256]{1,0:T(8,128)(2,1)S(1)} collective-permute-done((bf16[200,256]{1,0:T(8,128)(2,1)S(1)}, bf16[200,256]{1,0:T(8,128)(2,1)S(1)}, u32[]{:S(2)}, u32[]{:S(2)}) %collective-permute-start.22) | collective-permute-done | bytes 102432 | tf_op jit(solution)/shard_map/ppermute | solution.py:797
  110.1 9.2 %collective-permute-done.24.refs_1_ = bf16[200,512]{1,0:T(8,128)(2,1)S(1)} collective-permute-done((bf16[200,512]{1,0:T(8,128)(2,1)S(1)}, bf16[200,512]{1,0:T(8,128)(2,1)S(1)}, u32[]{:S(2)}, u32[]{:S(2)}) %collective-permute-start.24) | collective-permute-done | bytes 204832 | tf_op jit(solution)/shard_map/ppermute | solution.py:797
  119.6 2.8 %collective-permute-start.25 = (bf16[200,512]{1,0:T(8,128)(2,1)S(1)}, bf16[200,512]{1,0:T(8,128)(2,1)S(1)}, u32[]{:S(2)}, u32[]{:S(2)}) collective-permute-start(bf16[200,512]{1,0:T(8,128)(2,1)S(1)} %tail_near_sum.1.refs_2_.refs_1_), channel_id=1, source_target_pairs={{0,2},{1,3},{2,0},{3,1},{4,6},{5,7},{6,4},{7,5},{8,10},{9,11},{10,... | collective-permute-start | bytes 614408 | tf_op jit(solution)/shard_map/ppermute | solution.py:797
  122.4 3.4 %store.1 = bf16[4,64,64,256]{3,2,1,0:T(8,128)(2,1)} custom-call(bf16[4,64,64,256]{3,2,1,0:T(8,128)(2,1)S(1)} %get-tuple-element.247.source_ref, bf16[304,512]{1,0:T(8,128)(2,1)S(1)} %dense_far_sum.1.refs_16_.refs_0_.refs_3_), custom_call_target="tpu_custom_call" | custom-call | tf_op jit(solution)/shard_map/store/pallas_call | solution.py:784
  129.3 1.8 %finish.1 = (f32[64,512]{1,0:T(8,128)}, f32[64,512]{1,0:T(8,128)}, f32[64,512]{1,0:T(8,128)}, f32[256,512]{1,0:T(8,128)}, f32[64,2048]{1,0:T(8,128)}, /*index=5*...) custom-call(s32[5]{0:T(128)S(1)} %stack.23.refs_17_.place_ref.refs_0, ...), custom_call_target="tpu_custom_call" | custom-call | bytes 2608128 | tf_op jit(solution)/shard_map/finish/pallas_call | solution.py:954
  (56 shorter events, 20.6 us)
Async XLA Ops:
  0.7 12.3 %collective-permute-start.2 = (bf16[4,64,512]{2,1,0:T(8,128)(2,1)}, bf16[4,64,512]{2,1,0:T(8,128)(2,1)S(1)}, u32[]{:S(2)}, u32[]{:S(2)}) collective-permute-start(bf16[4,64,512]{2,1,0:T(8,128)(2,1)} %refs_12_.5), channel_id=1, source_target_pairs={{0,1},{1,0},{2,3},{3,2},{4,5},{5,4},{6,7},{7,6},{8,9},{9,8},{10,11... | collective-permute-start | bytes 786440 | tf_op jit(solution)/shard_map/ppermute | solution.py:797
  4.7 16.0 %collective-permute-start.1 = (bf16[2,64,512]{2,1,0:T(8,128)(2,1)S(1)}, bf16[2,64,512]{2,1,0:T(8,128)(2,1)S(1)}, u32[]{:S(2)}, u32[]{:S(2)}) collective-permute-start(bf16[2,64,512]{2,1,0:T(8,128)(2,1)S(1)} %slice.3), channel_id=1, source_target_pairs={{0,3},{1,2},{2,1},{3,0},{4,7},{5,6},{6,5},{7,4},{8,11},{9,10},{10,... | collective-permute-start | bytes 393224 | tf_op jit(solution)/shard_map/ppermute | solution.py:797
  7.2 13.5 %collective-permute-start = (bf16[2,64,512]{2,1,0:T(8,128)(2,1)S(1)}, bf16[2,64,512]{2,1,0:T(8,128)(2,1)S(1)}, u32[]{:S(2)}, u32[]{:S(2)}) collective-permute-start(bf16[2,64,512]{2,1,0:T(8,128)(2,1)S(1)} %slice.3), channel_id=1, source_target_pairs={{0,2},{1,3},{2,0},{3,1},{4,6},{5,7},{6,4},{7,5},{8,10},{9,11},{10,... | collective-permute-start | bytes 393224 | tf_op jit(solution)/shard_map/ppermute | solution.py:797
  7.5 13.2 %copy-start.3 = (s32[4]{0:T(128)S(1)}, s32[4]{0:T(128)}, u32[]{:S(2)}) copy-start(s32[4]{0:T(128)} %length_ref.3) | copy-start | bytes 52
  15.7 12.4 %collective-permute-start.4 = (bf16[2,64,512]{2,1,0:T(8,128)(2,1)S(1)}, bf16[2,64,512]{2,1,0:T(8,128)(2,1)S(1)}, u32[]{:S(2)}, u32[]{:S(2)}) collective-permute-start(bf16[2,64,512]{2,1,0:T(8,128)(2,1)S(1)} %get-tuple-element.155), channel_id=1, source_target_pairs={{0,3},{1,2},{2,1},{3,0},{4,7},{5,6},{6,5},{7,4},{8,11},{9,10},{10,... | collective-permute-start | bytes 393224 | tf_op jit(solution)/shard_map/ppermute | solution.py:797
  20.7 9.5 %collective-permute-start.3 = (bf16[2,64,512]{2,1,0:T(8,128)(2,1)S(1)}, bf16[2,64,512]{2,1,0:T(8,128)(2,1)S(1)}, u32[]{:S(2)}, u32[]{:S(2)}) collective-permute-start(bf16[2,64,512]{2,1,0:T(8,128)(2,1)S(1)} %get-tuple-element.155), channel_id=1, source_target_pairs={{0,2},{1,3},{2,0},{3,1},{4,6},{5,7},{6,4},{7,5},{8,10},{9,11},{10,... | collective-permute-start | bytes 393224 | tf_op jit(solution)/shard_map/ppermute | solution.py:797
  28.1 9.5 %copy-start.1 = (bf16[2,256,512]{2,1,0:T(8,128)(2,1)}, bf16[2,256,512]{2,1,0:T(8,128)(2,1)S(1)}, u32[]{:S(2)}) copy-start(bf16[2,256,512]{2,1,0:T(8,128)(2,1)S(1)} %get-tuple-element.208.refs_1_) | copy-start | bytes 1572868
  30.2 7.4 %copy-start = (bf16[4,64,512]{2,1,0:T(8,128)(2,1)S(1)}, bf16[4,64,512]{2,1,0:T(8,128)(2,1)}, u32[]{:S(2)}) copy-start(bf16[4,64,512]{2,1,0:T(8,128)(2,1)} %refs_12_.5) | copy-start | bytes 786436
  45.1 5.5 %collective-permute-start.5 = (bf16[4,9,64,512]{3,2,1,0:T(8,128)(2,1)S(1)}, bf16[4,9,64,512]{3,2,1,0:T(8,128)(2,1)S(1)}, u32[]{:S(2)}, u32[]{:S(2)}) collective-permute-start(bf16[4,9,64,512]{3,2,1,0:T(8,128)(2,1)S(1)} %get-tuple-element.185), channel_id=1, source_target_pairs={{0,4},{4,0},{8,12},{12,8},{16,20},{20,16},{24,28},{28,24},{1,5},{5... | collective-permute-start | bytes 7077896 | tf_op jit(solution)/shard_map/ppermute | solution.py:797
  45.2 5.4 %collective-permute-start.6 = (f32[8,512]{1,0:T(8,128)S(1)}, f32[8,512]{1,0:T(8,128)S(1)}, u32[]{:S(2)}, u32[]{:S(2)}) collective-permute-start(f32[8,512]{1,0:T(8,128)S(1)} %get-tuple-element.186.refs_3_), channel_id=1, source_target_pairs={{0,4},{4,0},{8,12},{12,8},{16,20},{20,16},{24,28},{28,24},{1,5},{5... | collective-permute-start | bytes 49160 | tf_op jit(solution)/shard_map/ppermute | solution.py:797
  51.7 22.4 %collective-permute-start.12 = (bf16[1160,256]{1,0:T(8,128)(2,1)S(1)}, bf16[1160,256]{1,0:T(8,128)(2,1)S(1)}, u32[]{:S(2)}, u32[]{:S(2)}) collective-permute-start(bf16[1160,256]{1,0:T(8,128)(2,1)S(1)} %get-tuple-element.224), channel_id=1, source_target_pairs={{0,16},{4,20},{8,24},{12,28},{16,0},{20,4},{24,8},{28,12},{1,17},{... | collective-permute-start | bytes 1781768 | tf_op jit(solution)/shard_map/ppermute | solution.py:797
  53.3 20.8 %collective-permute-start.11 = (bf16[1160,256]{1,0:T(8,128)(2,1)S(1)}, bf16[1160,256]{1,0:T(8,128)(2,1)S(1)}, u32[]{:S(2)}, u32[]{:S(2)}) collective-permute-start(bf16[1160,256]{1,0:T(8,128)(2,1)S(1)} %get-tuple-element.187.refs_2_), channel_id=1, source_target_pairs={{0,8},{4,12},{8,0},{12,4},{16,24},{20,28},{24,16},{28,20},{1,9},{5... | collective-permute-start | bytes 1781768 | tf_op jit(solution)/shard_map/ppermute | solution.py:797
  59.7 7.8 %collective-permute-start.7 = (bf16[2,2,64,512]{3,2,1,0:T(8,128)(2,1)S(1)}, bf16[2,2,64,512]{3,2,1,0:T(8,128)(2,1)S(1)}, u32[]{:S(2)}, u32[]{:S(2)}) collective-permute-start(bf16[2,2,64,512]{3,2,1,0:T(8,128)(2,1)S(1)} %get-tuple-element.202), channel_id=1, source_target_pairs={{0,1},{1,0},{2,3},{3,2},{4,5},{5,4},{6,7},{7,6},{8,9},{9,8},{10,11... | collective-permute-start | bytes 786440 | tf_op jit(solution)/shard_map/ppermute | solution.py:797
  67.5 7.8 %collective-permute-start.10 = (bf16[2,64,512]{2,1,0:T(8,128)(2,1)S(1)}, bf16[2,64,512]{2,1,0:T(8,128)(2,1)S(1)}, u32[]{:S(2)}, u32[]{:S(2)}) collective-permute-start(bf16[2,64,512]{2,1,0:T(8,128)(2,1)S(1)} %cross_first.1.refs_2_), channel_id=1, source_target_pairs={{0,2},{1,3},{2,0},{3,1},{4,6},{5,7},{6,4},{7,5},{8,10},{9,11},{10,... | collective-permute-start | bytes 393224 | tf_op jit(solution)/shard_map/ppermute | solution.py:797
  69.0 6.2 %copy-start.2 = (bf16[2,256,512]{2,1,0:T(8,128)(2,1)S(1)}, bf16[2,256,512]{2,1,0:T(8,128)(2,1)}, u32[]{:S(2)}) copy-start(bf16[2,256,512]{2,1,0:T(8,128)(2,1)} %copy-done.1) | copy-start | bytes 1572868
  77.4 3.8 %collective-permute-start.13 = (bf16[4,3,64,512]{3,2,1,0:T(8,128)(2,1)S(1)}, bf16[4,3,64,512]{3,2,1,0:T(8,128)(2,1)S(1)}, u32[]{:S(2)}, u32[]{:S(2)}) collective-permute-start(bf16[4,3,64,512]{3,2,1,0:T(8,128)(2,1)S(1)} %get-tuple-element.228), channel_id=1, source_target_pairs={{0,4},{4,0},{8,12},{12,8},{16,20},{20,16},{24,28},{28,24},{1,5},{5... | collective-permute-start | bytes 2359304 | tf_op jit(solution)/shard_map/ppermute | solution.py:797
  77.5 9.9 %collective-permute-start.17 = (bf16[584,256]{1,0:T(8,128)(2,1)S(1)}, bf16[584,256]{1,0:T(8,128)(2,1)S(1)}, u32[]{:S(2)}, u32[]{:S(2)}) collective-permute-start(bf16[584,256]{1,0:T(8,128)(2,1)S(1)} %get-tuple-element.234), channel_id=1, source_target_pairs={{0,8},{4,12},{8,0},{12,4},{16,24},{20,28},{24,16},{28,20},{1,9},{5... | collective-permute-start | bytes 897032 | tf_op jit(solution)/shard_map/ppermute | solution.py:797
  78.1 9.3 %collective-permute-start.16 = (bf16[584,256]{1,0:T(8,128)(2,1)S(1)}, bf16[584,256]{1,0:T(8,128)(2,1)S(1)}, u32[]{:S(2)}, u32[]{:S(2)}) collective-permute-start(bf16[584,256]{1,0:T(8,128)(2,1)S(1)} %get-tuple-element.226.refs_16_), channel_id=1, source_target_pairs={{0,16},{4,20},{8,24},{12,28},{16,0},{20,4},{24,8},{28,12},{1,17},{... | collective-permute-start | bytes 897032 | tf_op jit(solution)/shard_map/ppermute | solution.py:797
  78.6 1.4 %collective-permute-start.14 = (f32[8,512]{1,0:T(8,128)S(1)}, f32[8,512]{1,0:T(8,128)S(1)}, u32[]{:S(2)}, u32[]{:S(2)}) collective-permute-start(f32[8,512]{1,0:T(8,128)S(1)} %get-tuple-element.229.refs_3_), channel_id=1, source_target_pairs={{0,4},{4,0},{8,12},{12,8},{16,20},{20,16},{24,28},{28,24},{1,5},{5... | collective-permute-start | bytes 49160 | tf_op jit(solution)/shard_map/ppermute | solution.py:797
  78.6 6.3 %collective-permute-start.8 = (bf16[2,1,64,512]{3,2,1,0:T(8,128)(2,1)S(1)}, bf16[2,1,64,512]{3,2,1,0:T(8,128)(2,1)S(1)}, u32[]{:S(2)}, u32[]{:S(2)}) collective-permute-start(bf16[2,1,64,512]{3,2,1,0:T(8,128)(2,1)S(1)} %get-tuple-element.204), channel_id=1, source_target_pairs={{0,1},{1,0},{2,3},{3,2},{4,5},{5,4},{6,7},{7,6},{8,9},{9,8},{10,11... | collective-permute-start | bytes 393224 | tf_op jit(solution)/shard_map/ppermute | solution.py:797
  80.0 7.3 %collective-permute-start.9 = (bf16[2,1,64,512]{3,2,1,0:T(8,128)(2,1)S(1)}, bf16[2,1,64,512]{3,2,1,0:T(8,128)(2,1)S(1)}, u32[]{:S(2)}, u32[]{:S(2)}) collective-permute-start(bf16[2,1,64,512]{3,2,1,0:T(8,128)(2,1)S(1)} %get-tuple-element.205), channel_id=1, source_target_pairs={{0,1},{1,0},{2,3},{3,2},{4,5},{5,4},{6,7},{7,6},{8,9},{9,8},{10,11... | collective-permute-start | bytes 393224 | tf_op jit(solution)/shard_map/ppermute | solution.py:797
  88.1 13.1 %collective-permute-start.18 = (bf16[304,512]{1,0:T(8,128)(2,1)S(1)}, bf16[304,512]{1,0:T(8,128)(2,1)S(1)}, u32[]{:S(2)}, u32[]{:S(2)}) collective-permute-start(bf16[304,512]{1,0:T(8,128)(2,1)S(1)} %get-tuple-element.237), channel_id=1, source_target_pairs={{0,1},{1,0},{2,3},{3,2},{4,5},{5,4},{6,7},{7,6},{8,9},{9,8},{10,11... | collective-permute-start | bytes 933896 | tf_op jit(solution)/shard_map/ppermute | solution.py:797
  89.6 6.3 %collective-permute-start.20 = (bf16[392,256]{1,0:T(8,128)(2,1)S(1)}, bf16[392,256]{1,0:T(8,128)(2,1)S(1)}, u32[]{:S(2)}, u32[]{:S(2)}) collective-permute-start(bf16[392,256]{1,0:T(8,128)(2,1)S(1)} %get-tuple-element.240), channel_id=1, source_target_pairs={{0,16},{4,20},{8,24},{12,28},{16,0},{20,4},{24,8},{28,12},{1,17},{... | collective-permute-start | bytes 602120 | tf_op jit(solution)/shard_map/ppermute | solution.py:797
  91.1 6.1 %collective-permute-start.19 = (bf16[392,256]{1,0:T(8,128)(2,1)S(1)}, bf16[392,256]{1,0:T(8,128)(2,1)S(1)}, u32[]{:S(2)}, u32[]{:S(2)}) collective-permute-start(bf16[392,256]{1,0:T(8,128)(2,1)S(1)} %get-tuple-element.230.refs_4_), channel_id=1, source_target_pairs={{0,8},{4,12},{8,0},{12,4},{16,24},{20,28},{24,16},{28,20},{1,9},{5... | collective-permute-start | bytes 602120 | tf_op jit(solution)/shard_map/ppermute | solution.py:797
  92.6 8.7 %collective-permute-start.15 = (bf16[2,64,512]{2,1,0:T(8,128)(2,1)S(1)}, bf16[2,64,512]{2,1,0:T(8,128)(2,1)S(1)}, u32[]{:S(2)}, u32[]{:S(2)}) collective-permute-start(bf16[2,64,512]{2,1,0:T(8,128)(2,1)S(1)} %cross_second.1.refs_6_), channel_id=1, source_target_pairs={{0,2},{1,3},{2,0},{3,1},{4,6},{5,7},{6,4},{7,5},{8,10},{9,11},{10,... | collective-permute-start | bytes 393224 | tf_op jit(solution)/shard_map/ppermute | solution.py:797
  101.9 17.5 %collective-permute-start.21 = (bf16[304,512]{1,0:T(8,128)(2,1)S(1)}, bf16[304,512]{1,0:T(8,128)(2,1)S(1)}, u32[]{:S(2)}, u32[]{:S(2)}) collective-permute-start(bf16[304,512]{1,0:T(8,128)(2,1)S(1)} %dense_near_sum.1.refs_5_.refs_0_), channel_id=1, source_target_pairs={{0,2},{1,3},{2,0},{3,1},{4,6},{5,7},{6,4},{7,5},{8,10},{9,11},{10,... | collective-permute-start | bytes 933896 | tf_op jit(solution)/shard_map/ppermute | solution.py:797
  103.0 4.7 %collective-permute-start.23 = (bf16[200,256]{1,0:T(8,128)(2,1)S(1)}, bf16[200,256]{1,0:T(8,128)(2,1)S(1)}, u32[]{:S(2)}, u32[]{:S(2)}) collective-permute-start(bf16[200,256]{1,0:T(8,128)(2,1)S(1)} %get-tuple-element.245), channel_id=1, source_target_pairs={{0,8},{4,12},{8,0},{12,4},{16,24},{20,28},{24,16},{28,20},{1,9},{5... | collective-permute-start | bytes 307208 | tf_op jit(solution)/shard_map/ppermute | solution.py:797
  104.4 4.7 %collective-permute-start.22 = (bf16[200,256]{1,0:T(8,128)(2,1)S(1)}, bf16[200,256]{1,0:T(8,128)(2,1)S(1)}, u32[]{:S(2)}, u32[]{:S(2)}) collective-permute-start(bf16[200,256]{1,0:T(8,128)(2,1)S(1)} %get-tuple-element.242.refs_3_), channel_id=1, source_target_pairs={{0,16},{4,20},{8,24},{12,28},{16,0},{20,4},{24,8},{28,12},{1,17},{... | collective-permute-start | bytes 307208 | tf_op jit(solution)/shard_map/ppermute | solution.py:797
  109.2 10.2 %collective-permute-start.24 = (bf16[200,512]{1,0:T(8,128)(2,1)S(1)}, bf16[200,512]{1,0:T(8,128)(2,1)S(1)}, u32[]{:S(2)}, u32[]{:S(2)}) collective-permute-start(bf16[200,512]{1,0:T(8,128)(2,1)S(1)} %tail_sum_second.1.refs_0_), channel_id=1, source_target_pairs={{0,1},{1,0},{2,3},{3,2},{4,5},{5,4},{6,7},{7,6},{8,9},{9,8},{10,11... | collective-permute-start | bytes 614408 | tf_op jit(solution)/shard_map/ppermute | solution.py:797
  119.5 9.8 %collective-permute-start.26 = (bf16[304,512]{1,0:T(8,128)(2,1)S(1)}, bf16[304,512]{1,0:T(8,128)(2,1)S(1)}, u32[]{:S(2)}, u32[]{:S(2)}) collective-permute-start(bf16[304,512]{1,0:T(8,128)(2,1)S(1)} %dense_far_sum.1.refs_16_.refs_0_.refs_3_), channel_id=1, source_target_pairs={{0,1},{1,0},{2,3},{3,2},{4,5},{5,4},{6,7},{7,6},{8,9},{9,8},{10,11... | collective-permute-start | bytes 933896 | tf_op jit(solution)/shard_map/ppermute | solution.py:797
  119.6 8.6 %collective-permute-start.25 = (bf16[200,512]{1,0:T(8,128)(2,1)S(1)}, bf16[200,512]{1,0:T(8,128)(2,1)S(1)}, u32[]{:S(2)}, u32[]{:S(2)}) collective-permute-start(bf16[200,512]{1,0:T(8,128)(2,1)S(1)} %tail_near_sum.1.refs_2_.refs_1_), channel_id=1, source_target_pairs={{0,2},{1,3},{2,0},{3,1},{4,6},{5,7},{6,4},{7,5},{8,10},{9,11},{10,... | collective-permute-start | bytes 614408 | tf_op jit(solution)/shard_map/ppermute | solution.py:797

commit v9 on v8

--- a/solution.py
+++ b/solution.py
@@ -877,14 +877,14 @@
     total_ref[:size, half:] = (left_y_ref[...] + came_y_ref[:size].astype(F32)).astype(BF16)
     vectors = vectors_ref[...].astype(F32) + get_vectors(came_x_ref, came_y_ref)
     total_ref[size : size + VECTOR_ROWS] = vectors.astype(BF16)
+    filled = size + VECTOR_ROWS
+    if filled < total_ref.shape[0]:
+        total_ref[filled:] = jnp.zeros((total_ref.shape[0] - filled, 2 * half), BF16)
 
 
 def third_cut_kernel(place_ref, *refs):
     third_sum_kernel(*refs[:-1])
     total_ref, sent_ref = refs[-2:]
-    filled = refs[0].shape[0] + VECTOR_ROWS
-    if filled < total_ref.shape[0]:
-        total_ref[filled:] = jnp.zeros((total_ref.shape[0] - filled, total_ref.shape[1]), BF16)
     half = sent_ref.shape[0]
     away = pl.multiple_of((1 - (place_ref[1] & 1)) * half, half)
     sent_ref[...] = total_ref[pl.ds(away, half)]
@@ -1007,7 +1007,8 @@
 
 def sum_second(pieces, name, after=()):
     size, half = pieces[0].shape
-    shape = shape_of((size + VECTOR_ROWS, 2 * half), BF16)
+    rows = -(-(size + VECTOR_ROWS) // 32) * 32
+    shape = shape_of((rows, 2 * half), BF16)
     return small_call(third_sum_kernel, None, pieces, [shape], name + "_sum_second", after)[0]
 
 

time: 132 us -> 131 us (level)
  transfers between devices with their start and end apart: 27 -> 27, of which waited for: 13 -> 13; matrix products, arithmetic and copies ran while one was open for 1% -> 1% of each run, Pallas kernels for 32% -> 33%
where the time goes in v9:
time: 131 us; the launch traced here: 130 us
  Pallas kernels  63.3 us (48%)
  starting transfers between devices  33.6 us (26%)
  waiting for transfers between devices  31.5 us (24%)
    ppermute x27, starting transfers between devices, swap(): return lax.ppermute(value, axis, [(i, i ^ mask) for i in range(size)])  33.6 us
    ppermute x27, waiting for transfers between devices, swap(): return lax.ppermute(value, axis, [(i, i ^ mask) for i in range(size)])  31.5 us
    pallas_call x4, Pallas kernels, attention_backward(): pl.pallas_call(functools.partial(backward_kernel, head_size, 4, first, ba...  19.7 us
    pallas_call x2, Pallas kernels, attention_forward(): pl.pallas_call(functools.partial(forward_kernel, head_size, 4, first, len...  14.8 us
    pallas_call x14, Pallas kernels, small_call(): pl.pallas_call(body, grid_spec=pltpu.PrefetchScalarGridSpec(num_scalar_pr...  9.76 us
    pallas_call x1, Pallas kernels, dense(): pl.pallas_call(functools.partial(dense_kernel, len(mixed)), grid_spec=plt...  7.5 us
    pallas_call x1, Pallas kernels, load(): pl.pallas_call(functools.partial(load_kernel, count, starts), in_specs=[p...  5.43 us
    pallas_call x1, Pallas kernels, store(): pl.pallas_call(store_kernel, in_specs=[near_spec()] + [pl.BlockSpec(memor...  3.4 us
  transfers between devices with their start and end apart: 27, of which 13 were waited for; matrix products, arithmetic and copies ran while one was open for 1% of the time, Pallas kernels for 33%

profile of v9, /device:TPU:0, one launch (start us, length us, event | category | flops | bytes accessed | tf_op | source)
XLA Modules:
  0.0 130.5 jit_solution(12907982272143921531)
XLA Ops:
  0.7 3.1 %collective-permute-start.2 = (bf16[4,64,512]{2,1,0:T(8,128)(2,1)}, bf16[4,64,512]{2,1,0:T(8,128)(2,1)S(1)}, u32[]{:S(2)}, u32[]{:S(2)}) collective-permute-start(bf16[4,64,512]{2,1,0:T(8,128)(2,1)} %refs_12_.5), channel_id=1, source_target_pairs={{0,1},{1,0},{2,3},{3,2},{4,5},{5,4},{6,7},{7,6},{8,9},{9,8},{10,11... | collective-permute-start | bytes 786440 | tf_op jit(solution)/shard_map/ppermute | solution.py:797
  4.7 2.5 %collective-permute-start.1 = (bf16[2,64,512]{2,1,0:T(8,128)(2,1)S(1)}, bf16[2,64,512]{2,1,0:T(8,128)(2,1)S(1)}, u32[]{:S(2)}, u32[]{:S(2)}) collective-permute-start(bf16[2,64,512]{2,1,0:T(8,128)(2,1)S(1)} %slice.3), channel_id=1, source_target_pairs={{0,3},{1,2},{2,1},{3,0},{4,7},{5,6},{6,5},{7,4},{8,11},{9,10},{10,... | collective-permute-start | bytes 393224 | tf_op jit(solution)/shard_map/ppermute | solution.py:797
  7.5 5.4 %load_first.1 = (bf16[4,64,64,256]{3,2,1,0:T(8,128)(2,1)S(1)}, bf16[512,512]{1,0:T(8,128)(2,1)S(1)}, bf16[512,512]{1,0:T(8,128)(2,1)S(1)}, bf16[512,512]{1,0:T(8...) custom-call(bf16[4,64,64,256]{3,2,1,0:T(8,128)(2,1)} %refs_0_.1, ...), custom_call_target="tpu_custom_call" | custom-call | tf_op jit(solution)/shard_map/load_first/pallas_call | solution.py:98
  13.0 2.7 %near_half.1 = (bf16[2,256,512]{2,1,0:T(8,128)(2,1)S(1)}, bf16[2,256,512]{2,1,0:T(8,128)(2,1)S(1)}, bf16[2,4,256,128]{3,2,1,0:T(8,128)(2,1)S(1)}, bf16[2,4,256,2...) custom-call(s32[5]{0:T(128)S(1)} %stack.23.refs_17_.place_ref.refs_0, ...), custom_call_target="tpu_custom_call" | custom-call | tf_op jit(solution)/shard_map/near_half/pallas_call | solution.py:198
  15.7 5.0 %collective-permute-start.4 = (bf16[2,64,512]{2,1,0:T(8,128)(2,1)S(1)}, bf16[2,64,512]{2,1,0:T(8,128)(2,1)S(1)}, u32[]{:S(2)}, u32[]{:S(2)}) collective-permute-start(bf16[2,64,512]{2,1,0:T(8,128)(2,1)S(1)} %get-tuple-element.155), channel_id=1, source_target_pairs={{0,3},{1,2},{2,1},{3,0},{4,7},{5,6},{6,5},{7,4},{8,11},{9,10},{10,... | collective-permute-start | bytes 393224 | tf_op jit(solution)/shard_map/ppermute | solution.py:797
  20.7 7.4 %attention_forward.2 = (bf16[4,64,64,256]{3,2,1,0:T(8,128)(2,1)}, bf16[2,64,64,256]{3,2,1,0:T(8,128)(2,1)S(1)}, f32[2,4,64,128]{3,2,1,0:T(8,128)S(1)}, f32[2,4,6...) custom-call(s32[5]{0:T(128)S(1)} %stack.23.refs_17_.place_ref.refs_0, ...), custom_call_target="tpu_custom_call", output_to_operand_aliasing={{4}: (11, {}), {5}: (12, {}), {6}: (13, {}), {7}: (14, {})} | custom-call | flops 1610612736 | bytes 12582912 | tf_op jit(solution)/shard_map/attention_forward/pallas_call | solution.py:321
  28.1 2.1 %collective-permute-done.3.two_ref = bf16[2,64,512]{2,1,0:T(8,128)(2,1)S(1)} collective-permute-done((bf16[2,64,512]{2,1,0:T(8,128)(2,1)S(1)}, bf16[2,64,512]{2,1,0:T(8,128)(2,1)S(1)}, u32[]{:S(2)}, u32[]{:S(2)}) %collective-permute-start.3) | collective-permute-done | bytes 131104 | tf_op jit(solution)/shard_map/ppermute | solution.py:797
  30.2 7.4 %attention_forward.3 = (bf16[4,64,64,256]{3,2,1,0:T(8,128)(2,1)}, bf16[2,64,64,256]{3,2,1,0:T(8,128)(2,1)S(1)}, f32[2,4,64,128]{3,2,1,0:T(8,128)S(1)}, f32[2,4,6...) custom-call(s32[5]{0:T(128)S(1)} %stack.23.refs_17_.place_ref.refs_0, ...), custom_call_target="tpu_custom_call", output_to_operand_aliasing={{4}: (11, {}), {5}: (12, {}), {6}: (13, {}), {7}: (14, {}),... | custom-call | flops 1610612736 | bytes 12582912 | tf_op jit(solution)/shard_map/attention_forward/pallas_call | solution.py:321
  37.6 7.5 %dense.1 = (bf16[4,64,512]{2,1,0:T(8,128)(2,1)}, bf16[4,9,64,512]{3,2,1,0:T(8,128)(2,1)S(1)}, bf16[4,9,64,512]{3,2,1,0:T(8,128)(2,1)S(1)}, f32[4,64,512]{2,1,0:T...) custom-call(s32[5]{0:T(128)S(1)} %stack.23.refs_17_.place_ref.refs_0_, ...), custom_call_target="tpu_custom_call" | custom-call | flops 3221225472 | bytes 12582912 | tf_op jit(solution)/shard_map/dense/pallas_call | solution.py:531
  45.7 4.9 %attention_backward.4 = (bf16[4,64,64,256]{3,2,1,0:T(8,128)(2,1)S(1)}, bf16[2,1,64,512]{3,2,1,0:T(8,128)(2,1)S(1)}, bf16[1,64,512]{2,1,0:T(8,128)(2,1)S(1)}, f32...) custom-call(s32[5]{0:T(128)S(1)} %stack.23.refs_17_.place_ref.refs_0, ...), custom_call_target="tpu_custom_call" | custom-call | flops 1610612736 | bytes 6291456 | tf_op jit(solution)/shard_map/attention_backward/pallas_call | solution.py:727
  51.7 1.6 %collective-permute-start.12 = (bf16[1160,256]{1,0:T(8,128)(2,1)S(1)}, bf16[1160,256]{1,0:T(8,128)(2,1)S(1)}, u32[]{:S(2)}, u32[]{:S(2)}) collective-permute-start(bf16[1160,256]{1,0:T(8,128)(2,1)S(1)} %get-tuple-element.224), channel_id=1, source_target_pairs={{0,16},{4,20},{8,24},{12,28},{16,0},{20,4},{24,8},{28,12},{1,17},{... | collective-permute-start | bytes 1781768 | tf_op jit(solution)/shard_map/ppermute | solution.py:797
  53.3 1.5 %collective-permute-start.11 = (bf16[1160,256]{1,0:T(8,128)(2,1)S(1)}, bf16[1160,256]{1,0:T(8,128)(2,1)S(1)}, u32[]{:S(2)}, u32[]{:S(2)}) collective-permute-start(bf16[1160,256]{1,0:T(8,128)(2,1)S(1)} %get-tuple-element.187.refs_2_), channel_id=1, source_target_pairs={{0,8},{4,12},{8,0},{12,4},{16,24},{20,28},{24,16},{28,20},{1,9},{5... | collective-permute-start | bytes 1781768 | tf_op jit(solution)/shard_map/ppermute | solution.py:797
  54.8 4.9 %attention_backward.5 = (bf16[4,64,64,256]{3,2,1,0:T(8,128)(2,1)S(1)}, bf16[2,2,64,512]{3,2,1,0:T(8,128)(2,1)S(1)}, bf16[1,64,512]{2,1,0:T(8,128)(2,1)S(1)}, f32...) custom-call(s32[5]{0:T(128)S(1)} %stack.23.refs_17_.place_ref.refs_0, ...), custom_call_target="tpu_custom_call", output_to_operand_aliasing={{0}: (13, {}), {4}: (14, {})} | custom-call | flops 1610612736 | bytes 6291456 | tf_op jit(solution)/shard_map/attention_backward/pallas_call | solution.py:727
  59.7 4.9 %attention_backward.6 = (bf16[4,64,64,256]{3,2,1,0:T(8,128)(2,1)S(1)}, bf16[2,1,64,512]{3,2,1,0:T(8,128)(2,1)S(1)}, bf16[1,64,512]{2,1,0:T(8,128)(2,1)S(1)}, f32...) custom-call(s32[5]{0:T(128)S(1)} %stack.23.refs_17_.place_ref.refs_0, ...), custom_call_target="tpu_custom_call", output_to_operand_aliasing={{0}: (13, {}), {4}: (14, {})} | custom-call | flops 1610612736 | bytes 6291456 | tf_op jit(solution)/shard_map/attention_backward/pallas_call | solution.py:727
  64.6 2.8 %collective-permute-done.7.refs_2_.refs_4_.refs_5_ = bf16[2,2,64,512]{3,2,1,0:T(8,128)(2,1)S(1)} collective-permute-done((bf16[2,2,64,512]{3,2,1,0:T(8,128)(2,1)S(1)}, bf16[2,2,64,512]{3,2,1,0:T(8,128)(2,1)S(1)}, u32[]{:S(2)}, u32[]{:S(2)}) %collective-permute-start.7) | collective-permute-done | bytes 262176 | tf_op jit(solution)/shard_map/ppermute | solution.py:797
  67.5 1.5 %collective-permute-start.10 = (bf16[2,64,512]{2,1,0:T(8,128)(2,1)S(1)}, bf16[2,64,512]{2,1,0:T(8,128)(2,1)S(1)}, u32[]{:S(2)}, u32[]{:S(2)}) collective-permute-start(bf16[2,64,512]{2,1,0:T(8,128)(2,1)S(1)} %cross_first.1.refs_2_), channel_id=1, source_target_pairs={{0,2},{1,3},{2,0},{3,1},{4,6},{5,7},{6,4},{7,5},{8,10},{9,11},{10,... | collective-permute-start | bytes 393224 | tf_op jit(solution)/shard_map/ppermute | solution.py:797
  69.0 5.1 %attention_backward.7 = (bf16[4,64,64,256]{3,2,1,0:T(8,128)(2,1)S(1)}, bf16[2,1,64,512]{3,2,1,0:T(8,128)(2,1)S(1)}, bf16[1,64,512]{2,1,0:T(8,128)(2,1)S(1)}, f32...) custom-call(s32[5]{0:T(128)S(1)} %stack.23.refs_17_.place_ref.refs_0, ...), custom_call_target="tpu_custom_call", output_to_operand_aliasing={{0}: (13, {}), {4}: (14, {})} | custom-call | flops 1610612736 | bytes 6291456 | tf_op jit(solution)/shard_map/attention_backward/pallas_call | solution.py:727
  75.3 2.1 %attention_weights.1 = (bf16[4,3,64,512]{3,2,1,0:T(8,128)(2,1)S(1)}, bf16[4,3,64,512]{3,2,1,0:T(8,128)(2,1)S(1)}) custom-call(s32[5]{0:T(128)S(1)} %stack.23.refs_17_.place_ref.refs_0_, bf16[2,256,512]{2,1,0:T(8,128)(2,1)S(1)} %copy-done.2, bf16[2,256,512]{2,1,0:T(8,128)(2,1)S(1)} %get-tuple-element.209.refs_2_, ...), custom_call_target="tpu_custom_call" | custom-call | bytes 4980736 | tf_op jit(solution)/shard_map/attention_weights/pallas_call | solution.py:954
  81.9 3.0 %collective-permute-done.8.refs_2_.refs_6_ = bf16[2,1,64,512]{3,2,1,0:T(8,128)(2,1)S(1)} collective-permute-done((bf16[2,1,64,512]{3,2,1,0:T(8,128)(2,1)S(1)}, bf16[2,1,64,512]{3,2,1,0:T(8,128)(2,1)S(1)}, u32[]{:S(2)}, u32[]{:S(2)}) %collective-permute-start.8) | collective-permute-done | bytes 131104 | tf_op jit(solution)/shard_map/ppermute | solution.py:797
  84.9 2.4 %collective-permute-done.9.refs_3_.refs_7_ = bf16[2,1,64,512]{3,2,1,0:T(8,128)(2,1)S(1)} collective-permute-done((bf16[2,1,64,512]{3,2,1,0:T(8,128)(2,1)S(1)}, bf16[2,1,64,512]{3,2,1,0:T(8,128)(2,1)S(1)}, u32[]{:S(2)}, u32[]{:S(2)}) %collective-permute-start.9) | collective-permute-done | bytes 131104 | tf_op jit(solution)/shard_map/ppermute | solution.py:797
  88.1 1.5 %collective-permute-start.18 = (bf16[304,512]{1,0:T(8,128)(2,1)S(1)}, bf16[304,512]{1,0:T(8,128)(2,1)S(1)}, u32[]{:S(2)}, u32[]{:S(2)}) collective-permute-start(bf16[304,512]{1,0:T(8,128)(2,1)S(1)} %get-tuple-element.237), channel_id=1, source_target_pairs={{0,1},{1,0},{2,3},{3,2},{4,5},{5,4},{6,7},{7,6},{8,9},{9,8},{10,11... | collective-permute-start | bytes 933896 | tf_op jit(solution)/shard_map/ppermute | solution.py:797
  89.6 1.5 %collective-permute-start.20 = (bf16[392,256]{1,0:T(8,128)(2,1)S(1)}, bf16[392,256]{1,0:T(8,128)(2,1)S(1)}, u32[]{:S(2)}, u32[]{:S(2)}) collective-permute-start(bf16[392,256]{1,0:T(8,128)(2,1)S(1)} %get-tuple-element.240), channel_id=1, source_target_pairs={{0,16},{4,20},{8,24},{12,28},{16,0},{20,4},{24,8},{28,12},{1,17},{... | collective-permute-start | bytes 602120 | tf_op jit(solution)/shard_map/ppermute | solution.py:797
  91.1 1.5 %collective-permute-start.19 = (bf16[392,256]{1,0:T(8,128)(2,1)S(1)}, bf16[392,256]{1,0:T(8,128)(2,1)S(1)}, u32[]{:S(2)}, u32[]{:S(2)}) collective-permute-start(bf16[392,256]{1,0:T(8,128)(2,1)S(1)} %get-tuple-element.230.refs_4_), channel_id=1, source_target_pairs={{0,8},{4,12},{8,0},{12,4},{16,24},{20,28},{24,16},{28,20},{1,9},{5... | collective-permute-start | bytes 602120 | tf_op jit(solution)/shard_map/ppermute | solution.py:797
  92.6 1.8 %collective-permute-start.15 = (bf16[2,64,512]{2,1,0:T(8,128)(2,1)S(1)}, bf16[2,64,512]{2,1,0:T(8,128)(2,1)S(1)}, u32[]{:S(2)}, u32[]{:S(2)}) collective-permute-start(bf16[2,64,512]{2,1,0:T(8,128)(2,1)S(1)} %cross_second.1.refs_6_), channel_id=1, source_target_pairs={{0,2},{1,3},{2,0},{3,1},{4,6},{5,7},{6,4},{7,5},{8,10},{9,11},{10,... | collective-permute-start | bytes 393224 | tf_op jit(solution)/shard_map/ppermute | solution.py:797
  94.4 1.5 %collective-permute-done.20.refs_4_ = bf16[392,256]{1,0:T(8,128)(2,1)S(1)} collective-permute-done((bf16[392,256]{1,0:T(8,128)(2,1)S(1)}, bf16[392,256]{1,0:T(8,128)(2,1)S(1)}, u32[]{:S(2)}, u32[]{:S(2)}) %collective-permute-start.20) | collective-permute-done | bytes 200736 | tf_op jit(solution)/shard_map/ppermute | solution.py:797
  97.8 1.6 %collective-permute-start.23 = (bf16[200,256]{1,0:T(8,128)(2,1)S(1)}, bf16[200,256]{1,0:T(8,128)(2,1)S(1)}, u32[]{:S(2)}, u32[]{:S(2)}) collective-permute-start(bf16[200,256]{1,0:T(8,128)(2,1)S(1)} %get-tuple-element.245), channel_id=1, source_target_pairs={{0,8},{4,12},{8,0},{12,4},{16,24},{20,28},{24,16},{28,20},{1,9},{5... | collective-permute-start | bytes 307208 | tf_op jit(solution)/shard_map/ppermute | solution.py:797
  104.8 8.8 %collective-permute-done.24.refs_1_ = bf16[224,512]{1,0:T(8,128)(2,1)S(1)} collective-permute-done((bf16[224,512]{1,0:T(8,128)(2,1)S(1)}, bf16[224,512]{1,0:T(8,128)(2,1)S(1)}, u32[]{:S(2)}, u32[]{:S(2)}) %collective-permute-start.24) | collective-permute-done | bytes 229408 | tf_op jit(solution)/shard_map/ppermute | solution.py:797
  113.6 2.4 %collective-permute-done.21.refs_1_ = bf16[304,512]{1,0:T(8,128)(2,1)S(1)} collective-permute-done((bf16[304,512]{1,0:T(8,128)(2,1)S(1)}, bf16[304,512]{1,0:T(8,128)(2,1)S(1)}, u32[]{:S(2)}, u32[]{:S(2)}) %collective-permute-start.21) | collective-permute-done | bytes 311328 | tf_op jit(solution)/shard_map/ppermute | solution.py:797
  116.3 3.4 %collective-permute-start.25 = (bf16[224,512]{1,0:T(8,128)(2,1)S(1)}, bf16[224,512]{1,0:T(8,128)(2,1)S(1)}, u32[]{:S(2)}, u32[]{:S(2)}) collective-permute-start(bf16[224,512]{1,0:T(8,128)(2,1)S(1)} %tail_near_sum.1.refs_2_.refs_1_), channel_id=1, source_target_pairs={{0,2},{1,3},{2,0},{3,1},{4,6},{5,7},{6,4},{7,5},{8,10},{9,11},{10,... | collective-permute-start | bytes 688136 | tf_op jit(solution)/shard_map/ppermute | solution.py:797
  119.7 3.4 %store.1 = bf16[4,64,64,256]{3,2,1,0:T(8,128)(2,1)} custom-call(bf16[4,64,64,256]{3,2,1,0:T(8,128)(2,1)S(1)} %get-tuple-element.247.source_ref, bf16[304,512]{1,0:T(8,128)(2,1)S(1)} %dense_far_sum.1.refs_16_.refs_0_.refs_3_), custom_call_target="tpu_custom_call" | custom-call | tf_op jit(solution)/shard_map/store/pallas_call | solution.py:784
  124.2 3.2 %collective-permute-done.25.refs_2_ = bf16[224,512]{1,0:T(8,128)(2,1)S(1)} collective-permute-done((bf16[224,512]{1,0:T(8,128)(2,1)S(1)}, bf16[224,512]{1,0:T(8,128)(2,1)S(1)}, u32[]{:S(2)}, u32[]{:S(2)}) %collective-permute-start.25) | collective-permute-done | bytes 229408 | tf_op jit(solution)/shard_map/ppermute | solution.py:797
  128.6 1.8 %finish.1 = (f32[64,512]{1,0:T(8,128)}, f32[64,512]{1,0:T(8,128)}, f32[64,512]{1,0:T(8,128)}, f32[256,512]{1,0:T(8,128)}, f32[64,2048]{1,0:T(8,128)}, /*index=5*...) custom-call(s32[5]{0:T(128)S(1)} %stack.23.refs_17_.place_ref.refs_0, ...), custom_call_target="tpu_custom_call" | custom-call | bytes 2657280 | tf_op jit(solution)/shard_map/finish/pallas_call | solution.py:954
  (56 shorter events, 19.3 us)
Async XLA Ops:
  0.7 12.3 %collective-permute-start.2 = (bf16[4,64,512]{2,1,0:T(8,128)(2,1)}, bf16[4,64,512]{2,1,0:T(8,128)(2,1)S(1)}, u32[]{:S(2)}, u32[]{:S(2)}) collective-permute-start(bf16[4,64,512]{2,1,0:T(8,128)(2,1)} %refs_12_.5), channel_id=1, source_target_pairs={{0,1},{1,0},{2,3},{3,2},{4,5},{5,4},{6,7},{7,6},{8,9},{9,8},{10,11... | collective-permute-start | bytes 786440 | tf_op jit(solution)/shard_map/ppermute | solution.py:797
  4.7 16.0 %collective-permute-start.1 = (bf16[2,64,512]{2,1,0:T(8,128)(2,1)S(1)}, bf16[2,64,512]{2,1,0:T(8,128)(2,1)S(1)}, u32[]{:S(2)}, u32[]{:S(2)}) collective-permute-start(bf16[2,64,512]{2,1,0:T(8,128)(2,1)S(1)} %slice.3), channel_id=1, source_target_pairs={{0,3},{1,2},{2,1},{3,0},{4,7},{5,6},{6,5},{7,4},{8,11},{9,10},{10,... | collective-permute-start | bytes 393224 | tf_op jit(solution)/shard_map/ppermute | solution.py:797
  7.2 13.5 %collective-permute-start = (bf16[2,64,512]{2,1,0:T(8,128)(2,1)S(1)}, bf16[2,64,512]{2,1,0:T(8,128)(2,1)S(1)}, u32[]{:S(2)}, u32[]{:S(2)}) collective-permute-start(bf16[2,64,512]{2,1,0:T(8,128)(2,1)S(1)} %slice.3), channel_id=1, source_target_pairs={{0,2},{1,3},{2,0},{3,1},{4,6},{5,7},{6,4},{7,5},{8,10},{9,11},{10,... | collective-permute-start | bytes 393224 | tf_op jit(solution)/shard_map/ppermute | solution.py:797
  7.5 13.2 %copy-start.3 = (s32[4]{0:T(128)S(1)}, s32[4]{0:T(128)}, u32[]{:S(2)}) copy-start(s32[4]{0:T(128)} %length_ref.3) | copy-start | bytes 52
  15.7 12.4 %collective-permute-start.4 = (bf16[2,64,512]{2,1,0:T(8,128)(2,1)S(1)}, bf16[2,64,512]{2,1,0:T(8,128)(2,1)S(1)}, u32[]{:S(2)}, u32[]{:S(2)}) collective-permute-start(bf16[2,64,512]{2,1,0:T(8,128)(2,1)S(1)} %get-tuple-element.155), channel_id=1, source_target_pairs={{0,3},{1,2},{2,1},{3,0},{4,7},{5,6},{6,5},{7,4},{8,11},{9,10},{10,... | collective-permute-start | bytes 393224 | tf_op jit(solution)/shard_map/ppermute | solution.py:797
  20.7 9.5 %collective-permute-start.3 = (bf16[2,64,512]{2,1,0:T(8,128)(2,1)S(1)}, bf16[2,64,512]{2,1,0:T(8,128)(2,1)S(1)}, u32[]{:S(2)}, u32[]{:S(2)}) collective-permute-start(bf16[2,64,512]{2,1,0:T(8,128)(2,1)S(1)} %get-tuple-element.155), channel_id=1, source_target_pairs={{0,2},{1,3},{2,0},{3,1},{4,6},{5,7},{6,4},{7,5},{8,10},{9,11},{10,... | collective-permute-start | bytes 393224 | tf_op jit(solution)/shard_map/ppermute | solution.py:797
  28.1 9.5 %copy-start.1 = (bf16[2,256,512]{2,1,0:T(8,128)(2,1)}, bf16[2,256,512]{2,1,0:T(8,128)(2,1)S(1)}, u32[]{:S(2)}) copy-start(bf16[2,256,512]{2,1,0:T(8,128)(2,1)S(1)} %get-tuple-element.208.refs_1_) | copy-start | bytes 1572868
  30.2 7.4 %copy-start = (bf16[4,64,512]{2,1,0:T(8,128)(2,1)S(1)}, bf16[4,64,512]{2,1,0:T(8,128)(2,1)}, u32[]{:S(2)}) copy-start(bf16[4,64,512]{2,1,0:T(8,128)(2,1)} %refs_12_.5) | copy-start | bytes 786436
  45.1 5.5 %collective-permute-start.5 = (bf16[4,9,64,512]{3,2,1,0:T(8,128)(2,1)S(1)}, bf16[4,9,64,512]{3,2,1,0:T(8,128)(2,1)S(1)}, u32[]{:S(2)}, u32[]{:S(2)}) collective-permute-start(bf16[4,9,64,512]{3,2,1,0:T(8,128)(2,1)S(1)} %get-tuple-element.185), channel_id=1, source_target_pairs={{0,4},{4,0},{8,12},{12,8},{16,20},{20,16},{24,28},{28,24},{1,5},{5... | collective-permute-start | bytes 7077896 | tf_op jit(solution)/shard_map/ppermute | solution.py:797
  45.2 5.4 %collective-permute-start.6 = (f32[8,512]{1,0:T(8,128)S(1)}, f32[8,512]{1,0:T(8,128)S(1)}, u32[]{:S(2)}, u32[]{:S(2)}) collective-permute-start(f32[8,512]{1,0:T(8,128)S(1)} %get-tuple-element.186.refs_3_), channel_id=1, source_target_pairs={{0,4},{4,0},{8,12},{12,8},{16,20},{20,16},{24,28},{28,24},{1,5},{5... | collective-permute-start | bytes 49160 | tf_op jit(solution)/shard_map/ppermute | solution.py:797
  51.7 22.4 %collective-permute-start.12 = (bf16[1160,256]{1,0:T(8,128)(2,1)S(1)}, bf16[1160,256]{1,0:T(8,128)(2,1)S(1)}, u32[]{:S(2)}, u32[]{:S(2)}) collective-permute-start(bf16[1160,256]{1,0:T(8,128)(2,1)S(1)} %get-tuple-element.224), channel_id=1, source_target_pairs={{0,16},{4,20},{8,24},{12,28},{16,0},{20,4},{24,8},{28,12},{1,17},{... | collective-permute-start | bytes 1781768 | tf_op jit(solution)/shard_map/ppermute | solution.py:797
  53.3 20.8 %collective-permute-start.11 = (bf16[1160,256]{1,0:T(8,128)(2,1)S(1)}, bf16[1160,256]{1,0:T(8,128)(2,1)S(1)}, u32[]{:S(2)}, u32[]{:S(2)}) collective-permute-start(bf16[1160,256]{1,0:T(8,128)(2,1)S(1)} %get-tuple-element.187.refs_2_), channel_id=1, source_target_pairs={{0,8},{4,12},{8,0},{12,4},{16,24},{20,28},{24,16},{28,20},{1,9},{5... | collective-permute-start | bytes 1781768 | tf_op jit(solution)/shard_map/ppermute | solution.py:797
  59.7 7.8 %collective-permute-start.7 = (bf16[2,2,64,512]{3,2,1,0:T(8,128)(2,1)S(1)}, bf16[2,2,64,512]{3,2,1,0:T(8,128)(2,1)S(1)}, u32[]{:S(2)}, u32[]{:S(2)}) collective-permute-start(bf16[2,2,64,512]{3,2,1,0:T(8,128)(2,1)S(1)} %get-tuple-element.202), channel_id=1, source_target_pairs={{0,1},{1,0},{2,3},{3,2},{4,5},{5,4},{6,7},{7,6},{8,9},{9,8},{10,11... | collective-permute-start | bytes 786440 | tf_op jit(solution)/shard_map/ppermute | solution.py:797
  67.5 7.8 %collective-permute-start.10 = (bf16[2,64,512]{2,1,0:T(8,128)(2,1)S(1)}, bf16[2,64,512]{2,1,0:T(8,128)(2,1)S(1)}, u32[]{:S(2)}, u32[]{:S(2)}) collective-permute-start(bf16[2,64,512]{2,1,0:T(8,128)(2,1)S(1)} %cross_first.1.refs_2_), channel_id=1, source_target_pairs={{0,2},{1,3},{2,0},{3,1},{4,6},{5,7},{6,4},{7,5},{8,10},{9,11},{10,... | collective-permute-start | bytes 393224 | tf_op jit(solution)/shard_map/ppermute | solution.py:797
  69.0 6.2 %copy-start.2 = (bf16[2,256,512]{2,1,0:T(8,128)(2,1)S(1)}, bf16[2,256,512]{2,1,0:T(8,128)(2,1)}, u32[]{:S(2)}) copy-start(bf16[2,256,512]{2,1,0:T(8,128)(2,1)} %copy-done.1) | copy-start | bytes 1572868
  77.4 3.8 %collective-permute-start.13 = (bf16[4,3,64,512]{3,2,1,0:T(8,128)(2,1)S(1)}, bf16[4,3,64,512]{3,2,1,0:T(8,128)(2,1)S(1)}, u32[]{:S(2)}, u32[]{:S(2)}) collective-permute-start(bf16[4,3,64,512]{3,2,1,0:T(8,128)(2,1)S(1)} %get-tuple-element.228), channel_id=1, source_target_pairs={{0,4},{4,0},{8,12},{12,8},{16,20},{20,16},{24,28},{28,24},{1,5},{5... | collective-permute-start | bytes 2359304 | tf_op jit(solution)/shard_map/ppermute | solution.py:797
  77.5 9.9 %collective-permute-start.17 = (bf16[584,256]{1,0:T(8,128)(2,1)S(1)}, bf16[584,256]{1,0:T(8,128)(2,1)S(1)}, u32[]{:S(2)}, u32[]{:S(2)}) collective-permute-start(bf16[584,256]{1,0:T(8,128)(2,1)S(1)} %get-tuple-element.234), channel_id=1, source_target_pairs={{0,8},{4,12},{8,0},{12,4},{16,24},{20,28},{24,16},{28,20},{1,9},{5... | collective-permute-start | bytes 897032 | tf_op jit(solution)/shard_map/ppermute | solution.py:797
  78.1 9.3 %collective-permute-start.16 = (bf16[584,256]{1,0:T(8,128)(2,1)S(1)}, bf16[584,256]{1,0:T(8,128)(2,1)S(1)}, u32[]{:S(2)}, u32[]{:S(2)}) collective-permute-start(bf16[584,256]{1,0:T(8,128)(2,1)S(1)} %get-tuple-element.226.refs_16_), channel_id=1, source_target_pairs={{0,16},{4,20},{8,24},{12,28},{16,0},{20,4},{24,8},{28,12},{1,17},{... | collective-permute-start | bytes 897032 | tf_op jit(solution)/shard_map/ppermute | solution.py:797
  78.6 1.4 %collective-permute-start.14 = (f32[8,512]{1,0:T(8,128)S(1)}, f32[8,512]{1,0:T(8,128)S(1)}, u32[]{:S(2)}, u32[]{:S(2)}) collective-permute-start(f32[8,512]{1,0:T(8,128)S(1)} %get-tuple-element.229.refs_3_), channel_id=1, source_target_pairs={{0,4},{4,0},{8,12},{12,8},{16,20},{20,16},{24,28},{28,24},{1,5},{5... | collective-permute-start | bytes 49160 | tf_op jit(solution)/shard_map/ppermute | solution.py:797
  78.6 6.3 %collective-permute-start.8 = (bf16[2,1,64,512]{3,2,1,0:T(8,128)(2,1)S(1)}, bf16[2,1,64,512]{3,2,1,0:T(8,128)(2,1)S(1)}, u32[]{:S(2)}, u32[]{:S(2)}) collective-permute-start(bf16[2,1,64,512]{3,2,1,0:T(8,128)(2,1)S(1)} %get-tuple-element.204), channel_id=1, source_target_pairs={{0,1},{1,0},{2,3},{3,2},{4,5},{5,4},{6,7},{7,6},{8,9},{9,8},{10,11... | collective-permute-start | bytes 393224 | tf_op jit(solution)/shard_map/ppermute | solution.py:797
  80.0 7.3 %collective-permute-start.9 = (bf16[2,1,64,512]{3,2,1,0:T(8,128)(2,1)S(1)}, bf16[2,1,64,512]{3,2,1,0:T(8,128)(2,1)S(1)}, u32[]{:S(2)}, u32[]{:S(2)}) collective-permute-start(bf16[2,1,64,512]{3,2,1,0:T(8,128)(2,1)S(1)} %get-tuple-element.205), channel_id=1, source_target_pairs={{0,1},{1,0},{2,3},{3,2},{4,5},{5,4},{6,7},{7,6},{8,9},{9,8},{10,11... | collective-permute-start | bytes 393224 | tf_op jit(solution)/shard_map/ppermute | solution.py:797
  88.1 13.1 %collective-permute-start.18 = (bf16[304,512]{1,0:T(8,128)(2,1)S(1)}, bf16[304,512]{1,0:T(8,128)(2,1)S(1)}, u32[]{:S(2)}, u32[]{:S(2)}) collective-permute-start(bf16[304,512]{1,0:T(8,128)(2,1)S(1)} %get-tuple-element.237), channel_id=1, source_target_pairs={{0,1},{1,0},{2,3},{3,2},{4,5},{5,4},{6,7},{7,6},{8,9},{9,8},{10,11... | collective-permute-start | bytes 933896 | tf_op jit(solution)/shard_map/ppermute | solution.py:797
  89.6 6.3 %collective-permute-start.20 = (bf16[392,256]{1,0:T(8,128)(2,1)S(1)}, bf16[392,256]{1,0:T(8,128)(2,1)S(1)}, u32[]{:S(2)}, u32[]{:S(2)}) collective-permute-start(bf16[392,256]{1,0:T(8,128)(2,1)S(1)} %get-tuple-element.240), channel_id=1, source_target_pairs={{0,16},{4,20},{8,24},{12,28},{16,0},{20,4},{24,8},{28,12},{1,17},{... | collective-permute-start | bytes 602120 | tf_op jit(solution)/shard_map/ppermute | solution.py:797
  91.1 6.1 %collective-permute-start.19 = (bf16[392,256]{1,0:T(8,128)(2,1)S(1)}, bf16[392,256]{1,0:T(8,128)(2,1)S(1)}, u32[]{:S(2)}, u32[]{:S(2)}) collective-permute-start(bf16[392,256]{1,0:T(8,128)(2,1)S(1)} %get-tuple-element.230.refs_4_), channel_id=1, source_target_pairs={{0,8},{4,12},{8,0},{12,4},{16,24},{20,28},{24,16},{28,20},{1,9},{5... | collective-permute-start | bytes 602120 | tf_op jit(solution)/shard_map/ppermute | solution.py:797
  92.6 8.7 %collective-permute-start.15 = (bf16[2,64,512]{2,1,0:T(8,128)(2,1)S(1)}, bf16[2,64,512]{2,1,0:T(8,128)(2,1)S(1)}, u32[]{:S(2)}, u32[]{:S(2)}) collective-permute-start(bf16[2,64,512]{2,1,0:T(8,128)(2,1)S(1)} %cross_second.1.refs_6_), channel_id=1, source_target_pairs={{0,2},{1,3},{2,0},{3,1},{4,6},{5,7},{6,4},{7,5},{8,10},{9,11},{10,... | collective-permute-start | bytes 393224 | tf_op jit(solution)/shard_map/ppermute | solution.py:797
  97.8 5.2 %collective-permute-start.23 = (bf16[200,256]{1,0:T(8,128)(2,1)S(1)}, bf16[200,256]{1,0:T(8,128)(2,1)S(1)}, u32[]{:S(2)}, u32[]{:S(2)}) collective-permute-start(bf16[200,256]{1,0:T(8,128)(2,1)S(1)} %get-tuple-element.245), channel_id=1, source_target_pairs={{0,8},{4,12},{8,0},{12,4},{16,24},{20,28},{24,16},{28,20},{1,9},{5... | collective-permute-start | bytes 307208 | tf_op jit(solution)/shard_map/ppermute | solution.py:797
  99.3 4.7 %collective-permute-start.22 = (bf16[200,256]{1,0:T(8,128)(2,1)S(1)}, bf16[200,256]{1,0:T(8,128)(2,1)S(1)}, u32[]{:S(2)}, u32[]{:S(2)}) collective-permute-start(bf16[200,256]{1,0:T(8,128)(2,1)S(1)} %get-tuple-element.242.refs_3_), channel_id=1, source_target_pairs={{0,16},{4,20},{8,24},{12,28},{16,0},{20,4},{24,8},{28,12},{1,17},{... | collective-permute-start | bytes 307208 | tf_op jit(solution)/shard_map/ppermute | solution.py:797
  101.9 14.1 %collective-permute-start.21 = (bf16[304,512]{1,0:T(8,128)(2,1)S(1)}, bf16[304,512]{1,0:T(8,128)(2,1)S(1)}, u32[]{:S(2)}, u32[]{:S(2)}) collective-permute-start(bf16[304,512]{1,0:T(8,128)(2,1)S(1)} %dense_near_sum.1.refs_5_.refs_0_), channel_id=1, source_target_pairs={{0,2},{1,3},{2,0},{3,1},{4,6},{5,7},{6,4},{7,5},{8,10},{9,11},{10,... | collective-permute-start | bytes 933896 | tf_op jit(solution)/shard_map/ppermute | solution.py:797
  104.0 9.5 %collective-permute-start.24 = (bf16[224,512]{1,0:T(8,128)(2,1)S(1)}, bf16[224,512]{1,0:T(8,128)(2,1)S(1)}, u32[]{:S(2)}, u32[]{:S(2)}) collective-permute-start(bf16[224,512]{1,0:T(8,128)(2,1)S(1)} %tail_sum_second.1.refs_0_), channel_id=1, source_target_pairs={{0,1},{1,0},{2,3},{3,2},{4,5},{5,4},{6,7},{7,6},{8,9},{9,8},{10,11... | collective-permute-start | bytes 688136 | tf_op jit(solution)/shard_map/ppermute | solution.py:797
  116.1 12.5 %collective-permute-start.26 = (bf16[304,512]{1,0:T(8,128)(2,1)S(1)}, bf16[304,512]{1,0:T(8,128)(2,1)S(1)}, u32[]{:S(2)}, u32[]{:S(2)}) collective-permute-start(bf16[304,512]{1,0:T(8,128)(2,1)S(1)} %dense_far_sum.1.refs_16_.refs_0_.refs_3_), channel_id=1, source_target_pairs={{0,1},{1,0},{2,3},{3,2},{4,5},{5,4},{6,7},{7,6},{8,9},{9,8},{10,11... | collective-permute-start | bytes 933896 | tf_op jit(solution)/shard_map/ppermute | solution.py:797
  116.3 11.1 %collective-permute-start.25 = (bf16[224,512]{1,0:T(8,128)(2,1)S(1)}, bf16[224,512]{1,0:T(8,128)(2,1)S(1)}, u32[]{:S(2)}, u32[]{:S(2)}) collective-permute-start(bf16[224,512]{1,0:T(8,128)(2,1)S(1)} %tail_near_sum.1.refs_2_.refs_1_), channel_id=1, source_target_pairs={{0,2},{1,3},{2,0},{3,1},{4,6},{5,7},{6,4},{7,5},{8,10},{9,11},{10,... | collective-permute-start | bytes 688136 | tf_op jit(solution)/shard_map/ppermute | solution.py:797

commit v10 on v9

--- a/solution.py
+++ b/solution.py
@@ -1345,7 +1345,7 @@
             near_sum_kernel, place, [dense_total, came], [came], "dense_near_sum", (held, far2)
         )[0]
         far = swap(mine, "rows", 2)
-        total = sum_second(pieces, "tail", (mine,))
+        total = sum_second(pieces, "tail")
         tail_came = swap(total, "rows", 1)
         total = small_call(add_kernel, None, [total, tail_came], [total], "tail_near_sum")[0]
         tail_came = swap(total, "rows", 2)

time: 131 us -> 131 us (level)
  no operation moved by 1% of the time
where the time goes in v10:
time: 131 us; the launch traced here: 130 us
  Pallas kernels  63.3 us (48%)
  starting transfers between devices  33.6 us (26%)
  waiting for transfers between devices  31.5 us (24%)
    ppermute x27, starting transfers between devices, swap(): return lax.ppermute(value, axis, [(i, i ^ mask) for i in range(size)])  33.6 us
    ppermute x27, waiting for transfers between devices, swap(): return lax.ppermute(value, axis, [(i, i ^ mask) for i in range(size)])  31.5 us
    pallas_call x4, Pallas kernels, attention_backward(): pl.pallas_call(functools.partial(backward_kernel, head_size, 4, first, ba...  19.7 us
    pallas_call x2, Pallas kernels, attention_forward(): pl.pallas_call(functools.partial(forward_kernel, head_size, 4, first, len...  14.8 us
    pallas_call x14, Pallas kernels, small_call(): pl.pallas_call(body, grid_spec=pltpu.PrefetchScalarGridSpec(num_scalar_pr...  9.76 us
    pallas_call x1, Pallas kernels, dense(): pl.pallas_call(functools.partial(dense_kernel, len(mixed)), grid_spec=plt...  7.5 us
    pallas_call x1, Pallas kernels, load(): pl.pallas_call(functools.partial(load_kernel, count, starts), in_specs=[p...  5.43 us
    pallas_call x1, Pallas kernels, store(): pl.pallas_call(store_kernel, in_specs=[near_spec()] + [pl.BlockSpec(memor...  3.4 us
  transfers between devices with their start and end apart: 27, of which 13 were waited for; matrix products, arithmetic and copies ran while one was open for 1% of the time, Pallas kernels for 33%

profile of v10, /device:TPU:0, one launch (start us, length us, event | category | flops | bytes accessed | tf_op | source)
XLA Modules:
  0.0 130.5 jit_solution(12165116120317638600)
XLA Ops:
  0.7 3.1 %collective-permute-start.2 = (bf16[4,64,512]{2,1,0:T(8,128)(2,1)}, bf16[4,64,512]{2,1,0:T(8,128)(2,1)S(1)}, u32[]{:S(2)}, u32[]{:S(2)}) collective-permute-start(bf16[4,64,512]{2,1,0:T(8,128)(2,1)} %refs_12_.5), channel_id=1, source_target_pairs={{0,1},{1,0},{2,3},{3,2},{4,5},{5,4},{6,7},{7,6},{8,9},{9,8},{10,11... | collective-permute-start | bytes 786440 | tf_op jit(solution)/shard_map/ppermute | solution.py:797
  4.7 2.5 %collective-permute-start.1 = (bf16[2,64,512]{2,1,0:T(8,128)(2,1)S(1)}, bf16[2,64,512]{2,1,0:T(8,128)(2,1)S(1)}, u32[]{:S(2)}, u32[]{:S(2)}) collective-permute-start(bf16[2,64,512]{2,1,0:T(8,128)(2,1)S(1)} %slice.3), channel_id=1, source_target_pairs={{0,3},{1,2},{2,1},{3,0},{4,7},{5,6},{6,5},{7,4},{8,11},{9,10},{10,... | collective-permute-start | bytes 393224 | tf_op jit(solution)/shard_map/ppermute | solution.py:797
  7.5 5.4 %load_first.1 = (bf16[4,64,64,256]{3,2,1,0:T(8,128)(2,1)S(1)}, bf16[512,512]{1,0:T(8,128)(2,1)S(1)}, bf16[512,512]{1,0:T(8,128)(2,1)S(1)}, bf16[512,512]{1,0:T(8...) custom-call(bf16[4,64,64,256]{3,2,1,0:T(8,128)(2,1)} %refs_0_.1, ...), custom_call_target="tpu_custom_call" | custom-call | tf_op jit(solution)/shard_map/load_first/pallas_call | solution.py:98
  13.0 2.7 %near_half.1 = (bf16[2,256,512]{2,1,0:T(8,128)(2,1)S(1)}, bf16[2,256,512]{2,1,0:T(8,128)(2,1)S(1)}, bf16[2,4,256,128]{3,2,1,0:T(8,128)(2,1)S(1)}, bf16[2,4,256,2...) custom-call(s32[5]{0:T(128)S(1)} %stack.23.refs_17_.place_ref.refs_0, ...), custom_call_target="tpu_custom_call" | custom-call | tf_op jit(solution)/shard_map/near_half/pallas_call | solution.py:198
  15.7 5.0 %collective-permute-start.4 = (bf16[2,64,512]{2,1,0:T(8,128)(2,1)S(1)}, bf16[2,64,512]{2,1,0:T(8,128)(2,1)S(1)}, u32[]{:S(2)}, u32[]{:S(2)}) collective-permute-start(bf16[2,64,512]{2,1,0:T(8,128)(2,1)S(1)} %get-tuple-element.155), channel_id=1, source_target_pairs={{0,3},{1,2},{2,1},{3,0},{4,7},{5,6},{6,5},{7,4},{8,11},{9,10},{10,... | collective-permute-start | bytes 393224 | tf_op jit(solution)/shard_map/ppermute | solution.py:797
  20.7 7.4 %attention_forward.2 = (bf16[4,64,64,256]{3,2,1,0:T(8,128)(2,1)}, bf16[2,64,64,256]{3,2,1,0:T(8,128)(2,1)S(1)}, f32[2,4,64,128]{3,2,1,0:T(8,128)S(1)}, f32[2,4,6...) custom-call(s32[5]{0:T(128)S(1)} %stack.23.refs_17_.place_ref.refs_0, ...), custom_call_target="tpu_custom_call", output_to_operand_aliasing={{4}: (11, {}), {5}: (12, {}), {6}: (13, {}), {7}: (14, {})} | custom-call | flops 1610612736 | bytes 12582912 | tf_op jit(solution)/shard_map/attention_forward/pallas_call | solution.py:321
  28.1 2.1 %collective-permute-done.3.two_ref = bf16[2,64,512]{2,1,0:T(8,128)(2,1)S(1)} collective-permute-done((bf16[2,64,512]{2,1,0:T(8,128)(2,1)S(1)}, bf16[2,64,512]{2,1,0:T(8,128)(2,1)S(1)}, u32[]{:S(2)}, u32[]{:S(2)}) %collective-permute-start.3) | collective-permute-done | bytes 131104 | tf_op jit(solution)/shard_map/ppermute | solution.py:797
  30.2 7.4 %attention_forward.3 = (bf16[4,64,64,256]{3,2,1,0:T(8,128)(2,1)}, bf16[2,64,64,256]{3,2,1,0:T(8,128)(2,1)S(1)}, f32[2,4,64,128]{3,2,1,0:T(8,128)S(1)}, f32[2,4,6...) custom-call(s32[5]{0:T(128)S(1)} %stack.23.refs_17_.place_ref.refs_0, ...), custom_call_target="tpu_custom_call", output_to_operand_aliasing={{4}: (11, {}), {5}: (12, {}), {6}: (13, {}), {7}: (14, {}),... | custom-call | flops 1610612736 | bytes 12582912 | tf_op jit(solution)/shard_map/attention_forward/pallas_call | solution.py:321
  37.6 7.5 %dense.1 = (bf16[4,64,512]{2,1,0:T(8,128)(2,1)}, bf16[4,9,64,512]{3,2,1,0:T(8,128)(2,1)S(1)}, bf16[4,9,64,512]{3,2,1,0:T(8,128)(2,1)S(1)}, f32[4,64,512]{2,1,0:T...) custom-call(s32[5]{0:T(128)S(1)} %stack.23.refs_17_.place_ref.refs_0_, ...), custom_call_target="tpu_custom_call" | custom-call | flops 3221225472 | bytes 12582912 | tf_op jit(solution)/shard_map/dense/pallas_call | solution.py:531
  45.7 4.9 %attention_backward.4 = (bf16[4,64,64,256]{3,2,1,0:T(8,128)(2,1)S(1)}, bf16[2,1,64,512]{3,2,1,0:T(8,128)(2,1)S(1)}, bf16[1,64,512]{2,1,0:T(8,128)(2,1)S(1)}, f32...) custom-call(s32[5]{0:T(128)S(1)} %stack.23.refs_17_.place_ref.refs_0, ...), custom_call_target="tpu_custom_call" | custom-call | flops 1610612736 | bytes 6291456 | tf_op jit(solution)/shard_map/attention_backward/pallas_call | solution.py:727
  51.7 1.6 %collective-permute-start.12 = (bf16[1160,256]{1,0:T(8,128)(2,1)S(1)}, bf16[1160,256]{1,0:T(8,128)(2,1)S(1)}, u32[]{:S(2)}, u32[]{:S(2)}) collective-permute-start(bf16[1160,256]{1,0:T(8,128)(2,1)S(1)} %get-tuple-element.224), channel_id=1, source_target_pairs={{0,16},{4,20},{8,24},{12,28},{16,0},{20,4},{24,8},{28,12},{1,17},{... | collective-permute-start | bytes 1781768 | tf_op jit(solution)/shard_map/ppermute | solution.py:797
  53.3 1.5 %collective-permute-start.11 = (bf16[1160,256]{1,0:T(8,128)(2,1)S(1)}, bf16[1160,256]{1,0:T(8,128)(2,1)S(1)}, u32[]{:S(2)}, u32[]{:S(2)}) collective-permute-start(bf16[1160,256]{1,0:T(8,128)(2,1)S(1)} %get-tuple-element.187.refs_2_), channel_id=1, source_target_pairs={{0,8},{4,12},{8,0},{12,4},{16,24},{20,28},{24,16},{28,20},{1,9},{5... | collective-permute-start | bytes 1781768 | tf_op jit(solution)/shard_map/ppermute | solution.py:797
  54.8 4.9 %attention_backward.5 = (bf16[4,64,64,256]{3,2,1,0:T(8,128)(2,1)S(1)}, bf16[2,2,64,512]{3,2,1,0:T(8,128)(2,1)S(1)}, bf16[1,64,512]{2,1,0:T(8,128)(2,1)S(1)}, f32...) custom-call(s32[5]{0:T(128)S(1)} %stack.23.refs_17_.place_ref.refs_0, ...), custom_call_target="tpu_custom_call", output_to_operand_aliasing={{0}: (13, {}), {4}: (14, {})} | custom-call | flops 1610612736 | bytes 6291456 | tf_op jit(solution)/shard_map/attention_backward/pallas_call | solution.py:727
  59.7 4.9 %attention_backward.6 = (bf16[4,64,64,256]{3,2,1,0:T(8,128)(2,1)S(1)}, bf16[2,1,64,512]{3,2,1,0:T(8,128)(2,1)S(1)}, bf16[1,64,512]{2,1,0:T(8,128)(2,1)S(1)}, f32...) custom-call(s32[5]{0:T(128)S(1)} %stack.23.refs_17_.place_ref.refs_0, ...), custom_call_target="tpu_custom_call", output_to_operand_aliasing={{0}: (13, {}), {4}: (14, {})} | custom-call | flops 1610612736 | bytes 6291456 | tf_op jit(solution)/shard_map/attention_backward/pallas_call | solution.py:727
  64.6 2.8 %collective-permute-done.7.refs_2_.refs_4_.refs_5_ = bf16[2,2,64,512]{3,2,1,0:T(8,128)(2,1)S(1)} collective-permute-done((bf16[2,2,64,512]{3,2,1,0:T(8,128)(2,1)S(1)}, bf16[2,2,64,512]{3,2,1,0:T(8,128)(2,1)S(1)}, u32[]{:S(2)}, u32[]{:S(2)}) %collective-permute-start.7) | collective-permute-done | bytes 262176 | tf_op jit(solution)/shard_map/ppermute | solution.py:797
  67.5 1.5 %collective-permute-start.10 = (bf16[2,64,512]{2,1,0:T(8,128)(2,1)S(1)}, bf16[2,64,512]{2,1,0:T(8,128)(2,1)S(1)}, u32[]{:S(2)}, u32[]{:S(2)}) collective-permute-start(bf16[2,64,512]{2,1,0:T(8,128)(2,1)S(1)} %cross_first.1.refs_2_), channel_id=1, source_target_pairs={{0,2},{1,3},{2,0},{3,1},{4,6},{5,7},{6,4},{7,5},{8,10},{9,11},{10,... | collective-permute-start | bytes 393224 | tf_op jit(solution)/shard_map/ppermute | solution.py:797
  69.0 5.1 %attention_backward.7 = (bf16[4,64,64,256]{3,2,1,0:T(8,128)(2,1)S(1)}, bf16[2,1,64,512]{3,2,1,0:T(8,128)(2,1)S(1)}, bf16[1,64,512]{2,1,0:T(8,128)(2,1)S(1)}, f32...) custom-call(s32[5]{0:T(128)S(1)} %stack.23.refs_17_.place_ref.refs_0, ...), custom_call_target="tpu_custom_call", output_to_operand_aliasing={{0}: (13, {}), {4}: (14, {})} | custom-call | flops 1610612736 | bytes 6291456 | tf_op jit(solution)/shard_map/attention_backward/pallas_call | solution.py:727
  75.3 2.1 %attention_weights.1 = (bf16[4,3,64,512]{3,2,1,0:T(8,128)(2,1)S(1)}, bf16[4,3,64,512]{3,2,1,0:T(8,128)(2,1)S(1)}) custom-call(s32[5]{0:T(128)S(1)} %stack.23.refs_17_.place_ref.refs_0_, bf16[2,256,512]{2,1,0:T(8,128)(2,1)S(1)} %copy-done.2, bf16[2,256,512]{2,1,0:T(8,128)(2,1)S(1)} %get-tuple-element.209.refs_2_, ...), custom_call_target="tpu_custom_call" | custom-call | bytes 4980736 | tf_op jit(solution)/shard_map/attention_weights/pallas_call | solution.py:954
  81.9 3.0 %collective-permute-done.8.refs_2_.refs_6_ = bf16[2,1,64,512]{3,2,1,0:T(8,128)(2,1)S(1)} collective-permute-done((bf16[2,1,64,512]{3,2,1,0:T(8,128)(2,1)S(1)}, bf16[2,1,64,512]{3,2,1,0:T(8,128)(2,1)S(1)}, u32[]{:S(2)}, u32[]{:S(2)}) %collective-permute-start.8) | collective-permute-done | bytes 131104 | tf_op jit(solution)/shard_map/ppermute | solution.py:797
  84.9 2.4 %collective-permute-done.9.refs_3_.refs_7_ = bf16[2,1,64,512]{3,2,1,0:T(8,128)(2,1)S(1)} collective-permute-done((bf16[2,1,64,512]{3,2,1,0:T(8,128)(2,1)S(1)}, bf16[2,1,64,512]{3,2,1,0:T(8,128)(2,1)S(1)}, u32[]{:S(2)}, u32[]{:S(2)}) %collective-permute-start.9) | collective-permute-done | bytes 131104 | tf_op jit(solution)/shard_map/ppermute | solution.py:797
  88.1 1.5 %collective-permute-start.18 = (bf16[304,512]{1,0:T(8,128)(2,1)S(1)}, bf16[304,512]{1,0:T(8,128)(2,1)S(1)}, u32[]{:S(2)}, u32[]{:S(2)}) collective-permute-start(bf16[304,512]{1,0:T(8,128)(2,1)S(1)} %get-tuple-element.237), channel_id=1, source_target_pairs={{0,1},{1,0},{2,3},{3,2},{4,5},{5,4},{6,7},{7,6},{8,9},{9,8},{10,11... | collective-permute-start | bytes 933896 | tf_op jit(solution)/shard_map/ppermute | solution.py:797
  89.6 1.5 %collective-permute-start.20 = (bf16[392,256]{1,0:T(8,128)(2,1)S(1)}, bf16[392,256]{1,0:T(8,128)(2,1)S(1)}, u32[]{:S(2)}, u32[]{:S(2)}) collective-permute-start(bf16[392,256]{1,0:T(8,128)(2,1)S(1)} %get-tuple-element.240), channel_id=1, source_target_pairs={{0,16},{4,20},{8,24},{12,28},{16,0},{20,4},{24,8},{28,12},{1,17},{... | collective-permute-start | bytes 602120 | tf_op jit(solution)/shard_map/ppermute | solution.py:797
  91.1 1.5 %collective-permute-start.19 = (bf16[392,256]{1,0:T(8,128)(2,1)S(1)}, bf16[392,256]{1,0:T(8,128)(2,1)S(1)}, u32[]{:S(2)}, u32[]{:S(2)}) collective-permute-start(bf16[392,256]{1,0:T(8,128)(2,1)S(1)} %get-tuple-element.230.refs_4_), channel_id=1, source_target_pairs={{0,8},{4,12},{8,0},{12,4},{16,24},{20,28},{24,16},{28,20},{1,9},{5... | collective-permute-start | bytes 602120 | tf_op jit(solution)/shard_map/ppermute | solution.py:797
  92.6 1.8 %collective-permute-start.15 = (bf16[2,64,512]{2,1,0:T(8,128)(2,1)S(1)}, bf16[2,64,512]{2,1,0:T(8,128)(2,1)S(1)}, u32[]{:S(2)}, u32[]{:S(2)}) collective-permute-start(bf16[2,64,512]{2,1,0:T(8,128)(2,1)S(1)} %cross_second.1.refs_6_), channel_id=1, source_target_pairs={{0,2},{1,3},{2,0},{3,1},{4,6},{5,7},{6,4},{7,5},{8,10},{9,11},{10,... | collective-permute-start | bytes 393224 | tf_op jit(solution)/shard_map/ppermute | solution.py:797
  94.4 1.5 %collective-permute-done.20.refs_4_ = bf16[392,256]{1,0:T(8,128)(2,1)S(1)} collective-permute-done((bf16[392,256]{1,0:T(8,128)(2,1)S(1)}, bf16[392,256]{1,0:T(8,128)(2,1)S(1)}, u32[]{:S(2)}, u32[]{:S(2)}) %collective-permute-start.20) | collective-permute-done | bytes 200736 | tf_op jit(solution)/shard_map/ppermute | solution.py:797
  97.8 1.6 %collective-permute-start.23 = (bf16[200,256]{1,0:T(8,128)(2,1)S(1)}, bf16[200,256]{1,0:T(8,128)(2,1)S(1)}, u32[]{:S(2)}, u32[]{:S(2)}) collective-permute-start(bf16[200,256]{1,0:T(8,128)(2,1)S(1)} %get-tuple-element.245), channel_id=1, source_target_pairs={{0,8},{4,12},{8,0},{12,4},{16,24},{20,28},{24,16},{28,20},{1,9},{5... | collective-permute-start | bytes 307208 | tf_op jit(solution)/shard_map/ppermute | solution.py:797
  104.7 8.8 %collective-permute-done.24.refs_1_ = bf16[224,512]{1,0:T(8,128)(2,1)S(1)} collective-permute-done((bf16[224,512]{1,0:T(8,128)(2,1)S(1)}, bf16[224,512]{1,0:T(8,128)(2,1)S(1)}, u32[]{:S(2)}, u32[]{:S(2)}) %collective-permute-start.24) | collective-permute-done | bytes 229408 | tf_op jit(solution)/shard_map/ppermute | solution.py:797
  113.6 2.4 %collective-permute-done.21.refs_1_ = bf16[304,512]{1,0:T(8,128)(2,1)S(1)} collective-permute-done((bf16[304,512]{1,0:T(8,128)(2,1)S(1)}, bf16[304,512]{1,0:T(8,128)(2,1)S(1)}, u32[]{:S(2)}, u32[]{:S(2)}) %collective-permute-start.21) | collective-permute-done | bytes 311328 | tf_op jit(solution)/shard_map/ppermute | solution.py:797
  116.3 3.4 %collective-permute-start.25 = (bf16[224,512]{1,0:T(8,128)(2,1)S(1)}, bf16[224,512]{1,0:T(8,128)(2,1)S(1)}, u32[]{:S(2)}, u32[]{:S(2)}) collective-permute-start(bf16[224,512]{1,0:T(8,128)(2,1)S(1)} %tail_near_sum.1.refs_2_.refs_1_), channel_id=1, source_target_pairs={{0,2},{1,3},{2,0},{3,1},{4,6},{5,7},{6,4},{7,5},{8,10},{9,11},{10,... | collective-permute-start | bytes 688136 | tf_op jit(solution)/shard_map/ppermute | solution.py:797
  119.7 3.4 %store.1 = bf16[4,64,64,256]{3,2,1,0:T(8,128)(2,1)} custom-call(bf16[4,64,64,256]{3,2,1,0:T(8,128)(2,1)S(1)} %get-tuple-element.247.source_ref, bf16[304,512]{1,0:T(8,128)(2,1)S(1)} %dense_far_sum.1.refs_16_.refs_0_.refs_3_), custom_call_target="tpu_custom_call" | custom-call | tf_op jit(solution)/shard_map/store/pallas_call | solution.py:784
  124.2 3.2 %collective-permute-done.25.refs_2_ = bf16[224,512]{1,0:T(8,128)(2,1)S(1)} collective-permute-done((bf16[224,512]{1,0:T(8,128)(2,1)S(1)}, bf16[224,512]{1,0:T(8,128)(2,1)S(1)}, u32[]{:S(2)}, u32[]{:S(2)}) %collective-permute-start.25) | collective-permute-done | bytes 229408 | tf_op jit(solution)/shard_map/ppermute | solution.py:797
  128.6 1.8 %finish.1 = (f32[64,512]{1,0:T(8,128)}, f32[64,512]{1,0:T(8,128)}, f32[64,512]{1,0:T(8,128)}, f32[256,512]{1,0:T(8,128)}, f32[64,2048]{1,0:T(8,128)}, /*index=5*...) custom-call(s32[5]{0:T(128)S(1)} %stack.23.refs_17_.place_ref.refs_0, ...), custom_call_target="tpu_custom_call" | custom-call | bytes 2657280 | tf_op jit(solution)/shard_map/finish/pallas_call | solution.py:954
  (56 shorter events, 19.3 us)
Async XLA Ops:
  0.7 12.3 %collective-permute-start.2 = (bf16[4,64,512]{2,1,0:T(8,128)(2,1)}, bf16[4,64,512]{2,1,0:T(8,128)(2,1)S(1)}, u32[]{:S(2)}, u32[]{:S(2)}) collective-permute-start(bf16[4,64,512]{2,1,0:T(8,128)(2,1)} %refs_12_.5), channel_id=1, source_target_pairs={{0,1},{1,0},{2,3},{3,2},{4,5},{5,4},{6,7},{7,6},{8,9},{9,8},{10,11... | collective-permute-start | bytes 786440 | tf_op jit(solution)/shard_map/ppermute | solution.py:797
  4.7 16.0 %collective-permute-start.1 = (bf16[2,64,512]{2,1,0:T(8,128)(2,1)S(1)}, bf16[2,64,512]{2,1,0:T(8,128)(2,1)S(1)}, u32[]{:S(2)}, u32[]{:S(2)}) collective-permute-start(bf16[2,64,512]{2,1,0:T(8,128)(2,1)S(1)} %slice.3), channel_id=1, source_target_pairs={{0,3},{1,2},{2,1},{3,0},{4,7},{5,6},{6,5},{7,4},{8,11},{9,10},{10,... | collective-permute-start | bytes 393224 | tf_op jit(solution)/shard_map/ppermute | solution.py:797
  7.2 13.5 %collective-permute-start = (bf16[2,64,512]{2,1,0:T(8,128)(2,1)S(1)}, bf16[2,64,512]{2,1,0:T(8,128)(2,1)S(1)}, u32[]{:S(2)}, u32[]{:S(2)}) collective-permute-start(bf16[2,64,512]{2,1,0:T(8,128)(2,1)S(1)} %slice.3), channel_id=1, source_target_pairs={{0,2},{1,3},{2,0},{3,1},{4,6},{5,7},{6,4},{7,5},{8,10},{9,11},{10,... | collective-permute-start | bytes 393224 | tf_op jit(solution)/shard_map/ppermute | solution.py:797
  7.5 13.2 %copy-start.3 = (s32[4]{0:T(128)S(1)}, s32[4]{0:T(128)}, u32[]{:S(2)}) copy-start(s32[4]{0:T(128)} %length_ref.3) | copy-start | bytes 52
  15.7 12.4 %collective-permute-start.4 = (bf16[2,64,512]{2,1,0:T(8,128)(2,1)S(1)}, bf16[2,64,512]{2,1,0:T(8,128)(2,1)S(1)}, u32[]{:S(2)}, u32[]{:S(2)}) collective-permute-start(bf16[2,64,512]{2,1,0:T(8,128)(2,1)S(1)} %get-tuple-element.155), channel_id=1, source_target_pairs={{0,3},{1,2},{2,1},{3,0},{4,7},{5,6},{6,5},{7,4},{8,11},{9,10},{10,... | collective-permute-start | bytes 393224 | tf_op jit(solution)/shard_map/ppermute | solution.py:797
  20.7 9.5 %collective-permute-start.3 = (bf16[2,64,512]{2,1,0:T(8,128)(2,1)S(1)}, bf16[2,64,512]{2,1,0:T(8,128)(2,1)S(1)}, u32[]{:S(2)}, u32[]{:S(2)}) collective-permute-start(bf16[2,64,512]{2,1,0:T(8,128)(2,1)S(1)} %get-tuple-element.155), channel_id=1, source_target_pairs={{0,2},{1,3},{2,0},{3,1},{4,6},{5,7},{6,4},{7,5},{8,10},{9,11},{10,... | collective-permute-start | bytes 393224 | tf_op jit(solution)/shard_map/ppermute | solution.py:797
  28.1 9.5 %copy-start.1 = (bf16[2,256,512]{2,1,0:T(8,128)(2,1)}, bf16[2,256,512]{2,1,0:T(8,128)(2,1)S(1)}, u32[]{:S(2)}) copy-start(bf16[2,256,512]{2,1,0:T(8,128)(2,1)S(1)} %get-tuple-element.208.refs_1_) | copy-start | bytes 1572868
  30.2 7.4 %copy-start = (bf16[4,64,512]{2,1,0:T(8,128)(2,1)S(1)}, bf16[4,64,512]{2,1,0:T(8,128)(2,1)}, u32[]{:S(2)}) copy-start(bf16[4,64,512]{2,1,0:T(8,128)(2,1)} %refs_12_.5) | copy-start | bytes 786436
  45.1 5.5 %collective-permute-start.5 = (bf16[4,9,64,512]{3,2,1,0:T(8,128)(2,1)S(1)}, bf16[4,9,64,512]{3,2,1,0:T(8,128)(2,1)S(1)}, u32[]{:S(2)}, u32[]{:S(2)}) collective-permute-start(bf16[4,9,64,512]{3,2,1,0:T(8,128)(2,1)S(1)} %get-tuple-element.185), channel_id=1, source_target_pairs={{0,4},{4,0},{8,12},{12,8},{16,20},{20,16},{24,28},{28,24},{1,5},{5... | collective-permute-start | bytes 7077896 | tf_op jit(solution)/shard_map/ppermute | solution.py:797
  45.2 5.4 %collective-permute-start.6 = (f32[8,512]{1,0:T(8,128)S(1)}, f32[8,512]{1,0:T(8,128)S(1)}, u32[]{:S(2)}, u32[]{:S(2)}) collective-permute-start(f32[8,512]{1,0:T(8,128)S(1)} %get-tuple-element.186.refs_3_), channel_id=1, source_target_pairs={{0,4},{4,0},{8,12},{12,8},{16,20},{20,16},{24,28},{28,24},{1,5},{5... | collective-permute-start | bytes 49160 | tf_op jit(solution)/shard_map/ppermute | solution.py:797
  51.7 22.4 %collective-permute-start.12 = (bf16[1160,256]{1,0:T(8,128)(2,1)S(1)}, bf16[1160,256]{1,0:T(8,128)(2,1)S(1)}, u32[]{:S(2)}, u32[]{:S(2)}) collective-permute-start(bf16[1160,256]{1,0:T(8,128)(2,1)S(1)} %get-tuple-element.224), channel_id=1, source_target_pairs={{0,16},{4,20},{8,24},{12,28},{16,0},{20,4},{24,8},{28,12},{1,17},{... | collective-permute-start | bytes 1781768 | tf_op jit(solution)/shard_map/ppermute | solution.py:797
  53.3 20.8 %collective-permute-start.11 = (bf16[1160,256]{1,0:T(8,128)(2,1)S(1)}, bf16[1160,256]{1,0:T(8,128)(2,1)S(1)}, u32[]{:S(2)}, u32[]{:S(2)}) collective-permute-start(bf16[1160,256]{1,0:T(8,128)(2,1)S(1)} %get-tuple-element.187.refs_2_), channel_id=1, source_target_pairs={{0,8},{4,12},{8,0},{12,4},{16,24},{20,28},{24,16},{28,20},{1,9},{5... | collective-permute-start | bytes 1781768 | tf_op jit(solution)/shard_map/ppermute | solution.py:797
  59.7 7.8 %collective-permute-start.7 = (bf16[2,2,64,512]{3,2,1,0:T(8,128)(2,1)S(1)}, bf16[2,2,64,512]{3,2,1,0:T(8,128)(2,1)S(1)}, u32[]{:S(2)}, u32[]{:S(2)}) collective-permute-start(bf16[2,2,64,512]{3,2,1,0:T(8,128)(2,1)S(1)} %get-tuple-element.202), channel_id=1, source_target_pairs={{0,1},{1,0},{2,3},{3,2},{4,5},{5,4},{6,7},{7,6},{8,9},{9,8},{10,11... | collective-permute-start | bytes 786440 | tf_op jit(solution)/shard_map/ppermute | solution.py:797
  67.5 7.8 %collective-permute-start.10 = (bf16[2,64,512]{2,1,0:T(8,128)(2,1)S(1)}, bf16[2,64,512]{2,1,0:T(8,128)(2,1)S(1)}, u32[]{:S(2)}, u32[]{:S(2)}) collective-permute-start(bf16[2,64,512]{2,1,0:T(8,128)(2,1)S(1)} %cross_first.1.refs_2_), channel_id=1, source_target_pairs={{0,2},{1,3},{2,0},{3,1},{4,6},{5,7},{6,4},{7,5},{8,10},{9,11},{10,... | collective-permute-start | bytes 393224 | tf_op jit(solution)/shard_map/ppermute | solution.py:797
  69.0 6.2 %copy-start.2 = (bf16[2,256,512]{2,1,0:T(8,128)(2,1)S(1)}, bf16[2,256,512]{2,1,0:T(8,128)(2,1)}, u32[]{:S(2)}) copy-start(bf16[2,256,512]{2,1,0:T(8,128)(2,1)} %copy-done.1) | copy-start | bytes 1572868
  77.4 3.8 %collective-permute-start.13 = (bf16[4,3,64,512]{3,2,1,0:T(8,128)(2,1)S(1)}, bf16[4,3,64,512]{3,2,1,0:T(8,128)(2,1)S(1)}, u32[]{:S(2)}, u32[]{:S(2)}) collective-permute-start(bf16[4,3,64,512]{3,2,1,0:T(8,128)(2,1)S(1)} %get-tuple-element.228), channel_id=1, source_target_pairs={{0,4},{4,0},{8,12},{12,8},{16,20},{20,16},{24,28},{28,24},{1,5},{5... | collective-permute-start | bytes 2359304 | tf_op jit(solution)/shard_map/ppermute | solution.py:797
  77.5 9.9 %collective-permute-start.17 = (bf16[584,256]{1,0:T(8,128)(2,1)S(1)}, bf16[584,256]{1,0:T(8,128)(2,1)S(1)}, u32[]{:S(2)}, u32[]{:S(2)}) collective-permute-start(bf16[584,256]{1,0:T(8,128)(2,1)S(1)} %get-tuple-element.234), channel_id=1, source_target_pairs={{0,8},{4,12},{8,0},{12,4},{16,24},{20,28},{24,16},{28,20},{1,9},{5... | collective-permute-start | bytes 897032 | tf_op jit(solution)/shard_map/ppermute | solution.py:797
  78.1 9.3 %collective-permute-start.16 = (bf16[584,256]{1,0:T(8,128)(2,1)S(1)}, bf16[584,256]{1,0:T(8,128)(2,1)S(1)}, u32[]{:S(2)}, u32[]{:S(2)}) collective-permute-start(bf16[584,256]{1,0:T(8,128)(2,1)S(1)} %get-tuple-element.226.refs_16_), channel_id=1, source_target_pairs={{0,16},{4,20},{8,24},{12,28},{16,0},{20,4},{24,8},{28,12},{1,17},{... | collective-permute-start | bytes 897032 | tf_op jit(solution)/shard_map/ppermute | solution.py:797
  78.6 1.4 %collective-permute-start.14 = (f32[8,512]{1,0:T(8,128)S(1)}, f32[8,512]{1,0:T(8,128)S(1)}, u32[]{:S(2)}, u32[]{:S(2)}) collective-permute-start(f32[8,512]{1,0:T(8,128)S(1)} %get-tuple-element.229.refs_3_), channel_id=1, source_target_pairs={{0,4},{4,0},{8,12},{12,8},{16,20},{20,16},{24,28},{28,24},{1,5},{5... | collective-permute-start | bytes 49160 | tf_op jit(solution)/shard_map/ppermute | solution.py:797
  78.6 6.3 %collective-permute-start.8 = (bf16[2,1,64,512]{3,2,1,0:T(8,128)(2,1)S(1)}, bf16[2,1,64,512]{3,2,1,0:T(8,128)(2,1)S(1)}, u32[]{:S(2)}, u32[]{:S(2)}) collective-permute-start(bf16[2,1,64,512]{3,2,1,0:T(8,128)(2,1)S(1)} %get-tuple-element.204), channel_id=1, source_target_pairs={{0,1},{1,0},{2,3},{3,2},{4,5},{5,4},{6,7},{7,6},{8,9},{9,8},{10,11... | collective-permute-start | bytes 393224 | tf_op jit(solution)/shard_map/ppermute | solution.py:797
  80.0 7.3 %collective-permute-start.9 = (bf16[2,1,64,512]{3,2,1,0:T(8,128)(2,1)S(1)}, bf16[2,1,64,512]{3,2,1,0:T(8,128)(2,1)S(1)}, u32[]{:S(2)}, u32[]{:S(2)}) collective-permute-start(bf16[2,1,64,512]{3,2,1,0:T(8,128)(2,1)S(1)} %get-tuple-element.205), channel_id=1, source_target_pairs={{0,1},{1,0},{2,3},{3,2},{4,5},{5,4},{6,7},{7,6},{8,9},{9,8},{10,11... | collective-permute-start | bytes 393224 | tf_op jit(solution)/shard_map/ppermute | solution.py:797
  88.1 13.1 %collective-permute-start.18 = (bf16[304,512]{1,0:T(8,128)(2,1)S(1)}, bf16[304,512]{1,0:T(8,128)(2,1)S(1)}, u32[]{:S(2)}, u32[]{:S(2)}) collective-permute-start(bf16[304,512]{1,0:T(8,128)(2,1)S(1)} %get-tuple-element.237), channel_id=1, source_target_pairs={{0,1},{1,0},{2,3},{3,2},{4,5},{5,4},{6,7},{7,6},{8,9},{9,8},{10,11... | collective-permute-start | bytes 933896 | tf_op jit(solution)/shard_map/ppermute | solution.py:797
  89.6 6.3 %collective-permute-start.20 = (bf16[392,256]{1,0:T(8,128)(2,1)S(1)}, bf16[392,256]{1,0:T(8,128)(2,1)S(1)}, u32[]{:S(2)}, u32[]{:S(2)}) collective-permute-start(bf16[392,256]{1,0:T(8,128)(2,1)S(1)} %get-tuple-element.240), channel_id=1, source_target_pairs={{0,16},{4,20},{8,24},{12,28},{16,0},{20,4},{24,8},{28,12},{1,17},{... | collective-permute-start | bytes 602120 | tf_op jit(solution)/shard_map/ppermute | solution.py:797
  91.1 6.1 %collective-permute-start.19 = (bf16[392,256]{1,0:T(8,128)(2,1)S(1)}, bf16[392,256]{1,0:T(8,128)(2,1)S(1)}, u32[]{:S(2)}, u32[]{:S(2)}) collective-permute-start(bf16[392,256]{1,0:T(8,128)(2,1)S(1)} %get-tuple-element.230.refs_4_), channel_id=1, source_target_pairs={{0,8},{4,12},{8,0},{12,4},{16,24},{20,28},{24,16},{28,20},{1,9},{5... | collective-permute-start | bytes 602120 | tf_op jit(solution)/shard_map/ppermute | solution.py:797
  92.6 8.7 %collective-permute-start.15 = (bf16[2,64,512]{2,1,0:T(8,128)(2,1)S(1)}, bf16[2,64,512]{2,1,0:T(8,128)(2,1)S(1)}, u32[]{:S(2)}, u32[]{:S(2)}) collective-permute-start(bf16[2,64,512]{2,1,0:T(8,128)(2,1)S(1)} %cross_second.1.refs_6_), channel_id=1, source_target_pairs={{0,2},{1,3},{2,0},{3,1},{4,6},{5,7},{6,4},{7,5},{8,10},{9,11},{10,... | collective-permute-start | bytes 393224 | tf_op jit(solution)/shard_map/ppermute | solution.py:797
  97.8 5.2 %collective-permute-start.23 = (bf16[200,256]{1,0:T(8,128)(2,1)S(1)}, bf16[200,256]{1,0:T(8,128)(2,1)S(1)}, u32[]{:S(2)}, u32[]{:S(2)}) collective-permute-start(bf16[200,256]{1,0:T(8,128)(2,1)S(1)} %get-tuple-element.245), channel_id=1, source_target_pairs={{0,8},{4,12},{8,0},{12,4},{16,24},{20,28},{24,16},{28,20},{1,9},{5... | collective-permute-start | bytes 307208 | tf_op jit(solution)/shard_map/ppermute | solution.py:797
  99.3 4.7 %collective-permute-start.22 = (bf16[200,256]{1,0:T(8,128)(2,1)S(1)}, bf16[200,256]{1,0:T(8,128)(2,1)S(1)}, u32[]{:S(2)}, u32[]{:S(2)}) collective-permute-start(bf16[200,256]{1,0:T(8,128)(2,1)S(1)} %get-tuple-element.242.refs_3_), channel_id=1, source_target_pairs={{0,16},{4,20},{8,24},{12,28},{16,0},{20,4},{24,8},{28,12},{1,17},{... | collective-permute-start | bytes 307208 | tf_op jit(solution)/shard_map/ppermute | solution.py:797
  101.9 14.1 %collective-permute-start.21 = (bf16[304,512]{1,0:T(8,128)(2,1)S(1)}, bf16[304,512]{1,0:T(8,128)(2,1)S(1)}, u32[]{:S(2)}, u32[]{:S(2)}) collective-permute-start(bf16[304,512]{1,0:T(8,128)(2,1)S(1)} %dense_near_sum.1.refs_0_), channel_id=1, source_target_pairs={{0,2},{1,3},{2,0},{3,1},{4,6},{5,7},{6,4},{7,5},{8,10},{9,11},{10,... | collective-permute-start | bytes 933896 | tf_op jit(solution)/shard_map/ppermute | solution.py:797
  104.0 9.5 %collective-permute-start.24 = (bf16[224,512]{1,0:T(8,128)(2,1)S(1)}, bf16[224,512]{1,0:T(8,128)(2,1)S(1)}, u32[]{:S(2)}, u32[]{:S(2)}) collective-permute-start(bf16[224,512]{1,0:T(8,128)(2,1)S(1)} %tail_sum_second.1.refs_0_), channel_id=1, source_target_pairs={{0,1},{1,0},{2,3},{3,2},{4,5},{5,4},{6,7},{7,6},{8,9},{9,8},{10,11... | collective-permute-start | bytes 688136 | tf_op jit(solution)/shard_map/ppermute | solution.py:797
  116.1 12.5 %collective-permute-start.26 = (bf16[304,512]{1,0:T(8,128)(2,1)S(1)}, bf16[304,512]{1,0:T(8,128)(2,1)S(1)}, u32[]{:S(2)}, u32[]{:S(2)}) collective-permute-start(bf16[304,512]{1,0:T(8,128)(2,1)S(1)} %dense_far_sum.1.refs_16_.refs_0_.refs_3_), channel_id=1, source_target_pairs={{0,1},{1,0},{2,3},{3,2},{4,5},{5,4},{6,7},{7,6},{8,9},{9,8},{10,11... | collective-permute-start | bytes 933896 | tf_op jit(solution)/shard_map/ppermute | solution.py:797
  116.3 11.1 %collective-permute-start.25 = (bf16[224,512]{1,0:T(8,128)(2,1)S(1)}, bf16[224,512]{1,0:T(8,128)(2,1)S(1)}, u32[]{:S(2)}, u32[]{:S(2)}) collective-permute-start(bf16[224,512]{1,0:T(8,128)(2,1)S(1)} %tail_near_sum.1.refs_2_.refs_1_), channel_id=1, source_target_pairs={{0,2},{1,3},{2,0},{3,1},{4,6},{5,7},{6,4},{7,5},{8,10},{9,11},{10,... | collective-permute-start | bytes 688136 | tf_op jit(solution)/shard_map/ppermute | solution.py:797
